TPU v7x, 512 devices: a whole 4x4x16 slice. The times are simulated.
512 devices in a mesh: chan: 64 (over y, x, z_hi, core), freq: 8 (over z_lo).
Axes of the slice: x: 4, y: 4, z: 16 (z_hi: 2, z_lo: 8; z = z_hi * 8 + z_lo), core: 2. Of those that a mesh axis runs over, the one named last changes fastest.
Arguments:
- spectra: bfloat16 [256, 2, 16, 8192], P('freq', None, None, 'chan'), may hold values from -20 to 20
- model: bfloat16 [256, 2, 8, 8192], P('freq', None, None, 'chan'), may hold values from -6 to 6
- channel_ok: int32 [8192], replicated, may hold values 0 or 1
- limits: int32 [64], replicated, may hold values from 128 to 1024, as said below
Outputs:
- adjoint: float32 [256, 2, 16, 8192], P('freq', None, None, 'chan')
- misfit: float32 [], replicated
Inputs may be any that keep to these rules, and one draw needn't show every extreme that they name: `limits`: one block has the limit 128 and another the limit 1024.
All inputs are finite; a program needn't handle non-finite values.
Results may differ from a plain program's by a relative error of at most 0.00053.
Values may be sent and summed in bfloat16 or wider, within the bound.
A program may use at most 64 MiB of HBM per device.

v0:
```python
import jax
import jax.numpy as jnp
from jax import lax
from jax.sharding import PartitionSpec as P

F = 256
W = 16
BAND = 1024


def shifted(x, axis, by):
    peers = lax.axis_size(axis)
    return lax.ppermute(x, axis, [(i, (i + by) % peers) for i in range(peers)])


def pair_terms(first_block, second_block, ok_first, ok_second, limit_first, shift_blocks):
    bin_count = first_block.shape[0]
    row_count = first_block.shape[2]
    block_width = first_block.shape[3]
    row_scale = jnp.concatenate(
        [jnp.full((W,), 1.0 / W, jnp.float32), jnp.full((row_count - W,), -1.0, jnp.float32)]
    ).astype(jnp.bfloat16)
    scaled = first_block * row_scale[None, None, :, None]
    stacked_left = jnp.stack(
        [
            scaled.reshape(bin_count, 2 * row_count, block_width),
            jnp.concatenate([scaled[:, 1], -scaled[:, 0]], axis=1),
        ],
        axis=0,
    )
    right_rows = second_block.reshape(bin_count, 2 * row_count, block_width)
    cross_spec = jnp.einsum(
        "xfrc,frd->xfcd", stacked_left, right_rows, preferred_element_type=jnp.float32
    )
    row_index = lax.broadcasted_iota(jnp.int32, (block_width, block_width), 0)
    col_index = lax.broadcasted_iota(jnp.int32, (block_width, block_width), 1)
    offset = shift_blocks * block_width + col_index - row_index
    inside = ((offset >= 1) & (offset <= limit_first)).astype(jnp.float32)
    live_mask = ok_first[:, None] * ok_second[None, :] * inside
    residual = cross_spec * live_mask[None, None]
    piece_loss = 0.5 * jnp.sum(residual * residual)
    rounded = residual.astype(jnp.bfloat16)
    far_spec = second_block[:, :, :W].reshape(bin_count, 2 * W, block_width)
    near_spec = first_block[:, :, :W].reshape(bin_count, 2 * W, block_width)
    toward = jnp.einsum("xfcd,fvd->xfvc", rounded, far_spec, preferred_element_type=jnp.float32)
    first_real = toward[0, :, :W] - toward[1, :, W:]
    first_imag = toward[0, :, W:] + toward[1, :, :W]
    backward = jnp.einsum("xfcd,fvc->xfvd", rounded, near_spec, preferred_element_type=jnp.float32)
    second_real = backward[0, :, :W] + backward[1, :, W:]
    second_imag = backward[0, :, W:] - backward[1, :, :W]
    return (
        piece_loss,
        jnp.stack([first_real, first_imag], axis=1),
        jnp.stack([second_real, second_imag], axis=1),
    )


def shards(spectra, model, channel_ok, limits):
    payload = jnp.concatenate([spectra, model], axis=2)
    block_width = spectra.shape[3]
    band_blocks = BAND // block_width
    block_total = lax.axis_size("chan")
    block_index = lax.axis_index("chan")
    ok_all = channel_ok.astype(jnp.float32)

    def flags_of(move):
        start = (block_index + move) % block_total * block_width
        return lax.dynamic_slice_in_dim(ok_all, start, block_width)

    ok_own = flags_of(0)
    limit_own = lax.dynamic_index_in_dim(limits, block_index % block_total, keepdims=False)
    misfit_sum, near_terms, far_terms = pair_terms(payload, payload, ok_own, ok_own, limit_own, 0)
    adjoint_acc = near_terms + far_terms
    for s in range(1, band_blocks + 1):
        ahead_block = shifted(payload, "chan", -s)
        piece_loss, near_terms, far_terms = pair_terms(
            payload, ahead_block, ok_own, flags_of(s), limit_own, s
        )
        misfit_sum = misfit_sum + piece_loss
        adjoint_acc = adjoint_acc + near_terms
        adjoint_acc = adjoint_acc + shifted(far_terms, "chan", s)
    misfit_total = lax.psum(misfit_sum, ("chan", "freq"))
    misfit = misfit_total / float(F * block_width * block_total * BAND)
    return (adjoint_acc * (1.0 / W), misfit)


def solution(mesh):
    return jax.shard_map(
        shards,
        mesh=mesh,
        in_specs=(P("freq", None, None, "chan"), P("freq", None, None, "chan"), P(), P()),
        out_specs=(P("freq", None, None, "chan"), P()),
        check_vma=False,
    )
```

profile of v0, /device:TPU:1, one launch (start us, length us, event | category | flops | bytes accessed | tf_op | source)
XLA Modules:
  0.0 475.2 jit_solution(15571919331790536662)
XLA Ops:
  4.0 7.9 %collective-permute-start.14 = (bf16[32,2,24,128]{3,2,0,1:T(8,128)(2,1)}, bf16[32,2,24,128]{3,2,0,1:T(8,128)(2,1)S(1)}, u32[]{:S(2)}, u32[]{:S(2)}) collective-permute-start(bf16[32,2,24,128]{3,2,0,1:T(8,128)(2,1)} %get-tuple-element.61), channel_id=1, source_target_pairs={{0,448},{8,456},{16,464},{24,472},{32,480},{40,488},{48,496},{56,5... | collective-permute-start | bytes 1179656 | tf_op jit(solution)/shard_map/ppermute | solution.py:13
  12.0 16.2 %collective-permute-start.12 = (bf16[32,2,24,128]{3,2,0,1:T(8,128)(2,1)}, bf16[32,2,24,128]{3,2,0,1:T(8,128)(2,1)S(1)}, u32[]{:S(2)}, u32[]{:S(2)}) collective-permute-start(bf16[32,2,24,128]{3,2,0,1:T(8,128)(2,1)} %get-tuple-element.61), channel_id=1, source_target_pairs={{0,456},{8,464},{16,472},{24,480},{32,488},{40,496},{48,504},{56,0... | collective-permute-start | bytes 1179656 | tf_op jit(solution)/shard_map/ppermute | solution.py:13
  28.2 1.9 collective-permute-start.10
  30.1 5.4 %collective-permute-start.8 = (bf16[32,2,24,128]{3,2,0,1:T(8,128)(2,1)}, bf16[32,2,24,128]{3,2,0,1:T(8,128)(2,1)S(1)}, u32[]{:S(2)}, u32[]{:S(2)}) collective-permute-start(bf16[32,2,24,128]{3,2,0,1:T(8,128)(2,1)} %get-tuple-element.61), channel_id=1, source_target_pairs={{0,472},{8,480},{16,488},{24,496},{32,504},{40,0},{48,8},{56,16},{... | collective-permute-start | bytes 1179656 | tf_op jit(solution)/shard_map/ppermute | solution.py:13
  35.5 1.9 collective-permute-start.6
  39.7 1.9 multiply_reduce_fusion.8
  43.6 12.0 %collective-permute-start.4 = (bf16[32,2,24,128]{3,2,0,1:T(8,128)(2,1)}, bf16[32,2,24,128]{3,2,0,1:T(8,128)(2,1)S(1)}, u32[]{:S(2)}, u32[]{:S(2)}) collective-permute-start(bf16[32,2,24,128]{3,2,0,1:T(8,128)(2,1)} %get-tuple-element.61), channel_id=1, source_target_pairs={{0,488},{8,496},{16,504},{24,0},{32,8},{40,16},{48,24},{56,32},{64... | collective-permute-start | bytes 1179656 | tf_op jit(solution)/shard_map/ppermute | solution.py:13
  55.7 1.9 multiply_reduce_fusion
  59.8 14.1 %collective-permute-start.2 = (bf16[32,2,24,128]{3,2,0,1:T(8,128)(2,1)}, bf16[32,2,24,128]{3,2,0,1:T(8,128)(2,1)S(1)}, u32[]{:S(2)}, u32[]{:S(2)}) collective-permute-start(bf16[32,2,24,128]{3,2,0,1:T(8,128)(2,1)} %get-tuple-element.61), channel_id=1, source_target_pairs={{0,496},{8,504},{16,0},{24,8},{32,16},{40,24},{48,32},{56,40},{64,... | collective-permute-start | bytes 1179656 | tf_op jit(solution)/shard_map/ppermute | solution.py:13
  73.9 2.0 multiply_reduce_fusion.1
  78.1 1.9 collective-permute-start
  80.1 2.0 multiply_reduce_fusion.2
  85.2 25.0 %collective-permute-start.15 = (f32[32,2,16,128]{3,2,0,1:T(8,128)}, f32[32,2,16,128]{3,2,0,1:T(8,128)}, u32[]{:S(2)}, u32[]{:S(2)}) collective-permute-start(f32[32,2,16,128]{3,2,0,1:T(8,128)} %pad_maximum_fusion.8), channel_id=1, source_target_pairs={{0,64},{8,72},{16,80},{24,88},{32,96},{40,104},{48,112},{56,120},{... | collective-permute-start | bytes 1572872 | tf_op jit(solution)/shard_map/ppermute | solution.py:13
  110.2 2.0 multiply_reduce_fusion.3
  115.2 3.5 collective-permute-start.13
  118.8 2.0 multiply_reduce_fusion.4
  123.8 46.2 %collective-permute-start.11 = (f32[32,2,16,128]{3,2,0,1:T(8,128)}, f32[32,2,16,128]{3,2,0,1:T(8,128)}, u32[]{:S(2)}, u32[]{:S(2)}) collective-permute-start(f32[32,2,16,128]{3,2,0,1:T(8,128)} %pad_maximum_fusion.6), channel_id=1, source_target_pairs={{0,48},{8,56},{16,64},{24,72},{32,80},{40,88},{48,96},{56,104},{64... | collective-permute-start | bytes 1572872 | tf_op jit(solution)/shard_map/ppermute | solution.py:13
  170.1 1.9 multiply_reduce_fusion.5
  175.1 1.9 collective-permute-start.9
  177.0 1.9 multiply_reduce_fusion.6
  183.1 23.0 %collective-permute-start.7 = (f32[32,2,16,128]{3,2,0,1:T(8,128)}, f32[32,2,16,128]{3,2,0,1:T(8,128)}, u32[]{:S(2)}, u32[]{:S(2)}) collective-permute-start(f32[32,2,16,128]{3,2,0,1:T(8,128)} %pad_maximum_fusion.4), channel_id=1, source_target_pairs={{0,32},{8,40},{16,48},{24,56},{32,64},{40,72},{48,80},{56,88},{64,... | collective-permute-start | bytes 1572872 | tf_op jit(solution)/shard_map/ppermute | solution.py:13
  206.1 2.0 multiply_reduce_fusion.7
  216.3 150.5 %psum.7 = f32[]{:T(128)} all-reduce(f32[]{:T(128)S(6)} %add.578), channel_id=1, replica_groups=mesh['chan'=64,'freq'=8] {'chan','freq'}, use_global_device_ids=true, to_apply=%region_9.10 | all-reduce | flops 1 | bytes 8 | tf_op jit(solution)/shard_map/psum | solution.py:82
  366.8 1.9 pad_maximum_fusion.3
  368.7 1.9 pad_maximum_fusion.2
  372.2 1.5 fusion.49
  373.8 2.4 collective-permute-start.5
  376.2 10.2 %collective-permute-start.3 = (f32[32,2,16,128]{3,2,0,1:T(8,128)S(1)}, f32[32,2,16,128]{3,2,0,1:T(8,128)S(1)}, u32[]{:S(2)}, u32[]{:S(2)}) collective-permute-start(f32[32,2,16,128]{3,2,0,1:T(8,128)S(1)} %copy-done.19), channel_id=1, source_target_pairs={{0,16},{8,24},{16,32},{24,40},{32,48},{40,56},{48,64},{56,72},{64,... | collective-permute-start | bytes 1572872 | tf_op jit(solution)/shard_map/ppermute | solution.py:13
  386.4 11.8 %collective-permute-start.1 = (f32[32,2,16,128]{3,2,0,1:T(8,128)S(1)}, f32[32,2,16,128]{3,2,0,1:T(8,128)S(1)}, u32[]{:S(2)}, u32[]{:S(2)}) collective-permute-start(f32[32,2,16,128]{3,2,0,1:T(8,128)S(1)} %copy-done.20), channel_id=1, source_target_pairs={{0,8},{8,16},{16,24},{24,32},{32,40},{40,48},{48,56},{56,64},{64,7... | collective-permute-start | bytes 1572872 | tf_op jit(solution)/shard_map/ppermute | solution.py:13
  398.9 30.2 %collective-permute-done.5 = f32[32,2,16,128]{3,2,0,1:T(8,128)S(1)} collective-permute-done((f32[32,2,16,128]{3,2,0,1:T(8,128)S(1)}, f32[32,2,16,128]{3,2,0,1:T(8,128)S(1)}, u32[]{:S(2)}, u32[]{:S(2)}) %collective-permute-start.5) | collective-permute-done | bytes 524320 | tf_op jit(solution)/shard_map/ppermute | solution.py:13
  429.3 41.5 %collective-permute-done.1 = f32[32,2,16,128]{3,2,0,1:T(8,128)S(1)} collective-permute-done((f32[32,2,16,128]{3,2,0,1:T(8,128)S(1)}, f32[32,2,16,128]{3,2,0,1:T(8,128)S(1)}, u32[]{:S(2)}, u32[]{:S(2)}) %collective-permute-start.1) | collective-permute-done | bytes 524320 | tf_op jit(solution)/shard_map/ppermute | solution.py:13
  470.9 2.3 fusion.110
  (145 shorter events, 33.5 us)
Async XLA Ops:
  0.6 37.1 %copy-start.22 = (bf16[24]{0:T(256)(128)(2,1)S(1)}, bf16[24]{0:T(256)(128)(2,1)}, u32[]{:S(2)}) copy-start(bf16[24]{0:T(256)(128)(2,1)} %constant.88.clone.1) | copy-start | bytes 148
  0.6 37.0 %copy-start.21 = (s32[8192]{0:T(1024)S(1)}, s32[8192]{0:T(1024)}, u32[]{:S(2)}) copy-start(s32[8192]{0:T(1024)} %param.6) | copy-start | bytes 98308
  0.7 37.1 %copy-start.23 = (s32[64]{0:T(128)S(1)}, s32[64]{0:T(128)}, u32[]{:S(2)}) copy-start(s32[64]{0:T(128)} %param.7) | copy-start | bytes 772
  4.0 39.6 %collective-permute-start.14 = (bf16[32,2,24,128]{3,2,0,1:T(8,128)(2,1)}, bf16[32,2,24,128]{3,2,0,1:T(8,128)(2,1)S(1)}, u32[]{:S(2)}, u32[]{:S(2)}) collective-permute-start(bf16[32,2,24,128]{3,2,0,1:T(8,128)(2,1)} %get-tuple-element.61), channel_id=1, source_target_pairs={{0,448},{8,456},{16,464},{24,472},{32,480},{40,488},{48,496},{56,5... | collective-permute-start | bytes 1179656 | tf_op jit(solution)/shard_map/ppermute | solution.py:13
  12.0 47.8 %collective-permute-start.12 = (bf16[32,2,24,128]{3,2,0,1:T(8,128)(2,1)}, bf16[32,2,24,128]{3,2,0,1:T(8,128)(2,1)S(1)}, u32[]{:S(2)}, u32[]{:S(2)}) collective-permute-start(bf16[32,2,24,128]{3,2,0,1:T(8,128)(2,1)} %get-tuple-element.61), channel_id=1, source_target_pairs={{0,456},{8,464},{16,472},{24,480},{32,488},{40,496},{48,504},{56,0... | collective-permute-start | bytes 1179656 | tf_op jit(solution)/shard_map/ppermute | solution.py:13
  28.2 50.0 %collective-permute-start.10 = (bf16[32,2,24,128]{3,2,0,1:T(8,128)(2,1)}, bf16[32,2,24,128]{3,2,0,1:T(8,128)(2,1)S(1)}, u32[]{:S(2)}, u32[]{:S(2)}) collective-permute-start(bf16[32,2,24,128]{3,2,0,1:T(8,128)(2,1)} %get-tuple-element.61), channel_id=1, source_target_pairs={{0,464},{8,472},{16,480},{24,488},{32,496},{40,504},{48,0},{56,8},... | collective-permute-start | bytes 1179656 | tf_op jit(solution)/shard_map/ppermute | solution.py:13
  30.1 55.0 %collective-permute-start.8 = (bf16[32,2,24,128]{3,2,0,1:T(8,128)(2,1)}, bf16[32,2,24,128]{3,2,0,1:T(8,128)(2,1)S(1)}, u32[]{:S(2)}, u32[]{:S(2)}) collective-permute-start(bf16[32,2,24,128]{3,2,0,1:T(8,128)(2,1)} %get-tuple-element.61), channel_id=1, source_target_pairs={{0,472},{8,480},{16,488},{24,496},{32,504},{40,0},{48,8},{56,16},{... | collective-permute-start | bytes 1179656 | tf_op jit(solution)/shard_map/ppermute | solution.py:13
  35.5 79.7 %collective-permute-start.6 = (bf16[32,2,24,128]{3,2,0,1:T(8,128)(2,1)}, bf16[32,2,24,128]{3,2,0,1:T(8,128)(2,1)S(1)}, u32[]{:S(2)}, u32[]{:S(2)}) collective-permute-start(bf16[32,2,24,128]{3,2,0,1:T(8,128)(2,1)} %get-tuple-element.61), channel_id=1, source_target_pairs={{0,480},{8,488},{16,496},{24,504},{32,0},{40,8},{48,16},{56,24},{6... | collective-permute-start | bytes 1179656 | tf_op jit(solution)/shard_map/ppermute | solution.py:13
  43.6 80.1 %collective-permute-start.4 = (bf16[32,2,24,128]{3,2,0,1:T(8,128)(2,1)}, bf16[32,2,24,128]{3,2,0,1:T(8,128)(2,1)S(1)}, u32[]{:S(2)}, u32[]{:S(2)}) collective-permute-start(bf16[32,2,24,128]{3,2,0,1:T(8,128)(2,1)} %get-tuple-element.61), channel_id=1, source_target_pairs={{0,488},{8,496},{16,504},{24,0},{32,8},{40,16},{48,24},{56,32},{64... | collective-permute-start | bytes 1179656 | tf_op jit(solution)/shard_map/ppermute | solution.py:13
  59.8 115.3 %collective-permute-start.2 = (bf16[32,2,24,128]{3,2,0,1:T(8,128)(2,1)}, bf16[32,2,24,128]{3,2,0,1:T(8,128)(2,1)S(1)}, u32[]{:S(2)}, u32[]{:S(2)}) collective-permute-start(bf16[32,2,24,128]{3,2,0,1:T(8,128)(2,1)} %get-tuple-element.61), channel_id=1, source_target_pairs={{0,496},{8,504},{16,0},{24,8},{32,16},{40,24},{48,32},{56,40},{64,... | collective-permute-start | bytes 1179656 | tf_op jit(solution)/shard_map/ppermute | solution.py:13
  78.1 104.9 %collective-permute-start = (bf16[32,2,24,128]{3,2,0,1:T(8,128)(2,1)}, bf16[32,2,24,128]{3,2,0,1:T(8,128)(2,1)S(1)}, u32[]{:S(2)}, u32[]{:S(2)}) collective-permute-start(bf16[32,2,24,128]{3,2,0,1:T(8,128)(2,1)} %get-tuple-element.61), channel_id=1, source_target_pairs={{0,504},{8,0},{16,8},{24,16},{32,24},{40,32},{48,40},{56,48},{64,5... | collective-permute-start | bytes 1179656 | tf_op jit(solution)/shard_map/ppermute | solution.py:13
  85.2 288.6 %collective-permute-start.15 = (f32[32,2,16,128]{3,2,0,1:T(8,128)}, f32[32,2,16,128]{3,2,0,1:T(8,128)}, u32[]{:S(2)}, u32[]{:S(2)}) collective-permute-start(f32[32,2,16,128]{3,2,0,1:T(8,128)} %pad_maximum_fusion.8), channel_id=1, source_target_pairs={{0,64},{8,72},{16,80},{24,88},{32,96},{40,104},{48,112},{56,120},{... | collective-permute-start | bytes 1572872 | tf_op jit(solution)/shard_map/ppermute | solution.py:13
  115.2 261.0 %collective-permute-start.13 = (f32[32,2,16,128]{3,2,0,1:T(8,128)}, f32[32,2,16,128]{3,2,0,1:T(8,128)}, u32[]{:S(2)}, u32[]{:S(2)}) collective-permute-start(f32[32,2,16,128]{3,2,0,1:T(8,128)} %pad_maximum_fusion.7), channel_id=1, source_target_pairs={{0,56},{8,64},{16,72},{24,80},{32,88},{40,96},{48,104},{56,112},{6... | collective-permute-start | bytes 1572872 | tf_op jit(solution)/shard_map/ppermute | solution.py:13
  123.8 262.6 %collective-permute-start.11 = (f32[32,2,16,128]{3,2,0,1:T(8,128)}, f32[32,2,16,128]{3,2,0,1:T(8,128)}, u32[]{:S(2)}, u32[]{:S(2)}) collective-permute-start(f32[32,2,16,128]{3,2,0,1:T(8,128)} %pad_maximum_fusion.6), channel_id=1, source_target_pairs={{0,48},{8,56},{16,64},{24,72},{32,80},{40,88},{48,96},{56,104},{64... | collective-permute-start | bytes 1572872 | tf_op jit(solution)/shard_map/ppermute | solution.py:13
  175.1 223.8 %collective-permute-start.9 = (f32[32,2,16,128]{3,2,0,1:T(8,128)}, f32[32,2,16,128]{3,2,0,1:T(8,128)}, u32[]{:S(2)}, u32[]{:S(2)}) collective-permute-start(f32[32,2,16,128]{3,2,0,1:T(8,128)} %pad_maximum_fusion.5), channel_id=1, source_target_pairs={{0,40},{8,48},{16,56},{24,64},{32,72},{40,80},{48,88},{56,96},{64,... | collective-permute-start | bytes 1572872 | tf_op jit(solution)/shard_map/ppermute | solution.py:13
  183.1 215.8 %collective-permute-start.7 = (f32[32,2,16,128]{3,2,0,1:T(8,128)}, f32[32,2,16,128]{3,2,0,1:T(8,128)}, u32[]{:S(2)}, u32[]{:S(2)}) collective-permute-start(f32[32,2,16,128]{3,2,0,1:T(8,128)} %pad_maximum_fusion.4), channel_id=1, source_target_pairs={{0,32},{8,40},{16,48},{24,56},{32,64},{40,72},{48,80},{56,88},{64,... | collective-permute-start | bytes 1572872 | tf_op jit(solution)/shard_map/ppermute | solution.py:13
  215.5 155.1 %copy-start.15 = (f32[32,1,16,128]{3,2,0,1:T(8,128)S(1)}, f32[32,1,16,128]{3,2,0,1:T(8,128)}, u32[]{:S(2)}) copy-start(f32[32,1,16,128]{3,2,0,1:T(8,128)} %get-tuple-element.28) | copy-start | bytes 786436
  373.8 55.3 %collective-permute-start.5 = (f32[32,2,16,128]{3,2,0,1:T(8,128)S(1)}, f32[32,2,16,128]{3,2,0,1:T(8,128)S(1)}, u32[]{:S(2)}, u32[]{:S(2)}) collective-permute-start(f32[32,2,16,128]{3,2,0,1:T(8,128)S(1)} %copy-done.18), channel_id=1, source_target_pairs={{0,24},{8,32},{16,40},{24,48},{32,56},{40,64},{48,72},{56,80},{64,... | collective-permute-start | bytes 1572872 | tf_op jit(solution)/shard_map/ppermute | solution.py:13
  376.2 53.1 %collective-permute-start.3 = (f32[32,2,16,128]{3,2,0,1:T(8,128)S(1)}, f32[32,2,16,128]{3,2,0,1:T(8,128)S(1)}, u32[]{:S(2)}, u32[]{:S(2)}) collective-permute-start(f32[32,2,16,128]{3,2,0,1:T(8,128)S(1)} %copy-done.19), channel_id=1, source_target_pairs={{0,16},{8,24},{16,32},{24,40},{32,48},{40,56},{48,64},{56,72},{64,... | collective-permute-start | bytes 1572872 | tf_op jit(solution)/shard_map/ppermute | solution.py:13
  386.4 84.4 %collective-permute-start.1 = (f32[32,2,16,128]{3,2,0,1:T(8,128)S(1)}, f32[32,2,16,128]{3,2,0,1:T(8,128)S(1)}, u32[]{:S(2)}, u32[]{:S(2)}) collective-permute-start(f32[32,2,16,128]{3,2,0,1:T(8,128)S(1)} %copy-done.20), channel_id=1, source_target_pairs={{0,8},{8,16},{16,24},{24,32},{32,40},{40,48},{48,56},{56,64},{64,7... | collective-permute-start | bytes 1572872 | tf_op jit(solution)/shard_map/ppermute | solution.py:13
  398.3 72.5 %copy-start.3 = (f32[32,1,16,128]{3,2,0,1:T(8,128)S(1)}, f32[32,1,16,128]{3,2,0,1:T(8,128)}, u32[]{:S(2)}) copy-start(f32[32,1,16,128]{3,2,0,1:T(8,128)} %get-tuple-element.25) | copy-start | bytes 786436
  398.3 72.5 %copy-start.4 = (f32[32,1,16,128]{3,2,0,1:T(8,128)S(1)}, f32[32,1,16,128]{3,2,0,1:T(8,128)}, u32[]{:S(2)}) copy-start(f32[32,1,16,128]{3,2,0,1:T(8,128)} %get-tuple-element.55) | copy-start | bytes 786436
  398.3 72.5 %copy-start.5 = (f32[32,1,16,128]{3,2,0,1:T(8,128)S(1)}, f32[32,1,16,128]{3,2,0,1:T(8,128)}, u32[]{:S(2)}) copy-start(f32[32,1,16,128]{3,2,0,1:T(8,128)} %get-tuple-element.50) | copy-start | bytes 786436
  398.3 72.5 %copy-start.6 = (f32[32,1,16,128]{3,2,0,1:T(8,128)S(1)}, f32[32,1,16,128]{3,2,0,1:T(8,128)}, u32[]{:S(2)}) copy-start(f32[32,1,16,128]{3,2,0,1:T(8,128)} %get-tuple-element.51) | copy-start | bytes 786436
  398.3 72.5 %copy-start.7 = (f32[32,1,16,128]{3,2,0,1:T(8,128)S(1)}, f32[32,1,16,128]{3,2,0,1:T(8,128)}, u32[]{:S(2)}) copy-start(f32[32,1,16,128]{3,2,0,1:T(8,128)} %get-tuple-element.46) | copy-start | bytes 786436
  398.3 72.5 %copy-start.8 = (f32[32,1,16,128]{3,2,0,1:T(8,128)S(1)}, f32[32,1,16,128]{3,2,0,1:T(8,128)}, u32[]{:S(2)}) copy-start(f32[32,1,16,128]{3,2,0,1:T(8,128)} %get-tuple-element.47) | copy-start | bytes 786436
  398.3 72.5 %copy-start.9 = (f32[32,1,16,128]{3,2,0,1:T(8,128)S(1)}, f32[32,1,16,128]{3,2,0,1:T(8,128)}, u32[]{:S(2)}) copy-start(f32[32,1,16,128]{3,2,0,1:T(8,128)} %get-tuple-element.42) | copy-start | bytes 786436
  398.3 72.5 %copy-start.10 = (f32[32,1,16,128]{3,2,0,1:T(8,128)S(1)}, f32[32,1,16,128]{3,2,0,1:T(8,128)}, u32[]{:S(2)}) copy-start(f32[32,1,16,128]{3,2,0,1:T(8,128)} %get-tuple-element.43) | copy-start | bytes 786436
  398.4 72.5 %copy-start.11 = (f32[32,1,16,128]{3,2,0,1:T(8,128)S(1)}, f32[32,1,16,128]{3,2,0,1:T(8,128)}, u32[]{:S(2)}) copy-start(f32[32,1,16,128]{3,2,0,1:T(8,128)} %get-tuple-element.38) | copy-start | bytes 786436
  398.4 72.5 %copy-start.12 = (f32[32,1,16,128]{3,2,0,1:T(8,128)S(1)}, f32[32,1,16,128]{3,2,0,1:T(8,128)}, u32[]{:S(2)}) copy-start(f32[32,1,16,128]{3,2,0,1:T(8,128)} %get-tuple-element.39) | copy-start | bytes 786436
  398.4 72.5 %copy-start.13 = (f32[32,1,16,128]{3,2,0,1:T(8,128)S(1)}, f32[32,1,16,128]{3,2,0,1:T(8,128)}, u32[]{:S(2)}) copy-start(f32[32,1,16,128]{3,2,0,1:T(8,128)} %get-tuple-element.34) | copy-start | bytes 786436
  398.4 72.5 %copy-start.14 = (f32[32,1,16,128]{3,2,0,1:T(8,128)S(1)}, f32[32,1,16,128]{3,2,0,1:T(8,128)}, u32[]{:S(2)}) copy-start(f32[32,1,16,128]{3,2,0,1:T(8,128)} %get-tuple-element.35) | copy-start | bytes 786436
  (8 other events, 79.6 us)
where the time goes:
time: 483 us; the launch traced here: 475 us
  starting transfers between devices  185 us (38%)
  blocking collectives  151 us (31%)
  waiting for transfers between devices  71.9 us (15%)
  matrix products  29.5 us (6%)
  other arithmetic  23 us (5%)
  between operations  9.07 us (2%)
  local copies, waits for them, and re-layouts  5.73 us (1%)
    ppermute x16, starting transfers between devices, shifted(): return lax.ppermute(x, axis, [(i, (i + by) % peers) for i in range(peers)])  185 us
    psum x1, blocking collectives, shards(): misfit_total = lax.psum(misfit_sum, ('chan', 'freq'))  151 us
    ppermute x16, waiting for transfers between devices, shifted(): return lax.ppermute(x, axis, [(i, (i + by) % peers) for i in range(peers)])  71.9 us
    dot_general x9, matrix products, pair_terms(): jnp.einsum('xfrc,frd->xfcd', stacked_left, right_rows, preferred_element_...  17.4 us
  transfers between devices with their start and end apart: 16, of which 3 were waited for; matrix products, arithmetic and copies ran while one was open for 11% of the time, Pallas kernels for 0%

commit v1 on v0

v1 whole, which is shorter than its diff:
```python
import jax
import jax.numpy as jnp
from jax import lax
from jax.sharding import PartitionSpec as P

F = 256
W = 16
BAND = 1024
GROUP = 4


def permute(x, pairs):
    return lax.ppermute(x, "chan", pairs)


def shift_pairs(peers, by):
    return [(i, (i + by) % peers) for i in range(peers)]


def group_pairs(peers, t):
    return [(i, (i // GROUP) * GROUP + (i % GROUP + t) % GROUP) for i in range(peers)]


def exchange(chunks, j, peers):
    rel = jnp.roll(chunks, -j, axis=0)
    got = [rel[0]] + [permute(rel[t], group_pairs(peers, t)) for t in range(1, GROUP)]
    got = jnp.stack(got, axis=0)
    order = (j - jnp.arange(GROUP)) % GROUP
    return jnp.take(got, order, axis=0)


def pair_terms(first, second, ok_first, ok_second, limit_first, shift_blocks):
    row_count = first.shape[2]
    block_width = first.shape[4]
    row_scale = jnp.concatenate(
        [jnp.full((W,), 1.0 / W, jnp.float32), jnp.full((row_count - W,), -1.0, jnp.float32)]
    ).astype(jnp.bfloat16)
    scaled = first * row_scale[None, None, :, None, None]
    fb = first.shape[0]
    nb = first.shape[3]
    stacked_left = jnp.stack(
        [
            scaled.reshape(fb, 2 * row_count, nb, block_width),
            jnp.concatenate([scaled[:, 1], -scaled[:, 0]], axis=1),
        ],
        axis=0,
    )
    right_rows = second.reshape(fb, 2 * row_count, nb, block_width)
    cross_spec = jnp.einsum(
        "xfrbc,frbd->xfbcd", stacked_left, right_rows, preferred_element_type=jnp.float32
    )
    row_index = lax.broadcasted_iota(jnp.int32, (block_width, block_width), 0)
    col_index = lax.broadcasted_iota(jnp.int32, (block_width, block_width), 1)
    offset = shift_blocks * block_width + col_index - row_index
    inside = ((offset[None] >= 1) & (offset[None] <= limit_first[:, None, None])).astype(jnp.float32)
    live_mask = ok_first[:, :, None] * ok_second[:, None, :] * inside
    residual = cross_spec * live_mask[None, None]
    piece_loss = 0.5 * jnp.sum(residual * residual)
    rounded = residual.astype(jnp.bfloat16)
    far_spec = second[:, :, :W].reshape(fb, 2 * W, nb, block_width)
    near_spec = first[:, :, :W].reshape(fb, 2 * W, nb, block_width)
    toward = jnp.einsum("xfbcd,fvbd->xfvbc", rounded, far_spec, preferred_element_type=jnp.float32)
    first_real = toward[0, :, :W] - toward[1, :, W:]
    first_imag = toward[0, :, W:] + toward[1, :, :W]
    backward = jnp.einsum("xfbcd,fvbc->xfvbd", rounded, near_spec, preferred_element_type=jnp.float32)
    second_real = backward[0, :, :W] + backward[1, :, W:]
    second_imag = backward[0, :, W:] - backward[1, :, :W]
    return (
        piece_loss,
        jnp.stack([first_real, first_imag], axis=1),
        jnp.stack([second_real, second_imag], axis=1),
    )


def shards(spectra, model, channel_ok, limits):
    payload = jnp.concatenate([spectra, model], axis=2)
    fl, _, rows, bw = payload.shape
    peers = lax.axis_size("chan")
    me = lax.axis_index("chan")
    j = me % GROUP
    column = me // GROUP
    sub = fl // GROUP
    band_blocks = BAND // bw
    halo_cols = -(-band_blocks // GROUP)
    span = GROUP * bw

    chunks = payload.reshape(GROUP, sub, 2, rows, bw)
    mine = exchange(chunks, j, peers)
    own = jnp.transpose(mine, (1, 2, 3, 0, 4)).reshape(sub, 2, rows, span)

    parts = [own] + [permute(own, shift_pairs(peers, -GROUP * h)) for h in range(1, halo_cols + 1)]
    ext = jnp.concatenate(parts, axis=3)
    total = ext.shape[3]

    ok_all = channel_ok.astype(jnp.float32)
    ok_wide = jnp.concatenate([ok_all, ok_all[:total]])
    ok_ext = lax.dynamic_slice_in_dim(ok_wide, column * span, total)
    lim = lax.dynamic_slice_in_dim(limits, column * GROUP, GROUP)

    first = ext[:, :, :, :span].reshape(sub, 2, rows, GROUP, bw)
    ok_first = ok_ext[:span].reshape(GROUP, bw)
    misfit_sum = jnp.zeros((), jnp.float32)
    near_acc = jnp.zeros((sub, 2, W, GROUP, bw), jnp.float32)
    far_acc = jnp.zeros((sub, 2, W, total), jnp.float32)
    for s in range(band_blocks + 1):
        second = ext[:, :, :, s * bw : s * bw + span].reshape(sub, 2, rows, GROUP, bw)
        ok_second = ok_ext[s * bw : s * bw + span].reshape(GROUP, bw)
        piece_loss, near_terms, far_terms = pair_terms(first, second, ok_first, ok_second, lim, s)
        misfit_sum = misfit_sum + piece_loss
        near_acc = near_acc + near_terms
        far_flat = far_terms.reshape(sub, 2, W, span)
        far_acc = far_acc + jnp.pad(far_flat, ((0, 0), (0, 0), (0, 0), (s * bw, total - span - s * bw)))
    adj = near_acc.reshape(sub, 2, W, span) + far_acc[:, :, :, :span]
    for h in range(1, halo_cols + 1):
        adj = adj + permute(far_acc[:, :, :, h * span : (h + 1) * span], shift_pairs(peers, GROUP * h))
    adj = adj * (1.0 / W)

    blocks = jnp.transpose(adj.reshape(sub, 2, W, GROUP, bw), (3, 0, 1, 2, 4))
    back = exchange(blocks, j, peers)
    adjoint = back.reshape(fl, 2, W, bw)

    misfit_total = lax.psum(misfit_sum, ("chan", "freq"))
    misfit = misfit_total / float(F * bw * peers * BAND)
    return adjoint, misfit


def solution(mesh):
    return jax.shard_map(
        shards,
        mesh=mesh,
        in_specs=(P("freq", None, None, "chan"), P("freq", None, None, "chan"), P(), P()),
        out_specs=(P("freq", None, None, "chan"), P()),
        check_vma=False,
    )
```

time: 483 us -> 334 us (0.69)
  starting transfers between devices: 185 us -> 57.9 us
  local copies, waits for them, and re-layouts: 5.73 us -> 71.9 us
  blocking collectives: 151 us -> 102 us
  waiting for transfers between devices: 71.9 us -> 38 us
    ppermute x16 -> x10, starting transfers between devices: 185 us -> 57.9 us  [permute(): return lax.ppermute(x, 'chan', pairs)]
    psum x1, blocking collectives: 151 us -> 102 us  [shards(): misfit_total = lax.psum(misfit_sum, ('chan', 'freq'))]
    ppermute x16 -> x10, waiting for transfers between devices: 71.9 us -> 38 us  [permute(): return lax.ppermute(x, 'chan', pairs)]
    reshape x0 -> x10, local copies, waits for them, and re-layouts: none -> 15.2 us  [the longest x8 12.8 us: shards(): second = ext[:, :, :, s * bw:s * bw + span].reshape(sub, 2, rows, GROUP, bw)]
    sub x0 -> x18, local copies, waits for them, and re-layouts: none -> 12 us  [the longest x9 6.6 us: pair_terms(): first_real = toward[0, :, :W] - toward[1, :, W:]]
    slice x16 -> x30, local copies, waits for them, and re-layouts: 1.75 us -> 13.6 us  [the longest x23 7.92 us: pair_terms(): far_spec = second[:, :, :W].reshape(fb, 2 * W, nb, block_width)]
    add x0 -> x18, local copies, waits for them, and re-layouts: none -> 11.1 us  [the longest x9 6.62 us: pair_terms(): first_imag = toward[0, :, W:] + toward[1, :, :W]]
    another operation x0 -> x8, local copies, waits for them, and re-layouts: none -> 9.99 us  [pair_terms(): right_rows = second.reshape(fb, 2 * row_count, nb, block_width)]
  transfers between devices with their start and end apart: 16 -> 10, of which waited for: 3 -> 4; matrix products, arithmetic and copies ran while one was open for 11% -> 4% of each run, Pallas kernels for 0% -> 0%
where the time goes in v1:
time: 334 us; the launch traced here: 330 us
  blocking collectives  102 us (31%)
  local copies, waits for them, and re-layouts  71.9 us (22%)
  starting transfers between devices  57.9 us (17%)
  waiting for transfers between devices  38 us (11%)
  matrix products  31.7 us (9%)
  other arithmetic  19.6 us (6%)
  between operations  9.45 us (3%)
    psum x1, blocking collectives, shards(): misfit_total = lax.psum(misfit_sum, ('chan', 'freq'))  102 us
    ppermute x10, starting transfers between devices, permute(): return lax.ppermute(x, 'chan', pairs)  57.9 us
    ppermute x10, waiting for transfers between devices, permute(): return lax.ppermute(x, 'chan', pairs)  38 us
    dot_general x9, matrix products, pair_terms(): jnp.einsum('xfrbc,frbd->xfbcd', stacked_left, right_rows, preferred_eleme...  19.3 us
    reshape x8, local copies, waits for them, and re-layouts, shards(): second = ext[:, :, :, s * bw:s * bw + span].reshape(sub, 2, rows, GROUP, bw)  12.8 us
    another operation x8, local copies, waits for them, and re-layouts, pair_terms(): right_rows = second.reshape(fb, 2 * row_count, nb, block_width)  9.99 us
    slice x23, local copies, waits for them, and re-layouts, pair_terms(): far_spec = second[:, :, :W].reshape(fb, 2 * W, nb, block_width)  7.92 us
    dot_general x9, matrix products, pair_terms(): jnp.einsum('xfbcd,fvbc->xfvbd', rounded, near_spec, preferred_element_typ...  7.82 us
  transfers between devices with their start and end apart: 10, of which 4 were waited for; matrix products, arithmetic and copies ran while one was open for 4% of the time, Pallas kernels for 0%

profile of v1, /device:TPU:1, one launch (start us, length us, event | category | flops | bytes accessed | tf_op | source)
XLA Modules:
  0.0 330.2 jit_solution(5131253265094476053)
XLA Ops:
  2.6 16.3 %collective-permute-start.1 = (bf16[8,2,24,128]{3,2,1,0:T(8,128)(2,1)}, bf16[8,2,24,128]{3,2,1,0:T(8,128)(2,1)S(1)}, u32[]{:S(2)}, u32[]{:S(2)}) collective-permute-start(bf16[8,2,24,128]{3,2,1,0:T(8,128)(2,1)} %get-tuple-element.57), channel_id=1, source_target_pairs={{0,16},{8,24},{16,0},{24,8},{32,48},{40,56},{48,32},{56,40},{64,80... | collective-permute-start | bytes 294920 | tf_op jit(solution)/shard_map/ppermute | solution.py:13
  18.9 4.8 %collective-permute-start = (bf16[8,2,24,128]{3,2,1,0:T(8,128)(2,1)S(1)}, bf16[8,2,24,128]{3,2,1,0:T(8,128)(2,1)S(1)}, u32[]{:S(2)}, u32[]{:S(2)}) collective-permute-start(bf16[8,2,24,128]{3,2,1,0:T(8,128)(2,1)S(1)} %get-tuple-element.58), channel_id=1, source_target_pairs={{0,8},{8,16},{16,24},{24,0},{32,40},{40,48},{48,56},{56,32},{64,72... | collective-permute-start | bytes 294920 | tf_op jit(solution)/shard_map/ppermute | solution.py:13
  23.6 1.9 collective-permute-start.2
  29.6 9.8 %collective-permute-done.2 = bf16[8,2,24,128]{3,2,1,0:T(8,128)(2,1)} collective-permute-done((bf16[8,2,24,128]{3,2,1,0:T(8,128)(2,1)S(1)}, bf16[8,2,24,128]{3,2,1,0:T(8,128)(2,1)}, u32[]{:S(2)}, u32[]{:S(2)}) %collective-permute-start.2) | collective-permute-done | bytes 98336 | tf_op jit(solution)/shard_map/ppermute | solution.py:13
  45.5 1.9 reshape.1311
  47.4 7.6 %collective-permute-start.4 = (bf16[8,2,24,512]{3,2,1,0:T(8,128)(2,1)}, bf16[8,2,24,512]{3,2,1,0:T(8,128)(2,1)S(1)}, u32[]{:S(2)}, u32[]{:S(2)}) collective-permute-start(bf16[8,2,24,512]{3,2,1,0:T(8,128)(2,1)} %reshape.1311), channel_id=1, source_target_pairs={{0,448},{8,456},{16,464},{24,472},{32,480},{40,488},{48,496},{56,5... | collective-permute-start | bytes 1179656 | tf_op jit(solution)/shard_map/ppermute | solution.py:13
  55.0 3.2 collective-permute-start.3
  59.4 2.9 multiply_reduce_fusion.8
  68.1 4.6 %collective-permute-done.3 = bf16[8,2,24,512]{3,2,1,0:T(8,128)(2,1)S(1)} collective-permute-done((bf16[8,2,24,512]{3,2,1,0:T(8,128)(2,1)}, bf16[8,2,24,512]{3,2,1,0:T(8,128)(2,1)S(1)}, u32[]{:S(2)}, u32[]{:S(2)}) %collective-permute-start.3) | collective-permute-done | bytes 393248 | tf_op jit(solution)/shard_map/ppermute | solution.py:13
  81.1 1.8 reshape.1316
  84.6 2.3 fusion.72
  88.5 1.9 reshape.1320
  90.4 1.9 reshape_reshape.30
  92.3 1.9 reshape.1324
  108.5 1.9 multiply_reduce_fusion.6
  115.1 2.0 multiply_reduce_fusion.5
  122.7 3.0 multiply_reduce_fusion.4
  129.2 1.9 multiply_reduce_fusion.3
  135.2 1.9 multiply_reduce_fusion.2
  142.0 1.9 multiply_reduce_fusion.1
  148.8 1.9 multiply_reduce_fusion.7
  154.5 1.9 multiply_reduce_fusion
  158.9 4.2 %fusion.9 = f32[8,2,16,1536]{3,1,2,0:T(2,128)S(1)} fusion(f32[8,1,16,512]{3,1,2,0:T(1,128)S(1)} %bitcast.366, f32[8,1,16,512]{3,1,2,0:T(1,128)S(1)} %bitcast.364, f32[8,1,16,512]{3,1,2,0:T(1,128)S(1)} %bitcast.360, f32[8,1,16,512]{3,1,2,0:T(1,128)S(1)} %bitcast.359, f32[8,1,16,512]{3,1,2,0:T(1,128)S(1)} %bitcast.357, f32[8,1,16,512]{3,1,2,0:T(1,128)S(1)} %bitcast.356, ...), kind=kLoop, calls=%fused_computation.37 | loop fusion | flops 22806528 | bytes 6291456 | tf_op jit(solution)/shard_map/add | solution.py:112
  163.7 1.9 collective-permute-start.5
  165.6 4.7 %collective-permute-start.6 = (f32[8,2,16,512]{3,1,2,0:T(2,128)S(1)}, f32[8,2,16,512]{3,1,2,0:T(2,128)S(1)}, u32[]{:S(2)}, u32[]{:S(2)}) collective-permute-start(f32[8,2,16,512]{3,1,2,0:T(2,128)S(1)} %get-tuple-element.5), channel_id=1, source_target_pairs={{0,64},{8,72},{16,80},{24,88},{32,96},{40,104},{48,112},{56,120},{... | collective-permute-start | bytes 1572872 | tf_op jit(solution)/shard_map/ppermute | solution.py:13
  171.3 10.8 %collective-permute-done.5 = f32[8,2,16,512]{3,1,2,0:T(2,128)S(1)} collective-permute-done((f32[8,2,16,512]{3,1,2,0:T(2,128)S(1)}, f32[8,2,16,512]{3,1,2,0:T(2,128)S(1)}, u32[]{:S(2)}, u32[]{:S(2)}) %collective-permute-start.5) | collective-permute-done | bytes 524320 | tf_op jit(solution)/shard_map/ppermute | solution.py:13
  182.1 12.8 %collective-permute-done.6 = f32[8,2,16,512]{3,1,2,0:T(2,128)S(1)} collective-permute-done((f32[8,2,16,512]{3,1,2,0:T(2,128)S(1)}, f32[8,2,16,512]{3,1,2,0:T(2,128)S(1)}, u32[]{:S(2)}, u32[]{:S(2)}) %collective-permute-start.6) | collective-permute-done | bytes 524320 | tf_op jit(solution)/shard_map/ppermute | solution.py:13
  195.0 4.5 %fusion.38 = f32[8,2,16,512]{3,1,2,0:T(2,128)S(1)} fusion(f32[8,2,16,512]{3,1,2,0:T(2,128)S(1)} %collective-permute-done.6, f32[8,2,16,512]{3,1,2,0:T(2,128)S(1)} %collective-permute-done.5, f32[8,2,16,1536]{3,1,2,0:T(2,128)S(1)} %fusion.9, f32[8,1,16,512]{3,1,2,0:T(1,128)S(1)} %bitcast.380, f32[8,1,16,512]{3,1,2,0:T(1,128)S(1)} %bitcast.379, ...), kind=kLoop, calls=%fused_computation.80 | loop fusion | flops 2752512 | bytes 6815744 | tf_op jit(solution)/shard_map/mul | solution.py:116
  200.8 3.2 collective-permute-start.9
  204.1 1.9 collective-permute-start.8
  206.0 12.3 %collective-permute-start.7 = (f32[8,2,16,128]{3,1,2,0:T(2,128)S(1)}, f32[8,2,16,128]{3,1,2,0:T(2,128)S(1)}, u32[]{:S(2)}, u32[]{:S(2)}) collective-permute-start(f32[8,2,16,128]{3,1,2,0:T(2,128)S(1)} %bitcast.386), channel_id=1, source_target_pairs={{0,8},{8,16},{16,24},{24,0},{32,40},{40,48},{48,56},{56,32},{64,72... | collective-permute-start | bytes 393224 | tf_op jit(solution)/shard_map/ppermute | solution.py:13
  224.0 101.7 %psum.7 = f32[]{:T(128)} all-reduce(f32[]{:T(128)S(6)} %add.589), channel_id=1, replica_groups=mesh['chan'=64,'freq'=8] {'chan','freq'}, use_global_device_ids=true, to_apply=%region_9.10 | all-reduce | flops 1 | bytes 8 | tf_op jit(solution)/shard_map/psum | solution.py:122
  (259 shorter events, 83.6 us)
Async XLA Ops:
  0.6 26.7 %copy-start.45 = (s32[8192]{0:T(1024)S(1)}, s32[8192]{0:T(1024)}, u32[]{:S(2)}) copy-start(s32[8192]{0:T(1024)} %param.6) | copy-start | bytes 98308
  0.6 27.3 %copy-start.46 = (s32[64]{0:T(128)S(1)}, s32[64]{0:T(128)}, u32[]{:S(2)}) copy-start(s32[64]{0:T(128)} %param.7) | copy-start | bytes 772
  2.6 26.9 %collective-permute-start.1 = (bf16[8,2,24,128]{3,2,1,0:T(8,128)(2,1)}, bf16[8,2,24,128]{3,2,1,0:T(8,128)(2,1)S(1)}, u32[]{:S(2)}, u32[]{:S(2)}) collective-permute-start(bf16[8,2,24,128]{3,2,1,0:T(8,128)(2,1)} %get-tuple-element.57), channel_id=1, source_target_pairs={{0,16},{8,24},{16,0},{24,8},{32,48},{40,56},{48,32},{56,40},{64,80... | collective-permute-start | bytes 294920 | tf_op jit(solution)/shard_map/ppermute | solution.py:13
  18.9 10.7 %collective-permute-start = (bf16[8,2,24,128]{3,2,1,0:T(8,128)(2,1)S(1)}, bf16[8,2,24,128]{3,2,1,0:T(8,128)(2,1)S(1)}, u32[]{:S(2)}, u32[]{:S(2)}) collective-permute-start(bf16[8,2,24,128]{3,2,1,0:T(8,128)(2,1)S(1)} %get-tuple-element.58), channel_id=1, source_target_pairs={{0,8},{8,16},{16,24},{24,0},{32,40},{40,48},{48,56},{56,32},{64,72... | collective-permute-start | bytes 294920 | tf_op jit(solution)/shard_map/ppermute | solution.py:13
  23.6 15.7 %collective-permute-start.2 = (bf16[8,2,24,128]{3,2,1,0:T(8,128)(2,1)S(1)}, bf16[8,2,24,128]{3,2,1,0:T(8,128)(2,1)}, u32[]{:S(2)}, u32[]{:S(2)}) collective-permute-start(bf16[8,2,24,128]{3,2,1,0:T(8,128)(2,1)S(1)} %get-tuple-element.59), channel_id=1, source_target_pairs={{0,24},{8,0},{16,8},{24,16},{32,56},{40,32},{48,40},{56,48},{64,88... | collective-permute-start | bytes 294920 | tf_op jit(solution)/shard_map/ppermute | solution.py:13
  47.4 25.4 %collective-permute-start.4 = (bf16[8,2,24,512]{3,2,1,0:T(8,128)(2,1)}, bf16[8,2,24,512]{3,2,1,0:T(8,128)(2,1)S(1)}, u32[]{:S(2)}, u32[]{:S(2)}) collective-permute-start(bf16[8,2,24,512]{3,2,1,0:T(8,128)(2,1)} %reshape.1311), channel_id=1, source_target_pairs={{0,448},{8,456},{16,464},{24,472},{32,480},{40,488},{48,496},{56,5... | collective-permute-start | bytes 1179656 | tf_op jit(solution)/shard_map/ppermute | solution.py:13
  55.0 17.7 %collective-permute-start.3 = (bf16[8,2,24,512]{3,2,1,0:T(8,128)(2,1)}, bf16[8,2,24,512]{3,2,1,0:T(8,128)(2,1)S(1)}, u32[]{:S(2)}, u32[]{:S(2)}) collective-permute-start(bf16[8,2,24,512]{3,2,1,0:T(8,128)(2,1)} %reshape.1311), channel_id=1, source_target_pairs={{0,480},{8,488},{16,496},{24,504},{32,0},{40,8},{48,16},{56,24},{6... | collective-permute-start | bytes 1179656 | tf_op jit(solution)/shard_map/ppermute | solution.py:13
  88.5 9.3 %copy-start.1 = (bf16[8,2,24,512]{3,2,1,0:T(8,128)(2,1)S(1)}, bf16[8,2,24,512]{3,2,1,0:T(8,128)(2,1)}, u32[]{:S(2)}) copy-start(bf16[8,2,24,512]{3,2,1,0:T(8,128)(2,1)} %copy-done) | copy-start | bytes 1179652
  102.3 3.7 %slice-start.1 = ((bf16[8,2,24,4,128]{4,3,2,1,0:T(4,128)(2,1)}), bf16[8,2,16,4,128]{4,3,2,1,0:T(4,128)(2,1)S(1)}, s32[]{:S(2)}) async-start(bf16[8,2,24,4,128]{4,3,2,1,0:T(4,128)(2,1)} %reshape.1316), calls=%async_computation.1 | async-start | bytes 524288 | tf_op jit(solution)/shard_map/slice | solution.py:60
  102.3 3.8 %slice-start = ((bf16[8,2,24,4,128]{4,3,2,1,0:T(4,128)(2,1)}), bf16[8,2,16,4,128]{4,3,2,1,0:T(4,128)(2,1)S(1)}, s32[]{:S(2)}) async-start(bf16[8,2,24,4,128]{4,3,2,1,0:T(4,128)(2,1)} %reshape.1314), calls=%async_computation | async-start | bytes 524288 | tf_op jit(solution)/shard_map/slice | solution.py:60
  163.1 7.2 %copy-start.14 = (bf16[8,2,16,4,128]{4,2,1,3,0:T(8,128)(2,1)S(1)}, bf16[8,2,16,4,128]{4,2,1,3,0:T(8,128)(2,1)}, u32[]{:S(2)}) copy-start(bf16[8,2,16,4,128]{4,2,1,3,0:T(8,128)(2,1)} %copy.71) | copy-start | bytes 786436
  163.7 18.4 %collective-permute-start.5 = (f32[8,2,16,512]{3,1,2,0:T(2,128)S(1)}, f32[8,2,16,512]{3,1,2,0:T(2,128)S(1)}, u32[]{:S(2)}, u32[]{:S(2)}) collective-permute-start(f32[8,2,16,512]{3,1,2,0:T(2,128)S(1)} %get-tuple-element.4), channel_id=1, source_target_pairs={{0,32},{8,40},{16,48},{24,56},{32,64},{40,72},{48,80},{56,88},{64,... | collective-permute-start | bytes 1572872 | tf_op jit(solution)/shard_map/ppermute | solution.py:13
  165.6 29.2 %collective-permute-start.6 = (f32[8,2,16,512]{3,1,2,0:T(2,128)S(1)}, f32[8,2,16,512]{3,1,2,0:T(2,128)S(1)}, u32[]{:S(2)}, u32[]{:S(2)}) collective-permute-start(f32[8,2,16,512]{3,1,2,0:T(2,128)S(1)} %get-tuple-element.5), channel_id=1, source_target_pairs={{0,64},{8,72},{16,80},{24,88},{32,96},{40,104},{48,112},{56,120},{... | collective-permute-start | bytes 1572872 | tf_op jit(solution)/shard_map/ppermute | solution.py:13
  170.3 24.5 %copy-start.39 = (f32[1,8,16,4,128]{4,3,0,2,1:T(4,128)S(1)}, f32[1,8,16,4,128]{4,3,0,2,1:T(4,128)}, u32[]{:S(2)}) copy-start(f32[1,8,16,4,128]{4,3,0,2,1:T(4,128)} %copy.64) | copy-start | bytes 786436
  170.4 24.5 %copy-start.40 = (f32[1,8,16,4,128]{4,3,0,2,1:T(4,128)S(1)}, f32[1,8,16,4,128]{4,3,0,2,1:T(4,128)}, u32[]{:S(2)}) copy-start(f32[1,8,16,4,128]{4,3,0,2,1:T(4,128)} %copy.65) | copy-start | bytes 786436
  170.4 24.5 %copy-start.41 = (f32[1,8,16,4,128]{4,3,0,2,1:T(4,128)S(1)}, f32[1,8,16,4,128]{4,3,0,2,1:T(4,128)}, u32[]{:S(2)}) copy-start(f32[1,8,16,4,128]{4,3,0,2,1:T(4,128)} %copy.69) | copy-start | bytes 786436
  170.4 24.5 %copy-start.42 = (f32[1,8,16,4,128]{4,3,0,2,1:T(4,128)S(1)}, f32[1,8,16,4,128]{4,3,0,2,1:T(4,128)}, u32[]{:S(2)}) copy-start(f32[1,8,16,4,128]{4,3,0,2,1:T(4,128)} %copy.70) | copy-start | bytes 786436
  170.4 24.5 %copy-start.43 = (f32[1,8,16,4,128]{4,3,0,2,1:T(4,128)S(1)}, f32[1,8,16,4,128]{4,3,0,2,1:T(4,128)}, u32[]{:S(2)}) copy-start(f32[1,8,16,4,128]{4,3,0,2,1:T(4,128)} %copy.39) | copy-start | bytes 786436
  170.4 24.5 %copy-start.44 = (f32[1,8,16,4,128]{4,3,0,2,1:T(4,128)S(1)}, f32[1,8,16,4,128]{4,3,0,2,1:T(4,128)}, u32[]{:S(2)}) copy-start(f32[1,8,16,4,128]{4,3,0,2,1:T(4,128)} %copy.40) | copy-start | bytes 786436
  170.9 24.0 %copy-start.29 = (f32[1,8,16,4,128]{4,3,0,2,1:T(4,128)S(1)}, f32[1,8,16,4,128]{4,3,0,2,1:T(4,128)}, u32[]{:S(2)}) copy-start(f32[1,8,16,4,128]{4,3,0,2,1:T(4,128)} %copy.33) | copy-start | bytes 786436
  170.9 24.0 %copy-start.30 = (f32[1,8,16,4,128]{4,3,0,2,1:T(4,128)S(1)}, f32[1,8,16,4,128]{4,3,0,2,1:T(4,128)}, u32[]{:S(2)}) copy-start(f32[1,8,16,4,128]{4,3,0,2,1:T(4,128)} %copy.34) | copy-start | bytes 786436
  170.9 24.0 %copy-start.31 = (f32[1,8,16,4,128]{4,3,0,2,1:T(4,128)S(1)}, f32[1,8,16,4,128]{4,3,0,2,1:T(4,128)}, u32[]{:S(2)}) copy-start(f32[1,8,16,4,128]{4,3,0,2,1:T(4,128)} %copy.44) | copy-start | bytes 786436
  170.9 24.0 %copy-start.32 = (f32[1,8,16,4,128]{4,3,0,2,1:T(4,128)S(1)}, f32[1,8,16,4,128]{4,3,0,2,1:T(4,128)}, u32[]{:S(2)}) copy-start(f32[1,8,16,4,128]{4,3,0,2,1:T(4,128)} %copy.45) | copy-start | bytes 786436
  170.9 24.0 %copy-start.33 = (f32[1,8,16,4,128]{4,3,0,2,1:T(4,128)S(1)}, f32[1,8,16,4,128]{4,3,0,2,1:T(4,128)}, u32[]{:S(2)}) copy-start(f32[1,8,16,4,128]{4,3,0,2,1:T(4,128)} %copy.49) | copy-start | bytes 786436
  170.9 24.0 %copy-start.34 = (f32[1,8,16,4,128]{4,3,0,2,1:T(4,128)S(1)}, f32[1,8,16,4,128]{4,3,0,2,1:T(4,128)}, u32[]{:S(2)}) copy-start(f32[1,8,16,4,128]{4,3,0,2,1:T(4,128)} %copy.50) | copy-start | bytes 786436
  171.0 24.0 %copy-start.35 = (f32[1,8,16,4,128]{4,3,0,2,1:T(4,128)S(1)}, f32[1,8,16,4,128]{4,3,0,2,1:T(4,128)}, u32[]{:S(2)}) copy-start(f32[1,8,16,4,128]{4,3,0,2,1:T(4,128)} %copy.54) | copy-start | bytes 786436
  171.0 24.0 %copy-start.36 = (f32[1,8,16,4,128]{4,3,0,2,1:T(4,128)S(1)}, f32[1,8,16,4,128]{4,3,0,2,1:T(4,128)}, u32[]{:S(2)}) copy-start(f32[1,8,16,4,128]{4,3,0,2,1:T(4,128)} %copy.55) | copy-start | bytes 786436
  171.0 24.0 %copy-start.37 = (f32[1,8,16,4,128]{4,3,0,2,1:T(4,128)S(1)}, f32[1,8,16,4,128]{4,3,0,2,1:T(4,128)}, u32[]{:S(2)}) copy-start(f32[1,8,16,4,128]{4,3,0,2,1:T(4,128)} %copy.59) | copy-start | bytes 786436
  171.0 24.0 %copy-start.38 = (f32[1,8,16,4,128]{4,3,0,2,1:T(4,128)S(1)}, f32[1,8,16,4,128]{4,3,0,2,1:T(4,128)}, u32[]{:S(2)}) copy-start(f32[1,8,16,4,128]{4,3,0,2,1:T(4,128)} %copy.60) | copy-start | bytes 786436
  200.8 125.6 %collective-permute-start.9 = (f32[8,2,16,128]{3,1,2,0:T(2,128)S(1)}, f32[8,2,16,128]{3,1,2,0:T(2,128)S(1)}, u32[]{:S(2)}, u32[]{:S(2)}) collective-permute-start(f32[8,2,16,128]{3,1,2,0:T(2,128)S(1)} %bitcast.390), channel_id=1, source_target_pairs={{0,24},{8,0},{16,8},{24,16},{32,56},{40,32},{48,40},{56,48},{64,88... | collective-permute-start | bytes 393224 | tf_op jit(solution)/shard_map/ppermute | solution.py:13
  204.1 122.3 %collective-permute-start.8 = (f32[8,2,16,128]{3,1,2,0:T(2,128)S(1)}, f32[8,2,16,128]{3,1,2,0:T(2,128)S(1)}, u32[]{:S(2)}, u32[]{:S(2)}) collective-permute-start(f32[8,2,16,128]{3,1,2,0:T(2,128)S(1)} %bitcast.388), channel_id=1, source_target_pairs={{0,16},{8,24},{16,0},{24,8},{32,48},{40,56},{48,32},{56,40},{64,80... | collective-permute-start | bytes 393224 | tf_op jit(solution)/shard_map/ppermute | solution.py:13
  206.0 120.4 %collective-permute-start.7 = (f32[8,2,16,128]{3,1,2,0:T(2,128)S(1)}, f32[8,2,16,128]{3,1,2,0:T(2,128)S(1)}, u32[]{:S(2)}, u32[]{:S(2)}) collective-permute-start(f32[8,2,16,128]{3,1,2,0:T(2,128)S(1)} %bitcast.386), channel_id=1, source_target_pairs={{0,8},{8,16},{16,24},{24,0},{32,40},{40,48},{48,56},{56,32},{64,72... | collective-permute-start | bytes 393224 | tf_op jit(solution)/shard_map/ppermute | solution.py:13
  (30 other events, 49.7 us)

commit v2 on v1

v2 whole, which is shorter than its diff:
```python
import jax
import jax.numpy as jnp
from jax import lax
from jax.sharding import PartitionSpec as P

F = 256
W = 16
BAND = 1024
GROUP = 4


def permute(x, pairs):
    return lax.ppermute(x, "chan", pairs)


def shift_pairs(peers, by):
    return [(i, (i + by) % peers) for i in range(peers)]


def group_pairs(peers, t):
    return [(i, (i // GROUP) * GROUP + (i % GROUP + t) % GROUP) for i in range(peers)]


def exchange(chunks, j, peers):
    rel = jnp.roll(chunks, -j, axis=0)
    got = [rel[0]] + [permute(rel[t], group_pairs(peers, t)) for t in range(1, GROUP)]
    got = jnp.stack(got, axis=0)
    order = (j - jnp.arange(GROUP)) % GROUP
    return jnp.take(got, order, axis=0)


def pair_terms(first, second, ok_first, ok_second, limit_first, shift_blocks):
    fb, nb, _, row_count, block_width = first.shape
    row_scale = jnp.concatenate(
        [jnp.full((W,), 1.0 / W, jnp.float32), jnp.full((row_count - W,), -1.0, jnp.float32)]
    ).astype(jnp.bfloat16)
    scaled = first * row_scale[None, None, None, :, None]
    stacked_left = jnp.stack(
        [
            scaled.reshape(fb, nb, 2 * row_count, block_width),
            jnp.concatenate([scaled[:, :, 1], -scaled[:, :, 0]], axis=2),
        ],
        axis=2,
    )
    right_rows = second.reshape(fb, nb, 2 * row_count, block_width)
    cross_spec = jnp.einsum(
        "fbxrc,fbrd->fbxcd", stacked_left, right_rows, preferred_element_type=jnp.float32
    )
    row_index = lax.broadcasted_iota(jnp.int32, (block_width, block_width), 0)
    col_index = lax.broadcasted_iota(jnp.int32, (block_width, block_width), 1)
    offset = shift_blocks * block_width + col_index - row_index
    inside = ((offset[None] >= 1) & (offset[None] <= limit_first[:, None, None])).astype(jnp.float32)
    live_mask = ok_first[:, :, None] * ok_second[:, None, :] * inside
    residual = cross_spec * live_mask[None, :, None]
    piece_loss = 0.5 * jnp.sum(residual * residual)
    rounded = residual.astype(jnp.bfloat16)
    far_spec = second[:, :, :, :W].reshape(fb, nb, 2 * W, block_width)
    near_spec = first[:, :, :, :W].reshape(fb, nb, 2 * W, block_width)
    toward = jnp.einsum("fbxcd,fbvd->fbxvc", rounded, far_spec, preferred_element_type=jnp.float32)
    first_real = toward[:, :, 0, :W] - toward[:, :, 1, W:]
    first_imag = toward[:, :, 0, W:] + toward[:, :, 1, :W]
    backward = jnp.einsum("fbxcd,fbvc->fbxvd", rounded, near_spec, preferred_element_type=jnp.float32)
    second_real = backward[:, :, 0, :W] + backward[:, :, 1, W:]
    second_imag = backward[:, :, 0, W:] - backward[:, :, 1, :W]
    return (
        piece_loss,
        jnp.stack([first_real, first_imag], axis=2),
        jnp.stack([second_real, second_imag], axis=2),
    )


def global_sum(v, mesh_shape):
    for axis in ("chan", "freq"):
        n = mesh_shape[axis]
        bit = 1
        while bit < n:
            v = v + lax.ppermute(v, axis, [(i, i ^ bit) for i in range(n)])
            bit *= 2
    return v


def shards(spectra, model, channel_ok, limits, mesh_shape):
    payload = jnp.concatenate([spectra, model], axis=2)
    fl, _, rows, bw = payload.shape
    peers = lax.axis_size("chan")
    me = lax.axis_index("chan")
    j = me % GROUP
    column = me // GROUP
    sub = fl // GROUP
    band_blocks = BAND // bw
    halo_cols = -(-band_blocks // GROUP)
    nblk = GROUP * (1 + halo_cols)

    chunks = payload.reshape(GROUP, sub, 2, rows, bw)
    mine = exchange(chunks, j, peers)
    own = jnp.transpose(mine, (1, 0, 2, 3, 4))

    parts = [own] + [permute(own, shift_pairs(peers, -GROUP * h)) for h in range(1, halo_cols + 1)]
    ext = jnp.concatenate(parts, axis=1)

    ok_all = channel_ok.astype(jnp.float32)
    ok_wide = jnp.concatenate([ok_all, ok_all[: nblk * bw]])
    ok_ext = lax.dynamic_slice_in_dim(ok_wide, column * GROUP * bw, nblk * bw).reshape(nblk, bw)
    lim = lax.dynamic_slice_in_dim(limits, column * GROUP, GROUP)

    first = ext[:, :GROUP]
    ok_first = ok_ext[:GROUP]
    misfit_sum = jnp.zeros((), jnp.float32)
    near_acc = jnp.zeros((sub, GROUP, 2, W, bw), jnp.float32)
    far_acc = jnp.zeros((sub, nblk, 2, W, bw), jnp.float32)
    for s in range(band_blocks + 1):
        second = ext[:, s : s + GROUP]
        piece_loss, near_terms, far_terms = pair_terms(
            first, second, ok_first, ok_ext[s : s + GROUP], lim, s
        )
        misfit_sum = misfit_sum + piece_loss
        near_acc = near_acc + near_terms
        far_acc = far_acc.at[:, s : s + GROUP].add(far_terms)
    misfit_total = global_sum(misfit_sum, mesh_shape)
    adj = near_acc + far_acc[:, :GROUP]
    for h in range(1, halo_cols + 1):
        adj = adj + permute(far_acc[:, h * GROUP : (h + 1) * GROUP], shift_pairs(peers, GROUP * h))
    adj = adj * (1.0 / W)

    blocks = jnp.transpose(adj, (1, 0, 2, 3, 4))
    back = exchange(blocks, j, peers)
    adjoint = back.reshape(fl, 2, W, bw)

    misfit = misfit_total / float(F * bw * peers * BAND)
    return adjoint, misfit


def solution(mesh):
    mesh_shape = dict(mesh.shape)
    return jax.shard_map(
        lambda *a: shards(*a, mesh_shape),
        mesh=mesh,
        in_specs=(P("freq", None, None, "chan"), P("freq", None, None, "chan"), P(), P()),
        out_specs=(P("freq", None, None, "chan"), P()),
        check_vma=False,
    )
```

time: 334 us -> 224 us (0.67)
  the two profiles are of different devices: /device:TPU:1 before, /device:TPU:32 now
where the time goes in v2:
time: 224 us
  starting transfers between devices  102 us (46%)
  waiting for transfers between devices  64 us (29%)
  matrix products  29.9 us (13%)
  between operations  13.8 us (6%)
  other arithmetic  9.69 us (4%)
  local copies, waits for them, and re-layouts  3.97 us (2%)
    ppermute x10, starting transfers between devices, permute(): return lax.ppermute(x, 'chan', pairs)  61.7 us
    ppermute x9, starting transfers between devices, global_sum(): v = v + lax.ppermute(v, axis, [(i, i ^ bit) for i in range(n)])  40.4 us
    ppermute x10, waiting for transfers between devices, permute(): return lax.ppermute(x, 'chan', pairs)  37.4 us
    ppermute x9, waiting for transfers between devices, global_sum(): v = v + lax.ppermute(v, axis, [(i, i ^ bit) for i in range(n)])  26.7 us
    dot_general x9, matrix products, pair_terms(): jnp.einsum('fbxrc,fbrd->fbxcd', stacked_left, right_rows, preferred_eleme...  18.3 us
    dot_general x9, matrix products, pair_terms(): jnp.einsum('fbxcd,fbvd->fbxvc', rounded, far_spec, preferred_element_type...  7.65 us
  transfers between devices with their start and end apart: 19, of which 11 were waited for; matrix products, arithmetic and copies ran while one was open for 3% of the time, Pallas kernels for 0%

profile of v2, /device:TPU:32, one launch (start us, length us, event | category | flops | bytes accessed | tf_op | source)
XLA Modules:
  0.0 223.5 jit_solution(8712067716067047452)
XLA Ops:
  1.9 14.8 %collective-permute-start.1 = (bf16[8,2,24,128]{3,2,1,0:T(8,128)(2,1)S(1)}, bf16[8,2,24,128]{3,2,1,0:T(8,128)(2,1)S(1)}, u32[]{:S(2)}, u32[]{:S(2)}) collective-permute-start(bf16[8,2,24,128]{3,2,1,0:T(8,128)(2,1)S(1)} %get-tuple-element.172), channel_id=1, source_target_pairs={{0,16},{8,24},{16,0},{24,8},{32,48},{40,56},{48,32},{56,40},{64,80... | collective-permute-start | bytes 294920 | tf_op jit(solution)/shard_map/ppermute | solution.py:13
  18.7 12.4 %collective-permute-start.2 = (bf16[8,2,24,128]{3,2,1,0:T(8,128)(2,1)S(1)}, bf16[8,2,24,128]{3,2,1,0:T(8,128)(2,1)S(1)}, u32[]{:S(2)}, u32[]{:S(2)}) collective-permute-start(bf16[8,2,24,128]{3,2,1,0:T(8,128)(2,1)S(1)} %get-tuple-element.174), channel_id=1, source_target_pairs={{0,24},{8,0},{16,8},{24,16},{32,56},{40,32},{48,40},{56,48},{64,88... | collective-permute-start | bytes 294920 | tf_op jit(solution)/shard_map/ppermute | solution.py:13
  37.2 7.1 %collective-permute-start.3 = (bf16[8,4,2,24,128]{4,3,1,0,2:T(8,128)(2,1)S(1)}, bf16[8,4,2,24,128]{4,3,1,0,2:T(8,128)(2,1)S(1)}, u32[]{:S(2)}, u32[]{:S(2)}) collective-permute-start(bf16[8,4,2,24,128]{4,3,1,0,2:T(8,128)(2,1)S(1)} %get-tuple-element.111), channel_id=1, source_target_pairs={{0,480},{8,488},{16,496},{24,504},{32,0},{40,8},{48,16},{56,24},{6... | collective-permute-start | bytes 1179656 | tf_op jit(solution)/shard_map/ppermute | solution.py:13
  44.3 2.7 %collective-permute-start.4 = (bf16[8,4,2,24,128]{4,3,1,0,2:T(8,128)(2,1)S(1)}, bf16[8,4,2,24,128]{4,3,1,0,2:T(8,128)(2,1)S(1)}, u32[]{:S(2)}, u32[]{:S(2)}) collective-permute-start(bf16[8,4,2,24,128]{4,3,1,0,2:T(8,128)(2,1)S(1)} %get-tuple-element.111), channel_id=1, source_target_pairs={{0,448},{8,456},{16,464},{24,472},{32,480},{40,488},{48,496},{56,5... | collective-permute-start | bytes 1179656 | tf_op jit(solution)/shard_map/ppermute | solution.py:13
  49.3 12.7 %collective-permute-done.3 = bf16[8,4,2,24,128]{4,3,1,0,2:T(8,128)(2,1)S(1)} collective-permute-done((bf16[8,4,2,24,128]{4,3,1,0,2:T(8,128)(2,1)S(1)}, bf16[8,4,2,24,128]{4,3,1,0,2:T(8,128)(2,1)S(1)}, u32[]{:S(2)}, u32[]{:S(2)}) %collective-permute-start.3) | collective-permute-done | bytes 393248 | tf_op jit(solution)/shard_map/ppermute | solution.py:13
  64.5 2.0 multiply_reduce_fusion.3
  68.0 2.1 multiply_reduce_fusion.2
  71.5 2.0 multiply_reduce_fusion.1
  74.9 2.0 multiply_reduce_fusion.6
  78.6 2.1 multiply_reduce_fusion.7
  95.8 5.5 %collective-permute-start.6 = (f32[8,4,2,16,128]{4,3,2,1,0:T(8,128)S(1)}, f32[8,4,2,16,128]{4,3,2,1,0:T(8,128)S(1)}, u32[]{:S(2)}, u32[]{:S(2)}) collective-permute-start(f32[8,4,2,16,128]{4,3,2,1,0:T(8,128)S(1)} %get-tuple-element.113), channel_id=1, source_target_pairs={{0,64},{8,72},{16,80},{24,88},{32,96},{40,104},{48,112},{56,120},{... | collective-permute-start | bytes 1572872 | tf_op jit(solution)/shard_map/ppermute | solution.py:13
  101.5 12.2 %collective-permute-done.5 = f32[8,4,2,16,128]{4,3,2,1,0:T(8,128)S(1)} collective-permute-done((f32[8,4,2,16,128]{4,3,2,1,0:T(8,128)S(1)}, f32[8,4,2,16,128]{4,3,2,1,0:T(8,128)S(1)}, u32[]{:S(2)}, u32[]{:S(2)}) %collective-permute-start.5) | collective-permute-done | bytes 524320 | tf_op jit(solution)/shard_map/ppermute | solution.py:13
  113.7 12.4 %collective-permute-done.6 = f32[8,4,2,16,128]{4,3,2,1,0:T(8,128)S(1)} collective-permute-done((f32[8,4,2,16,128]{4,3,2,1,0:T(8,128)S(1)}, f32[8,4,2,16,128]{4,3,2,1,0:T(8,128)S(1)}, u32[]{:S(2)}, u32[]{:S(2)}) %collective-permute-start.6) | collective-permute-done | bytes 524320 | tf_op jit(solution)/shard_map/ppermute | solution.py:13
  126.9 4.0 %collective-permute-start.9 = (f32[8,2,16,128]{3,2,1,0:T(8,128)S(1)}, f32[8,2,16,128]{3,2,1,0:T(8,128)S(1)}, u32[]{:S(2)}, u32[]{:S(2)}) collective-permute-start(f32[8,2,16,128]{3,2,1,0:T(8,128)S(1)} %get-tuple-element.163), channel_id=1, source_target_pairs={{0,24},{8,0},{16,8},{24,16},{32,56},{40,32},{48,40},{56,48},{64,88... | collective-permute-start | bytes 393224 | tf_op jit(solution)/shard_map/ppermute | solution.py:13
  131.0 9.4 %collective-permute-start.8 = (f32[8,2,16,128]{3,2,1,0:T(8,128)S(1)}, f32[8,2,16,128]{3,2,1,0:T(8,128)S(1)}, u32[]{:S(2)}, u32[]{:S(2)}) collective-permute-start(f32[8,2,16,128]{3,2,1,0:T(8,128)S(1)} %get-tuple-element.164), channel_id=1, source_target_pairs={{0,16},{8,24},{16,0},{24,8},{32,48},{40,56},{48,32},{56,40},{64,80... | collective-permute-start | bytes 393224 | tf_op jit(solution)/shard_map/ppermute | solution.py:13
  148.0 6.2 %collective-permute-start.10 = (f32[]{:T(128)}, f32[]{:T(128)}, u32[]{:S(2)}, u32[]{:S(2)}) collective-permute-start(f32[]{:T(128)} %add.429), channel_id=1, source_target_pairs={{0,8},{8,0},{16,24},{24,16},{32,40},{40,32},{48,56},{56,48},{64,72... | collective-permute-start | bytes 20 | tf_op jit(solution)/shard_map/ppermute | solution.py:77
  154.9 10.7 %collective-permute-start.11 = (f32[]{:T(128)}, f32[]{:T(128)}, u32[]{:S(2)}, u32[]{:S(2)}) collective-permute-start(f32[]{:T(128)} %add.430), channel_id=1, source_target_pairs={{0,16},{8,24},{16,0},{24,8},{32,48},{40,56},{48,32},{56,40},{64,80... | collective-permute-start | bytes 20 | tf_op jit(solution)/shard_map/ppermute | solution.py:77
  165.6 3.6 %collective-permute-done.11 = f32[]{:T(128)} collective-permute-done((f32[]{:T(128)}, f32[]{:T(128)}, u32[]{:S(2)}, u32[]{:S(2)}) %collective-permute-start.11) | collective-permute-done | bytes 36 | tf_op jit(solution)/shard_map/ppermute | solution.py:77
  169.7 3.2 %collective-permute-start.12 = (f32[]{:T(128)}, f32[]{:T(128)}, u32[]{:S(2)}, u32[]{:S(2)}) collective-permute-start(f32[]{:T(128)} %add.431), channel_id=1, source_target_pairs={{0,32},{8,40},{16,48},{24,56},{32,0},{40,8},{48,16},{56,24},{64,96... | collective-permute-start | bytes 20 | tf_op jit(solution)/shard_map/ppermute | solution.py:77
  173.0 2.3 %collective-permute-done.12 = f32[]{:T(128)} collective-permute-done((f32[]{:T(128)}, f32[]{:T(128)}, u32[]{:S(2)}, u32[]{:S(2)}) %collective-permute-start.12) | collective-permute-done | bytes 36 | tf_op jit(solution)/shard_map/ppermute | solution.py:77
  175.9 3.2 %collective-permute-start.13 = (f32[]{:T(128)}, f32[]{:T(128)}, u32[]{:S(2)}, u32[]{:S(2)}) collective-permute-start(f32[]{:T(128)} %add.432), channel_id=1, source_target_pairs={{0,64},{8,72},{16,80},{24,88},{32,96},{40,104},{48,112},{56,120},{... | collective-permute-start | bytes 20 | tf_op jit(solution)/shard_map/ppermute | solution.py:77
  179.1 3.8 %collective-permute-done.13 = f32[]{:T(128)} collective-permute-done((f32[]{:T(128)}, f32[]{:T(128)}, u32[]{:S(2)}, u32[]{:S(2)}) %collective-permute-start.13) | collective-permute-done | bytes 36 | tf_op jit(solution)/shard_map/ppermute | solution.py:77
  183.6 3.2 %collective-permute-start.14 = (f32[]{:T(128)}, f32[]{:T(128)}, u32[]{:S(2)}, u32[]{:S(2)}) collective-permute-start(f32[]{:T(128)} %add.433), channel_id=1, source_target_pairs={{0,128},{8,136},{16,144},{24,152},{32,160},{40,168},{48,176},{56,1... | collective-permute-start | bytes 20 | tf_op jit(solution)/shard_map/ppermute | solution.py:77
  186.8 2.3 %collective-permute-done.14 = f32[]{:T(128)} collective-permute-done((f32[]{:T(128)}, f32[]{:T(128)}, u32[]{:S(2)}, u32[]{:S(2)}) %collective-permute-start.14) | collective-permute-done | bytes 36 | tf_op jit(solution)/shard_map/ppermute | solution.py:77
  189.8 3.2 %collective-permute-start.15 = (f32[]{:T(128)}, f32[]{:T(128)}, u32[]{:S(2)}, u32[]{:S(2)}) collective-permute-start(f32[]{:T(128)} %add.434), channel_id=1, source_target_pairs={{0,256},{8,264},{16,272},{24,280},{32,288},{40,296},{48,304},{56,3... | collective-permute-start | bytes 20 | tf_op jit(solution)/shard_map/ppermute | solution.py:77
  193.0 3.8 %collective-permute-done.15 = f32[]{:T(128)} collective-permute-done((f32[]{:T(128)}, f32[]{:T(128)}, u32[]{:S(2)}, u32[]{:S(2)}) %collective-permute-start.15) | collective-permute-done | bytes 36 | tf_op jit(solution)/shard_map/ppermute | solution.py:77
  197.4 3.2 %collective-permute-start.16 = (f32[]{:T(128)}, f32[]{:T(128)}, u32[]{:S(2)}, u32[]{:S(2)}) collective-permute-start(f32[]{:T(128)} %add.435), channel_id=1, source_target_pairs={{0,1},{1,0},{2,3},{3,2},{4,5},{5,4},{6,7},{7,6},{8,9},{9,8},{10,11... | collective-permute-start | bytes 20 | tf_op jit(solution)/shard_map/ppermute | solution.py:77
  200.6 2.3 %collective-permute-done.16 = f32[]{:T(128)} collective-permute-done((f32[]{:T(128)}, f32[]{:T(128)}, u32[]{:S(2)}, u32[]{:S(2)}) %collective-permute-start.16) | collective-permute-done | bytes 36 | tf_op jit(solution)/shard_map/ppermute | solution.py:77
  203.6 3.2 %collective-permute-start.17 = (f32[]{:T(128)}, f32[]{:T(128)}, u32[]{:S(2)}, u32[]{:S(2)}) collective-permute-start(f32[]{:T(128)} %add.436), channel_id=1, source_target_pairs={{0,2},{1,3},{2,0},{3,1},{4,6},{5,7},{6,4},{7,5},{8,10},{9,11},{10,... | collective-permute-start | bytes 20 | tf_op jit(solution)/shard_map/ppermute | solution.py:77
  206.8 3.2 %collective-permute-done.17 = f32[]{:T(128)} collective-permute-done((f32[]{:T(128)}, f32[]{:T(128)}, u32[]{:S(2)}, u32[]{:S(2)}) %collective-permute-start.17) | collective-permute-done | bytes 36 | tf_op jit(solution)/shard_map/ppermute | solution.py:77
  210.7 4.3 %collective-permute-start.18 = (f32[]{:T(128)}, f32[]{:T(128)}, u32[]{:S(2)}, u32[]{:S(2)}) collective-permute-start(f32[]{:T(128)} %add.437), channel_id=1, source_target_pairs={{0,4},{1,5},{2,6},{3,7},{4,0},{5,1},{6,2},{7,3},{8,12},{9,13},{10,... | collective-permute-start | bytes 20 | tf_op jit(solution)/shard_map/ppermute | solution.py:77
  214.9 5.2 %collective-permute-done.18 = f32[]{:T(128)} collective-permute-done((f32[]{:T(128)}, f32[]{:T(128)}, u32[]{:S(2)}, u32[]{:S(2)}) %collective-permute-start.18) | collective-permute-done | bytes 36 | tf_op jit(solution)/shard_map/ppermute | solution.py:77
  (129 shorter events, 39.1 us)
Async XLA Ops:
  1.9 33.6 %collective-permute-start.1 = (bf16[8,2,24,128]{3,2,1,0:T(8,128)(2,1)S(1)}, bf16[8,2,24,128]{3,2,1,0:T(8,128)(2,1)S(1)}, u32[]{:S(2)}, u32[]{:S(2)}) collective-permute-start(bf16[8,2,24,128]{3,2,1,0:T(8,128)(2,1)S(1)} %get-tuple-element.172), channel_id=1, source_target_pairs={{0,16},{8,24},{16,0},{24,8},{32,48},{40,56},{48,32},{56,40},{64,80... | collective-permute-start | bytes 294920 | tf_op jit(solution)/shard_map/ppermute | solution.py:13
  16.8 18.8 %collective-permute-start = (bf16[8,2,24,128]{3,2,1,0:T(8,128)(2,1)S(1)}, bf16[8,2,24,128]{3,2,1,0:T(8,128)(2,1)S(1)}, u32[]{:S(2)}, u32[]{:S(2)}) collective-permute-start(bf16[8,2,24,128]{3,2,1,0:T(8,128)(2,1)S(1)} %get-tuple-element.173), channel_id=1, source_target_pairs={{0,8},{8,16},{16,24},{24,0},{32,40},{40,48},{48,56},{56,32},{64,72... | collective-permute-start | bytes 294920 | tf_op jit(solution)/shard_map/ppermute | solution.py:13
  18.7 16.9 %collective-permute-start.2 = (bf16[8,2,24,128]{3,2,1,0:T(8,128)(2,1)S(1)}, bf16[8,2,24,128]{3,2,1,0:T(8,128)(2,1)S(1)}, u32[]{:S(2)}, u32[]{:S(2)}) collective-permute-start(bf16[8,2,24,128]{3,2,1,0:T(8,128)(2,1)S(1)} %get-tuple-element.174), channel_id=1, source_target_pairs={{0,24},{8,0},{16,8},{24,16},{32,56},{40,32},{48,40},{56,48},{64,88... | collective-permute-start | bytes 294920 | tf_op jit(solution)/shard_map/ppermute | solution.py:13
  37.2 24.8 %collective-permute-start.3 = (bf16[8,4,2,24,128]{4,3,1,0,2:T(8,128)(2,1)S(1)}, bf16[8,4,2,24,128]{4,3,1,0,2:T(8,128)(2,1)S(1)}, u32[]{:S(2)}, u32[]{:S(2)}) collective-permute-start(bf16[8,4,2,24,128]{4,3,1,0,2:T(8,128)(2,1)S(1)} %get-tuple-element.111), channel_id=1, source_target_pairs={{0,480},{8,488},{16,496},{24,504},{32,0},{40,8},{48,16},{56,24},{6... | collective-permute-start | bytes 1179656 | tf_op jit(solution)/shard_map/ppermute | solution.py:13
  44.3 17.8 %collective-permute-start.4 = (bf16[8,4,2,24,128]{4,3,1,0,2:T(8,128)(2,1)S(1)}, bf16[8,4,2,24,128]{4,3,1,0,2:T(8,128)(2,1)S(1)}, u32[]{:S(2)}, u32[]{:S(2)}) collective-permute-start(bf16[8,4,2,24,128]{4,3,1,0,2:T(8,128)(2,1)S(1)} %get-tuple-element.111), channel_id=1, source_target_pairs={{0,448},{8,456},{16,464},{24,472},{32,480},{40,488},{48,496},{56,5... | collective-permute-start | bytes 1179656 | tf_op jit(solution)/shard_map/ppermute | solution.py:13
  93.8 19.9 %collective-permute-start.5 = (f32[8,4,2,16,128]{4,3,2,1,0:T(8,128)S(1)}, f32[8,4,2,16,128]{4,3,2,1,0:T(8,128)S(1)}, u32[]{:S(2)}, u32[]{:S(2)}) collective-permute-start(f32[8,4,2,16,128]{4,3,2,1,0:T(8,128)S(1)} %get-tuple-element.112), channel_id=1, source_target_pairs={{0,32},{8,40},{16,48},{24,56},{32,64},{40,72},{48,80},{56,88},{64,... | collective-permute-start | bytes 1572872 | tf_op jit(solution)/shard_map/ppermute | solution.py:13
  95.8 30.4 %collective-permute-start.6 = (f32[8,4,2,16,128]{4,3,2,1,0:T(8,128)S(1)}, f32[8,4,2,16,128]{4,3,2,1,0:T(8,128)S(1)}, u32[]{:S(2)}, u32[]{:S(2)}) collective-permute-start(f32[8,4,2,16,128]{4,3,2,1,0:T(8,128)S(1)} %get-tuple-element.113), channel_id=1, source_target_pairs={{0,64},{8,72},{16,80},{24,88},{32,96},{40,104},{48,112},{56,120},{... | collective-permute-start | bytes 1572872 | tf_op jit(solution)/shard_map/ppermute | solution.py:13
  126.9 93.8 %collective-permute-start.9 = (f32[8,2,16,128]{3,2,1,0:T(8,128)S(1)}, f32[8,2,16,128]{3,2,1,0:T(8,128)S(1)}, u32[]{:S(2)}, u32[]{:S(2)}) collective-permute-start(f32[8,2,16,128]{3,2,1,0:T(8,128)S(1)} %get-tuple-element.163), channel_id=1, source_target_pairs={{0,24},{8,0},{16,8},{24,16},{32,56},{40,32},{48,40},{56,48},{64,88... | collective-permute-start | bytes 393224 | tf_op jit(solution)/shard_map/ppermute | solution.py:13
  131.0 89.8 %collective-permute-start.8 = (f32[8,2,16,128]{3,2,1,0:T(8,128)S(1)}, f32[8,2,16,128]{3,2,1,0:T(8,128)S(1)}, u32[]{:S(2)}, u32[]{:S(2)}) collective-permute-start(f32[8,2,16,128]{3,2,1,0:T(8,128)S(1)} %get-tuple-element.164), channel_id=1, source_target_pairs={{0,16},{8,24},{16,0},{24,8},{32,48},{40,56},{48,32},{56,40},{64,80... | collective-permute-start | bytes 393224 | tf_op jit(solution)/shard_map/ppermute | solution.py:13
  140.4 80.4 %collective-permute-start.7 = (f32[8,2,16,128]{3,2,1,0:T(8,128)S(1)}, f32[8,2,16,128]{3,2,1,0:T(8,128)S(1)}, u32[]{:S(2)}, u32[]{:S(2)}) collective-permute-start(f32[8,2,16,128]{3,2,1,0:T(8,128)S(1)} %get-tuple-element.165), channel_id=1, source_target_pairs={{0,8},{8,16},{16,24},{24,0},{32,40},{40,48},{48,56},{56,32},{64,72... | collective-permute-start | bytes 393224 | tf_op jit(solution)/shard_map/ppermute | solution.py:13
  148.0 6.2 %collective-permute-start.10 = (f32[]{:T(128)}, f32[]{:T(128)}, u32[]{:S(2)}, u32[]{:S(2)}) collective-permute-start(f32[]{:T(128)} %add.429), channel_id=1, source_target_pairs={{0,8},{8,0},{16,24},{24,16},{32,40},{40,32},{48,56},{56,48},{64,72... | collective-permute-start | bytes 20 | tf_op jit(solution)/shard_map/ppermute | solution.py:77
  154.9 14.3 %collective-permute-start.11 = (f32[]{:T(128)}, f32[]{:T(128)}, u32[]{:S(2)}, u32[]{:S(2)}) collective-permute-start(f32[]{:T(128)} %add.430), channel_id=1, source_target_pairs={{0,16},{8,24},{16,0},{24,8},{32,48},{40,56},{48,32},{56,40},{64,80... | collective-permute-start | bytes 20 | tf_op jit(solution)/shard_map/ppermute | solution.py:77
  169.7 5.5 %collective-permute-start.12 = (f32[]{:T(128)}, f32[]{:T(128)}, u32[]{:S(2)}, u32[]{:S(2)}) collective-permute-start(f32[]{:T(128)} %add.431), channel_id=1, source_target_pairs={{0,32},{8,40},{16,48},{24,56},{32,0},{40,8},{48,16},{56,24},{64,96... | collective-permute-start | bytes 20 | tf_op jit(solution)/shard_map/ppermute | solution.py:77
  175.9 7.0 %collective-permute-start.13 = (f32[]{:T(128)}, f32[]{:T(128)}, u32[]{:S(2)}, u32[]{:S(2)}) collective-permute-start(f32[]{:T(128)} %add.432), channel_id=1, source_target_pairs={{0,64},{8,72},{16,80},{24,88},{32,96},{40,104},{48,112},{56,120},{... | collective-permute-start | bytes 20 | tf_op jit(solution)/shard_map/ppermute | solution.py:77
  183.6 5.5 %collective-permute-start.14 = (f32[]{:T(128)}, f32[]{:T(128)}, u32[]{:S(2)}, u32[]{:S(2)}) collective-permute-start(f32[]{:T(128)} %add.433), channel_id=1, source_target_pairs={{0,128},{8,136},{16,144},{24,152},{32,160},{40,168},{48,176},{56,1... | collective-permute-start | bytes 20 | tf_op jit(solution)/shard_map/ppermute | solution.py:77
  189.8 7.0 %collective-permute-start.15 = (f32[]{:T(128)}, f32[]{:T(128)}, u32[]{:S(2)}, u32[]{:S(2)}) collective-permute-start(f32[]{:T(128)} %add.434), channel_id=1, source_target_pairs={{0,256},{8,264},{16,272},{24,280},{32,288},{40,296},{48,304},{56,3... | collective-permute-start | bytes 20 | tf_op jit(solution)/shard_map/ppermute | solution.py:77
  197.4 5.5 %collective-permute-start.16 = (f32[]{:T(128)}, f32[]{:T(128)}, u32[]{:S(2)}, u32[]{:S(2)}) collective-permute-start(f32[]{:T(128)} %add.435), channel_id=1, source_target_pairs={{0,1},{1,0},{2,3},{3,2},{4,5},{5,4},{6,7},{7,6},{8,9},{9,8},{10,11... | collective-permute-start | bytes 20 | tf_op jit(solution)/shard_map/ppermute | solution.py:77
  203.6 6.4 %collective-permute-start.17 = (f32[]{:T(128)}, f32[]{:T(128)}, u32[]{:S(2)}, u32[]{:S(2)}) collective-permute-start(f32[]{:T(128)} %add.436), channel_id=1, source_target_pairs={{0,2},{1,3},{2,0},{3,1},{4,6},{5,7},{6,4},{7,5},{8,10},{9,11},{10,... | collective-permute-start | bytes 20 | tf_op jit(solution)/shard_map/ppermute | solution.py:77
  210.7 9.4 %collective-permute-start.18 = (f32[]{:T(128)}, f32[]{:T(128)}, u32[]{:S(2)}, u32[]{:S(2)}) collective-permute-start(f32[]{:T(128)} %add.437), channel_id=1, source_target_pairs={{0,4},{1,5},{2,6},{3,7},{4,0},{5,1},{6,2},{7,3},{8,12},{9,13},{10,... | collective-permute-start | bytes 20 | tf_op jit(solution)/shard_map/ppermute | solution.py:77

commit v3 on v2

--- a/solution.py
+++ b/solution.py
@@ -1,7 +1,10 @@
 import jax
 import jax.numpy as jnp
 from jax import lax
+from jax.experimental import pallas as pl
+from jax.experimental.pallas import tpu as pltpu
 from jax.sharding import PartitionSpec as P
+import functools
 
 F = 256
 W = 16
@@ -69,14 +72,77 @@
     )
 
 
+MESH = pl.DeviceIdType.MESH
+
+def sum_kernel(n_col, n_f, val_ref, out_ref, slots1, slots2, stage, send1, recv1, send2, recv2):
+    c = lax.axis_index("chan")
+    f = lax.axis_index("freq")
+    k = c // GROUP
+    j = c % GROUP
+    g1 = GROUP * n_f
+    me1 = j * n_f + f
+
+    def dev1(slot):
+        return (k * GROUP + slot // n_f, slot % n_f)
+
+    def dev2(col):
+        return (col * GROUP + j, f)
+
+    barrier = pltpu.get_barrier_semaphore()
+    for t in range(1, g1):
+        pl.semaphore_signal(barrier, 1, device_id=dev1((me1 + t) % g1), device_id_type=MESH)
+    for t in range(1, n_col):
+        pl.semaphore_signal(barrier, 1, device_id=dev2((k + t) % n_col), device_id_type=MESH)
+    pl.semaphore_wait(barrier, g1 - 1 + n_col - 1)
+
+    def gather(src, slots, sends, recvs, count, mine, dev):
+        out = []
+        for t in range(1, count):
+            peer = (mine + t) % count
+            cp = pltpu.make_async_remote_copy(
+                src_ref=src, dst_ref=slots.at[mine], send_sem=sends.at[peer],
+                recv_sem=recvs.at[mine], device_id=dev(peer), device_id_type=MESH)
+            cp.start()
+            out.append(cp)
+        slots[mine] = src[...]
+        for t in range(1, count):
+            peer = (mine + t) % count
+            pltpu.make_async_remote_copy(
+                src_ref=src, dst_ref=slots.at[peer], send_sem=sends.at[peer],
+                recv_sem=recvs.at[peer], device_id=dev(peer), device_id_type=MESH).wait_recv()
+        for cp in out:
+            cp.wait_send()
+        acc = slots[0]
+        for s in range(1, count):
+            acc = acc + slots[s]
+        return acc
+
+    stage[...] = gather(val_ref, slots1, send1, recv1, g1, me1, dev1)
+    out_ref[...] = gather(stage, slots2, send2, recv2, n_col, k, dev2)
+
+
 def global_sum(v, mesh_shape):
-    for axis in ("chan", "freq"):
-        n = mesh_shape[axis]
-        bit = 1
-        while bit < n:
-            v = v + lax.ppermute(v, axis, [(i, i ^ bit) for i in range(n)])
-            bit *= 2
-    return v
+    n_col = mesh_shape["chan"] // GROUP
+    n_f = mesh_shape["freq"]
+    g1 = GROUP * n_f
+    tile = jnp.full((8, 128), v, jnp.float32)
+    out = pl.pallas_call(
+        functools.partial(sum_kernel, n_col, n_f),
+        out_shape=jax.ShapeDtypeStruct((8, 128), jnp.float32),
+        in_specs=[pl.BlockSpec(memory_space=pltpu.VMEM)],
+        out_specs=pl.BlockSpec(memory_space=pltpu.VMEM),
+        scratch_shapes=[
+            pltpu.VMEM((g1, 8, 128), jnp.float32),
+            pltpu.VMEM((n_col, 8, 128), jnp.float32),
+            pltpu.VMEM((8, 128), jnp.float32),
+            pltpu.SemaphoreType.DMA((g1,)),
+            pltpu.SemaphoreType.DMA((g1,)),
+            pltpu.SemaphoreType.DMA((n_col,)),
+            pltpu.SemaphoreType.DMA((n_col,)),
+        ],
+        compiler_params=pltpu.CompilerParams(collective_id=0, has_side_effects=True),
+    )(tile)
+    return out[0, 0]
 
 
 def shards(spectra, model, channel_ok, limits, mesh_shape):

time: 224 us -> 181 us (0.81)
  the two profiles are of different devices: /device:TPU:32 before, /device:TPU:1 now
where the time goes in v3:
time: 181 us; the launch traced here: 179 us
  starting transfers between devices  57.7 us (32%)
  waiting for transfers between devices  44.5 us (25%)
  matrix products  30.7 us (17%)
  Pallas kernels  21.5 us (12%)
  other arithmetic  9.68 us (5%)
  between operations  8.94 us (5%)
  local copies, waits for them, and re-layouts  5.77 us (3%)
    ppermute x10, starting transfers between devices, permute(): return lax.ppermute(x, 'chan', pairs)  57.7 us
    ppermute x10, waiting for transfers between devices, permute(): return lax.ppermute(x, 'chan', pairs)  44.5 us
    pallas_call x1, Pallas kernels, global_sum(): pl.pallas_call(functools.partial(sum_kernel, n_col, n_f), out_shape=jax.S...  21.5 us
    dot_general x9, matrix products, pair_terms(): jnp.einsum('fbxrc,fbrd->fbxcd', stacked_left, right_rows, preferred_eleme...  18.4 us
    dot_general x9, matrix products, pair_terms(): jnp.einsum('fbxcd,fbvd->fbxvc', rounded, far_spec, preferred_element_type...  7.87 us
    dot_general x9, matrix products, pair_terms(): jnp.einsum('fbxcd,fbvc->fbxvd', rounded, near_spec, preferred_element_typ...  4.38 us
  transfers between devices with their start and end apart: 10, of which 4 were waited for; matrix products, arithmetic and copies ran while one was open for 5% of the time, Pallas kernels for 12%

profile of v3, /device:TPU:1, one launch (start us, length us, event | category | flops | bytes accessed | tf_op | source)
XLA Modules:
  0.0 178.8 jit_solution(640703642327325259)
XLA Ops:
  0.7 1.1 pad_maximum_fusion.3
  1.9 16.3 %collective-permute-start.1 = (bf16[8,2,24,128]{3,2,1,0:T(8,128)(2,1)S(1)}, bf16[8,2,24,128]{3,2,1,0:T(8,128)(2,1)S(1)}, u32[]{:S(2)}, u32[]{:S(2)}) collective-permute-start(bf16[8,2,24,128]{3,2,1,0:T(8,128)(2,1)S(1)} %get-tuple-element.172), channel_id=1, source_target_pairs={{0,16},{8,24},{16,0},{24,8},{32,48},{40,56},{48,32},{56,40},{64,80... | collective-permute-start | bytes 294920 | tf_op jit(solution)/shard_map/ppermute | solution.py:16
  18.2 4.8 %collective-permute-start = (bf16[8,2,24,128]{3,2,1,0:T(8,128)(2,1)S(1)}, bf16[8,2,24,128]{3,2,1,0:T(8,128)(2,1)S(1)}, u32[]{:S(2)}, u32[]{:S(2)}) collective-permute-start(bf16[8,2,24,128]{3,2,1,0:T(8,128)(2,1)S(1)} %get-tuple-element.173), channel_id=1, source_target_pairs={{0,8},{8,16},{16,24},{24,0},{32,40},{40,48},{48,56},{56,32},{64,72... | collective-permute-start | bytes 294920 | tf_op jit(solution)/shard_map/ppermute | solution.py:16
  23.0 1.9 %collective-permute-start.2 = (bf16[8,2,24,128]{3,2,1,0:T(8,128)(2,1)S(1)}, bf16[8,2,24,128]{3,2,1,0:T(8,128)(2,1)S(1)}, u32[]{:S(2)}, u32[]{:S(2)}) collective-permute-start(bf16[8,2,24,128]{3,2,1,0:T(8,128)(2,1)S(1)} %get-tuple-element.174), channel_id=1, source_target_pairs={{0,24},{8,0},{16,8},{24,16},{32,56},{40,32},{48,40},{56,48},{64,88... | collective-permute-start | bytes 294920 | tf_op jit(solution)/shard_map/ppermute | solution.py:16
  28.3 1.1 multiply_select_fusion
  29.5 9.3 %collective-permute-done.2 = bf16[8,2,24,128]{3,2,1,0:T(8,128)(2,1)S(1)} collective-permute-done((bf16[8,2,24,128]{3,2,1,0:T(8,128)(2,1)S(1)}, bf16[8,2,24,128]{3,2,1,0:T(8,128)(2,1)S(1)}, u32[]{:S(2)}, u32[]{:S(2)}) %collective-permute-start.2) | collective-permute-done | bytes 98336 | tf_op jit(solution)/shard_map/ppermute | solution.py:16
  40.4 7.1 %collective-permute-start.3 = (bf16[8,4,2,24,128]{4,3,1,0,2:T(8,128)(2,1)S(1)}, bf16[8,4,2,24,128]{4,3,1,0,2:T(8,128)(2,1)S(1)}, u32[]{:S(2)}, u32[]{:S(2)}) collective-permute-start(bf16[8,4,2,24,128]{4,3,1,0,2:T(8,128)(2,1)S(1)} %get-tuple-element.111), channel_id=1, source_target_pairs={{0,480},{8,488},{16,496},{24,504},{32,0},{40,8},{48,16},{56,24},{6... | collective-permute-start | bytes 1179656 | tf_op jit(solution)/shard_map/ppermute | solution.py:16
  47.5 2.4 %collective-permute-start.4 = (bf16[8,4,2,24,128]{4,3,1,0,2:T(8,128)(2,1)S(1)}, bf16[8,4,2,24,128]{4,3,1,0,2:T(8,128)(2,1)S(1)}, u32[]{:S(2)}, u32[]{:S(2)}) collective-permute-start(bf16[8,4,2,24,128]{4,3,1,0,2:T(8,128)(2,1)S(1)} %get-tuple-element.111), channel_id=1, source_target_pairs={{0,448},{8,456},{16,464},{24,472},{32,480},{40,488},{48,496},{56,5... | collective-permute-start | bytes 1179656 | tf_op jit(solution)/shard_map/ppermute | solution.py:16
  50.2 2.0 %multiply_reduce_fusion.8 = (f32[]{:T(128)}, f32[8,4,2,128,128]{4,3,2,1,0:T(8,128)S(1)}) fusion(f32[4,128,128]{2,1,0:T(8,128)S(1)} %get-tuple-element.189, bf16[8,4,48,128,1]{3,2,4,1,0:T(8,128)(2,1)S(1)} %bitcast.242, bf16[8,4,1,48,128]{4,3,2,1,0:T(8,128)(2,1)S(1)} %maximum_bitcast_fusion, bf16[8,4,1,48,128]{4,3,2,1,0:T(8,128)(2,1)S(1)} %bitcast.215), kind=kOutput, calls=%fused_computation.10 | convolution fusion | flops 104202240 | bytes 5636100 | tf_op jit(solution)/shard_map/fbxrc,fbrd->fbxcd/dot_general | solution.py:49
  52.2 11.8 %collective-permute-done.3 = bf16[8,4,2,24,128]{4,3,1,0,2:T(8,128)(2,1)S(1)} collective-permute-done((bf16[8,4,2,24,128]{4,3,1,0,2:T(8,128)(2,1)S(1)}, bf16[8,4,2,24,128]{4,3,1,0,2:T(8,128)(2,1)S(1)}, u32[]{:S(2)}, u32[]{:S(2)}) %collective-permute-start.3) | collective-permute-done | bytes 393248 | tf_op jit(solution)/shard_map/ppermute | solution.py:16
  65.2 0.9 convolution_bitcast_fusion.17
  66.6 2.0 %multiply_reduce_fusion.3 = (f32[]{:T(128)}, f32[8,4,2,128,128]{4,3,2,1,0:T(8,128)S(1)}) fusion(f32[4,128,128]{2,1,0:T(8,128)S(1)} %get-tuple-element.188, bf16[8,4,48,128,1]{3,2,4,1,0:T(8,128)(2,1)S(1)} %bitcast.240, bf16[8,4,1,48,128]{4,3,2,1,0:T(8,128)(2,1)S(1)} %maximum_bitcast_fusion, bf16[8,4,1,48,128]{4,3,2,1,0:T(8,128)(2,1)S(1)} %bitcast.216), kind=kOutput, calls=%fused_computation.5 | convolution fusion | flops 104202240 | bytes 5636100 | tf_op jit(solution)/shard_map/fbxrc,fbrd->fbxcd/dot_general | solution.py:49
  69.1 0.9 convolution_bitcast_fusion.12
  70.1 2.1 %multiply_reduce_fusion.2 = (f32[]{:T(128)}, f32[8,4,2,128,128]{4,3,2,1,0:T(8,128)S(1)}) fusion(f32[4,128,128]{2,1,0:T(8,128)S(1)} %get-tuple-element.191, bf16[8,4,48,128,1]{3,2,4,1,0:T(8,128)(2,1)S(1)} %bitcast.238, bf16[8,4,1,48,128]{4,3,2,1,0:T(8,128)(2,1)S(1)} %maximum_bitcast_fusion, bf16[8,4,1,48,128]{4,3,2,1,0:T(8,128)(2,1)S(1)} %bitcast.217), kind=kOutput, calls=%fused_computation.4 | convolution fusion | flops 104202240 | bytes 5636100 | tf_op jit(solution)/shard_map/fbxrc,fbrd->fbxcd/dot_general | solution.py:49
  73.7 2.0 %multiply_reduce_fusion.1 = (f32[]{:T(128)}, f32[8,4,2,128,128]{4,3,2,1,0:T(8,128)S(1)}) fusion(f32[4,128,128]{2,1,0:T(8,128)S(1)} %get-tuple-element.190, bf16[8,4,48,128,1]{3,2,4,1,0:T(8,128)(2,1)S(1)} %bitcast.237, bf16[8,4,1,48,128]{4,3,2,1,0:T(8,128)(2,1)S(1)} %maximum_bitcast_fusion, bf16[8,4,1,48,128]{4,3,2,1,0:T(8,128)(2,1)S(1)} %bitcast.218), kind=kOutput, calls=%fused_computation.3 | convolution fusion | flops 104202240 | bytes 5636100 | tf_op jit(solution)/shard_map/fbxrc,fbrd->fbxcd/dot_general | solution.py:49
  77.3 2.0 %multiply_reduce_fusion.6 = (f32[]{:T(128)}, f32[8,4,2,128,128]{4,3,2,1,0:T(8,128)S(1)}) fusion(f32[4,128,128]{2,1,0:T(8,128)S(1)} %get-tuple-element.185, bf16[8,4,48,128,1]{3,2,4,1,0:T(8,128)(2,1)S(1)} %bitcast.236, bf16[8,4,1,48,128]{4,3,2,1,0:T(8,128)(2,1)S(1)} %maximum_bitcast_fusion, bf16[8,4,1,48,128]{4,3,2,1,0:T(8,128)(2,1)S(1)} %bitcast.219), kind=kOutput, calls=%fused_computation.8 | convolution fusion | flops 104202240 | bytes 5636100 | tf_op jit(solution)/shard_map/fbxrc,fbrd->fbxcd/dot_general | solution.py:49
  79.8 1.0 convolution_bitcast_fusion.15
  81.0 2.1 %multiply_reduce_fusion.7 = (f32[]{:T(128)}, f32[8,4,2,128,128]{4,3,2,1,0:T(8,128)S(1)}) fusion(f32[4,128,128]{2,1,0:T(8,128)S(1)} %get-tuple-element.192, bf16[8,4,48,128,1]{3,2,4,1,0:T(8,128)(2,1)S(1)} %bitcast.235, bf16[8,4,1,48,128]{4,3,2,1,0:T(8,128)(2,1)S(1)} %maximum_bitcast_fusion, bf16[8,4,1,48,128]{4,3,2,1,0:T(8,128)(2,1)S(1)} %bitcast.220), kind=kOutput, calls=%fused_computation.9 | convolution fusion | flops 104202240 | bytes 5636100 | tf_op jit(solution)/shard_map/fbxrc,fbrd->fbxcd/dot_general | solution.py:49
  84.5 2.0 %multiply_reduce_fusion.5 = (f32[]{:T(128)}, f32[8,4,2,128,128]{4,3,2,1,0:T(8,128)S(1)}) fusion(f32[4,128,128]{2,1,0:T(8,128)S(1)} %get-tuple-element.186, bf16[8,4,48,128,1]{3,2,4,1,0:T(8,128)(2,1)S(1)} %bitcast.234, bf16[8,4,1,48,128]{4,3,2,1,0:T(8,128)(2,1)S(1)} %maximum_bitcast_fusion, bf16[8,4,1,48,128]{4,3,2,1,0:T(8,128)(2,1)S(1)} %bitcast.221), kind=kOutput, calls=%fused_computation.7 | convolution fusion | flops 104202240 | bytes 5636100 | tf_op jit(solution)/shard_map/fbxrc,fbrd->fbxcd/dot_general | solution.py:49
  87.0 0.9 convolution_bitcast_fusion.14
  88.1 2.1 %multiply_reduce_fusion = (f32[]{:T(128)}, f32[8,4,2,128,128]{4,3,2,1,0:T(8,128)S(1)}) fusion(f32[4,128,128]{2,1,0:T(8,128)S(1)} %get-tuple-element.184, bf16[8,4,48,128,1]{3,2,4,1,0:T(8,128)(2,1)S(1)} %bitcast.241, bf16[8,4,1,48,128]{4,3,2,1,0:T(8,128)(2,1)S(1)} %maximum_bitcast_fusion, bf16[8,4,1,48,128]{4,3,2,1,0:T(8,128)(2,1)S(1)} %bitcast.222), kind=kOutput, calls=%fused_computation.2 | convolution fusion | flops 104202240 | bytes 5636100 | tf_op jit(solution)/shard_map/fbxrc,fbrd->fbxcd/dot_general | solution.py:49
  91.7 2.1 %multiply_reduce_fusion.4 = (f32[]{:T(128)}, f32[8,4,2,128,128]{4,3,2,1,0:T(8,128)S(1)}) fusion(f32[4,128,128]{2,1,0:T(8,128)S(1)} %get-tuple-element.187, bf16[8,4,48,128,1]{3,2,4,1,0:T(8,128)(2,1)S(1)} %bitcast.239, bf16[8,4,1,48,128]{4,3,2,1,0:T(8,128)(2,1)S(1)} %maximum_bitcast_fusion, bf16[8,4,1,48,128]{4,3,2,1,0:T(8,128)(2,1)S(1)} %bitcast.223), kind=kOutput, calls=%fused_computation.6 | convolution fusion | flops 104202240 | bytes 5636100 | tf_op jit(solution)/shard_map/fbxrc,fbrd->fbxcd/dot_general | solution.py:49
  96.6 1.9 %collective-permute-start.5 = (f32[8,4,2,16,128]{4,3,2,1,0:T(8,128)S(1)}, f32[8,4,2,16,128]{4,3,2,1,0:T(8,128)S(1)}, u32[]{:S(2)}, u32[]{:S(2)}) collective-permute-start(f32[8,4,2,16,128]{4,3,2,1,0:T(8,128)S(1)} %get-tuple-element.112), channel_id=1, source_target_pairs={{0,32},{8,40},{16,48},{24,56},{32,64},{40,72},{48,80},{56,88},{64,... | collective-permute-start | bytes 1572872 | tf_op jit(solution)/shard_map/ppermute | solution.py:16
  98.5 4.9 %collective-permute-start.6 = (f32[8,4,2,16,128]{4,3,2,1,0:T(8,128)S(1)}, f32[8,4,2,16,128]{4,3,2,1,0:T(8,128)S(1)}, u32[]{:S(2)}, u32[]{:S(2)}) collective-permute-start(f32[8,4,2,16,128]{4,3,2,1,0:T(8,128)S(1)} %get-tuple-element.113), channel_id=1, source_target_pairs={{0,64},{8,72},{16,80},{24,88},{32,96},{40,104},{48,112},{56,120},{... | collective-permute-start | bytes 1572872 | tf_op jit(solution)/shard_map/ppermute | solution.py:16
  103.7 11.3 %collective-permute-done.5 = f32[8,4,2,16,128]{4,3,2,1,0:T(8,128)S(1)} collective-permute-done((f32[8,4,2,16,128]{4,3,2,1,0:T(8,128)S(1)}, f32[8,4,2,16,128]{4,3,2,1,0:T(8,128)S(1)}, u32[]{:S(2)}, u32[]{:S(2)}) %collective-permute-start.5) | collective-permute-done | bytes 524320 | tf_op jit(solution)/shard_map/ppermute | solution.py:16
  115.0 12.1 %collective-permute-done.6 = f32[8,4,2,16,128]{4,3,2,1,0:T(8,128)S(1)} collective-permute-done((f32[8,4,2,16,128]{4,3,2,1,0:T(8,128)S(1)}, f32[8,4,2,16,128]{4,3,2,1,0:T(8,128)S(1)}, u32[]{:S(2)}, u32[]{:S(2)}) %collective-permute-start.6) | collective-permute-done | bytes 524320 | tf_op jit(solution)/shard_map/ppermute | solution.py:16
  127.9 4.1 %collective-permute-start.9 = (f32[8,2,16,128]{3,2,1,0:T(8,128)S(1)}, f32[8,2,16,128]{3,2,1,0:T(8,128)S(1)}, u32[]{:S(2)}, u32[]{:S(2)}) collective-permute-start(f32[8,2,16,128]{3,2,1,0:T(8,128)S(1)} %get-tuple-element.163), channel_id=1, source_target_pairs={{0,24},{8,0},{16,8},{24,16},{32,56},{40,32},{48,40},{56,48},{64,88... | collective-permute-start | bytes 393224 | tf_op jit(solution)/shard_map/ppermute | solution.py:16
  132.0 1.9 %collective-permute-start.8 = (f32[8,2,16,128]{3,2,1,0:T(8,128)S(1)}, f32[8,2,16,128]{3,2,1,0:T(8,128)S(1)}, u32[]{:S(2)}, u32[]{:S(2)}) collective-permute-start(f32[8,2,16,128]{3,2,1,0:T(8,128)S(1)} %get-tuple-element.164), channel_id=1, source_target_pairs={{0,16},{8,24},{16,0},{24,8},{32,48},{40,56},{48,32},{56,40},{64,80... | collective-permute-start | bytes 393224 | tf_op jit(solution)/shard_map/ppermute | solution.py:16
  133.9 12.3 %collective-permute-start.7 = (f32[8,2,16,128]{3,2,1,0:T(8,128)S(1)}, f32[8,2,16,128]{3,2,1,0:T(8,128)S(1)}, u32[]{:S(2)}, u32[]{:S(2)}) collective-permute-start(f32[8,2,16,128]{3,2,1,0:T(8,128)S(1)} %get-tuple-element.165), channel_id=1, source_target_pairs={{0,8},{8,16},{16,24},{24,0},{32,40},{40,48},{48,56},{56,32},{64,72... | collective-permute-start | bytes 393224 | tf_op jit(solution)/shard_map/ppermute | solution.py:16
  152.6 21.5 %shard_map.59 = f32[8,128]{1,0:T(8,128)} custom-call(f32[8,128]{1,0:T(8,128)} %broadcast_in_dim.29.val_ref), custom_call_target="tpu_custom_call" | custom-call | tf_op jit(solution)/shard_map/pallas_call | solution.py:129
  174.1 1.2 slice.899
  176.8 0.9 bitcast_select_fusion
  (114 shorter events, 19.9 us)
Async XLA Ops:
  1.9 27.5 %collective-permute-start.1 = (bf16[8,2,24,128]{3,2,1,0:T(8,128)(2,1)S(1)}, bf16[8,2,24,128]{3,2,1,0:T(8,128)(2,1)S(1)}, u32[]{:S(2)}, u32[]{:S(2)}) collective-permute-start(bf16[8,2,24,128]{3,2,1,0:T(8,128)(2,1)S(1)} %get-tuple-element.172), channel_id=1, source_target_pairs={{0,16},{8,24},{16,0},{24,8},{32,48},{40,56},{48,32},{56,40},{64,80... | collective-permute-start | bytes 294920 | tf_op jit(solution)/shard_map/ppermute | solution.py:16
  18.2 11.2 %collective-permute-start = (bf16[8,2,24,128]{3,2,1,0:T(8,128)(2,1)S(1)}, bf16[8,2,24,128]{3,2,1,0:T(8,128)(2,1)S(1)}, u32[]{:S(2)}, u32[]{:S(2)}) collective-permute-start(bf16[8,2,24,128]{3,2,1,0:T(8,128)(2,1)S(1)} %get-tuple-element.173), channel_id=1, source_target_pairs={{0,8},{8,16},{16,24},{24,0},{32,40},{40,48},{48,56},{56,32},{64,72... | collective-permute-start | bytes 294920 | tf_op jit(solution)/shard_map/ppermute | solution.py:16
  23.0 15.8 %collective-permute-start.2 = (bf16[8,2,24,128]{3,2,1,0:T(8,128)(2,1)S(1)}, bf16[8,2,24,128]{3,2,1,0:T(8,128)(2,1)S(1)}, u32[]{:S(2)}, u32[]{:S(2)}) collective-permute-start(bf16[8,2,24,128]{3,2,1,0:T(8,128)(2,1)S(1)} %get-tuple-element.174), channel_id=1, source_target_pairs={{0,24},{8,0},{16,8},{24,16},{32,56},{40,32},{48,40},{56,48},{64,88... | collective-permute-start | bytes 294920 | tf_op jit(solution)/shard_map/ppermute | solution.py:16
  40.4 23.6 %collective-permute-start.3 = (bf16[8,4,2,24,128]{4,3,1,0,2:T(8,128)(2,1)S(1)}, bf16[8,4,2,24,128]{4,3,1,0,2:T(8,128)(2,1)S(1)}, u32[]{:S(2)}, u32[]{:S(2)}) collective-permute-start(bf16[8,4,2,24,128]{4,3,1,0,2:T(8,128)(2,1)S(1)} %get-tuple-element.111), channel_id=1, source_target_pairs={{0,480},{8,488},{16,496},{24,504},{32,0},{40,8},{48,16},{56,24},{6... | collective-permute-start | bytes 1179656 | tf_op jit(solution)/shard_map/ppermute | solution.py:16
  47.5 16.7 %collective-permute-start.4 = (bf16[8,4,2,24,128]{4,3,1,0,2:T(8,128)(2,1)S(1)}, bf16[8,4,2,24,128]{4,3,1,0,2:T(8,128)(2,1)S(1)}, u32[]{:S(2)}, u32[]{:S(2)}) collective-permute-start(bf16[8,4,2,24,128]{4,3,1,0,2:T(8,128)(2,1)S(1)} %get-tuple-element.111), channel_id=1, source_target_pairs={{0,448},{8,456},{16,464},{24,472},{32,480},{40,488},{48,496},{56,5... | collective-permute-start | bytes 1179656 | tf_op jit(solution)/shard_map/ppermute | solution.py:16
  96.6 18.4 %collective-permute-start.5 = (f32[8,4,2,16,128]{4,3,2,1,0:T(8,128)S(1)}, f32[8,4,2,16,128]{4,3,2,1,0:T(8,128)S(1)}, u32[]{:S(2)}, u32[]{:S(2)}) collective-permute-start(f32[8,4,2,16,128]{4,3,2,1,0:T(8,128)S(1)} %get-tuple-element.112), channel_id=1, source_target_pairs={{0,32},{8,40},{16,48},{24,56},{32,64},{40,72},{48,80},{56,88},{64,... | collective-permute-start | bytes 1572872 | tf_op jit(solution)/shard_map/ppermute | solution.py:16
  98.5 28.6 %collective-permute-start.6 = (f32[8,4,2,16,128]{4,3,2,1,0:T(8,128)S(1)}, f32[8,4,2,16,128]{4,3,2,1,0:T(8,128)S(1)}, u32[]{:S(2)}, u32[]{:S(2)}) collective-permute-start(f32[8,4,2,16,128]{4,3,2,1,0:T(8,128)S(1)} %get-tuple-element.113), channel_id=1, source_target_pairs={{0,64},{8,72},{16,80},{24,88},{32,96},{40,104},{48,112},{56,120},{... | collective-permute-start | bytes 1572872 | tf_op jit(solution)/shard_map/ppermute | solution.py:16
  127.9 48.1 %collective-permute-start.9 = (f32[8,2,16,128]{3,2,1,0:T(8,128)S(1)}, f32[8,2,16,128]{3,2,1,0:T(8,128)S(1)}, u32[]{:S(2)}, u32[]{:S(2)}) collective-permute-start(f32[8,2,16,128]{3,2,1,0:T(8,128)S(1)} %get-tuple-element.163), channel_id=1, source_target_pairs={{0,24},{8,0},{16,8},{24,16},{32,56},{40,32},{48,40},{56,48},{64,88... | collective-permute-start | bytes 393224 | tf_op jit(solution)/shard_map/ppermute | solution.py:16
  132.0 44.0 %collective-permute-start.8 = (f32[8,2,16,128]{3,2,1,0:T(8,128)S(1)}, f32[8,2,16,128]{3,2,1,0:T(8,128)S(1)}, u32[]{:S(2)}, u32[]{:S(2)}) collective-permute-start(f32[8,2,16,128]{3,2,1,0:T(8,128)S(1)} %get-tuple-element.164), channel_id=1, source_target_pairs={{0,16},{8,24},{16,0},{24,8},{32,48},{40,56},{48,32},{56,40},{64,80... | collective-permute-start | bytes 393224 | tf_op jit(solution)/shard_map/ppermute | solution.py:16
  133.9 42.1 %collective-permute-start.7 = (f32[8,2,16,128]{3,2,1,0:T(8,128)S(1)}, f32[8,2,16,128]{3,2,1,0:T(8,128)S(1)}, u32[]{:S(2)}, u32[]{:S(2)}) collective-permute-start(f32[8,2,16,128]{3,2,1,0:T(8,128)S(1)} %get-tuple-element.165), channel_id=1, source_target_pairs={{0,8},{8,16},{16,24},{24,0},{32,40},{40,48},{48,56},{56,32},{64,72... | collective-permute-start | bytes 393224 | tf_op jit(solution)/shard_map/ppermute | solution.py:16

commit v4 on v3

--- a/solution.py
+++ b/solution.py
@@ -155,37 +155,43 @@
     sub = fl // GROUP
     band_blocks = BAND // bw
     halo_cols = -(-band_blocks // GROUP)
-    nblk = GROUP * (1 + halo_cols)
+    nblk = GROUP * (1 + 2 * halo_cols)
 
     chunks = payload.reshape(GROUP, sub, 2, rows, bw)
     mine = exchange(chunks, j, peers)
     own = jnp.transpose(mine, (1, 0, 2, 3, 4))
 
-    parts = [own] + [permute(own, shift_pairs(peers, -GROUP * h)) for h in range(1, halo_cols + 1)]
-    ext = jnp.concatenate(parts, axis=1)
+    ahead = [permute(own, shift_pairs(peers, -GROUP * h)) for h in range(1, halo_cols + 1)]
+    behind = [permute(own, shift_pairs(peers, GROUP * h)) for h in range(halo_cols, 0, -1)]
+    ext = jnp.concatenate(behind + [own] + ahead, axis=1)
+    base = GROUP * halo_cols
+    start_col = (column - halo_cols) % (peers // GROUP)
 
     ok_all = channel_ok.astype(jnp.float32)
     ok_wide = jnp.concatenate([ok_all, ok_all[: nblk * bw]])
-    ok_ext = lax.dynamic_slice_in_dim(ok_wide, column * GROUP * bw, nblk * bw).reshape(nblk, bw)
-    lim = lax.dynamic_slice_in_dim(limits, column * GROUP, GROUP)
-
-    first = ext[:, :GROUP]
-    ok_first = ok_ext[:GROUP]
+    ok_ext = lax.dynamic_slice_in_dim(ok_wide, start_col * GROUP * bw, nblk * bw).reshape(nblk, bw)
+    lim_wide = jnp.concatenate([limits, limits[:nblk]])
+    lim_ext = lax.dynamic_slice_in_dim(lim_wide, start_col * GROUP, nblk)
+
+    own_blk = slice(base, base + GROUP)
     misfit_sum = jnp.zeros((), jnp.float32)
-    near_acc = jnp.zeros((sub, GROUP, 2, W, bw), jnp.float32)
-    far_acc = jnp.zeros((sub, nblk, 2, W, bw), jnp.float32)
+    adj = jnp.zeros((sub, GROUP, 2, W, bw), jnp.float32)
     for s in range(band_blocks + 1):
-        second = ext[:, s : s + GROUP]
+        ahead_blk = slice(base + s, base + s + GROUP)
         piece_loss, near_terms, far_terms = pair_terms(
-            first, second, ok_first, ok_ext[s : s + GROUP], lim, s
+            ext[:, own_blk], ext[:, ahead_blk], ok_ext[own_blk], ok_ext[ahead_blk], lim_ext[own_blk], s
         )
         misfit_sum = misfit_sum + piece_loss
-        near_acc = near_acc + near_terms
-        far_acc = far_acc.at[:, s : s + GROUP].add(far_terms)
+        adj = adj + near_terms
+        if s == 0:
+            adj = adj + far_terms
+        else:
+            back_blk = slice(base - s, base - s + GROUP)
+            _, _, back_terms = pair_terms(
+                ext[:, back_blk], ext[:, own_blk], ok_ext[back_blk], ok_ext[own_blk], lim_ext[back_blk], s
+            )
+            adj = adj + back_terms
     misfit_total = global_sum(misfit_sum, mesh_shape)
-    adj = near_acc + far_acc[:, :GROUP]
-    for h in range(1, halo_cols + 1):
-        adj = adj + permute(far_acc[:, h * GROUP : (h + 1) * GROUP], shift_pairs(peers, GROUP * h))
     adj = adj * (1.0 / W)
 
     blocks = jnp.transpose(adj, (1, 0, 2, 3, 4))

time: 181 us -> 249 us (1.38)
  other arithmetic: 9.68 us -> 46.1 us
  waiting for transfers between devices: 44.5 us -> 12.9 us
  local copies, waits for them, and re-layouts: 5.77 us -> 33.9 us
  matrix products: 30.7 us -> 54.5 us
  starting transfers between devices: 57.7 us -> 64 us
  Pallas kernels: 21.5 us -> 26.1 us
    ppermute x10, waiting for transfers between devices: 44.5 us -> 12.9 us  [permute(): return lax.ppermute(x, 'chan', pairs)]
    dot_general x9, matrix products: 4.38 us -> 27.7 us  [pair_terms(): jnp.einsum('fbxcd,fbvc->fbxvd', rounded, near_spec, preferred_element_typ...]
    add x9, other arithmetic: 0.68 us -> 15.9 us  [pair_terms(): second_real = backward[:, :, 0, :W] + backward[:, :, 1, W:]]
    slice x8 -> x19, local copies, waits for them, and re-layouts: 1.01 us -> 13.4 us  [the longest x10 6.78 us: pair_terms(): near_spec = first[:, :, :, :W].reshape(fb, nb, 2 * W, block_width)]
    slice x11 -> x12, local copies, waits for them, and re-layouts: 0.32 us -> 7.8 us  [pair_terms(): far_spec = second[:, :, :, :W].reshape(fb, nb, 2 * W, block_width)]
    another operation x1 -> x9, other arithmetic: 0.04 us -> 6.52 us  [pair_terms(): jnp.stack([scaled.reshape(fb, nb, 2 * row_count, block_width), jnp.concat...]
    mul x1 -> x9, local copies, waits for them, and re-layouts: 0.04 us -> 6.42 us  [pair_terms(): scaled = first * row_scale[None, None, None, :, None]]
    ppermute x10, starting transfers between devices: 57.7 us -> 64 us  [permute(): return lax.ppermute(x, 'chan', pairs)]
  transfers between devices with their start and end apart: 10 -> 10, of which waited for: 4 -> 2; matrix products, arithmetic and copies ran while one was open for 5% -> 6% of each run, Pallas kernels for 12% -> 11%
where the time goes in v4:
time: 249 us; the launch traced here: 247 us
  starting transfers between devices  64 us (26%)
  matrix products  54.5 us (22%)
  other arithmetic  46.1 us (19%)
  local copies, waits for them, and re-layouts  33.9 us (14%)
  Pallas kernels  26.1 us (10%)
  waiting for transfers between devices  12.9 us (5%)
  between operations  9.09 us (4%)
    ppermute x10, starting transfers between devices, permute(): return lax.ppermute(x, 'chan', pairs)  64 us
    dot_general x9, matrix products, pair_terms(): jnp.einsum('fbxcd,fbvc->fbxvd', rounded, near_spec, preferred_element_typ...  27.7 us
    pallas_call x1, Pallas kernels, global_sum(): pl.pallas_call(functools.partial(sum_kernel, n_col, n_f), out_shape=jax.S...  26.1 us
    dot_general x9, matrix products, pair_terms(): jnp.einsum('fbxrc,fbrd->fbxcd', stacked_left, right_rows, preferred_eleme...  19.3 us
    add x9, other arithmetic, pair_terms(): second_real = backward[:, :, 0, :W] + backward[:, :, 1, W:]  15.9 us
    ppermute x10, waiting for transfers between devices, permute(): return lax.ppermute(x, 'chan', pairs)  12.9 us
    slice x12, local copies, waits for them, and re-layouts, pair_terms(): far_spec = second[:, :, :, :W].reshape(fb, nb, 2 * W, block_width)  7.8 us
    dot_general x9, matrix products, pair_terms(): jnp.einsum('fbxcd,fbvd->fbxvc', rounded, far_spec, preferred_element_type...  7.61 us
  transfers between devices with their start and end apart: 10, of which 2 were waited for; matrix products, arithmetic and copies ran while one was open for 6% of the time, Pallas kernels for 11%

profile of v4, /device:TPU:1, one launch (start us, length us, event | category | flops | bytes accessed | tf_op | source)
XLA Modules:
  0.0 246.6 jit_solution(11319262465499025232)
XLA Ops:
  2.0 8.8 %collective-permute-start.2 = (bf16[8,2,24,128]{3,2,1,0:T(8,128)(2,1)S(1)}, bf16[8,2,24,128]{3,2,1,0:T(8,128)(2,1)S(1)}, u32[]{:S(2)}, u32[]{:S(2)}) collective-permute-start(bf16[8,2,24,128]{3,2,1,0:T(8,128)(2,1)S(1)} %get-tuple-element.104), channel_id=1, source_target_pairs={{0,24},{8,0},{16,8},{24,16},{32,56},{40,32},{48,40},{56,48},{64,88... | collective-permute-start | bytes 294920 | tf_op jit(solution)/shard_map/ppermute | solution.py:16
  10.8 10.1 %collective-permute-start.1 = (bf16[8,2,24,128]{3,2,1,0:T(8,128)(2,1)S(1)}, bf16[8,2,24,128]{3,2,1,0:T(8,128)(2,1)S(1)}, u32[]{:S(2)}, u32[]{:S(2)}) collective-permute-start(bf16[8,2,24,128]{3,2,1,0:T(8,128)(2,1)S(1)} %get-tuple-element.102), channel_id=1, source_target_pairs={{0,16},{8,24},{16,0},{24,8},{32,48},{40,56},{48,32},{56,40},{64,80... | collective-permute-start | bytes 294920 | tf_op jit(solution)/shard_map/ppermute | solution.py:16
  20.8 12.0 %collective-permute-start = (bf16[8,2,24,128]{3,2,1,0:T(8,128)(2,1)S(1)}, bf16[8,2,24,128]{3,2,1,0:T(8,128)(2,1)S(1)}, u32[]{:S(2)}, u32[]{:S(2)}) collective-permute-start(bf16[8,2,24,128]{3,2,1,0:T(8,128)(2,1)S(1)} %get-tuple-element.103), channel_id=1, source_target_pairs={{0,8},{8,16},{16,24},{24,0},{32,40},{40,48},{48,56},{56,32},{64,72... | collective-permute-start | bytes 294920 | tf_op jit(solution)/shard_map/ppermute | solution.py:16
  40.4 4.7 %collective-permute-start.6 = (bf16[8,4,2,24,128]{4,3,1,0,2:T(8,128)(2,1)S(1)}, bf16[8,4,2,24,128]{4,3,1,0,2:T(8,128)(2,1)S(1)}, u32[]{:S(2)}, u32[]{:S(2)}) collective-permute-start(bf16[8,4,2,24,128]{4,3,1,0,2:T(8,128)(2,1)S(1)} %get-tuple-element.3), channel_id=1, source_target_pairs={{0,64},{8,72},{16,80},{24,88},{32,96},{40,104},{48,112},{56,120},{... | collective-permute-start | bytes 1179656 | tf_op jit(solution)/shard_map/ppermute | solution.py:16
  45.1 4.4 %collective-permute-start.5 = (bf16[8,4,2,24,128]{4,3,1,0,2:T(8,128)(2,1)S(1)}, bf16[8,4,2,24,128]{4,3,1,0,2:T(8,128)(2,1)S(1)}, u32[]{:S(2)}, u32[]{:S(2)}) collective-permute-start(bf16[8,4,2,24,128]{4,3,1,0,2:T(8,128)(2,1)S(1)} %get-tuple-element.3), channel_id=1, source_target_pairs={{0,448},{8,456},{16,464},{24,472},{32,480},{40,488},{48,496},{56,5... | collective-permute-start | bytes 1179656 | tf_op jit(solution)/shard_map/ppermute | solution.py:16
  49.4 4.6 %collective-permute-start.3 = (bf16[8,4,2,24,128]{4,3,1,0,2:T(8,128)(2,1)S(1)}, bf16[8,4,2,24,128]{4,3,1,0,2:T(8,128)(2,1)S(1)}, u32[]{:S(2)}, u32[]{:S(2)}) collective-permute-start(bf16[8,4,2,24,128]{4,3,1,0,2:T(8,128)(2,1)S(1)} %get-tuple-element.3), channel_id=1, source_target_pairs={{0,480},{8,488},{16,496},{24,504},{32,0},{40,8},{48,16},{56,24},{6... | collective-permute-start | bytes 1179656 | tf_op jit(solution)/shard_map/ppermute | solution.py:16
  54.1 2.1 collective-permute-start.4
  59.4 11.1 %collective-permute-done.3 = bf16[8,4,2,24,128]{4,3,1,0,2:T(8,128)(2,1)S(1)} collective-permute-done((bf16[8,4,2,24,128]{4,3,1,0,2:T(8,128)(2,1)S(1)}, bf16[8,4,2,24,128]{4,3,1,0,2:T(8,128)(2,1)S(1)}, u32[]{:S(2)}, u32[]{:S(2)}) %collective-permute-start.3) | collective-permute-done | bytes 393248 | tf_op jit(solution)/shard_map/ppermute | solution.py:16
  91.0 3.4 %fusion.24 = f32[8,4,2,32,128]{4,3,2,1,0:T(8,128)} fusion(bf16[8,4,32,128,1]{3,2,4,1,0:T(8,128)(2,1)} %bitcast.382, bf16[8,4,48,128,1]{3,2,4,1,0:T(8,128)(2,1)} %bitcast.348, f32[4,128,128]{2,1,0:T(8,128)} %get-tuple-element.148, bf16[8,4,1,48,128]{4,3,1,0,2:T(8,128)(2,1)} %maximum_bitcast_fusion.8, bf16[8,4,1,48,128]{4,3,1,0,2:T(8,128)(2,1)} %bitcast.379), kind=kOutput, calls=%fused_computation.54 | convolution fusion | flops 170262528 | bytes 2752512 | tf_op jit(solution)/shard_map/fbxcd,fbvc->fbxvd/dot_general | solution.py:65
  94.4 2.1 slice_add_fusion
  97.6 3.0 %multiply_reduce_fusion = (f32[]{:T(128)}, f32[8,4,2,128,128]{4,3,2,1,0:T(8,128)S(1)}) fusion(f32[4,128,128]{2,1,0:T(8,128)} %get-tuple-element.149, bf16[8,4,48,128,1]{3,2,4,1,0:T(8,128)(2,1)S(1)} %bitcast.359, bf16[8,4,1,48,128]{4,3,2,1,0:T(8,128)(2,1)S(1)} %maximum_bitcast_fusion, bf16[8,4,1,48,128]{4,3,2,1,0:T(8,128)(2,1)S(1)} %bitcast.337), kind=kOutput, calls=%fused_computation.2 | convolution fusion | flops 104202240 | bytes 5636100 | tf_op jit(solution)/shard_map/fbxrc,fbrd->fbxcd/dot_general | solution.py:49
  103.8 3.4 %fusion.25 = f32[8,4,2,32,128]{4,3,2,1,0:T(8,128)} fusion(bf16[8,4,32,128,1]{3,2,4,1,0:T(8,128)(2,1)} %bitcast.383, bf16[8,4,48,128,1]{3,2,4,1,0:T(8,128)(2,1)} %bitcast.349, f32[4,128,128]{2,1,0:T(8,128)} %get-tuple-element.118, bf16[8,4,1,48,128]{4,3,1,0,2:T(8,128)(2,1)} %maximum_bitcast_fusion.7, bf16[8,4,1,48,128]{4,3,1,0,2:T(8,128)(2,1)} %bitcast.380), kind=kOutput, calls=%fused_computation.55 | convolution fusion | flops 170262528 | bytes 2752512 | tf_op jit(solution)/shard_map/fbxcd,fbvc->fbxvd/dot_general | solution.py:65
  107.2 2.1 slice_add_fusion.2
  116.6 3.4 %fusion.26 = f32[8,4,2,32,128]{4,3,2,1,0:T(8,128)} fusion(bf16[8,4,32,128,1]{3,2,4,1,0:T(8,128)(2,1)} %bitcast.384, bf16[8,4,48,128,1]{3,2,4,1,0:T(8,128)(2,1)} %bitcast.350, f32[4,128,128]{2,1,0:T(8,128)} %get-tuple-element.146, bf16[8,4,1,48,128]{4,3,1,0,2:T(8,128)(2,1)} %maximum_bitcast_fusion.6, bf16[8,4,1,48,128]{4,3,1,0,2:T(8,128)(2,1)} %bitcast.378), kind=kOutput, calls=%fused_computation.56 | convolution fusion | flops 170262528 | bytes 2752512 | tf_op jit(solution)/shard_map/fbxcd,fbvc->fbxvd/dot_general | solution.py:65
  120.0 2.1 slice_add_fusion.4
  124.4 2.1 multiply_reduce_fusion.2
  129.8 3.4 %fusion.27 = f32[8,4,2,32,128]{4,3,2,1,0:T(8,128)} fusion(bf16[8,4,32,128,1]{3,2,4,1,0:T(8,128)(2,1)} %bitcast.385, bf16[8,4,48,128,1]{3,2,4,1,0:T(8,128)(2,1)} %bitcast.351, f32[4,128,128]{2,1,0:T(8,128)} %get-tuple-element.144, bf16[8,4,1,48,128]{4,3,1,0,2:T(8,128)(2,1)} %maximum_bitcast_fusion.5, bf16[8,4,1,48,128]{4,3,1,0,2:T(8,128)(2,1)} %bitcast.377), kind=kOutput, calls=%fused_computation.57 | convolution fusion | flops 170262528 | bytes 2752512 | tf_op jit(solution)/shard_map/fbxcd,fbvc->fbxvd/dot_general | solution.py:65
  133.2 2.1 slice_add_fusion.6
  137.3 2.1 multiply_reduce_fusion.3
  142.7 3.4 %fusion.28 = f32[8,4,2,32,128]{4,3,2,1,0:T(8,128)} fusion(bf16[8,4,32,128,1]{3,2,4,1,0:T(8,128)(2,1)} %bitcast.387, bf16[8,4,48,128,1]{3,2,4,1,0:T(8,128)(2,1)} %bitcast.352, f32[4,128,128]{2,1,0:T(8,128)} %get-tuple-element.112, bf16[8,4,1,48,128]{4,3,1,0,2:T(8,128)(2,1)} %maximum_bitcast_fusion.4, bf16[8,4,1,48,128]{4,3,1,0,2:T(8,128)(2,1)} %bitcast.376), kind=kOutput, calls=%fused_computation.58 | convolution fusion | flops 170262528 | bytes 2752512 | tf_op jit(solution)/shard_map/fbxcd,fbvc->fbxvd/dot_general | solution.py:65
  146.1 2.1 slice_add_fusion.8
  154.5 3.4 %fusion.29 = f32[8,4,2,32,128]{4,3,2,1,0:T(8,128)} fusion(bf16[8,4,32,128,1]{3,2,4,1,0:T(8,128)(2,1)} %bitcast.386, bf16[8,4,48,128,1]{3,2,4,1,0:T(8,128)(2,1)} %bitcast.353, f32[4,128,128]{2,1,0:T(8,128)} %get-tuple-element.142, bf16[8,4,1,48,128]{4,3,1,0,2:T(8,128)(2,1)} %maximum_bitcast_fusion.3, bf16[8,4,1,48,128]{4,3,1,0,2:T(8,128)(2,1)} %bitcast.375), kind=kOutput, calls=%fused_computation.59 | convolution fusion | flops 170262528 | bytes 2752512 | tf_op jit(solution)/shard_map/fbxcd,fbvc->fbxvd/dot_general | solution.py:65
  157.9 2.1 slice_add_fusion.10
  161.0 2.1 multiply_reduce_fusion.5
  166.4 3.5 %fusion.30 = f32[8,4,2,32,128]{4,3,2,1,0:T(8,128)} fusion(bf16[8,4,32,128,1]{3,2,4,1,0:T(8,128)(2,1)} %bitcast.388, bf16[8,4,48,128,1]{3,2,4,1,0:T(8,128)(2,1)S(1)} %bitcast.354, f32[4,128,128]{2,1,0:T(8,128)} %get-tuple-element.140, bf16[8,4,1,48,128]{4,3,1,0,2:T(8,128)(2,1)} %maximum_bitcast_fusion.2, bf16[8,4,1,48,128]{4,3,1,0,2:T(8,128)(2,1)} %bitcast.374), kind=kOutput, calls=%fused_computation.60 | convolution fusion | flops 170262528 | bytes 2752512 | tf_op jit(solution)/shard_map/fbxcd,fbvc->fbxvd/dot_general | solution.py:65
  169.9 2.1 slice_add_fusion.12
  174.0 2.1 multiply_reduce_fusion.6
  179.3 3.3 %fusion.31 = f32[8,4,2,32,128]{4,3,2,1,0:T(8,128)} fusion(bf16[8,4,32,128,1]{3,2,4,1,0:T(8,128)(2,1)} %bitcast.381, bf16[8,4,48,128,1]{3,2,4,1,0:T(8,128)(2,1)S(1)} %bitcast.355, f32[4,128,128]{2,1,0:T(8,128)} %get-tuple-element.106, bf16[8,4,1,48,128]{4,3,1,0,2:T(8,128)(2,1)} %maximum_bitcast_fusion.1, bf16[8,4,1,48,128]{4,3,1,0,2:T(8,128)(2,1)} %bitcast.373), kind=kOutput, calls=%fused_computation.61 | convolution fusion | flops 170262528 | bytes 2752512 | tf_op jit(solution)/shard_map/fbxcd,fbvc->fbxvd/dot_general | solution.py:65
  192.1 2.3 collective-permute-start.9
  194.4 6.0 %collective-permute-start.8 = (f32[8,2,16,128]{3,2,1,0:T(8,128)S(1)}, f32[8,2,16,128]{3,2,1,0:T(8,128)S(1)}, u32[]{:S(2)}, u32[]{:S(2)}) collective-permute-start(f32[8,2,16,128]{3,2,1,0:T(8,128)S(1)} %get-tuple-element.66), channel_id=1, source_target_pairs={{0,16},{8,24},{16,0},{24,8},{32,48},{40,56},{48,32},{56,40},{64,80... | collective-permute-start | bytes 393224 | tf_op jit(solution)/shard_map/ppermute | solution.py:16
  200.4 9.1 %collective-permute-start.7 = (f32[8,2,16,128]{3,2,1,0:T(8,128)S(1)}, f32[8,2,16,128]{3,2,1,0:T(8,128)S(1)}, u32[]{:S(2)}, u32[]{:S(2)}) collective-permute-start(f32[8,2,16,128]{3,2,1,0:T(8,128)S(1)} %get-tuple-element.67), channel_id=1, source_target_pairs={{0,8},{8,16},{16,24},{24,0},{32,40},{40,48},{48,56},{56,32},{64,72... | collective-permute-start | bytes 393224 | tf_op jit(solution)/shard_map/ppermute | solution.py:16
  216.0 26.1 %shard_map.59 = f32[8,128]{1,0:T(8,128)} custom-call(f32[8,128]{1,0:T(8,128)} %broadcast_in_dim.29.val_ref), custom_call_target="tpu_custom_call" | custom-call | tf_op jit(solution)/shard_map/pallas_call | solution.py:129
  (266 shorter events, 83.2 us)
Async XLA Ops:
  1.9 38.4 %copy-start.61 = (bf16[24]{0:T(256)(128)(2,1)S(1)}, bf16[24]{0:T(256)(128)(2,1)}, u32[]{:S(2)}) copy-start(bf16[24]{0:T(256)(128)(2,1)} %constant.142.clone.1) | copy-start | bytes 148
  2.0 37.6 %collective-permute-start.2 = (bf16[8,2,24,128]{3,2,1,0:T(8,128)(2,1)S(1)}, bf16[8,2,24,128]{3,2,1,0:T(8,128)(2,1)S(1)}, u32[]{:S(2)}, u32[]{:S(2)}) collective-permute-start(bf16[8,2,24,128]{3,2,1,0:T(8,128)(2,1)S(1)} %get-tuple-element.104), channel_id=1, source_target_pairs={{0,24},{8,0},{16,8},{24,16},{32,56},{40,32},{48,40},{56,48},{64,88... | collective-permute-start | bytes 294920 | tf_op jit(solution)/shard_map/ppermute | solution.py:16
  10.8 28.8 %collective-permute-start.1 = (bf16[8,2,24,128]{3,2,1,0:T(8,128)(2,1)S(1)}, bf16[8,2,24,128]{3,2,1,0:T(8,128)(2,1)S(1)}, u32[]{:S(2)}, u32[]{:S(2)}) collective-permute-start(bf16[8,2,24,128]{3,2,1,0:T(8,128)(2,1)S(1)} %get-tuple-element.102), channel_id=1, source_target_pairs={{0,16},{8,24},{16,0},{24,8},{32,48},{40,56},{48,32},{56,40},{64,80... | collective-permute-start | bytes 294920 | tf_op jit(solution)/shard_map/ppermute | solution.py:16
  20.8 18.7 %collective-permute-start = (bf16[8,2,24,128]{3,2,1,0:T(8,128)(2,1)S(1)}, bf16[8,2,24,128]{3,2,1,0:T(8,128)(2,1)S(1)}, u32[]{:S(2)}, u32[]{:S(2)}) collective-permute-start(bf16[8,2,24,128]{3,2,1,0:T(8,128)(2,1)S(1)} %get-tuple-element.103), channel_id=1, source_target_pairs={{0,8},{8,16},{16,24},{24,0},{32,40},{40,48},{48,56},{56,32},{64,72... | collective-permute-start | bytes 294920 | tf_op jit(solution)/shard_map/ppermute | solution.py:16
  40.4 17.9 %collective-permute-start.6 = (bf16[8,4,2,24,128]{4,3,1,0,2:T(8,128)(2,1)S(1)}, bf16[8,4,2,24,128]{4,3,1,0,2:T(8,128)(2,1)S(1)}, u32[]{:S(2)}, u32[]{:S(2)}) collective-permute-start(bf16[8,4,2,24,128]{4,3,1,0,2:T(8,128)(2,1)S(1)} %get-tuple-element.3), channel_id=1, source_target_pairs={{0,64},{8,72},{16,80},{24,88},{32,96},{40,104},{48,112},{56,120},{... | collective-permute-start | bytes 1179656 | tf_op jit(solution)/shard_map/ppermute | solution.py:16
  45.1 29.5 %collective-permute-start.5 = (bf16[8,4,2,24,128]{4,3,1,0,2:T(8,128)(2,1)S(1)}, bf16[8,4,2,24,128]{4,3,1,0,2:T(8,128)(2,1)S(1)}, u32[]{:S(2)}, u32[]{:S(2)}) collective-permute-start(bf16[8,4,2,24,128]{4,3,1,0,2:T(8,128)(2,1)S(1)} %get-tuple-element.3), channel_id=1, source_target_pairs={{0,448},{8,456},{16,464},{24,472},{32,480},{40,488},{48,496},{56,5... | collective-permute-start | bytes 1179656 | tf_op jit(solution)/shard_map/ppermute | solution.py:16
  49.4 21.0 %collective-permute-start.3 = (bf16[8,4,2,24,128]{4,3,1,0,2:T(8,128)(2,1)S(1)}, bf16[8,4,2,24,128]{4,3,1,0,2:T(8,128)(2,1)S(1)}, u32[]{:S(2)}, u32[]{:S(2)}) collective-permute-start(bf16[8,4,2,24,128]{4,3,1,0,2:T(8,128)(2,1)S(1)} %get-tuple-element.3), channel_id=1, source_target_pairs={{0,480},{8,488},{16,496},{24,504},{32,0},{40,8},{48,16},{56,24},{6... | collective-permute-start | bytes 1179656 | tf_op jit(solution)/shard_map/ppermute | solution.py:16
  54.1 18.2 %collective-permute-start.4 = (bf16[8,4,2,24,128]{4,3,1,0,2:T(8,128)(2,1)S(1)}, bf16[8,4,2,24,128]{4,3,1,0,2:T(8,128)(2,1)S(1)}, u32[]{:S(2)}, u32[]{:S(2)}) collective-permute-start(bf16[8,4,2,24,128]{4,3,1,0,2:T(8,128)(2,1)S(1)} %get-tuple-element.3), channel_id=1, source_target_pairs={{0,32},{8,40},{16,48},{24,56},{32,64},{40,72},{48,80},{56,88},{64,... | collective-permute-start | bytes 1179656 | tf_op jit(solution)/shard_map/ppermute | solution.py:16
  56.3 3.0 %copy-start.9 = (bf16[8,4,2,24,128]{4,3,2,1,0:T(8,128)(2,1)}, bf16[8,4,2,24,128]{4,3,2,1,0:T(8,128)(2,1)S(1)}, u32[]{:S(2)}) copy-start(bf16[8,4,2,24,128]{4,3,2,1,0:T(8,128)(2,1)S(1)} %copy.13) | copy-start | bytes 1179652
  74.6 3.9 %copy-start = (bf16[8,4,2,24,128]{4,3,1,0,2:T(8,128)(2,1)}, bf16[8,4,2,24,128]{4,3,1,0,2:T(8,128)(2,1)S(1)}, u32[]{:S(2)}) copy-start(bf16[8,4,2,24,128]{4,3,1,0,2:T(8,128)(2,1)S(1)} %collective-permute-done.5) | copy-start | bytes 1179652
  89.4 7.1 %slice-start = ((bf16[8,4,2,24,128]{4,3,1,0,2:T(8,128)(2,1)}), bf16[8,4,2,16,128]{4,3,1,0,2:T(8,128)(2,1)S(1)}, s32[]{:S(2)}) async-start(bf16[8,4,2,24,128]{4,3,1,0,2:T(8,128)(2,1)} %copy-done), calls=%async_computation | async-start | bytes 524288 | tf_op jit(solution)/shard_map/slice | solution.py:60
  94.4 6.2 %copy-start.5 = (f32[4,128,128]{2,1,0:T(8,128)S(1)}, f32[4,128,128]{2,1,0:T(8,128)}, u32[]{:S(2)}) copy-start(f32[4,128,128]{2,1,0:T(8,128)} %get-tuple-element.149) | copy-start | bytes 786436
  101.4 9.9 %copy-start.4 = (f32[4,128,128]{2,1,0:T(8,128)S(1)}, f32[4,128,128]{2,1,0:T(8,128)}, u32[]{:S(2)}) copy-start(f32[4,128,128]{2,1,0:T(8,128)} %get-tuple-element.117) | copy-start | bytes 786436
  114.2 10.2 %copy-start.8 = (f32[4,128,128]{2,1,0:T(8,128)S(1)}, f32[4,128,128]{2,1,0:T(8,128)}, u32[]{:S(2)}) copy-start(f32[4,128,128]{2,1,0:T(8,128)} %get-tuple-element.147) | copy-start | bytes 786436
  127.3 10.0 %copy-start.7 = (f32[4,128,128]{2,1,0:T(8,128)S(1)}, f32[4,128,128]{2,1,0:T(8,128)}, u32[]{:S(2)}) copy-start(f32[4,128,128]{2,1,0:T(8,128)} %get-tuple-element.145) | copy-start | bytes 786436
  140.2 9.0 %copy-start.6 = (f32[4,128,128]{2,1,0:T(8,128)S(1)}, f32[4,128,128]{2,1,0:T(8,128)}, u32[]{:S(2)}) copy-start(f32[4,128,128]{2,1,0:T(8,128)} %get-tuple-element.111) | copy-start | bytes 786436
  151.2 2.5 %copy-start.51 = (bf16[8,4,24,128]{3,2,1,0:T(8,128)(2,1)S(1)}, bf16[8,4,24,128]{3,2,1,0:T(8,128)(2,1)}, u32[]{:S(2)}) copy-start(bf16[8,4,24,128]{3,2,1,0:T(8,128)(2,1)} %get-tuple-element.182) | copy-start | bytes 589828
  151.2 2.5 %copy-start.52 = (bf16[8,4,24,128]{3,2,1,0:T(8,128)(2,1)S(1)}, bf16[8,4,24,128]{3,2,1,0:T(8,128)(2,1)}, u32[]{:S(2)}) copy-start(bf16[8,4,24,128]{3,2,1,0:T(8,128)(2,1)} %get-tuple-element.183) | copy-start | bytes 589828
  152.0 8.9 %copy-start.11 = (bf16[8,4,2,24,128]{4,3,1,0,2:T(8,128)(2,1)S(1)}, bf16[8,4,2,24,128]{4,3,1,0,2:T(8,128)(2,1)}, u32[]{:S(2)}) copy-start(bf16[8,4,2,24,128]{4,3,1,0,2:T(8,128)(2,1)} %get-tuple-element.48) | copy-start | bytes 1179652
  152.0 9.0 %copy-start.3 = (f32[4,128,128]{2,1,0:T(8,128)S(1)}, f32[4,128,128]{2,1,0:T(8,128)}, u32[]{:S(2)}) copy-start(f32[4,128,128]{2,1,0:T(8,128)} %get-tuple-element.143) | copy-start | bytes 786436
  163.1 3.3 %copy-start.10 = (bf16[8,4,2,24,128]{4,3,2,1,0:T(8,128)(2,1)S(1)}, bf16[8,4,2,24,128]{4,3,2,1,0:T(8,128)(2,1)}, u32[]{:S(2)}) copy-start(bf16[8,4,2,24,128]{4,3,2,1,0:T(8,128)(2,1)} %copy-done.9) | copy-start | bytes 1179652
  164.0 10.1 %copy-start.2 = (f32[4,128,128]{2,1,0:T(8,128)S(1)}, f32[4,128,128]{2,1,0:T(8,128)}, u32[]{:S(2)}) copy-start(f32[4,128,128]{2,1,0:T(8,128)} %get-tuple-element.141) | copy-start | bytes 786436
  177.0 9.0 %copy-start.1 = (f32[4,128,128]{2,1,0:T(8,128)S(1)}, f32[4,128,128]{2,1,0:T(8,128)}, u32[]{:S(2)}) copy-start(f32[4,128,128]{2,1,0:T(8,128)} %get-tuple-element.105) | copy-start | bytes 786436
  188.1 2.5 %copy-start.38 = (f32[8,4,1,16,128]{4,3,2,1,0:T(8,128)S(1)}, f32[8,4,1,16,128]{4,3,2,1,0:T(8,128)}, u32[]{:S(2)}) copy-start(f32[8,4,1,16,128]{4,3,2,1,0:T(8,128)} %get-tuple-element.16) | copy-start | bytes 786436
  188.1 2.6 %copy-start.39 = (f32[8,4,1,16,128]{4,3,2,1,0:T(8,128)S(1)}, f32[8,4,1,16,128]{4,3,2,1,0:T(8,128)}, u32[]{:S(2)}) copy-start(f32[8,4,1,16,128]{4,3,2,1,0:T(8,128)} %get-tuple-element.17) | copy-start | bytes 786436
  188.1 2.7 %copy-start.40 = (f32[8,4,1,16,128]{4,3,2,1,0:T(8,128)S(1)}, f32[8,4,1,16,128]{4,3,2,1,0:T(8,128)}, u32[]{:S(2)}) copy-start(f32[8,4,1,16,128]{4,3,2,1,0:T(8,128)} %get-tuple-element.14) | copy-start | bytes 786436
  188.2 2.7 %copy-start.41 = (f32[8,4,1,16,128]{4,3,2,1,0:T(8,128)S(1)}, f32[8,4,1,16,128]{4,3,2,1,0:T(8,128)}, u32[]{:S(2)}) copy-start(f32[8,4,1,16,128]{4,3,2,1,0:T(8,128)} %get-tuple-element.15) | copy-start | bytes 786436
  188.2 2.8 %copy-start.42 = (f32[8,4,1,16,128]{4,3,2,1,0:T(8,128)S(1)}, f32[8,4,1,16,128]{4,3,2,1,0:T(8,128)}, u32[]{:S(2)}) copy-start(f32[8,4,1,16,128]{4,3,2,1,0:T(8,128)} %get-tuple-element.12) | copy-start | bytes 786436
  188.2 2.9 %copy-start.43 = (f32[8,4,1,16,128]{4,3,2,1,0:T(8,128)S(1)}, f32[8,4,1,16,128]{4,3,2,1,0:T(8,128)}, u32[]{:S(2)}) copy-start(f32[8,4,1,16,128]{4,3,2,1,0:T(8,128)} %get-tuple-element.13) | copy-start | bytes 786436
  192.1 51.8 %collective-permute-start.9 = (f32[8,2,16,128]{3,2,1,0:T(8,128)S(1)}, f32[8,2,16,128]{3,2,1,0:T(8,128)S(1)}, u32[]{:S(2)}, u32[]{:S(2)}) collective-permute-start(f32[8,2,16,128]{3,2,1,0:T(8,128)S(1)} %get-tuple-element.65), channel_id=1, source_target_pairs={{0,24},{8,0},{16,8},{24,16},{32,56},{40,32},{48,40},{56,48},{64,88... | collective-permute-start | bytes 393224 | tf_op jit(solution)/shard_map/ppermute | solution.py:16
  194.4 49.5 %collective-permute-start.8 = (f32[8,2,16,128]{3,2,1,0:T(8,128)S(1)}, f32[8,2,16,128]{3,2,1,0:T(8,128)S(1)}, u32[]{:S(2)}, u32[]{:S(2)}) collective-permute-start(f32[8,2,16,128]{3,2,1,0:T(8,128)S(1)} %get-tuple-element.66), channel_id=1, source_target_pairs={{0,16},{8,24},{16,0},{24,8},{32,48},{40,56},{48,32},{56,40},{64,80... | collective-permute-start | bytes 393224 | tf_op jit(solution)/shard_map/ppermute | solution.py:16
  200.4 43.5 %collective-permute-start.7 = (f32[8,2,16,128]{3,2,1,0:T(8,128)S(1)}, f32[8,2,16,128]{3,2,1,0:T(8,128)S(1)}, u32[]{:S(2)}, u32[]{:S(2)}) collective-permute-start(f32[8,2,16,128]{3,2,1,0:T(8,128)S(1)} %get-tuple-element.67), channel_id=1, source_target_pairs={{0,8},{8,16},{16,24},{24,0},{32,40},{40,48},{48,56},{56,32},{64,72... | collective-permute-start | bytes 393224 | tf_op jit(solution)/shard_map/ppermute | solution.py:16
  (41 other events, 81.0 us)

commit v5 on v3

--- a/solution.py
+++ b/solution.py
@@ -9,6 +9,7 @@
 F = 256
 W = 16
 BAND = 1024
+CHUNKS = 2
 GROUP = 4
 
 
@@ -145,52 +146,52 @@
     return out[0, 0]
 
 
-def shards(spectra, model, channel_ok, limits, mesh_shape):
+def shards(spectra, model, channel_ok, limits, mesh_shape, n_chunks):
     payload = jnp.concatenate([spectra, model], axis=2)
     fl, _, rows, bw = payload.shape
     peers = lax.axis_size("chan")
     me = lax.axis_index("chan")
     j = me % GROUP
     column = me // GROUP
-    sub = fl // GROUP
+    sub = fl // GROUP // n_chunks
     band_blocks = BAND // bw
     halo_cols = -(-band_blocks // GROUP)
     nblk = GROUP * (1 + halo_cols)
-
-    chunks = payload.reshape(GROUP, sub, 2, rows, bw)
-    mine = exchange(chunks, j, peers)
-    own = jnp.transpose(mine, (1, 0, 2, 3, 4))
-
-    parts = [own] + [permute(own, shift_pairs(peers, -GROUP * h)) for h in range(1, halo_cols + 1)]
-    ext = jnp.concatenate(parts, axis=1)
 
     ok_all = channel_ok.astype(jnp.float32)
     ok_wide = jnp.concatenate([ok_all, ok_all[: nblk * bw]])
     ok_ext = lax.dynamic_slice_in_dim(ok_wide, column * GROUP * bw, nblk * bw).reshape(nblk, bw)
     lim = lax.dynamic_slice_in_dim(limits, column * GROUP, GROUP)
 
-    first = ext[:, :GROUP]
-    ok_first = ok_ext[:GROUP]
+    pieces = payload.reshape(GROUP, n_chunks, sub, 2, rows, bw)
     misfit_sum = jnp.zeros((), jnp.float32)
-    near_acc = jnp.zeros((sub, GROUP, 2, W, bw), jnp.float32)
-    far_acc = jnp.zeros((sub, nblk, 2, W, bw), jnp.float32)
-    for s in range(band_blocks + 1):
-        second = ext[:, s : s + GROUP]
-        piece_loss, near_terms, far_terms = pair_terms(
-            first, second, ok_first, ok_ext[s : s + GROUP], lim, s
-        )
-        misfit_sum = misfit_sum + piece_loss
-        near_acc = near_acc + near_terms
-        far_acc = far_acc.at[:, s : s + GROUP].add(far_terms)
+    outs = []
+    for c in range(n_chunks):
+        mine = exchange(pieces[:, c], j, peers)
+        own = jnp.transpose(mine, (1, 0, 2, 3, 4))
+        parts = [own] + [permute(own, shift_pairs(peers, -GROUP * h)) for h in range(1, halo_cols + 1)]
+        ext = jnp.concatenate(parts, axis=1)
+
+        first = ext[:, :GROUP]
+        ok_first = ok_ext[:GROUP]
+        near_acc = jnp.zeros((sub, GROUP, 2, W, bw), jnp.float32)
+        far_acc = jnp.zeros((sub, nblk, 2, W, bw), jnp.float32)
+        for s in range(band_blocks + 1):
+            second = ext[:, s : s + GROUP]
+            piece_loss, near_terms, far_terms = pair_terms(
+                first, second, ok_first, ok_ext[s : s + GROUP], lim, s
+            )
+            misfit_sum = misfit_sum + piece_loss
+            near_acc = near_acc + near_terms
+            far_acc = far_acc.at[:, s : s + GROUP].add(far_terms)
+        adj = near_acc + far_acc[:, :GROUP]
+        for h in range(1, halo_cols + 1):
+            adj = adj + permute(far_acc[:, h * GROUP : (h + 1) * GROUP], shift_pairs(peers, GROUP * h))
+        adj = adj * (1.0 / W)
+        blocks = jnp.transpose(adj, (1, 0, 2, 3, 4))
+        outs.append(exchange(blocks, j, peers))
     misfit_total = global_sum(misfit_sum, mesh_shape)
-    adj = near_acc + far_acc[:, :GROUP]
-    for h in range(1, halo_cols + 1):
-        adj = adj + permute(far_acc[:, h * GROUP : (h + 1) * GROUP], shift_pairs(peers, GROUP * h))
-    adj = adj * (1.0 / W)
-
-    blocks = jnp.transpose(adj, (1, 0, 2, 3, 4))
-    back = exchange(blocks, j, peers)
-    adjoint = back.reshape(fl, 2, W, bw)
+    adjoint = jnp.stack(outs, axis=1).reshape(fl, 2, W, bw)
 
     misfit = misfit_total / float(F * bw * peers * BAND)
     return adjoint, misfit
@@ -199,7 +200,7 @@
 def solution(mesh):
     mesh_shape = dict(mesh.shape)
     return jax.shard_map(
-        lambda *a: shards(*a, mesh_shape),
+        lambda *a: shards(*a, mesh_shape, CHUNKS),
         mesh=mesh,
         in_specs=(P("freq", None, None, "chan"), P("freq", None, None, "chan"), P(), P()),
         out_specs=(P("freq", None, None, "chan"), P()),

time: 181 us -> 237 us (1.31)
  the two profiles are of different devices: /device:TPU:1 before, /device:TPU:32 now
where the time goes in v5:
time: 237 us; the launch traced here: 236 us
  starting transfers between devices  115 us (49%)
  Pallas kernels  32.7 us (14%)
  matrix products  31.7 us (13%)
  other arithmetic  18.2 us (8%)
  waiting for transfers between devices  17.1 us (7%)
  between operations  15.4 us (6%)
  local copies, waits for them, and re-layouts  6.25 us (3%)
    ppermute x20, starting transfers between devices, permute(): return lax.ppermute(x, 'chan', pairs)  115 us
    pallas_call x1, Pallas kernels, global_sum(): pl.pallas_call(functools.partial(sum_kernel, n_col, n_f), out_shape=jax.S...  32.7 us
    dot_general x18, matrix products, pair_terms(): jnp.einsum('fbxrc,fbrd->fbxcd', stacked_left, right_rows, preferred_eleme...  17.6 us
    ppermute x20, waiting for transfers between devices, permute(): return lax.ppermute(x, 'chan', pairs)  17.1 us
    dot_general x18, matrix products, pair_terms(): jnp.einsum('fbxcd,fbvd->fbxvc', rounded, far_spec, preferred_element_type...  8.64 us
    sub x18, other arithmetic, pair_terms(): first_real = toward[:, :, 0, :W] - toward[:, :, 1, W:]  8.33 us
    dot_general x18, matrix products, pair_terms(): jnp.einsum('fbxcd,fbvc->fbxvd', rounded, near_spec, preferred_element_typ...  5.52 us
  transfers between devices with their start and end apart: 20, of which 5 were waited for; matrix products, arithmetic and copies ran while one was open for 5% of the time, Pallas kernels for 14%

profile of v5, /device:TPU:32, one launch (start us, length us, event | category | flops | bytes accessed | tf_op | source)
XLA Modules:
  0.0 236.5 jit_solution(17980343152923995038)
XLA Ops:
  1.9 14.8 %collective-permute-start.1 = (bf16[4,2,24,128]{3,2,1,0:T(8,128)(2,1)S(1)}, bf16[4,2,24,128]{3,2,1,0:T(8,128)(2,1)S(1)}, u32[]{:S(2)}, u32[]{:S(2)}) collective-permute-start(bf16[4,2,24,128]{3,2,1,0:T(8,128)(2,1)S(1)} %get-tuple-element.360), channel_id=1, source_target_pairs={{0,16},{8,24},{16,0},{24,8},{32,48},{40,56},{48,32},{56,40},{64,80... | collective-permute-start | bytes 147464 | tf_op jit(solution)/shard_map/ppermute | solution.py:17
  16.8 1.9 collective-permute-start
  18.7 12.4 %collective-permute-start.2 = (bf16[4,2,24,128]{3,2,1,0:T(8,128)(2,1)S(1)}, bf16[4,2,24,128]{3,2,1,0:T(8,128)(2,1)S(1)}, u32[]{:S(2)}, u32[]{:S(2)}) collective-permute-start(bf16[4,2,24,128]{3,2,1,0:T(8,128)(2,1)S(1)} %get-tuple-element.362), channel_id=1, source_target_pairs={{0,24},{8,0},{16,8},{24,16},{32,56},{40,32},{48,40},{56,48},{64,88... | collective-permute-start | bytes 147464 | tf_op jit(solution)/shard_map/ppermute | solution.py:17
  31.2 1.9 collective-permute-start.11
  33.1 2.1 collective-permute-start.10
  36.6 12.2 %collective-permute-start.12 = (bf16[4,2,24,128]{3,2,1,0:T(8,128)(2,1)S(1)}, bf16[4,2,24,128]{3,2,1,0:T(8,128)(2,1)S(1)}, u32[]{:S(2)}, u32[]{:S(2)}) collective-permute-start(bf16[4,2,24,128]{3,2,1,0:T(8,128)(2,1)S(1)} %get-tuple-element.371), channel_id=1, source_target_pairs={{0,24},{8,0},{16,8},{24,16},{32,56},{40,32},{48,40},{56,48},{64,88... | collective-permute-start | bytes 147464 | tf_op jit(solution)/shard_map/ppermute | solution.py:17
  51.5 7.1 %collective-permute-start.3 = (bf16[4,4,2,24,128]{4,3,1,0,2:T(8,128)(2,1)S(1)}, bf16[4,4,2,24,128]{4,3,1,0,2:T(8,128)(2,1)S(1)}, u32[]{:S(2)}, u32[]{:S(2)}) collective-permute-start(bf16[4,4,2,24,128]{4,3,1,0,2:T(8,128)(2,1)S(1)} %get-tuple-element.241), channel_id=1, source_target_pairs={{0,480},{8,488},{16,496},{24,504},{32,0},{40,8},{48,16},{56,24},{6... | collective-permute-start | bytes 589832 | tf_op jit(solution)/shard_map/ppermute | solution.py:17
  58.6 2.7 %collective-permute-start.4 = (bf16[4,4,2,24,128]{4,3,1,0,2:T(8,128)(2,1)S(1)}, bf16[4,4,2,24,128]{4,3,1,0,2:T(8,128)(2,1)S(1)}, u32[]{:S(2)}, u32[]{:S(2)}) collective-permute-start(bf16[4,4,2,24,128]{4,3,1,0,2:T(8,128)(2,1)S(1)} %get-tuple-element.241), channel_id=1, source_target_pairs={{0,448},{8,456},{16,464},{24,472},{32,480},{40,488},{48,496},{56,5... | collective-permute-start | bytes 589832 | tf_op jit(solution)/shard_map/ppermute | solution.py:17
  61.3 3.0 %collective-permute-start.13 = (bf16[4,4,2,24,128]{4,3,1,0,2:T(8,128)(2,1)S(1)}, bf16[4,4,2,24,128]{4,3,1,0,2:T(8,128)(2,1)S(1)}, u32[]{:S(2)}, u32[]{:S(2)}) collective-permute-start(bf16[4,4,2,24,128]{4,3,1,0,2:T(8,128)(2,1)S(1)} %get-tuple-element.391), channel_id=1, source_target_pairs={{0,480},{8,488},{16,496},{24,504},{32,0},{40,8},{48,16},{56,24},{6... | collective-permute-start | bytes 589832 | tf_op jit(solution)/shard_map/ppermute | solution.py:17
  64.4 4.1 %collective-permute-start.14 = (bf16[4,4,2,24,128]{4,3,1,0,2:T(8,128)(2,1)S(1)}, bf16[4,4,2,24,128]{4,3,1,0,2:T(8,128)(2,1)S(1)}, u32[]{:S(2)}, u32[]{:S(2)}) collective-permute-start(bf16[4,4,2,24,128]{4,3,1,0,2:T(8,128)(2,1)S(1)} %get-tuple-element.391), channel_id=1, source_target_pairs={{0,448},{8,456},{16,464},{24,472},{32,480},{40,488},{48,496},{56,5... | collective-permute-start | bytes 589832 | tf_op jit(solution)/shard_map/ppermute | solution.py:17
  71.1 2.4 %collective-permute-done.14 = bf16[4,4,2,24,128]{4,3,1,0,2:T(8,128)(2,1)S(1)} collective-permute-done((bf16[4,4,2,24,128]{4,3,1,0,2:T(8,128)(2,1)S(1)}, bf16[4,4,2,24,128]{4,3,1,0,2:T(8,128)(2,1)S(1)}, u32[]{:S(2)}, u32[]{:S(2)}) %collective-permute-start.14) | collective-permute-done | bytes 196640 | tf_op jit(solution)/shard_map/ppermute | solution.py:17
  77.7 1.5 multiply_reduce_fusion.3
  81.4 1.5 multiply_reduce_fusion.2
  85.2 1.5 multiply_reduce_fusion.1
  89.5 1.5 multiply_reduce_fusion.6
  99.1 1.5 multiply_reduce_fusion.5
  104.2 1.5 multiply_reduce_fusion
  109.4 1.5 multiply_reduce_fusion.4
  114.0 5.5 %collective-permute-start.15 = (f32[4,4,2,16,128]{4,3,2,1,0:T(8,128)}, f32[4,4,2,16,128]{4,3,2,1,0:T(8,128)}, u32[]{:S(2)}, u32[]{:S(2)}) collective-permute-start(f32[4,4,2,16,128]{4,3,2,1,0:T(8,128)} %get-tuple-element.246), channel_id=1, source_target_pairs={{0,32},{8,40},{16,48},{24,56},{32,64},{40,72},{48,80},{56,88},{64,... | collective-permute-start | bytes 786440 | tf_op jit(solution)/shard_map/ppermute | solution.py:17
  119.5 5.0 %collective-permute-start.16 = (f32[4,4,2,16,128]{4,3,2,1,0:T(8,128)}, f32[4,4,2,16,128]{4,3,2,1,0:T(8,128)}, u32[]{:S(2)}, u32[]{:S(2)}) collective-permute-start(f32[4,4,2,16,128]{4,3,2,1,0:T(8,128)} %get-tuple-element.247), channel_id=1, source_target_pairs={{0,64},{8,72},{16,80},{24,88},{32,96},{40,104},{48,112},{56,120},{... | collective-permute-start | bytes 786440 | tf_op jit(solution)/shard_map/ppermute | solution.py:17
  126.8 1.9 collective-permute-start.5
  128.7 2.2 collective-permute-start.6
  143.5 32.7 %shard_map.59 = f32[8,128]{1,0:T(8,128)} custom-call(f32[8,128]{1,0:T(8,128)} %broadcast_in_dim.17.val_ref), custom_call_target="tpu_custom_call" | custom-call | tf_op jit(solution)/shard_map/pallas_call | solution.py:130
  178.2 1.8 fusion.5
  181.6 7.5 %collective-permute-start.19 = (f32[4,2,16,128]{3,2,1,0:T(8,128)S(1)}, f32[4,2,16,128]{3,2,1,0:T(8,128)S(1)}, u32[]{:S(2)}, u32[]{:S(2)}) collective-permute-start(f32[4,2,16,128]{3,2,1,0:T(8,128)S(1)} %get-tuple-element.351), channel_id=1, source_target_pairs={{0,24},{8,0},{16,8},{24,16},{32,56},{40,32},{48,40},{56,48},{64,88... | collective-permute-start | bytes 196616 | tf_op jit(solution)/shard_map/ppermute | solution.py:17
  189.2 5.7 %collective-permute-start.18 = (f32[4,2,16,128]{3,2,1,0:T(8,128)S(1)}, f32[4,2,16,128]{3,2,1,0:T(8,128)S(1)}, u32[]{:S(2)}, u32[]{:S(2)}) collective-permute-start(f32[4,2,16,128]{3,2,1,0:T(8,128)S(1)} %get-tuple-element.352), channel_id=1, source_target_pairs={{0,16},{8,24},{16,0},{24,8},{32,48},{40,56},{48,32},{56,40},{64,80... | collective-permute-start | bytes 196616 | tf_op jit(solution)/shard_map/ppermute | solution.py:17
  194.8 1.9 collective-permute-start.17
  196.8 12.4 %collective-permute-start.9 = (f32[4,2,16,128]{3,2,1,0:T(8,128)S(1)}, f32[4,2,16,128]{3,2,1,0:T(8,128)S(1)}, u32[]{:S(2)}, u32[]{:S(2)}) collective-permute-start(f32[4,2,16,128]{3,2,1,0:T(8,128)S(1)} %get-tuple-element.347), channel_id=1, source_target_pairs={{0,24},{8,0},{16,8},{24,16},{32,56},{40,32},{48,40},{56,48},{64,88... | collective-permute-start | bytes 196616 | tf_op jit(solution)/shard_map/ppermute | solution.py:17
  209.1 8.9 %collective-permute-start.8 = (f32[4,2,16,128]{3,2,1,0:T(8,128)S(1)}, f32[4,2,16,128]{3,2,1,0:T(8,128)S(1)}, u32[]{:S(2)}, u32[]{:S(2)}) collective-permute-start(f32[4,2,16,128]{3,2,1,0:T(8,128)S(1)} %get-tuple-element.348), channel_id=1, source_target_pairs={{0,16},{8,24},{16,0},{24,8},{32,48},{40,56},{48,32},{56,40},{64,80... | collective-permute-start | bytes 196616 | tf_op jit(solution)/shard_map/ppermute | solution.py:17
  218.1 1.9 collective-permute-start.7
  220.6 5.6 %collective-permute-done.8 = f32[4,2,16,128]{3,2,1,0:T(8,128)S(1)} collective-permute-done((f32[4,2,16,128]{3,2,1,0:T(8,128)S(1)}, f32[4,2,16,128]{3,2,1,0:T(8,128)S(1)}, u32[]{:S(2)}, u32[]{:S(2)}) %collective-permute-start.8) | collective-permute-done | bytes 65568 | tf_op jit(solution)/shard_map/ppermute | solution.py:17
  226.2 7.6 %collective-permute-done.7 = f32[4,2,16,128]{3,2,1,0:T(8,128)S(1)} collective-permute-done((f32[4,2,16,128]{3,2,1,0:T(8,128)S(1)}, f32[4,2,16,128]{3,2,1,0:T(8,128)S(1)}, u32[]{:S(2)}, u32[]{:S(2)}) %collective-permute-start.7) | collective-permute-done | bytes 65568 | tf_op jit(solution)/shard_map/ppermute | solution.py:17
  (254 shorter events, 45.6 us)
Async XLA Ops:
  0.6 35.1 %copy-start.8 = (s32[8192]{0:T(1024)S(1)}, s32[8192]{0:T(1024)}, u32[]{:S(2)}) copy-start(s32[8192]{0:T(1024)} %param.50) | copy-start | bytes 98308
  0.6 35.2 %copy-start.10 = (s32[64]{0:T(128)S(1)}, s32[64]{0:T(128)}, u32[]{:S(2)}) copy-start(s32[64]{0:T(128)} %param.51) | copy-start | bytes 772
  1.9 34.7 %collective-permute-start.1 = (bf16[4,2,24,128]{3,2,1,0:T(8,128)(2,1)S(1)}, bf16[4,2,24,128]{3,2,1,0:T(8,128)(2,1)S(1)}, u32[]{:S(2)}, u32[]{:S(2)}) collective-permute-start(bf16[4,2,24,128]{3,2,1,0:T(8,128)(2,1)S(1)} %get-tuple-element.360), channel_id=1, source_target_pairs={{0,16},{8,24},{16,0},{24,8},{32,48},{40,56},{48,32},{56,40},{64,80... | collective-permute-start | bytes 147464 | tf_op jit(solution)/shard_map/ppermute | solution.py:17
  16.8 32.1 %collective-permute-start = (bf16[4,2,24,128]{3,2,1,0:T(8,128)(2,1)S(1)}, bf16[4,2,24,128]{3,2,1,0:T(8,128)(2,1)S(1)}, u32[]{:S(2)}, u32[]{:S(2)}) collective-permute-start(bf16[4,2,24,128]{3,2,1,0:T(8,128)(2,1)S(1)} %get-tuple-element.361), channel_id=1, source_target_pairs={{0,8},{8,16},{16,24},{24,0},{32,40},{40,48},{48,56},{56,32},{64,72... | collective-permute-start | bytes 147464 | tf_op jit(solution)/shard_map/ppermute | solution.py:17
  18.7 30.1 %collective-permute-start.2 = (bf16[4,2,24,128]{3,2,1,0:T(8,128)(2,1)S(1)}, bf16[4,2,24,128]{3,2,1,0:T(8,128)(2,1)S(1)}, u32[]{:S(2)}, u32[]{:S(2)}) collective-permute-start(bf16[4,2,24,128]{3,2,1,0:T(8,128)(2,1)S(1)} %get-tuple-element.362), channel_id=1, source_target_pairs={{0,24},{8,0},{16,8},{24,16},{32,56},{40,32},{48,40},{56,48},{64,88... | collective-permute-start | bytes 147464 | tf_op jit(solution)/shard_map/ppermute | solution.py:17
  31.2 18.3 %collective-permute-start.11 = (bf16[4,2,24,128]{3,2,1,0:T(8,128)(2,1)S(1)}, bf16[4,2,24,128]{3,2,1,0:T(8,128)(2,1)S(1)}, u32[]{:S(2)}, u32[]{:S(2)}) collective-permute-start(bf16[4,2,24,128]{3,2,1,0:T(8,128)(2,1)S(1)} %get-tuple-element.369), channel_id=1, source_target_pairs={{0,16},{8,24},{16,0},{24,8},{32,48},{40,56},{48,32},{56,40},{64,80... | collective-permute-start | bytes 147464 | tf_op jit(solution)/shard_map/ppermute | solution.py:17
  33.1 16.4 %collective-permute-start.10 = (bf16[4,2,24,128]{3,2,1,0:T(8,128)(2,1)S(1)}, bf16[4,2,24,128]{3,2,1,0:T(8,128)(2,1)S(1)}, u32[]{:S(2)}, u32[]{:S(2)}) collective-permute-start(bf16[4,2,24,128]{3,2,1,0:T(8,128)(2,1)S(1)} %get-tuple-element.370), channel_id=1, source_target_pairs={{0,8},{8,16},{16,24},{24,0},{32,40},{40,48},{48,56},{56,32},{64,72... | collective-permute-start | bytes 147464 | tf_op jit(solution)/shard_map/ppermute | solution.py:17
  36.2 15.0 %copy-start.9 = (bf16[24]{0:T(256)(128)(2,1)S(1)}, bf16[24]{0:T(256)(128)(2,1)}, u32[]{:S(2)}) copy-start(bf16[24]{0:T(256)(128)(2,1)} %constant.550.clone.1) | copy-start | bytes 148
  36.6 14.0 %collective-permute-start.12 = (bf16[4,2,24,128]{3,2,1,0:T(8,128)(2,1)S(1)}, bf16[4,2,24,128]{3,2,1,0:T(8,128)(2,1)S(1)}, u32[]{:S(2)}, u32[]{:S(2)}) collective-permute-start(bf16[4,2,24,128]{3,2,1,0:T(8,128)(2,1)S(1)} %get-tuple-element.371), channel_id=1, source_target_pairs={{0,24},{8,0},{16,8},{24,16},{32,56},{40,32},{48,40},{56,48},{64,88... | collective-permute-start | bytes 147464 | tf_op jit(solution)/shard_map/ppermute | solution.py:17
  51.5 22.1 %collective-permute-start.3 = (bf16[4,4,2,24,128]{4,3,1,0,2:T(8,128)(2,1)S(1)}, bf16[4,4,2,24,128]{4,3,1,0,2:T(8,128)(2,1)S(1)}, u32[]{:S(2)}, u32[]{:S(2)}) collective-permute-start(bf16[4,4,2,24,128]{4,3,1,0,2:T(8,128)(2,1)S(1)} %get-tuple-element.241), channel_id=1, source_target_pairs={{0,480},{8,488},{16,496},{24,504},{32,0},{40,8},{48,16},{56,24},{6... | collective-permute-start | bytes 589832 | tf_op jit(solution)/shard_map/ppermute | solution.py:17
  58.6 15.2 %collective-permute-start.4 = (bf16[4,4,2,24,128]{4,3,1,0,2:T(8,128)(2,1)S(1)}, bf16[4,4,2,24,128]{4,3,1,0,2:T(8,128)(2,1)S(1)}, u32[]{:S(2)}, u32[]{:S(2)}) collective-permute-start(bf16[4,4,2,24,128]{4,3,1,0,2:T(8,128)(2,1)S(1)} %get-tuple-element.241), channel_id=1, source_target_pairs={{0,448},{8,456},{16,464},{24,472},{32,480},{40,488},{48,496},{56,5... | collective-permute-start | bytes 589832 | tf_op jit(solution)/shard_map/ppermute | solution.py:17
  61.3 9.6 %collective-permute-start.13 = (bf16[4,4,2,24,128]{4,3,1,0,2:T(8,128)(2,1)S(1)}, bf16[4,4,2,24,128]{4,3,1,0,2:T(8,128)(2,1)S(1)}, u32[]{:S(2)}, u32[]{:S(2)}) collective-permute-start(bf16[4,4,2,24,128]{4,3,1,0,2:T(8,128)(2,1)S(1)} %get-tuple-element.391), channel_id=1, source_target_pairs={{0,480},{8,488},{16,496},{24,504},{32,0},{40,8},{48,16},{56,24},{6... | collective-permute-start | bytes 589832 | tf_op jit(solution)/shard_map/ppermute | solution.py:17
  64.4 9.1 %collective-permute-start.14 = (bf16[4,4,2,24,128]{4,3,1,0,2:T(8,128)(2,1)S(1)}, bf16[4,4,2,24,128]{4,3,1,0,2:T(8,128)(2,1)S(1)}, u32[]{:S(2)}, u32[]{:S(2)}) collective-permute-start(bf16[4,4,2,24,128]{4,3,1,0,2:T(8,128)(2,1)S(1)} %get-tuple-element.391), channel_id=1, source_target_pairs={{0,448},{8,456},{16,464},{24,472},{32,480},{40,488},{48,496},{56,5... | collective-permute-start | bytes 589832 | tf_op jit(solution)/shard_map/ppermute | solution.py:17
  114.0 64.2 %collective-permute-start.15 = (f32[4,4,2,16,128]{4,3,2,1,0:T(8,128)}, f32[4,4,2,16,128]{4,3,2,1,0:T(8,128)}, u32[]{:S(2)}, u32[]{:S(2)}) collective-permute-start(f32[4,4,2,16,128]{4,3,2,1,0:T(8,128)} %get-tuple-element.246), channel_id=1, source_target_pairs={{0,32},{8,40},{16,48},{24,56},{32,64},{40,72},{48,80},{56,88},{64,... | collective-permute-start | bytes 786440 | tf_op jit(solution)/shard_map/ppermute | solution.py:17
  119.5 58.7 %collective-permute-start.16 = (f32[4,4,2,16,128]{4,3,2,1,0:T(8,128)}, f32[4,4,2,16,128]{4,3,2,1,0:T(8,128)}, u32[]{:S(2)}, u32[]{:S(2)}) collective-permute-start(f32[4,4,2,16,128]{4,3,2,1,0:T(8,128)} %get-tuple-element.247), channel_id=1, source_target_pairs={{0,64},{8,72},{16,80},{24,88},{32,96},{40,104},{48,112},{56,120},{... | collective-permute-start | bytes 786440 | tf_op jit(solution)/shard_map/ppermute | solution.py:17
  126.8 53.3 %collective-permute-start.5 = (f32[4,4,2,16,128]{4,3,2,1,0:T(8,128)}, f32[4,4,2,16,128]{4,3,2,1,0:T(8,128)}, u32[]{:S(2)}, u32[]{:S(2)}) collective-permute-start(f32[4,4,2,16,128]{4,3,2,1,0:T(8,128)} %get-tuple-element.244), channel_id=1, source_target_pairs={{0,32},{8,40},{16,48},{24,56},{32,64},{40,72},{48,80},{56,88},{64,... | collective-permute-start | bytes 786440 | tf_op jit(solution)/shard_map/ppermute | solution.py:17
  128.7 51.4 %collective-permute-start.6 = (f32[4,4,2,16,128]{4,3,2,1,0:T(8,128)}, f32[4,4,2,16,128]{4,3,2,1,0:T(8,128)}, u32[]{:S(2)}, u32[]{:S(2)}) collective-permute-start(f32[4,4,2,16,128]{4,3,2,1,0:T(8,128)} %get-tuple-element.245), channel_id=1, source_target_pairs={{0,64},{8,72},{16,80},{24,88},{32,96},{40,104},{48,112},{56,120},{... | collective-permute-start | bytes 786440 | tf_op jit(solution)/shard_map/ppermute | solution.py:17
  176.2 3.9 %copy-start = (f32[4,4,1,16,128]{4,3,2,1,0:T(8,128)S(1)}, f32[4,4,1,16,128]{4,3,2,1,0:T(8,128)}, u32[]{:S(2)}) copy-start(f32[4,4,1,16,128]{4,3,2,1,0:T(8,128)} %get-tuple-element.258) | copy-start | bytes 393220
  176.2 3.9 %copy-start.1 = (f32[4,4,1,16,128]{4,3,2,1,0:T(8,128)S(1)}, f32[4,4,1,16,128]{4,3,2,1,0:T(8,128)}, u32[]{:S(2)}) copy-start(f32[4,4,1,16,128]{4,3,2,1,0:T(8,128)} %get-tuple-element.259) | copy-start | bytes 393220
  176.2 3.9 %copy-start.2 = (f32[4,4,1,16,128]{4,3,2,1,0:T(8,128)S(1)}, f32[4,4,1,16,128]{4,3,2,1,0:T(8,128)}, u32[]{:S(2)}) copy-start(f32[4,4,1,16,128]{4,3,2,1,0:T(8,128)} %get-tuple-element.248) | copy-start | bytes 393220
  176.2 3.9 %copy-start.3 = (f32[4,4,1,16,128]{4,3,2,1,0:T(8,128)S(1)}, f32[4,4,1,16,128]{4,3,2,1,0:T(8,128)}, u32[]{:S(2)}) copy-start(f32[4,4,1,16,128]{4,3,2,1,0:T(8,128)} %get-tuple-element.249) | copy-start | bytes 393220
  176.2 3.9 %copy-start.4 = (f32[4,4,1,16,128]{4,3,2,1,0:T(8,128)S(1)}, f32[4,4,1,16,128]{4,3,2,1,0:T(8,128)}, u32[]{:S(2)}) copy-start(f32[4,4,1,16,128]{4,3,2,1,0:T(8,128)} %get-tuple-element.256) | copy-start | bytes 393220
  176.2 3.9 %copy-start.5 = (f32[4,4,1,16,128]{4,3,2,1,0:T(8,128)S(1)}, f32[4,4,1,16,128]{4,3,2,1,0:T(8,128)}, u32[]{:S(2)}) copy-start(f32[4,4,1,16,128]{4,3,2,1,0:T(8,128)} %get-tuple-element.257) | copy-start | bytes 393220
  176.2 3.9 %copy-start.6 = (f32[4,4,1,16,128]{4,3,2,1,0:T(8,128)S(1)}, f32[4,4,1,16,128]{4,3,2,1,0:T(8,128)}, u32[]{:S(2)}) copy-start(f32[4,4,1,16,128]{4,3,2,1,0:T(8,128)} %get-tuple-element.264) | copy-start | bytes 393220
  176.2 3.9 %copy-start.7 = (f32[4,4,1,16,128]{4,3,2,1,0:T(8,128)S(1)}, f32[4,4,1,16,128]{4,3,2,1,0:T(8,128)}, u32[]{:S(2)}) copy-start(f32[4,4,1,16,128]{4,3,2,1,0:T(8,128)} %get-tuple-element.265) | copy-start | bytes 393220
  181.6 36.4 %collective-permute-start.19 = (f32[4,2,16,128]{3,2,1,0:T(8,128)S(1)}, f32[4,2,16,128]{3,2,1,0:T(8,128)S(1)}, u32[]{:S(2)}, u32[]{:S(2)}) collective-permute-start(f32[4,2,16,128]{3,2,1,0:T(8,128)S(1)} %get-tuple-element.351), channel_id=1, source_target_pairs={{0,24},{8,0},{16,8},{24,16},{32,56},{40,32},{48,40},{56,48},{64,88... | collective-permute-start | bytes 196616 | tf_op jit(solution)/shard_map/ppermute | solution.py:17
  189.2 30.8 %collective-permute-start.18 = (f32[4,2,16,128]{3,2,1,0:T(8,128)S(1)}, f32[4,2,16,128]{3,2,1,0:T(8,128)S(1)}, u32[]{:S(2)}, u32[]{:S(2)}) collective-permute-start(f32[4,2,16,128]{3,2,1,0:T(8,128)S(1)} %get-tuple-element.352), channel_id=1, source_target_pairs={{0,16},{8,24},{16,0},{24,8},{32,48},{40,56},{48,32},{56,40},{64,80... | collective-permute-start | bytes 196616 | tf_op jit(solution)/shard_map/ppermute | solution.py:17
  194.8 25.2 %collective-permute-start.17 = (f32[4,2,16,128]{3,2,1,0:T(8,128)S(1)}, f32[4,2,16,128]{3,2,1,0:T(8,128)S(1)}, u32[]{:S(2)}, u32[]{:S(2)}) collective-permute-start(f32[4,2,16,128]{3,2,1,0:T(8,128)S(1)} %get-tuple-element.353), channel_id=1, source_target_pairs={{0,8},{8,16},{16,24},{24,0},{32,40},{40,48},{48,56},{56,32},{64,72... | collective-permute-start | bytes 196616 | tf_op jit(solution)/shard_map/ppermute | solution.py:17
  196.8 23.8 %collective-permute-start.9 = (f32[4,2,16,128]{3,2,1,0:T(8,128)S(1)}, f32[4,2,16,128]{3,2,1,0:T(8,128)S(1)}, u32[]{:S(2)}, u32[]{:S(2)}) collective-permute-start(f32[4,2,16,128]{3,2,1,0:T(8,128)S(1)} %get-tuple-element.347), channel_id=1, source_target_pairs={{0,24},{8,0},{16,8},{24,16},{32,56},{40,32},{48,40},{56,48},{64,88... | collective-permute-start | bytes 196616 | tf_op jit(solution)/shard_map/ppermute | solution.py:17
  209.1 17.1 %collective-permute-start.8 = (f32[4,2,16,128]{3,2,1,0:T(8,128)S(1)}, f32[4,2,16,128]{3,2,1,0:T(8,128)S(1)}, u32[]{:S(2)}, u32[]{:S(2)}) collective-permute-start(f32[4,2,16,128]{3,2,1,0:T(8,128)S(1)} %get-tuple-element.348), channel_id=1, source_target_pairs={{0,16},{8,24},{16,0},{24,8},{32,48},{40,56},{48,32},{56,40},{64,80... | collective-permute-start | bytes 196616 | tf_op jit(solution)/shard_map/ppermute | solution.py:17
  218.1 15.7 %collective-permute-start.7 = (f32[4,2,16,128]{3,2,1,0:T(8,128)S(1)}, f32[4,2,16,128]{3,2,1,0:T(8,128)S(1)}, u32[]{:S(2)}, u32[]{:S(2)}) collective-permute-start(f32[4,2,16,128]{3,2,1,0:T(8,128)S(1)} %get-tuple-element.349), channel_id=1, source_target_pairs={{0,8},{8,16},{16,24},{24,0},{32,40},{40,48},{48,56},{56,32},{64,72... | collective-permute-start | bytes 196616 | tf_op jit(solution)/shard_map/ppermute | solution.py:17

commit v6 on v3

--- a/solution.py
+++ b/solution.py
@@ -74,7 +74,8 @@
 
 MESH = pl.DeviceIdType.MESH
 
-def sum_kernel(n_col, n_f, val_ref, out_ref, slots1, slots2, stage, send1, recv1, send2, recv2):
+def tail_kernel(n_col, n_f, blocks_ref, val_ref, out_ref, sum_ref,
+                got, slots1, slots2, stage, send_o, recv_o, send1, recv1, send2, recv2):
     c = lax.axis_index("chan")
     f = lax.axis_index("freq")
     k = c // GROUP
@@ -88,6 +89,9 @@
     def dev2(col):
         return (col * GROUP + j, f)
 
+    def devg(b):
+        return (k * GROUP + b, f)
+
     barrier = pltpu.get_barrier_semaphore()
     for t in range(1, g1):
         pl.semaphore_signal(barrier, 1, device_id=dev1((me1 + t) % g1), device_id_type=MESH)
@@ -95,7 +99,7 @@
         pl.semaphore_signal(barrier, 1, device_id=dev2((k + t) % n_col), device_id_type=MESH)
     pl.semaphore_wait(barrier, g1 - 1 + n_col - 1)
 
-    def gather(src, slots, sends, recvs, count, mine, dev):
+    def start_gather(src, slots, sends, recvs, count, mine, dev):
         out = []
         for t in range(1, count):
             peer = (mine + t) % count
@@ -104,45 +108,72 @@
                 recv_sem=recvs.at[mine], device_id=dev(peer), device_id_type=MESH)
             cp.start()
             out.append(cp)
+        return out
+
+    def finish_gather(src, slots, sends, recvs, count, mine, dev, started):
         slots[mine] = src[...]
         for t in range(1, count):
             peer = (mine + t) % count
             pltpu.make_async_remote_copy(
                 src_ref=src, dst_ref=slots.at[peer], send_sem=sends.at[peer],
                 recv_sem=recvs.at[peer], device_id=dev(peer), device_id_type=MESH).wait_recv()
-        for cp in out:
+        for cp in started:
             cp.wait_send()
         acc = slots[0]
         for s in range(1, count):
             acc = acc + slots[s]
         return acc
 
-    stage[...] = gather(val_ref, slots1, send1, recv1, g1, me1, dev1)
-    out_ref[...] = gather(stage, slots2, send2, recv2, n_col, k, dev2)
-
-
-def global_sum(v, mesh_shape):
+    first = start_gather(val_ref, slots1, send1, recv1, g1, me1, dev1)
+    outgoing = []
+    for t in range(1, GROUP):
+        b = (j + t) % GROUP
+        cp = pltpu.make_async_remote_copy(
+            src_ref=blocks_ref.at[b], dst_ref=got.at[j], send_sem=send_o.at[b],
+            recv_sem=recv_o.at[j], device_id=devg(b), device_id_type=MESH)
+        cp.start()
+        outgoing.append(cp)
+    stage[...] = finish_gather(val_ref, slots1, send1, recv1, g1, me1, dev1, first)
+    second = start_gather(stage, slots2, send2, recv2, n_col, k, dev2)
+    sum_ref[...] = finish_gather(stage, slots2, send2, recv2, n_col, k, dev2, second)
+    got[j] = blocks_ref[j]
+    for t in range(1, GROUP):
+        b = (j + t) % GROUP
+        pltpu.make_async_remote_copy(
+            src_ref=blocks_ref.at[b], dst_ref=got.at[b], send_sem=send_o.at[b],
+            recv_sem=recv_o.at[b], device_id=devg(b), device_id_type=MESH).wait_recv()
+    for cp in outgoing:
+        cp.wait_send()
+    out_ref[...] = got[...]
+
+
+def finish(blocks, v, mesh_shape):
     n_col = mesh_shape["chan"] // GROUP
     n_f = mesh_shape["freq"]
     g1 = GROUP * n_f
     tile = jnp.full((8, 128), v, jnp.float32)
-    out = pl.pallas_call(
-        functools.partial(sum_kernel, n_col, n_f),
-        out_shape=jax.ShapeDtypeStruct((8, 128), jnp.float32),
-        in_specs=[pl.BlockSpec(memory_space=pltpu.VMEM)],
-        out_specs=pl.BlockSpec(memory_space=pltpu.VMEM),
+    vmem = pl.BlockSpec(memory_space=pltpu.VMEM)
+    out, total = pl.pallas_call(
+        functools.partial(tail_kernel, n_col, n_f),
+        out_shape=(jax.ShapeDtypeStruct(blocks.shape, blocks.dtype),
+                   jax.ShapeDtypeStruct((8, 128), jnp.float32)),
+        in_specs=[vmem, vmem],
+        out_specs=(vmem, vmem),
         scratch_shapes=[
+            pltpu.VMEM(blocks.shape, blocks.dtype),
             pltpu.VMEM((g1, 8, 128), jnp.float32),
             pltpu.VMEM((n_col, 8, 128), jnp.float32),
             pltpu.VMEM((8, 128), jnp.float32),
+            pltpu.SemaphoreType.DMA((GROUP,)),
+            pltpu.SemaphoreType.DMA((GROUP,)),
             pltpu.SemaphoreType.DMA((g1,)),
             pltpu.SemaphoreType.DMA((g1,)),
             pltpu.SemaphoreType.DMA((n_col,)),
             pltpu.SemaphoreType.DMA((n_col,)),
         ],
         compiler_params=pltpu.CompilerParams(collective_id=0, has_side_effects=True),
-    )(tile)
-    return out[0, 0]
+    )(blocks, tile)
+    return out, total[0, 0]
 
 
 def shards(spectra, model, channel_ok, limits, mesh_shape):
@@ -182,14 +213,13 @@
         misfit_sum = misfit_sum + piece_loss
         near_acc = near_acc + near_terms
         far_acc = far_acc.at[:, s : s + GROUP].add(far_terms)
-    misfit_total = global_sum(misfit_sum, mesh_shape)
     adj = near_acc + far_acc[:, :GROUP]
     for h in range(1, halo_cols + 1):
         adj = adj + permute(far_acc[:, h * GROUP : (h + 1) * GROUP], shift_pairs(peers, GROUP * h))
     adj = adj * (1.0 / W)
 
     blocks = jnp.transpose(adj, (1, 0, 2, 3, 4))
-    back = exchange(blocks, j, peers)
+    back, misfit_total = finish(blocks, misfit_sum, mesh_shape)
     adjoint = back.reshape(fl, 2, W, bw)
 
     misfit = misfit_total / float(F * bw * peers * BAND)

time: 181 us -> 185 us (1.022)
  Pallas kernels: 21.5 us -> 44.9 us
  starting transfers between devices: 57.7 us -> 39.4 us
  waiting for transfers between devices: 44.5 us -> 38.3 us
  other arithmetic: 9.68 us -> 14.5 us
    pallas_call x1, Pallas kernels: 21.5 us -> 44.9 us  [finish(): pl.pallas_call(functools.partial(tail_kernel, n_col, n_f), out_shape=(jax...]
    ppermute x10 -> x7, starting transfers between devices: 57.7 us -> 39.4 us  [permute(): return lax.ppermute(x, 'chan', pairs)]
    ppermute x10 -> x7, waiting for transfers between devices: 44.5 us -> 38.3 us  [permute(): return lax.ppermute(x, 'chan', pairs)]
    sub x9, other arithmetic: 0.6 us -> 4.65 us  [pair_terms(): first_real = toward[:, :, 0, :W] - toward[:, :, 1, W:]]
    unnamed x1 -> x39, local copies, waits for them, and re-layouts: 0.04 us -> 2.77 us
    transpose x1, other arithmetic: 0.59 us -> 2.52 us  [shards(): blocks = jnp.transpose(adj, (1, 0, 2, 3, 4))]
  transfers between devices with their start and end apart: 10 -> 7, of which waited for: 4 -> 4; matrix products, arithmetic and copies ran while one was open for 5% -> 4% of each run, Pallas kernels for 12% -> 0%
where the time goes in v6:
time: 185 us; the launch traced here: 184 us
  Pallas kernels  44.9 us (24%)
  starting transfers between devices  39.4 us (21%)
  waiting for transfers between devices  38.3 us (21%)
  matrix products  31.5 us (17%)
  other arithmetic  14.5 us (8%)
  between operations  9.16 us (5%)
  local copies, waits for them, and re-layouts  6.25 us (3%)
    pallas_call x1, Pallas kernels, finish(): pl.pallas_call(functools.partial(tail_kernel, n_col, n_f), out_shape=(jax...  44.9 us
    ppermute x7, starting transfers between devices, permute(): return lax.ppermute(x, 'chan', pairs)  39.4 us
    ppermute x7, waiting for transfers between devices, permute(): return lax.ppermute(x, 'chan', pairs)  38.3 us
    dot_general x9, matrix products, pair_terms(): jnp.einsum('fbxrc,fbrd->fbxcd', stacked_left, right_rows, preferred_eleme...  18.6 us
    dot_general x9, matrix products, pair_terms(): jnp.einsum('fbxcd,fbvd->fbxvc', rounded, far_spec, preferred_element_type...  9.06 us
    sub x9, other arithmetic, pair_terms(): first_real = toward[:, :, 0, :W] - toward[:, :, 1, W:]  4.65 us
    dot_general x9, matrix products, pair_terms(): jnp.einsum('fbxcd,fbvc->fbxvd', rounded, near_spec, preferred_element_typ...  3.78 us
  transfers between devices with their start and end apart: 7, of which 4 were waited for; matrix products, arithmetic and copies ran while one was open for 4% of the time, Pallas kernels for 0%

profile of v6, /device:TPU:1, one launch (start us, length us, event | category | flops | bytes accessed | tf_op | source)
XLA Modules:
  0.0 183.9 jit_solution(5752353431234143434)
XLA Ops:
  0.7 1.1 pad_maximum_fusion.2
  2.0 16.3 %collective-permute-start.1 = (bf16[8,2,24,128]{3,2,1,0:T(8,128)(2,1)S(1)}, bf16[8,2,24,128]{3,2,1,0:T(8,128)(2,1)S(1)}, u32[]{:S(2)}, u32[]{:S(2)}) collective-permute-start(bf16[8,2,24,128]{3,2,1,0:T(8,128)(2,1)S(1)} %get-tuple-element.190), channel_id=1, source_target_pairs={{0,16},{8,24},{16,0},{24,8},{32,48},{40,56},{48,32},{56,40},{64,80... | collective-permute-start | bytes 294920 | tf_op jit(solution)/shard_map/ppermute | solution.py:16
  18.2 4.8 %collective-permute-start = (bf16[8,2,24,128]{3,2,1,0:T(8,128)(2,1)S(1)}, bf16[8,2,24,128]{3,2,1,0:T(8,128)(2,1)S(1)}, u32[]{:S(2)}, u32[]{:S(2)}) collective-permute-start(bf16[8,2,24,128]{3,2,1,0:T(8,128)(2,1)S(1)} %get-tuple-element.191), channel_id=1, source_target_pairs={{0,8},{8,16},{16,24},{24,0},{32,40},{40,48},{48,56},{56,32},{64,72... | collective-permute-start | bytes 294920 | tf_op jit(solution)/shard_map/ppermute | solution.py:16
  23.0 1.9 %collective-permute-start.2 = (bf16[8,2,24,128]{3,2,1,0:T(8,128)(2,1)S(1)}, bf16[8,2,24,128]{3,2,1,0:T(8,128)(2,1)S(1)}, u32[]{:S(2)}, u32[]{:S(2)}) collective-permute-start(bf16[8,2,24,128]{3,2,1,0:T(8,128)(2,1)S(1)} %get-tuple-element.192), channel_id=1, source_target_pairs={{0,24},{8,0},{16,8},{24,16},{32,56},{40,32},{48,40},{56,48},{64,88... | collective-permute-start | bytes 294920 | tf_op jit(solution)/shard_map/ppermute | solution.py:16
  25.6 0.9 multiply_select_fusion.1
  26.5 1.3 multiply_select_fusion
  27.9 10.9 %collective-permute-done.2 = bf16[8,2,24,128]{3,2,1,0:T(8,128)(2,1)S(1)} collective-permute-done((bf16[8,2,24,128]{3,2,1,0:T(8,128)(2,1)S(1)}, bf16[8,2,24,128]{3,2,1,0:T(8,128)(2,1)S(1)}, u32[]{:S(2)}, u32[]{:S(2)}) %collective-permute-start.2) | collective-permute-done | bytes 98336 | tf_op jit(solution)/shard_map/ppermute | solution.py:16
  39.8 7.1 %collective-permute-start.3 = (bf16[8,4,2,24,128]{4,3,1,0,2:T(8,128)(2,1)S(1)}, bf16[8,4,2,24,128]{4,3,1,0,2:T(8,128)(2,1)S(1)}, u32[]{:S(2)}, u32[]{:S(2)}) collective-permute-start(bf16[8,4,2,24,128]{4,3,1,0,2:T(8,128)(2,1)S(1)} %get-tuple-element.115), channel_id=1, source_target_pairs={{0,480},{8,488},{16,496},{24,504},{32,0},{40,8},{48,16},{56,24},{6... | collective-permute-start | bytes 1179656 | tf_op jit(solution)/shard_map/ppermute | solution.py:16
  46.9 2.4 %collective-permute-start.4 = (bf16[8,4,2,24,128]{4,3,1,0,2:T(8,128)(2,1)S(1)}, bf16[8,4,2,24,128]{4,3,1,0,2:T(8,128)(2,1)S(1)}, u32[]{:S(2)}, u32[]{:S(2)}) collective-permute-start(bf16[8,4,2,24,128]{4,3,1,0,2:T(8,128)(2,1)S(1)} %get-tuple-element.115), channel_id=1, source_target_pairs={{0,448},{8,456},{16,464},{24,472},{32,480},{40,488},{48,496},{56,5... | collective-permute-start | bytes 1179656 | tf_op jit(solution)/shard_map/ppermute | solution.py:16
  49.4 2.0 %multiply_reduce_fusion.8 = (f32[]{:T(128)}, bf16[8,4,2,128,128]{4,3,2,1,0:T(8,128)(2,1)S(1)}) fusion(f32[4,128,128]{2,1,0:T(8,128)S(1)} %get-tuple-element.207, bf16[8,4,48,128,1]{3,2,4,1,0:T(8,128)(2,1)S(1)} %bitcast.197, bf16[8,4,1,48,128]{4,3,2,1,0:T(8,128)(2,1)S(1)} %maximum_bitcast_fusion, bf16[8,4,1,48,128]{4,3,2,1,0:T(8,128)(2,1)S(1)} %bitcast.183), kind=kOutput, calls=%fused_computation.9 | convolution fusion | flops 105250816 | bytes 3538948 | tf_op jit(solution)/shard_map/fbxrc,fbrd->fbxcd/dot_general | solution.py:49
  51.4 11.9 %collective-permute-done.3 = bf16[8,4,2,24,128]{4,3,1,0,2:T(8,128)(2,1)S(1)} collective-permute-done((bf16[8,4,2,24,128]{4,3,1,0,2:T(8,128)(2,1)S(1)}, bf16[8,4,2,24,128]{4,3,1,0,2:T(8,128)(2,1)S(1)}, u32[]{:S(2)}, u32[]{:S(2)}) %collective-permute-start.3) | collective-permute-done | bytes 393248 | tf_op jit(solution)/shard_map/ppermute | solution.py:16
  64.6 2.1 %multiply_reduce_fusion.3 = (f32[]{:T(128)}, bf16[8,4,2,128,128]{4,3,2,1,0:T(8,128)(2,1)S(1)}) fusion(f32[4,128,128]{2,1,0:T(8,128)S(1)} %get-tuple-element.206, bf16[8,4,48,128,1]{3,2,4,1,0:T(8,128)(2,1)S(1)} %bitcast.199, bf16[8,4,1,48,128]{4,3,2,1,0:T(8,128)(2,1)S(1)} %maximum_bitcast_fusion, bf16[8,4,1,48,128]{4,3,2,1,0:T(8,128)(2,1)S(1)} %bitcast.184), kind=kOutput, calls=%fused_computation.4 | convolution fusion | flops 105250816 | bytes 3538948 | tf_op jit(solution)/shard_map/fbxrc,fbrd->fbxcd/dot_general | solution.py:49
  68.1 2.0 %multiply_reduce_fusion.2 = (f32[]{:T(128)}, bf16[8,4,2,128,128]{4,3,2,1,0:T(8,128)(2,1)S(1)}) fusion(f32[4,128,128]{2,1,0:T(8,128)S(1)} %get-tuple-element.209, bf16[8,4,48,128,1]{3,2,4,1,0:T(8,128)(2,1)S(1)} %bitcast.196, bf16[8,4,1,48,128]{4,3,2,1,0:T(8,128)(2,1)S(1)} %maximum_bitcast_fusion, bf16[8,4,1,48,128]{4,3,2,1,0:T(8,128)(2,1)S(1)} %bitcast.185), kind=kOutput, calls=%fused_computation.3 | convolution fusion | flops 105250816 | bytes 3538948 | tf_op jit(solution)/shard_map/fbxrc,fbrd->fbxcd/dot_general | solution.py:49
  71.5 2.0 %multiply_reduce_fusion.1 = (f32[]{:T(128)}, bf16[8,4,2,128,128]{4,3,2,1,0:T(8,128)(2,1)S(1)}) fusion(f32[4,128,128]{2,1,0:T(8,128)S(1)} %get-tuple-element.208, bf16[8,4,48,128,1]{3,2,4,1,0:T(8,128)(2,1)S(1)} %bitcast.195, bf16[8,4,1,48,128]{4,3,2,1,0:T(8,128)(2,1)S(1)} %maximum_bitcast_fusion, bf16[8,4,1,48,128]{4,3,2,1,0:T(8,128)(2,1)S(1)} %bitcast.186), kind=kOutput, calls=%fused_computation.2 | convolution fusion | flops 105250816 | bytes 3538948 | tf_op jit(solution)/shard_map/fbxrc,fbrd->fbxcd/dot_general | solution.py:49
  75.8 2.0 %multiply_reduce_fusion.6 = (f32[]{:T(128)}, bf16[8,4,2,128,128]{4,3,2,1,0:T(8,128)(2,1)S(1)}) fusion(f32[4,128,128]{2,1,0:T(8,128)S(1)} %copy-done.15, bf16[8,4,48,128,1]{3,2,4,1,0:T(8,128)(2,1)S(1)} %bitcast.194, bf16[8,4,1,48,128]{4,3,2,1,0:T(8,128)(2,1)S(1)} %maximum_bitcast_fusion, bf16[8,4,1,48,128]{4,3,2,1,0:T(8,128)(2,1)S(1)} %bitcast.187), kind=kOutput, calls=%fused_computation.7 | convolution fusion | flops 105250816 | bytes 3538948 | tf_op jit(solution)/shard_map/fbxrc,fbrd->fbxcd/dot_general | solution.py:49
  79.1 0.9 slice_subtract_fusion.15
  80.0 2.3 %multiply_reduce_fusion.7 = (f32[]{:T(128)}, bf16[8,4,2,128,128]{4,3,2,1,0:T(8,128)(2,1)S(1)}) fusion(f32[4,128,128]{2,1,0:T(8,128)S(1)} %copy-done.11, bf16[8,4,48,128,1]{3,2,4,1,0:T(8,128)(2,1)S(1)} %bitcast.193, bf16[8,4,1,48,128]{4,3,2,1,0:T(8,128)(2,1)S(1)} %maximum_bitcast_fusion, bf16[8,4,1,48,128]{4,3,2,1,0:T(8,128)(2,1)S(1)} %bitcast.188), kind=kOutput, calls=%fused_computation.8 | convolution fusion | flops 105250816 | bytes 3538948 | tf_op jit(solution)/shard_map/fbxrc,fbrd->fbxcd/dot_general | solution.py:49
  84.4 2.1 %multiply_reduce_fusion.5 = (f32[]{:T(128)}, bf16[8,4,2,128,128]{4,3,2,1,0:T(8,128)(2,1)S(1)}) fusion(f32[4,128,128]{2,1,0:T(8,128)S(1)} %copy-done.14, bf16[8,4,48,128,1]{3,2,4,1,0:T(8,128)(2,1)S(1)} %bitcast.192, bf16[8,4,1,48,128]{4,3,2,1,0:T(8,128)(2,1)S(1)} %maximum_bitcast_fusion, bf16[8,4,1,48,128]{4,3,2,1,0:T(8,128)(2,1)S(1)} %bitcast.189), kind=kOutput, calls=%fused_computation.6 | convolution fusion | flops 105250816 | bytes 3538948 | tf_op jit(solution)/shard_map/fbxrc,fbrd->fbxcd/dot_general | solution.py:49
  87.8 0.9 slice_subtract_fusion.14
  88.8 2.1 %multiply_reduce_fusion = (f32[]{:T(128)}, bf16[8,4,2,128,128]{4,3,2,1,0:T(8,128)(2,1)S(1)}) fusion(f32[4,128,128]{2,1,0:T(8,128)S(1)} %copy-done.13, bf16[8,4,48,128,1]{3,2,4,1,0:T(8,128)(2,1)S(1)} %bitcast.200, bf16[8,4,1,48,128]{4,3,2,1,0:T(8,128)(2,1)S(1)} %maximum_bitcast_fusion, bf16[8,4,1,48,128]{4,3,2,1,0:T(8,128)(2,1)S(1)} %bitcast.190), kind=kOutput, calls=%fused_computation.1 | convolution fusion | flops 105250816 | bytes 3538948 | tf_op jit(solution)/shard_map/fbxrc,fbrd->fbxcd/dot_general | solution.py:49
  92.2 0.9 slice_subtract_fusion.9
  93.1 2.0 %multiply_reduce_fusion.4 = (f32[]{:T(128)}, bf16[8,4,2,128,128]{4,3,2,1,0:T(8,128)(2,1)S(1)}) fusion(f32[4,128,128]{2,1,0:T(8,128)S(1)} %copy-done.12, bf16[8,4,48,128,1]{3,2,4,1,0:T(8,128)(2,1)S(1)} %bitcast.198, bf16[8,4,1,48,128]{4,3,2,1,0:T(8,128)(2,1)S(1)} %maximum_bitcast_fusion, bf16[8,4,1,48,128]{4,3,2,1,0:T(8,128)(2,1)S(1)} %bitcast.191), kind=kOutput, calls=%fused_computation.5 | convolution fusion | flops 105250816 | bytes 3538948 | tf_op jit(solution)/shard_map/fbxrc,fbrd->fbxcd/dot_general | solution.py:49
  99.0 1.1 fusion.148
  100.2 1.9 %collective-permute-start.5 = (f32[8,4,2,16,128]{4,3,2,0,1:T(8,128)}, f32[8,4,2,16,128]{4,3,2,0,1:T(8,128)}, u32[]{:S(2)}, u32[]{:S(2)}) collective-permute-start(f32[8,4,2,16,128]{4,3,2,0,1:T(8,128)} %get-tuple-element.134), channel_id=1, source_target_pairs={{0,32},{8,40},{16,48},{24,56},{32,64},{40,72},{48,80},{56,88},{64,... | collective-permute-start | bytes 1572872 | tf_op jit(solution)/shard_map/ppermute | solution.py:16
  102.1 4.9 %collective-permute-start.6 = (f32[8,4,2,16,128]{4,3,2,0,1:T(8,128)}, f32[8,4,2,16,128]{4,3,2,0,1:T(8,128)}, u32[]{:S(2)}, u32[]{:S(2)}) collective-permute-start(f32[8,4,2,16,128]{4,3,2,0,1:T(8,128)} %get-tuple-element.135), channel_id=1, source_target_pairs={{0,64},{8,72},{16,80},{24,88},{32,96},{40,104},{48,112},{56,120},{... | collective-permute-start | bytes 1572872 | tf_op jit(solution)/shard_map/ppermute | solution.py:16
  113.0 2.5 %fusion.36 = f32[8,4,2,32,128]{4,3,2,0,1:T(8,128)S(1)} fusion(bf16[8,4,2,128,128]{4,3,2,1,0:T(8,128)(2,1)} %copy-done, bf16[8,4,32,128,1]{3,2,1,0,4:T(8,128)(2,1)S(1)} %bitcast.172), kind=kOutput, calls=%fused_computation.57 | convolution fusion | flops 67108864 | bytes 3407872 | tf_op jit(solution)/shard_map/fbxcd,fbvd->fbxvc/dot_general | solution.py:62
  115.6 3.3 %collective-permute-done.5 = f32[8,4,2,16,128]{4,3,2,0,1:T(8,128)} collective-permute-done((f32[8,4,2,16,128]{4,3,2,0,1:T(8,128)}, f32[8,4,2,16,128]{4,3,2,0,1:T(8,128)}, u32[]{:S(2)}, u32[]{:S(2)}) %collective-permute-start.5) | collective-permute-done | bytes 524320 | tf_op jit(solution)/shard_map/ppermute | solution.py:16
  118.8 12.1 %collective-permute-done.6 = f32[8,4,2,16,128]{4,3,2,0,1:T(8,128)} collective-permute-done((f32[8,4,2,16,128]{4,3,2,0,1:T(8,128)}, f32[8,4,2,16,128]{4,3,2,0,1:T(8,128)}, u32[]{:S(2)}, u32[]{:S(2)}) %collective-permute-start.6) | collective-permute-done | bytes 524320 | tf_op jit(solution)/shard_map/ppermute | solution.py:16
  131.1 2.5 %fusion.93.blocks_ref = f32[4,8,2,16,128]{4,3,2,1,0:T(8,128)} fusion(f32[8,4,2,16,128]{4,3,2,0,1:T(8,128)} %collective-permute-done.6, f32[8,4,2,16,128]{4,3,2,0,1:T(8,128)} %collective-permute-done.5, f32[8,12,2,16,128]{4,3,2,0,1:T(8,128)S(1)} %fusion.94, f32[8,4,1,16,128]{4,3,2,0,1:T(8,128)S(1)} %get-tuple-element.153, ...), kind=kLoop, calls=%fused_computation.93 | loop fusion | flops 2752512 | bytes 6815744 | tf_op jit(solution)/shard_map/transpose | solution.py:221
  134.2 44.9 %shard_map.59 = (f32[4,8,2,16,128]{4,3,2,1,0:T(8,128)}, f32[8,128]{1,0:T(8,128)}) custom-call(f32[4,8,2,16,128]{4,3,2,1,0:T(8,128)} %fusion.93.blocks_ref, f32[8,128]{1,0:T(8,128)} %broadcast_in_dim.14.val_ref), custom_call_target="tpu_custom_call" | custom-call | tf_op jit(solution)/shard_map/pallas_call | solution.py:156
  179.1 1.2 slice.883
  180.9 1.9 %copy.229 = f32[32,2,16,128]{3,2,1,0:T(8,128)} copy(f32[32,2,16,128]{3,2,1,0:T(8,128)} %bitcast.182) | data formatting | bytes 1048576
  (140 shorter events, 18.4 us)
Async XLA Ops:
  0.6 24.7 %copy-start.16 = (s32[8192]{0:T(1024)S(1)}, s32[8192]{0:T(1024)}, u32[]{:S(2)}) copy-start(s32[8192]{0:T(1024)} %param.24) | copy-start | bytes 98308
  0.6 24.9 %copy-start.18 = (s32[64]{0:T(128)S(1)}, s32[64]{0:T(128)}, u32[]{:S(2)}) copy-start(s32[64]{0:T(128)} %param.25) | copy-start | bytes 772
  2.0 25.9 %collective-permute-start.1 = (bf16[8,2,24,128]{3,2,1,0:T(8,128)(2,1)S(1)}, bf16[8,2,24,128]{3,2,1,0:T(8,128)(2,1)S(1)}, u32[]{:S(2)}, u32[]{:S(2)}) collective-permute-start(bf16[8,2,24,128]{3,2,1,0:T(8,128)(2,1)S(1)} %get-tuple-element.190), channel_id=1, source_target_pairs={{0,16},{8,24},{16,0},{24,8},{32,48},{40,56},{48,32},{56,40},{64,80... | collective-permute-start | bytes 294920 | tf_op jit(solution)/shard_map/ppermute | solution.py:16
  18.2 9.6 %collective-permute-start = (bf16[8,2,24,128]{3,2,1,0:T(8,128)(2,1)S(1)}, bf16[8,2,24,128]{3,2,1,0:T(8,128)(2,1)S(1)}, u32[]{:S(2)}, u32[]{:S(2)}) collective-permute-start(bf16[8,2,24,128]{3,2,1,0:T(8,128)(2,1)S(1)} %get-tuple-element.191), channel_id=1, source_target_pairs={{0,8},{8,16},{16,24},{24,0},{32,40},{40,48},{48,56},{56,32},{64,72... | collective-permute-start | bytes 294920 | tf_op jit(solution)/shard_map/ppermute | solution.py:16
  23.0 15.8 %collective-permute-start.2 = (bf16[8,2,24,128]{3,2,1,0:T(8,128)(2,1)S(1)}, bf16[8,2,24,128]{3,2,1,0:T(8,128)(2,1)S(1)}, u32[]{:S(2)}, u32[]{:S(2)}) collective-permute-start(bf16[8,2,24,128]{3,2,1,0:T(8,128)(2,1)S(1)} %get-tuple-element.192), channel_id=1, source_target_pairs={{0,24},{8,0},{16,8},{24,16},{32,56},{40,32},{48,40},{56,48},{64,88... | collective-permute-start | bytes 294920 | tf_op jit(solution)/shard_map/ppermute | solution.py:16
  26.5 13.0 %copy-start.17 = (bf16[24]{0:T(256)(128)(2,1)S(1)}, bf16[24]{0:T(256)(128)(2,1)}, u32[]{:S(2)}) copy-start(bf16[24]{0:T(256)(128)(2,1)} %constant.341.clone.1) | copy-start | bytes 148
  39.8 23.6 %collective-permute-start.3 = (bf16[8,4,2,24,128]{4,3,1,0,2:T(8,128)(2,1)S(1)}, bf16[8,4,2,24,128]{4,3,1,0,2:T(8,128)(2,1)S(1)}, u32[]{:S(2)}, u32[]{:S(2)}) collective-permute-start(bf16[8,4,2,24,128]{4,3,1,0,2:T(8,128)(2,1)S(1)} %get-tuple-element.115), channel_id=1, source_target_pairs={{0,480},{8,488},{16,496},{24,504},{32,0},{40,8},{48,16},{56,24},{6... | collective-permute-start | bytes 1179656 | tf_op jit(solution)/shard_map/ppermute | solution.py:16
  46.9 16.7 %collective-permute-start.4 = (bf16[8,4,2,24,128]{4,3,1,0,2:T(8,128)(2,1)S(1)}, bf16[8,4,2,24,128]{4,3,1,0,2:T(8,128)(2,1)S(1)}, u32[]{:S(2)}, u32[]{:S(2)}) collective-permute-start(bf16[8,4,2,24,128]{4,3,1,0,2:T(8,128)(2,1)S(1)} %get-tuple-element.115), channel_id=1, source_target_pairs={{0,448},{8,456},{16,464},{24,472},{32,480},{40,488},{48,496},{56,5... | collective-permute-start | bytes 1179656 | tf_op jit(solution)/shard_map/ppermute | solution.py:16
  51.4 45.9 %copy-start = (bf16[8,4,2,128,128]{4,3,2,1,0:T(8,128)(2,1)}, bf16[8,4,2,128,128]{4,3,2,1,0:T(8,128)(2,1)S(1)}, u32[]{:S(2)}) copy-start(bf16[8,4,2,128,128]{4,3,2,1,0:T(8,128)(2,1)S(1)} %get-tuple-element.133) | copy-start | bytes 6291460
  74.8 1.0 copy-start.15
  79.0 1.0 copy-start.11
  83.5 1.0 copy-start.14
  87.7 1.0 copy-start.13
  92.1 1.0 copy-start.12
  100.2 18.7 %collective-permute-start.5 = (f32[8,4,2,16,128]{4,3,2,0,1:T(8,128)}, f32[8,4,2,16,128]{4,3,2,0,1:T(8,128)}, u32[]{:S(2)}, u32[]{:S(2)}) collective-permute-start(f32[8,4,2,16,128]{4,3,2,0,1:T(8,128)} %get-tuple-element.134), channel_id=1, source_target_pairs={{0,32},{8,40},{16,48},{24,56},{32,64},{40,72},{48,80},{56,88},{64,... | collective-permute-start | bytes 1572872 | tf_op jit(solution)/shard_map/ppermute | solution.py:16
  102.1 28.9 %collective-permute-start.6 = (f32[8,4,2,16,128]{4,3,2,0,1:T(8,128)}, f32[8,4,2,16,128]{4,3,2,0,1:T(8,128)}, u32[]{:S(2)}, u32[]{:S(2)}) collective-permute-start(f32[8,4,2,16,128]{4,3,2,0,1:T(8,128)} %get-tuple-element.135), channel_id=1, source_target_pairs={{0,64},{8,72},{16,80},{24,88},{32,96},{40,104},{48,112},{56,120},{... | collective-permute-start | bytes 1572872 | tf_op jit(solution)/shard_map/ppermute | solution.py:16
  112.9 18.1 %copy-start.1 = (f32[8,4,1,16,128]{4,3,2,0,1:T(8,128)S(1)}, f32[8,4,1,16,128]{4,3,2,0,1:T(8,128)}, u32[]{:S(2)}) copy-start(f32[8,4,1,16,128]{4,3,2,0,1:T(8,128)} %get-tuple-element.148) | copy-start | bytes 786436
  112.9 18.1 %copy-start.2 = (f32[8,4,1,16,128]{4,3,2,0,1:T(8,128)S(1)}, f32[8,4,1,16,128]{4,3,2,0,1:T(8,128)}, u32[]{:S(2)}) copy-start(f32[8,4,1,16,128]{4,3,2,0,1:T(8,128)} %get-tuple-element.149) | copy-start | bytes 786436
  112.9 18.1 %copy-start.3 = (f32[8,4,1,16,128]{4,3,2,0,1:T(8,128)S(1)}, f32[8,4,1,16,128]{4,3,2,0,1:T(8,128)}, u32[]{:S(2)}) copy-start(f32[8,4,1,16,128]{4,3,2,0,1:T(8,128)} %get-tuple-element.150) | copy-start | bytes 786436
  112.9 18.1 %copy-start.4 = (f32[8,4,1,16,128]{4,3,2,0,1:T(8,128)S(1)}, f32[8,4,1,16,128]{4,3,2,0,1:T(8,128)}, u32[]{:S(2)}) copy-start(f32[8,4,1,16,128]{4,3,2,0,1:T(8,128)} %get-tuple-element.151) | copy-start | bytes 786436
  112.9 18.1 %copy-start.5 = (f32[8,4,1,16,128]{4,3,2,0,1:T(8,128)S(1)}, f32[8,4,1,16,128]{4,3,2,0,1:T(8,128)}, u32[]{:S(2)}) copy-start(f32[8,4,1,16,128]{4,3,2,0,1:T(8,128)} %get-tuple-element.146) | copy-start | bytes 786436
  112.9 18.1 %copy-start.6 = (f32[8,4,1,16,128]{4,3,2,0,1:T(8,128)S(1)}, f32[8,4,1,16,128]{4,3,2,0,1:T(8,128)}, u32[]{:S(2)}) copy-start(f32[8,4,1,16,128]{4,3,2,0,1:T(8,128)} %get-tuple-element.147) | copy-start | bytes 786436
  112.9 18.1 %copy-start.7 = (f32[8,4,1,16,128]{4,3,2,0,1:T(8,128)S(1)}, f32[8,4,1,16,128]{4,3,2,0,1:T(8,128)}, u32[]{:S(2)}) copy-start(f32[8,4,1,16,128]{4,3,2,0,1:T(8,128)} %get-tuple-element.136) | copy-start | bytes 786436
  112.9 18.1 %copy-start.8 = (f32[8,4,1,16,128]{4,3,2,0,1:T(8,128)S(1)}, f32[8,4,1,16,128]{4,3,2,0,1:T(8,128)}, u32[]{:S(2)}) copy-start(f32[8,4,1,16,128]{4,3,2,0,1:T(8,128)} %get-tuple-element.137) | copy-start | bytes 786436
  112.9 18.1 %copy-start.9 = (f32[8,4,1,16,128]{4,3,2,0,1:T(8,128)S(1)}, f32[8,4,1,16,128]{4,3,2,0,1:T(8,128)}, u32[]{:S(2)}) copy-start(f32[8,4,1,16,128]{4,3,2,0,1:T(8,128)} %get-tuple-element.144) | copy-start | bytes 786436
  113.0 18.1 %copy-start.10 = (f32[8,4,1,16,128]{4,3,2,0,1:T(8,128)S(1)}, f32[8,4,1,16,128]{4,3,2,0,1:T(8,128)}, u32[]{:S(2)}) copy-start(f32[8,4,1,16,128]{4,3,2,0,1:T(8,128)} %get-tuple-element.145) | copy-start | bytes 786436

commit v7 on v6

--- a/solution.py
+++ b/solution.py
@@ -9,6 +9,7 @@
 F = 256
 W = 16
 BAND = 1024
+HALVES = 2
 GROUP = 4
 
 
@@ -74,6 +75,92 @@
 
 MESH = pl.DeviceIdType.MESH
 
+def head_kernel(n_halves, halo_cols, chunks_ref, out_ref, held, send_e, recv_e, send_h, recv_h, own_sem):
+    c = lax.axis_index("chan")
+    f = lax.axis_index("freq")
+    peers = lax.axis_size("chan")
+    k = c // GROUP
+    j = c % GROUP
+
+    def devg(b):
+        return (k * GROUP + b, f)
+
+    def devh(h, sign):
+        return ((c + sign * GROUP * h) % peers, f)
+
+    barrier = pltpu.get_barrier_semaphore()
+    for t in range(1, GROUP):
+        pl.semaphore_signal(barrier, 1, device_id=devg((j + t) % GROUP), device_id_type=MESH)
+    for h in range(1, halo_cols + 1):
+        pl.semaphore_signal(barrier, 1, device_id=devh(h, -1), device_id_type=MESH)
+        pl.semaphore_signal(barrier, 1, device_id=devh(h, 1), device_id_type=MESH)
+    pl.semaphore_wait(barrier, GROUP - 1 + 2 * halo_cols)
+
+    sends = []
+    locals_ = []
+    for half in range(n_halves):
+        for t in range(1, GROUP):
+            b = (j + t) % GROUP
+            cp = pltpu.make_async_remote_copy(
+                src_ref=chunks_ref.at[b, half], dst_ref=held.at[half, 0, j],
+                send_sem=send_e.at[half, b], recv_sem=recv_e.at[half, j],
+                device_id=devg(b), device_id_type=MESH)
+            cp.start()
+            sends.append(cp)
+        cp = pltpu.make_async_copy(chunks_ref.at[j, half], held.at[half, 0, j], own_sem.at[half])
+        cp.start()
+        locals_.append(cp)
+    for half in range(n_halves):
+        locals_[half].wait()
+        for t in range(1, GROUP):
+            b = (j + t) % GROUP
+            pltpu.make_async_remote_copy(
+                src_ref=chunks_ref.at[b, half], dst_ref=held.at[half, 0, b],
+                send_sem=send_e.at[half, b], recv_sem=recv_e.at[half, b],
+                device_id=devg(b), device_id_type=MESH).wait_recv()
+        for h in range(1, halo_cols + 1):
+            cp = pltpu.make_async_remote_copy(
+                src_ref=held.at[half, 0], dst_ref=held.at[half, h],
+                send_sem=send_h.at[half, h], recv_sem=recv_h.at[half, h],
+                device_id=devh(h, -1), device_id_type=MESH)
+            cp.start()
+            sends.append(cp)
+    for half in range(n_halves):
+        for h in range(1, halo_cols + 1):
+            pltpu.make_async_remote_copy(
+                src_ref=held.at[half, 0], dst_ref=held.at[half, h],
+                send_sem=send_h.at[half, h], recv_sem=recv_h.at[half, h],
+                device_id=devh(h, 1), device_id_type=MESH).wait_recv()
+    for cp in sends:
+        cp.wait_send()
+    out_ref[...] = held[...]
+
+
+def gather_columns(payload, halo_cols, n_halves):
+    fl, two, rows, bw = payload.shape
+    q = fl // GROUP // n_halves
+    chunks = payload.reshape(GROUP, n_halves, q, two, rows, bw)
+    shape = (n_halves, 1 + halo_cols, GROUP, q, two, rows, bw)
+    vmem = pl.BlockSpec(memory_space=pltpu.VMEM)
+    held = pl.pallas_call(
+        functools.partial(head_kernel, n_halves, halo_cols),
+        out_shape=jax.ShapeDtypeStruct(shape, payload.dtype),
+        in_specs=[vmem],
+        out_specs=vmem,
+        scratch_shapes=[
+            pltpu.VMEM(shape, payload.dtype),
+            pltpu.SemaphoreType.DMA((n_halves, GROUP)),
+            pltpu.SemaphoreType.DMA((n_halves, GROUP)),
+            pltpu.SemaphoreType.DMA((n_halves, 1 + halo_cols)),
+            pltpu.SemaphoreType.DMA((n_halves, 1 + halo_cols)),
+            pltpu.SemaphoreType.DMA((n_halves,)),
+        ],
+        compiler_params=pltpu.CompilerParams(collective_id=1, has_side_effects=True),
+    )(chunks)
+    held = jnp.transpose(held, (0, 3, 1, 2, 4, 5, 6))
+    return held.reshape(n_halves * q, (1 + halo_cols) * GROUP, two, rows, bw)
+
+
 def tail_kernel(n_col, n_f, blocks_ref, val_ref, out_ref, sum_ref,
                 got, slots1, slots2, stage, send_o, recv_o, send1, recv1, send2, recv2):
     c = lax.axis_index("chan")
@@ -188,12 +275,7 @@
     halo_cols = -(-band_blocks // GROUP)
     nblk = GROUP * (1 + halo_cols)
 
-    chunks = payload.reshape(GROUP, sub, 2, rows, bw)
-    mine = exchange(chunks, j, peers)
-    own = jnp.transpose(mine, (1, 0, 2, 3, 4))
-
-    parts = [own] + [permute(own, shift_pairs(peers, -GROUP * h)) for h in range(1, halo_cols + 1)]
-    ext = jnp.concatenate(parts, axis=1)
+    ext = gather_columns(payload, halo_cols, HALVES)
 
     ok_all = channel_ok.astype(jnp.float32)
     ok_wide = jnp.concatenate([ok_all, ok_all[: nblk * bw]])

time: 185 us -> 185 us (level)
  Pallas kernels: 44.9 us -> 94.5 us
  starting transfers between devices: 39.4 us -> 4.05 us
  waiting for transfers between devices: 38.3 us -> 5.84 us
  local copies, waits for them, and re-layouts: 6.25 us -> 15 us
  other arithmetic: 14.5 us -> 23.2 us
    pallas_call x0 -> x1, Pallas kernels: none -> 50.5 us  [gather_columns(): pl.pallas_call(functools.partial(head_kernel, n_halves, halo_cols), out_s...]
    ppermute x7 -> x2, starting transfers between devices: 39.4 us -> 4.05 us  [permute(): return lax.ppermute(x, 'chan', pairs)]
    ppermute x7 -> x2, waiting for transfers between devices: 38.3 us -> 5.84 us  [permute(): return lax.ppermute(x, 'chan', pairs)]
    unnamed x39 -> x79, local copies, waits for them, and re-layouts: 2.77 us -> 6.02 us
    ge x5, other arithmetic: 0.14 us -> 3.16 us  [pair_terms(): offset[None] >= 1]
    sub x5, other arithmetic: 0.06 us -> 2.63 us  [pair_terms(): offset = shift_blocks * block_width + col_index - row_index]
    sub x9, other arithmetic: 4.65 us -> 6.82 us  [pair_terms(): first_real = toward[:, :, 0, :W] - toward[:, :, 1, W:]]
  transfers between devices with their start and end apart: 7 -> 2, of which waited for: 4 -> 1; matrix products, arithmetic and copies ran while one was open for 4% -> 9% of each run, Pallas kernels for 0% -> 0%
where the time goes in v7:
time: 185 us; the launch traced here: 184 us
  Pallas kernels  94.5 us (51%)
  matrix products  32.4 us (18%)
  other arithmetic  23.2 us (13%)
  local copies, waits for them, and re-layouts  15 us (8%)
  between operations  8.82 us (5%)
  waiting for transfers between devices  5.84 us (3%)
  starting transfers between devices  4.05 us (2%)
    pallas_call x1, Pallas kernels, gather_columns(): pl.pallas_call(functools.partial(head_kernel, n_halves, halo_cols), out_s...  50.5 us
    pallas_call x1, Pallas kernels, finish(): pl.pallas_call(functools.partial(tail_kernel, n_col, n_f), out_shape=(jax...  44 us
    dot_general x9, matrix products, pair_terms(): jnp.einsum('fbxrc,fbrd->fbxcd', stacked_left, right_rows, preferred_eleme...  19.5 us
    dot_general x9, matrix products, pair_terms(): jnp.einsum('fbxcd,fbvd->fbxvc', rounded, far_spec, preferred_element_type...  9.01 us
    sub x9, other arithmetic, pair_terms(): first_real = toward[:, :, 0, :W] - toward[:, :, 1, W:]  6.82 us
    unnamed x79, local copies, waits for them, and re-layouts  6.02 us
    ppermute x2, waiting for transfers between devices, permute(): return lax.ppermute(x, 'chan', pairs)  5.84 us
    ppermute x2, starting transfers between devices, permute(): return lax.ppermute(x, 'chan', pairs)  4.05 us
  transfers between devices with their start and end apart: 2, of which 1 were waited for; matrix products, arithmetic and copies ran while one was open for 9% of the time, Pallas kernels for 0%

profile of v7, /device:TPU:1, one launch (start us, length us, event | category | flops | bytes accessed | tf_op | source)
XLA Modules:
  0.0 183.8 jit_solution(7476266206255664663)
XLA Ops:
  6.5 1.8 pad_maximum_fusion.1
  8.3 50.5 %shard_map.59 = bf16[2,3,4,4,2,24,128]{6,5,4,3,2,1,0:T(8,128)(2,1)} custom-call(bf16[4,2,4,2,24,128]{5,4,3,2,1,0:T(8,128)(2,1)} %bitcast.165), custom_call_target="tpu_custom_call" | custom-call | tf_op jit(solution)/shard_map/pallas_call | solution.py:145
  58.8 1.6 copy.25
  60.4 1.2 fusion.138
  61.6 1.6 fusion.139
  68.4 1.2 multiply_select_fusion.1
  69.6 3.2 %multiply_reduce_fusion.7 = (f32[]{:T(128)}, bf16[8,4,2,128,128]{4,3,2,1,0:T(8,128)(2,1)S(1)}) fusion(f32[4,128,128]{2,1,0:T(8,128)S(1)} %get-tuple-element.207, bf16[8,4,48,128,1]{3,2,4,1,0:T(8,128)(2,1)} %bitcast.182, bf16[8,4,1,48,128]{4,3,2,1,0:T(8,128)(2,1)S(1)} %maximum_bitcast_fusion, bf16[8,4,1,48,128]{4,3,2,1,0:T(8,128)(2,1)} %bitcast.183), kind=kOutput, calls=%fused_computation.7 | convolution fusion | flops 105250816 | bytes 3538948 | tf_op jit(solution)/shard_map/fbxrc,fbrd->fbxcd/dot_general | solution.py:50
  74.4 2.1 %multiply_reduce_fusion.6 = (f32[]{:T(128)}, bf16[8,4,2,128,128]{4,3,2,1,0:T(8,128)(2,1)S(1)}) fusion(f32[4,128,128]{2,1,0:T(8,128)S(1)} %get-tuple-element.200, bf16[8,4,48,128,1]{3,2,4,1,0:T(8,128)(2,1)S(1)} %bitcast.181, bf16[8,4,1,48,128]{4,3,2,1,0:T(8,128)(2,1)S(1)} %maximum_bitcast_fusion, bf16[8,4,1,48,128]{4,3,2,1,0:T(8,128)(2,1)S(1)} %bitcast.184), kind=kOutput, calls=%fused_computation.6 | convolution fusion | flops 105250816 | bytes 3538948 | tf_op jit(solution)/shard_map/fbxrc,fbrd->fbxcd/dot_general | solution.py:50
  77.5 2.1 %multiply_reduce_fusion.5 = (f32[]{:T(128)}, bf16[8,4,2,128,128]{4,3,2,1,0:T(8,128)(2,1)S(1)}) fusion(f32[4,128,128]{2,1,0:T(8,128)S(1)} %get-tuple-element.201, bf16[8,4,48,128,1]{3,2,4,1,0:T(8,128)(2,1)S(1)} %bitcast.180, bf16[8,4,1,48,128]{4,3,2,1,0:T(8,128)(2,1)S(1)} %maximum_bitcast_fusion, bf16[8,4,1,48,128]{4,3,2,1,0:T(8,128)(2,1)S(1)} %bitcast.185), kind=kOutput, calls=%fused_computation.5 | convolution fusion | flops 105250816 | bytes 3538948 | tf_op jit(solution)/shard_map/fbxrc,fbrd->fbxcd/dot_general | solution.py:50
  80.5 2.1 %multiply_reduce_fusion.4 = (f32[]{:T(128)}, bf16[8,4,2,128,128]{4,3,2,1,0:T(8,128)(2,1)S(1)}) fusion(f32[4,128,128]{2,1,0:T(8,128)S(1)} %get-tuple-element.202, bf16[8,4,48,128,1]{3,2,4,1,0:T(8,128)(2,1)S(1)} %bitcast.179, bf16[8,4,1,48,128]{4,3,2,1,0:T(8,128)(2,1)S(1)} %maximum_bitcast_fusion, bf16[8,4,1,48,128]{4,3,2,1,0:T(8,128)(2,1)S(1)} %bitcast.186), kind=kOutput, calls=%fused_computation.4 | convolution fusion | flops 105250816 | bytes 3538948 | tf_op jit(solution)/shard_map/fbxrc,fbrd->fbxcd/dot_general | solution.py:50
  83.6 2.0 %multiply_reduce_fusion.3 = (f32[]{:T(128)}, bf16[8,4,2,128,128]{4,3,2,1,0:T(8,128)(2,1)S(1)}) fusion(f32[4,128,128]{2,1,0:T(8,128)S(1)} %get-tuple-element.203, bf16[8,4,48,128,1]{3,2,4,1,0:T(8,128)(2,1)S(1)} %bitcast.178, bf16[8,4,1,48,128]{4,3,2,1,0:T(8,128)(2,1)S(1)} %maximum_bitcast_fusion, bf16[8,4,1,48,128]{4,3,2,1,0:T(8,128)(2,1)S(1)} %bitcast.187), kind=kOutput, calls=%fused_computation.3 | convolution fusion | flops 105250816 | bytes 3538948 | tf_op jit(solution)/shard_map/fbxrc,fbrd->fbxcd/dot_general | solution.py:50
  86.6 2.0 %multiply_reduce_fusion.2 = (f32[]{:T(128)}, bf16[8,4,2,128,128]{4,3,2,1,0:T(8,128)(2,1)S(1)}) fusion(f32[4,128,128]{2,1,0:T(8,128)S(1)} %get-tuple-element.206, bf16[8,4,48,128,1]{3,2,4,1,0:T(8,128)(2,1)S(1)} %bitcast.177, bf16[8,4,1,48,128]{4,3,2,1,0:T(8,128)(2,1)S(1)} %maximum_bitcast_fusion, bf16[8,4,1,48,128]{4,3,2,1,0:T(8,128)(2,1)S(1)} %bitcast.188), kind=kOutput, calls=%fused_computation.2 | convolution fusion | flops 105250816 | bytes 3538948 | tf_op jit(solution)/shard_map/fbxrc,fbrd->fbxcd/dot_general | solution.py:50
  89.3 2.1 %multiply_reduce_fusion.1 = (f32[]{:T(128)}, bf16[8,4,2,128,128]{4,3,2,1,0:T(8,128)(2,1)S(1)}) fusion(f32[4,128,128]{2,1,0:T(8,128)S(1)} %get-tuple-element.205, bf16[8,4,48,128,1]{3,2,4,1,0:T(8,128)(2,1)S(1)} %bitcast.176, bf16[8,4,1,48,128]{4,3,2,1,0:T(8,128)(2,1)S(1)} %maximum_bitcast_fusion, bf16[8,4,1,48,128]{4,3,2,1,0:T(8,128)(2,1)S(1)} %bitcast.189), kind=kOutput, calls=%fused_computation.1 | convolution fusion | flops 105250816 | bytes 3538948 | tf_op jit(solution)/shard_map/fbxrc,fbrd->fbxcd/dot_general | solution.py:50
  91.9 2.0 %multiply_reduce_fusion = (f32[]{:T(128)}, bf16[8,4,2,128,128]{4,3,2,1,0:T(8,128)(2,1)S(1)}) fusion(f32[4,128,128]{2,1,0:T(8,128)S(1)} %get-tuple-element.199, bf16[8,4,48,128,1]{3,2,4,1,0:T(8,128)(2,1)S(1)} %bitcast.175, bf16[8,4,1,48,128]{4,3,2,1,0:T(8,128)(2,1)S(1)} %maximum_bitcast_fusion, bf16[8,4,1,48,128]{4,3,2,1,0:T(8,128)(2,1)S(1)} %bitcast.190), kind=kOutput, calls=%fused_computation | convolution fusion | flops 105250816 | bytes 3538948 | tf_op jit(solution)/shard_map/fbxrc,fbrd->fbxcd/dot_general | solution.py:50
  94.4 2.0 %multiply_reduce_fusion.8 = (f32[]{:T(128)}, bf16[8,4,2,128,128]{4,3,2,1,0:T(8,128)(2,1)S(1)}) fusion(f32[4,128,128]{2,1,0:T(8,128)S(1)} %get-tuple-element.204, bf16[8,4,48,128,1]{3,2,4,1,0:T(8,128)(2,1)S(1)} %bitcast.164, bf16[8,4,1,48,128]{4,3,2,1,0:T(8,128)(2,1)S(1)} %maximum_bitcast_fusion, bf16[8,4,1,48,128]{4,3,2,1,0:T(8,128)(2,1)S(1)} %bitcast.191), kind=kOutput, calls=%fused_computation.8 | convolution fusion | flops 105250816 | bytes 3538948 | tf_op jit(solution)/shard_map/fbxrc,fbrd->fbxcd/dot_general | solution.py:50
  96.9 0.9 copy-done
  99.0 1.1 fusion.137
  100.1 1.9 %collective-permute-start = (f32[8,4,2,16,128]{4,3,2,0,1:T(8,128)}, f32[8,4,2,16,128]{4,3,2,0,1:T(8,128)}, u32[]{:S(2)}, u32[]{:S(2)}) collective-permute-start(f32[8,4,2,16,128]{4,3,2,0,1:T(8,128)} %get-tuple-element.132), channel_id=1, source_target_pairs={{0,32},{8,40},{16,48},{24,56},{32,64},{40,72},{48,80},{56,88},{64,... | collective-permute-start | bytes 1572872 | tf_op jit(solution)/shard_map/ppermute | solution.py:17
  102.0 2.1 %collective-permute-start.1 = (f32[8,4,2,16,128]{4,3,2,0,1:T(8,128)}, f32[8,4,2,16,128]{4,3,2,0,1:T(8,128)}, u32[]{:S(2)}, u32[]{:S(2)}) collective-permute-start(f32[8,4,2,16,128]{4,3,2,0,1:T(8,128)} %get-tuple-element.133), channel_id=1, source_target_pairs={{0,64},{8,72},{16,80},{24,88},{32,96},{40,104},{48,112},{56,120},{... | collective-permute-start | bytes 1572872 | tf_op jit(solution)/shard_map/ppermute | solution.py:17
  104.2 0.8 fusion.42
  105.0 0.9 slice_subtract_fusion.16
  106.7 0.9 slice_subtract_fusion.15
  110.7 0.8 fusion.66
  113.1 0.9 slice_subtract_fusion.11
  114.8 0.9 slice_subtract_fusion.10
  116.5 0.9 slice_subtract_fusion.9
  123.2 2.5 %fusion.36 = f32[8,4,2,32,128]{4,3,2,0,1:T(8,128)S(1)} fusion(bf16[8,4,2,128,128]{4,3,2,1,0:T(8,128)(2,1)} %copy-done, bf16[8,4,32,128,1]{3,2,1,0,4:T(8,128)(2,1)S(1)} %bitcast.162), kind=kOutput, calls=%fused_computation.56 | convolution fusion | flops 67108864 | bytes 3407872 | tf_op jit(solution)/shard_map/fbxcd,fbvd->fbxvc/dot_general | solution.py:63
  125.9 5.8 %collective-permute-done.1 = f32[8,4,2,16,128]{4,3,2,0,1:T(8,128)} collective-permute-done((f32[8,4,2,16,128]{4,3,2,0,1:T(8,128)}, f32[8,4,2,16,128]{4,3,2,0,1:T(8,128)}, u32[]{:S(2)}, u32[]{:S(2)}) %collective-permute-start.1) | collective-permute-done | bytes 524320 | tf_op jit(solution)/shard_map/ppermute | solution.py:17
  131.8 2.5 %fusion.93.blocks_ref = f32[4,8,2,16,128]{4,3,2,1,0:T(8,128)} fusion(f32[8,4,2,16,128]{4,3,2,0,1:T(8,128)} %collective-permute-done.1, f32[8,4,2,16,128]{4,3,2,0,1:T(8,128)} %collective-permute-done, f32[8,12,2,16,128]{4,3,2,0,1:T(8,128)S(1)} %fusion.94, f32[8,4,1,16,128]{4,3,2,0,1:T(8,128)S(1)} %get-tuple-element.169, ...), kind=kLoop, calls=%fused_computation.80 | loop fusion | flops 2752512 | bytes 6815744 | tf_op jit(solution)/shard_map/transpose | solution.py:303
  134.9 44.0 %shard_map.60 = (f32[4,8,2,16,128]{4,3,2,1,0:T(8,128)}, f32[8,128]{1,0:T(8,128)}) custom-call(f32[4,8,2,16,128]{4,3,2,1,0:T(8,128)} %fusion.93.blocks_ref, f32[8,128]{1,0:T(8,128)} %broadcast_in_dim.2.val_ref), custom_call_target="tpu_custom_call" | custom-call | tf_op jit(solution)/shard_map/pallas_call | solution.py:243
  178.9 1.2 slice.877
  180.8 1.9 %copy.211 = f32[32,2,16,128]{3,2,1,0:T(8,128)} copy(f32[32,2,16,128]{3,2,1,0:T(8,128)} %bitcast.174) | data formatting | bytes 1048576
  (143 shorter events, 27.6 us)
Async XLA Ops:
  61.6 1.6 copy-start.38
  72.7 0.9 copy-start.25
  72.7 0.9 copy-start.27
  72.7 0.9 copy-start.28
  72.7 0.9 copy-start.29
  72.7 0.9 copy-start.30
  72.8 0.9 copy-start.31
  72.8 0.9 copy-start.32
  73.2 1.0 copy-start.20
  73.3 1.2 copy-start.21
  76.5 1.0 copy-start.19
  79.5 1.0 copy-start.18
  82.6 1.0 copy-start.17
  85.6 1.0 copy-start.16
  96.4 1.3 copy-start
  98.8 5.4 %copy-start.2 = (bf16[8,4,2,16,128]{4,3,2,1,0:T(8,128)(2,1)S(1)}, bf16[8,4,2,16,128]{4,3,2,1,0:T(8,128)(2,1)}, u32[]{:S(2)}) copy-start(bf16[8,4,2,16,128]{4,3,2,1,0:T(8,128)(2,1)} %get-tuple-element.141) | copy-start | bytes 786436
  100.1 25.8 %collective-permute-start = (f32[8,4,2,16,128]{4,3,2,0,1:T(8,128)}, f32[8,4,2,16,128]{4,3,2,0,1:T(8,128)}, u32[]{:S(2)}, u32[]{:S(2)}) collective-permute-start(f32[8,4,2,16,128]{4,3,2,0,1:T(8,128)} %get-tuple-element.132), channel_id=1, source_target_pairs={{0,32},{8,40},{16,48},{24,56},{32,64},{40,72},{48,80},{56,88},{64,... | collective-permute-start | bytes 1572872 | tf_op jit(solution)/shard_map/ppermute | solution.py:17
  102.0 29.7 %collective-permute-start.1 = (f32[8,4,2,16,128]{4,3,2,0,1:T(8,128)}, f32[8,4,2,16,128]{4,3,2,0,1:T(8,128)}, u32[]{:S(2)}, u32[]{:S(2)}) collective-permute-start(f32[8,4,2,16,128]{4,3,2,0,1:T(8,128)} %get-tuple-element.133), channel_id=1, source_target_pairs={{0,64},{8,72},{16,80},{24,88},{32,96},{40,104},{48,112},{56,120},{... | collective-permute-start | bytes 1572872 | tf_op jit(solution)/shard_map/ppermute | solution.py:17
  104.2 1.7 copy-start.1
  123.1 8.6 %copy-start.3 = (f32[8,4,1,16,128]{4,3,2,0,1:T(8,128)S(1)}, f32[8,4,1,16,128]{4,3,2,0,1:T(8,128)}, u32[]{:S(2)}) copy-start(f32[8,4,1,16,128]{4,3,2,0,1:T(8,128)} %get-tuple-element.166) | copy-start | bytes 786436
  123.1 8.6 %copy-start.4 = (f32[8,4,1,16,128]{4,3,2,0,1:T(8,128)S(1)}, f32[8,4,1,16,128]{4,3,2,0,1:T(8,128)}, u32[]{:S(2)}) copy-start(f32[8,4,1,16,128]{4,3,2,0,1:T(8,128)} %get-tuple-element.167) | copy-start | bytes 786436
  123.1 8.6 %copy-start.5 = (f32[8,4,1,16,128]{4,3,2,0,1:T(8,128)S(1)}, f32[8,4,1,16,128]{4,3,2,0,1:T(8,128)}, u32[]{:S(2)}) copy-start(f32[8,4,1,16,128]{4,3,2,0,1:T(8,128)} %get-tuple-element.164) | copy-start | bytes 786436
  123.1 8.6 %copy-start.6 = (f32[8,4,1,16,128]{4,3,2,0,1:T(8,128)S(1)}, f32[8,4,1,16,128]{4,3,2,0,1:T(8,128)}, u32[]{:S(2)}) copy-start(f32[8,4,1,16,128]{4,3,2,0,1:T(8,128)} %get-tuple-element.165) | copy-start | bytes 786436
  123.1 8.6 %copy-start.7 = (f32[8,4,1,16,128]{4,3,2,0,1:T(8,128)S(1)}, f32[8,4,1,16,128]{4,3,2,0,1:T(8,128)}, u32[]{:S(2)}) copy-start(f32[8,4,1,16,128]{4,3,2,0,1:T(8,128)} %get-tuple-element.163) | copy-start | bytes 786436
  123.1 8.6 %copy-start.8 = (f32[8,4,1,16,128]{4,3,2,0,1:T(8,128)S(1)}, f32[8,4,1,16,128]{4,3,2,0,1:T(8,128)}, u32[]{:S(2)}) copy-start(f32[8,4,1,16,128]{4,3,2,0,1:T(8,128)} %get-tuple-element.161) | copy-start | bytes 786436
  123.1 8.6 %copy-start.9 = (f32[8,4,1,16,128]{4,3,2,0,1:T(8,128)S(1)}, f32[8,4,1,16,128]{4,3,2,0,1:T(8,128)}, u32[]{:S(2)}) copy-start(f32[8,4,1,16,128]{4,3,2,0,1:T(8,128)} %get-tuple-element.159) | copy-start | bytes 786436
  123.2 8.6 %copy-start.10 = (f32[8,4,1,16,128]{4,3,2,0,1:T(8,128)S(1)}, f32[8,4,1,16,128]{4,3,2,0,1:T(8,128)}, u32[]{:S(2)}) copy-start(f32[8,4,1,16,128]{4,3,2,0,1:T(8,128)} %get-tuple-element.156) | copy-start | bytes 786436
  123.2 8.6 %copy-start.11 = (f32[8,4,1,16,128]{4,3,2,0,1:T(8,128)S(1)}, f32[8,4,1,16,128]{4,3,2,0,1:T(8,128)}, u32[]{:S(2)}) copy-start(f32[8,4,1,16,128]{4,3,2,0,1:T(8,128)} %get-tuple-element.157) | copy-start | bytes 786436
  123.2 8.6 %copy-start.12 = (f32[8,4,1,16,128]{4,3,2,0,1:T(8,128)S(1)}, f32[8,4,1,16,128]{4,3,2,0,1:T(8,128)}, u32[]{:S(2)}) copy-start(f32[8,4,1,16,128]{4,3,2,0,1:T(8,128)} %get-tuple-element.154) | copy-start | bytes 786436
  123.2 8.6 %copy-start.13 = (f32[8,4,1,16,128]{4,3,2,0,1:T(8,128)S(1)}, f32[8,4,1,16,128]{4,3,2,0,1:T(8,128)}, u32[]{:S(2)}) copy-start(f32[8,4,1,16,128]{4,3,2,0,1:T(8,128)} %get-tuple-element.155) | copy-start | bytes 786436
  123.2 8.6 %copy-start.14 = (f32[8,4,1,16,128]{4,3,2,0,1:T(8,128)S(1)}, f32[8,4,1,16,128]{4,3,2,0,1:T(8,128)}, u32[]{:S(2)}) copy-start(f32[8,4,1,16,128]{4,3,2,0,1:T(8,128)} %get-tuple-element.152) | copy-start | bytes 786436
  123.2 8.6 %copy-start.15 = (f32[8,4,1,16,128]{4,3,2,0,1:T(8,128)S(1)}, f32[8,4,1,16,128]{4,3,2,0,1:T(8,128)}, u32[]{:S(2)}) copy-start(f32[8,4,1,16,128]{4,3,2,0,1:T(8,128)} %get-tuple-element.153) | copy-start | bytes 786436
  (9 other events, 7.7 us)

commit v8 on v7

--- a/solution.py
+++ b/solution.py
@@ -52,8 +52,8 @@
     )
     row_index = lax.broadcasted_iota(jnp.int32, (block_width, block_width), 0)
     col_index = lax.broadcasted_iota(jnp.int32, (block_width, block_width), 1)
-    offset = shift_blocks * block_width + col_index - row_index
-    inside = ((offset[None] >= 1) & (offset[None] <= limit_first[:, None, None])).astype(jnp.float32)
+    offset = shift_blocks[:, None, None] * block_width + col_index[None] - row_index[None]
+    inside = ((offset >= 1) & (offset <= limit_first[:, None, None])).astype(jnp.float32)
     live_mask = ok_first[:, :, None] * ok_second[:, None, :] * inside
     residual = cross_spec * live_mask[None, :, None]
     piece_loss = 0.5 * jnp.sum(residual * residual)
@@ -282,19 +282,30 @@
     ok_ext = lax.dynamic_slice_in_dim(ok_wide, column * GROUP * bw, nblk * bw).reshape(nblk, bw)
     lim = lax.dynamic_slice_in_dim(limits, column * GROUP, GROUP)
 
-    first = ext[:, :GROUP]
-    ok_first = ok_ext[:GROUP]
+    near_acc = [None] * GROUP
+    far_acc = [None] * nblk
     misfit_sum = jnp.zeros((), jnp.float32)
-    near_acc = jnp.zeros((sub, GROUP, 2, W, bw), jnp.float32)
-    far_acc = jnp.zeros((sub, nblk, 2, W, bw), jnp.float32)
-    for s in range(band_blocks + 1):
-        second = ext[:, s : s + GROUP]
+    span = band_blocks + 1
+    groups = [
+        [(bb, t) for bb in range(GROUP) for t in range(lo, hi) if bb <= t < bb + span]
+        for lo, hi in [(GROUP * h, GROUP * (h + 1)) for h in range(halo_cols, -1, -1)]
+    ]
+    for pairs in groups:
+        firsts = [bb for bb, _ in pairs]
+        seconds = [t for _, t in pairs]
+        first = jnp.stack([ext[:, bb] for bb in firsts], axis=1)
+        second = jnp.stack([ext[:, t] for t in seconds], axis=1)
+        shifts = jnp.array([t - bb for bb, t in pairs], jnp.int32)
         piece_loss, near_terms, far_terms = pair_terms(
-            first, second, ok_first, ok_ext[s : s + GROUP], lim, s
+            first, second, jnp.stack([ok_ext[bb] for bb in firsts]),
+            jnp.stack([ok_ext[t] for t in seconds]), jnp.stack([lim[bb] for bb in firsts]), shifts
         )
         misfit_sum = misfit_sum + piece_loss
-        near_acc = near_acc + near_terms
-        far_acc = far_acc.at[:, s : s + GROUP].add(far_terms)
+        for q, (bb, t) in enumerate(pairs):
+            near_acc[bb] = near_terms[:, q] if near_acc[bb] is None else near_acc[bb] + near_terms[:, q]
+            far_acc[t] = far_terms[:, q] if far_acc[t] is None else far_acc[t] + far_terms[:, q]
+    near_acc = jnp.stack(near_acc, axis=1)
+    far_acc = jnp.stack(far_acc, axis=1)
     adj = near_acc + far_acc[:, :GROUP]
     for h in range(1, halo_cols + 1):
         adj = adj + permute(far_acc[:, h * GROUP : (h + 1) * GROUP], shift_pairs(peers, GROUP * h))

time: 185 us -> 199 us (1.076)
  the two profiles are of different devices: /device:TPU:1 before, /device:TPU:257 now
where the time goes in v8:
time: 199 us; the launch traced here: 198 us
  Pallas kernels  98.5 us (49%)
  local copies, waits for them, and re-layouts  41.4 us (21%)
  matrix products  25 us (13%)
  other arithmetic  23.5 us (12%)
  between operations  5.21 us (3%)
  starting transfers between devices  4.42 us (2%)
    pallas_call x1, Pallas kernels, finish(): pl.pallas_call(functools.partial(tail_kernel, n_col, n_f), out_shape=(jax...  57.4 us
    pallas_call x1, Pallas kernels, gather_columns(): pl.pallas_call(functools.partial(head_kernel, n_halves, halo_cols), out_s...  41 us
    unnamed x121, local copies, waits for them, and re-layouts  17.2 us
    dot_general x3, matrix products, pair_terms(): jnp.einsum('fbxrc,fbrd->fbxcd', stacked_left, right_rows, preferred_eleme...  15.3 us
    another operation x3, local copies, waits for them, and re-layouts, shards(): jnp.stack([lim[bb] for bb in firsts])  11.8 us
    dot_general x3, matrix products, pair_terms(): jnp.einsum('fbxcd,fbvd->fbxvc', rounded, far_spec, preferred_element_type...  6.74 us
    mul x4, other arithmetic, pair_terms(): scaled = first * row_scale[None, None, None, :, None]  4.43 us
    ppermute x2, starting transfers between devices, permute(): return lax.ppermute(x, 'chan', pairs)  4.42 us
  transfers between devices with their start and end apart: 2, of which 0 were waited for; matrix products, arithmetic and copies ran while one was open for 21% of the time, Pallas kernels for 0%

profile of v8, /device:TPU:257, one launch (start us, length us, event | category | flops | bytes accessed | tf_op | source)
XLA Modules:
  0.0 198.0 jit_solution(6879553067291309272)
XLA Ops:
  2.7 1.8 pad_maximum_fusion.6
  4.5 41.0 %shard_map.86 = bf16[2,3,4,4,2,24,128]{6,5,4,3,2,1,0:T(8,128)(2,1)} custom-call(bf16[4,2,4,2,24,128]{5,4,3,2,1,0:T(8,128)(2,1)} %bitcast.173), custom_call_target="tpu_custom_call" | custom-call | tf_op jit(solution)/shard_map/pallas_call | solution.py:145
  45.5 1.6 copy.22
  48.7 1.1 fusion.185
  58.5 1.4 broadcast_multiply_fusion.2
  59.9 1.1 slice_bitcast_fusion.1
  61.0 1.1 maximum_bitcast_fusion.1
  62.1 1.5 broadcast_multiply_fusion.4
  63.8 2.8 %stack.156 = s32[10]{0:T(128)S(1)} concatenate(s32[2]{0:T(128)S(1)} %copy-done.28, s32[2]{0:T(128)S(1)} %copy-done.26, s32[1]{0:T(128)} %get-tuple-element.113, s32[2]{0:T(128)S(1)} %copy-done.24, s32[1]{0:T(128)} %get-tuple-element.112, s32[1]{0:T(128)} %get-tuple-element.112, s32[1]{0:T(128)} %get-tuple-element.112), dimensions={0} | concatenate | bytes 80 | tf_op jit(solution)/shard_map/stack | solution.py:301
  66.9 2.6 %pad_maximum_fusion.3 = (bf16[8,10,2,24,128]{4,3,2,1,0:T(8,128)(2,1)S(1)}, bf16[8,10,2,24,128]{4,3,2,1,0:T(8,128)(2,1)}) fusion(bf16[8,4,2,24,128]{4,3,2,1,0:T(8,128)(2,1)} %get-tuple-element.58, bf16[8,3,2,24,128]{4,3,2,1,0:T(8,128)(2,1)} %get-tuple-element.60, bf16[8,2,2,24,128]{4,3,2,1,0:T(8,128)(2,1)} %get-tuple-element.46, ...), kind=kLoop, calls=%fused_computation.179 | loop fusion | flops 2949120 | bytes 3932160 | tf_op jit(solution)/shard_map/stack | solution.py:297
  69.4 4.1 %multiply_reduce_fusion.2 = (f32[]{:T(128)}, bf16[8,10,2,128,128]{4,3,2,1,0:T(8,128)(2,1)S(1)}) fusion(f32[10,128,128]{2,1,0:T(8,128)S(1)} %multiply_select_fusion.2, bf16[8,10,48,128,1]{3,2,4,1,0:T(8,128)(2,1)S(1)} %bitcast.163, bf16[8,10,1,48,128]{4,3,2,1,0:T(8,128)(2,1)S(1)} %copy-done.15, bf16[8,10,1,48,128]{4,3,2,1,0:T(8,128)(2,1)S(1)} %copy-done.17), kind=kOutput, calls=%fused_computation.3 | convolution fusion | flops 263127040 | bytes 8847364 | tf_op jit(solution)/shard_map/fbxrc,fbrd->fbxcd/dot_general | solution.py:50
  74.3 1.5 copy-done.1
  77.0 2.1 %collective-permute-start.1 = (f32[8,4,2,16,128]{4,3,2,0,1:T(8,128)}, f32[8,4,2,16,128]{4,3,2,0,1:T(8,128)}, u32[]{:S(2)}, u32[]{:S(2)}) collective-permute-start(f32[8,4,2,16,128]{4,3,2,0,1:T(8,128)} %fusion.54), channel_id=1, source_target_pairs={{0,64},{8,72},{16,80},{24,88},{32,96},{40,104},{48,112},{56,120},{... | collective-permute-start | bytes 1572872 | tf_op jit(solution)/shard_map/ppermute | solution.py:17
  79.7 1.3 copy-done.13
  81.0 1.3 broadcast_multiply_fusion.1
  83.8 6.5 %stack.167 = s32[16]{0:T(128)S(1)} concatenate(s32[1]{0:T(128)} %get-tuple-element.111, s32[1]{0:T(128)} %get-tuple-element.111, s32[1]{0:T(128)} %get-tuple-element.111, s32[2]{0:T(128)S(1)} %copy-done.29, s32[1]{0:T(128)} %get-tuple-element.110, s32[1]{0:T(128)} %get-tuple-element.110, s32[2]{0:T(128)S(1)} %copy-done.27, s32[1]{0:T(128)} %get-tuple-element.113, ...), dimensions={0} | concatenate | bytes 128 | tf_op jit(solution)/shard_map/stack | solution.py:301
  90.4 2.5 %maximum_bitcast_fusion = bf16[8,16,1,48,128]{4,3,1,0,2:T(8,128)(2,1)} fusion(bf16[8,16,24,128]{3,2,1,0:T(8,128)(2,1)} %get-tuple-element.32, bf16[8,16,24,128]{3,2,1,0:T(8,128)(2,1)S(1)} %get-tuple-element.31), kind=kLoop, calls=%fused_computation.167 | loop fusion | flops 3145728 | bytes 3145728 | tf_op jit(solution)/shard_map/stack | solution.py:42
  93.3 7.2 %multiply_reduce_fusion = (f32[]{:T(128)}, bf16[8,16,2,128,128]{4,3,2,1,0:T(8,128)(2,1)S(1)}) fusion(f32[16,128,128]{2,1,0:T(8,128)S(1)} %multiply_select_fusion, bf16[8,16,48,128,1]{3,2,4,1,0:T(8,128)(2,1)S(1)} %bitcast.155, bf16[8,16,1,48,128]{4,3,1,0,2:T(8,128)(2,1)} %maximum_bitcast_fusion, bf16[8,16,1,48,128]{4,3,1,0,2:T(8,128)(2,1)} %broadcast_multiply_fusion.1), kind=kOutput, calls=%fused_computation | convolution fusion | flops 421003264 | bytes 14155780 | tf_op jit(solution)/shard_map/fbxrc,fbrd->fbxcd/dot_general | solution.py:50
  100.6 1.3 fusion.17
  101.8 2.1 %copy-done = bf16[8,16,2,128,128]{4,3,2,1,0:T(8,128)(2,1)} copy-done((bf16[8,16,2,128,128]{4,3,2,1,0:T(8,128)(2,1)}, bf16[8,16,2,128,128]{4,3,2,1,0:T(8,128)(2,1)S(1)}, u32[]{:S(2)}) %copy-start) | copy-done | bytes 8388632
  105.2 2.3 %collective-permute-start = (f32[8,4,2,16,128]{4,3,2,0,1:T(8,128)}, f32[8,4,2,16,128]{4,3,2,0,1:T(8,128)}, u32[]{:S(2)}, u32[]{:S(2)}) collective-permute-start(f32[8,4,2,16,128]{4,3,2,0,1:T(8,128)} %pad_maximum_fusion.5), channel_id=1, source_target_pairs={{0,32},{8,40},{16,48},{24,56},{32,64},{40,72},{48,80},{56,88},{64,... | collective-permute-start | bytes 1572872 | tf_op jit(solution)/shard_map/ppermute | solution.py:17
  107.6 2.5 %stack.176 = s32[10]{0:T(128)S(1)} concatenate(s32[1]{0:T(128)} %get-tuple-element.111, s32[1]{0:T(128)} %get-tuple-element.111, s32[1]{0:T(128)} %get-tuple-element.111, s32[2]{0:T(128)S(1)} %copy-done.29, s32[1]{0:T(128)} %get-tuple-element.110, s32[2]{0:T(128)S(1)} %copy-done.27, s32[2]{0:T(128)S(1)} %copy-done.25), dimensions={0} | concatenate | bytes 80 | tf_op jit(solution)/shard_map/stack | solution.py:301
  110.5 1.2 slice.915
  113.5 4.0 %multiply_reduce_fusion.1 = (f32[]{:T(128)}, bf16[8,10,2,128,128]{4,3,2,1,0:T(8,128)(2,1)S(1)}) fusion(f32[10,128,128]{2,1,0:T(8,128)S(1)} %multiply_select_fusion.1, bf16[8,10,48,128,1]{3,2,4,1,0:T(8,128)(2,1)S(1)} %bitcast.162, bf16[8,10,1,48,128]{4,3,1,0,2:T(8,128)(2,1)S(1)} %maximum_bitcast_fusion.2, bf16[8,10,1,48,128]{4,3,1,0,2:T(8,128)(2,1)S(1)} %copy-done.16), kind=kOutput, calls=%fused_computation.2 | convolution fusion | flops 263127040 | bytes 8847364 | tf_op jit(solution)/shard_map/fbxrc,fbrd->fbxcd/dot_general | solution.py:50
  118.3 1.9 fusion.32
  120.8 1.9 fusion.26
  123.9 3.0 %fusion.14 = f32[8,16,2,32,128]{4,3,2,0,1:T(8,128)S(1)} fusion(bf16[8,16,2,128,128]{4,3,2,1,0:T(8,128)(2,1)S(1)} %bitcast.151, bf16[8,16,32,128,1]{3,2,1,0,4:T(8,128)(2,1)S(1)} %bitcast.156), kind=kOutput, calls=%fused_computation.153 | convolution fusion | flops 268435456 | bytes 13631488 | tf_op jit(solution)/shard_map/fbxcd,fbvd->fbxvc/dot_general | solution.py:63
  130.5 2.1 %fusion.153 = (f32[8,1,2,16,128]{4,3,2,0,1:T(8,128)S(1)}, f32[8,1,2,16,128]{4,3,2,0,1:T(8,128)S(1)}, f32[8,1,2,16,128]{4,3,2,0,1:T(8,128)S(1)}) fusion(f32[8,10,1,16,128]{4,3,2,0,1:T(8,128)S(1)} %get-tuple-element.23, f32[8,10,1,16,128]{4,3,2,0,1:T(8,128)} %copy-done.4, f32[8,16,1,16,128]{4,3,2,0,1:T(8,128)} %copy-done.3, ...), kind=kLoop, calls=%fused_computation.322 | loop fusion | flops 1671168 | bytes 5111808 | tf_op jit(solution)/shard_map/add | solution.py:305
  132.9 2.2 %fusion.58.blocks_ref = f32[4,8,2,16,128]{4,3,2,1,0:T(8,128)} fusion(f32[8,4,2,16,128]{4,3,2,0,1:T(8,128)} %collective-permute-done.1, f32[8,4,2,16,128]{4,3,2,0,1:T(8,128)} %collective-permute-done, f32[8,1,2,16,128]{4,3,2,0,1:T(8,128)S(1)} %fusion.181, f32[8,1,2,16,128]{4,3,2,0,1:T(8,128)S(1)} %get-tuple-element.14, ...), kind=kLoop, calls=%fused_computation.218 | loop fusion | flops 1310720 | bytes 2621440 | tf_op jit(solution)/shard_map/transpose | solution.py:314
  135.7 57.4 %shard_map.87 = (f32[4,8,2,16,128]{4,3,2,1,0:T(8,128)}, f32[8,128]{1,0:T(8,128)}) custom-call(f32[4,8,2,16,128]{4,3,2,1,0:T(8,128)} %fusion.58.blocks_ref, f32[8,128]{1,0:T(8,128)} %broadcast_in_dim.2.val_ref), custom_call_target="tpu_custom_call" | custom-call | tf_op jit(solution)/shard_map/pallas_call | solution.py:243
  193.2 1.2 slice.800
  195.0 1.9 copy.194
  (172 shorter events, 25.4 us)
Async XLA Ops:
  48.0 1.7 copy-start.33
  48.0 2.4 %copy-start.18 = (s32[8192]{0:T(1024)S(1)}, s32[8192]{0:T(1024)}, u32[]{:S(2)}) copy-start(s32[8192]{0:T(1024)} %param.9) | copy-start | bytes 98308
  62.1 1.6 copy-start.23
  62.1 1.6 copy-start.30
  62.1 1.6 copy-start.31
  62.1 1.6 copy-start.32
  62.1 1.7 copy-start.24
  62.1 1.7 copy-start.26
  62.1 1.7 copy-start.28
  62.1 4.5 %copy-start.39 = (s32[10]{0:T(128)S(1)}, s32[10]{0:T(128)}, u32[]{:S(2)}) copy-start(s32[10]{0:T(128)} %constant.61) | copy-start | bytes 124
  62.1 4.7 %copy-start.14 = (bf16[8,4,2,24,128]{4,3,2,1,0:T(8,128)(2,1)S(1)}, bf16[8,4,2,24,128]{4,3,2,1,0:T(8,128)(2,1)}, u32[]{:S(2)}) copy-start(bf16[8,4,2,24,128]{4,3,2,1,0:T(8,128)(2,1)} %get-tuple-element.56) | copy-start | bytes 1179652
  66.8 2.6 %copy-start.15 = (bf16[8,10,1,48,128]{4,3,2,1,0:T(8,128)(2,1)S(1)}, bf16[8,10,1,48,128]{4,3,2,1,0:T(8,128)(2,1)}, u32[]{:S(2)}) copy-start(bf16[8,10,1,48,128]{4,3,2,1,0:T(8,128)(2,1)} %maximum_bitcast_fusion.1) | copy-start | bytes 2949124
  66.8 2.6 %copy-start.17 = (bf16[8,10,1,48,128]{4,3,2,1,0:T(8,128)(2,1)S(1)}, bf16[8,10,1,48,128]{4,3,2,1,0:T(8,128)(2,1)}, u32[]{:S(2)}) copy-start(bf16[8,10,1,48,128]{4,3,2,1,0:T(8,128)(2,1)} %get-tuple-element.107) | copy-start | bytes 2949124
  69.4 4.1 %copy-start.8 = (bf16[8,10,2,24,128]{4,3,2,1,0:T(8,128)(2,1)}, bf16[8,10,2,24,128]{4,3,2,1,0:T(8,128)(2,1)S(1)}, u32[]{:S(2)}) copy-start(bf16[8,10,2,24,128]{4,3,2,1,0:T(8,128)(2,1)S(1)} %get-tuple-element.117) | copy-start | bytes 2949124
  73.5 2.4 %copy-start.1 = (bf16[8,10,2,128,128]{4,3,2,1,0:T(8,128)(2,1)}, bf16[8,10,2,128,128]{4,3,2,1,0:T(8,128)(2,1)S(1)}, u32[]{:S(2)}) copy-start(bf16[8,10,2,128,128]{4,3,2,1,0:T(8,128)(2,1)S(1)} %get-tuple-element.11) | copy-start | bytes 15728644
  77.0 55.8 %collective-permute-start.1 = (f32[8,4,2,16,128]{4,3,2,0,1:T(8,128)}, f32[8,4,2,16,128]{4,3,2,0,1:T(8,128)}, u32[]{:S(2)}, u32[]{:S(2)}) collective-permute-start(f32[8,4,2,16,128]{4,3,2,0,1:T(8,128)} %fusion.54), channel_id=1, source_target_pairs={{0,64},{8,72},{16,80},{24,88},{32,96},{40,104},{48,112},{56,120},{... | collective-permute-start | bytes 1572872 | tf_op jit(solution)/shard_map/ppermute | solution.py:17
  79.5 1.4 copy-start.13
  90.3 2.5 %copy-start.19 = (f32[1,128]{1,0:T(1,128)S(1)}, f32[1,128]{1,0:T(1,128)}, u32[]{:S(2)}) copy-start(f32[1,128]{1,0:T(1,128)} %get-tuple-element.94) | copy-start | bytes 1540
  90.3 2.5 %copy-start.20 = (f32[1,128]{1,0:T(1,128)S(1)}, f32[1,128]{1,0:T(1,128)}, u32[]{:S(2)}) copy-start(f32[1,128]{1,0:T(1,128)} %get-tuple-element.95) | copy-start | bytes 1540
  90.3 2.5 %copy-start.21 = (f32[1,128]{1,0:T(1,128)S(1)}, f32[1,128]{1,0:T(1,128)}, u32[]{:S(2)}) copy-start(f32[1,128]{1,0:T(1,128)} %get-tuple-element.96) | copy-start | bytes 1540
  90.3 2.5 %copy-start.22 = (f32[1,128]{1,0:T(1,128)S(1)}, f32[1,128]{1,0:T(1,128)}, u32[]{:S(2)}) copy-start(f32[1,128]{1,0:T(1,128)} %get-tuple-element.97) | copy-start | bytes 1540
  90.4 2.6 %copy-start.37 = (s32[16]{0:T(128)S(1)}, s32[16]{0:T(128)}, u32[]{:S(2)}) copy-start(s32[16]{0:T(128)} %constant.62) | copy-start | bytes 196
  100.6 3.3 %copy-start = (bf16[8,16,2,128,128]{4,3,2,1,0:T(8,128)(2,1)}, bf16[8,16,2,128,128]{4,3,2,1,0:T(8,128)(2,1)S(1)}, u32[]{:S(2)}) copy-start(bf16[8,16,2,128,128]{4,3,2,1,0:T(8,128)(2,1)S(1)} %get-tuple-element.7) | copy-start | bytes 25165828
  104.4 6.0 %copy-start.9 = (bf16[8,10,2,24,128]{4,3,2,1,0:T(8,128)(2,1)S(1)}, bf16[8,10,2,24,128]{4,3,2,1,0:T(8,128)(2,1)}, u32[]{:S(2)}) copy-start(bf16[8,10,2,24,128]{4,3,2,1,0:T(8,128)(2,1)} %copy-done.8) | copy-start | bytes 2949124
  105.2 27.7 %collective-permute-start = (f32[8,4,2,16,128]{4,3,2,0,1:T(8,128)}, f32[8,4,2,16,128]{4,3,2,0,1:T(8,128)}, u32[]{:S(2)}, u32[]{:S(2)}) collective-permute-start(f32[8,4,2,16,128]{4,3,2,0,1:T(8,128)} %pad_maximum_fusion.5), channel_id=1, source_target_pairs={{0,32},{8,40},{16,48},{24,56},{32,64},{40,72},{48,80},{56,88},{64,... | collective-permute-start | bytes 1572872 | tf_op jit(solution)/shard_map/ppermute | solution.py:17
  118.3 2.2 %slice-start.2 = ((s8[5242880]{0:T(1024)(128)(4,1)}), s8[4194304]{0:T(1024)(128)(4,1)S(1)}, s32[]{:S(2)}) async-start(s8[5242880]{0:T(1024)(128)(4,1)} %bitcast.152), calls=%async_computation.2 | async-start | bytes 8388608
  118.3 2.5 %slice-start.3 = ((s8[5242880]{0:T(1024)(128)(4,1)}), s8[1048576]{0:T(1024)(128)(4,1)S(1)}, s32[]{:S(2)}) async-start(s8[5242880]{0:T(1024)(128)(4,1)} %bitcast.152), calls=%async_computation.3 | async-start | bytes 2097152
  120.2 2.7 %slice-start = ((s8[8388608]{0:T(1024)(128)(4,1)}), s8[4194304]{0:T(1024)(128)(4,1)S(1)}, s32[]{:S(2)}) async-start(s8[8388608]{0:T(1024)(128)(4,1)} %bitcast.150), calls=%async_computation | async-start | bytes 8388608
  120.4 6.8 %copy-start.4 = (f32[8,10,1,16,128]{4,3,2,0,1:T(8,128)}, f32[8,10,1,16,128]{4,3,2,0,1:T(8,128)S(1)}, u32[]{:S(2)}) copy-start(f32[8,10,1,16,128]{4,3,2,0,1:T(8,128)S(1)} %get-tuple-element.24) | copy-start | bytes 1966084
  120.8 3.1 %slice-start.1 = ((s8[8388608]{0:T(1024)(128)(4,1)}), s8[4194304]{0:T(1024)(128)(4,1)S(1)}, s32[]{:S(2)}) async-start(s8[8388608]{0:T(1024)(128)(4,1)} %bitcast.150), calls=%async_computation.1 | async-start | bytes 8388608
  122.9 4.3 %copy-start.5 = (f32[8,10,1,16,128]{4,3,2,0,1:T(8,128)}, f32[8,10,1,16,128]{4,3,2,0,1:T(8,128)S(1)}, u32[]{:S(2)}) copy-start(f32[8,10,1,16,128]{4,3,2,0,1:T(8,128)S(1)} %get-tuple-element.21) | copy-start | bytes 1966084
  122.9 4.3 %copy-start.6 = (f32[8,10,1,16,128]{4,3,2,0,1:T(8,128)}, f32[8,10,1,16,128]{4,3,2,0,1:T(8,128)S(1)}, u32[]{:S(2)}) copy-start(f32[8,10,1,16,128]{4,3,2,0,1:T(8,128)S(1)} %get-tuple-element.22) | copy-start | bytes 1966084
  (14 other events, 15.8 us)

commit v9 on v7

--- a/solution.py
+++ b/solution.py
@@ -286,18 +286,26 @@
     ok_first = ok_ext[:GROUP]
     misfit_sum = jnp.zeros((), jnp.float32)
     near_acc = jnp.zeros((sub, GROUP, 2, W, bw), jnp.float32)
-    far_acc = jnp.zeros((sub, nblk, 2, W, bw), jnp.float32)
-    for s in range(band_blocks + 1):
+    far_acc = [jnp.zeros((sub, 2, W, bw), jnp.float32) for _ in range(nblk)]
+    sent = []
+    for s in range(band_blocks, -1, -1):
         second = ext[:, s : s + GROUP]
         piece_loss, near_terms, far_terms = pair_terms(
             first, second, ok_first, ok_ext[s : s + GROUP], lim, s
         )
         misfit_sum = misfit_sum + piece_loss
         near_acc = near_acc + near_terms
-        far_acc = far_acc.at[:, s : s + GROUP].add(far_terms)
-    adj = near_acc + far_acc[:, :GROUP]
-    for h in range(1, halo_cols + 1):
-        adj = adj + permute(far_acc[:, h * GROUP : (h + 1) * GROUP], shift_pairs(peers, GROUP * h))
+        for bb in range(GROUP):
+            far_acc[s + bb] = far_acc[s + bb] + far_terms[:, bb]
+        for h in range(1, halo_cols + 1):
+            if s == max(GROUP * h - GROUP + 1, 0) and h * GROUP < nblk:
+                done = jnp.stack(far_acc[h * GROUP : (h + 1) * GROUP], axis=1)
+                done, ext = lax.optimization_barrier((done, ext))
+                first = ext[:, :GROUP]
+                sent.append(permute(done, shift_pairs(peers, GROUP * h)))
+    adj = near_acc + jnp.stack(far_acc[:GROUP], axis=1)
+    for part in sent:
+        adj = adj + part
     adj = adj * (1.0 / W)
 
     blocks = jnp.transpose(adj, (1, 0, 2, 3, 4))

time: 185 us -> 180 us (0.973)
  the two profiles are of different devices: /device:TPU:1 before, /device:TPU:257 now
where the time goes in v9:
time: 180 us; the launch traced here: 179 us
  Pallas kernels  98.4 us (55%)
  matrix products  29.4 us (16%)
  other arithmetic  24.7 us (14%)
  local copies, waits for them, and re-layouts  12.9 us (7%)
  between operations  8.89 us (5%)
  starting transfers between devices  4.42 us (2%)
    pallas_call x1, Pallas kernels, finish(): pl.pallas_call(functools.partial(tail_kernel, n_col, n_f), out_shape=(jax...  57.4 us
    pallas_call x1, Pallas kernels, gather_columns(): pl.pallas_call(functools.partial(head_kernel, n_halves, halo_cols), out_s...  41 us
    dot_general x9, matrix products, pair_terms(): jnp.einsum('fbxrc,fbrd->fbxcd', stacked_left, right_rows, preferred_eleme...  18.4 us
    dot_general x9, matrix products, pair_terms(): jnp.einsum('fbxcd,fbvd->fbxvc', rounded, far_spec, preferred_element_type...  7.28 us
    sub x9, other arithmetic, pair_terms(): first_real = toward[:, :, 0, :W] - toward[:, :, 1, W:]  6.91 us
    unnamed x67, local copies, waits for them, and re-layouts  4.64 us
    ppermute x2, starting transfers between devices, permute(): return lax.ppermute(x, 'chan', pairs)  4.42 us
    dot_general x9, matrix products, pair_terms(): jnp.einsum('fbxcd,fbvc->fbxvd', rounded, near_spec, preferred_element_typ...  3.73 us
  transfers between devices with their start and end apart: 2, of which 0 were waited for; matrix products, arithmetic and copies ran while one was open for 17% of the time, Pallas kernels for 0%

profile of v9, /device:TPU:257, one launch (start us, length us, event | category | flops | bytes accessed | tf_op | source)
XLA Modules:
  0.0 178.7 jit_solution(7878469224857629157)
XLA Ops:
  5.8 1.8 %pad_maximum_fusion.4 = bf16[32,2,24,128]{3,2,1,0:T(8,128)(2,1)} fusion(bf16[32,2,8,128]{3,2,1,0:T(8,128)(2,1)} %param.5, bf16[32,2,16,128]{3,2,1,0:T(8,128)(2,1)} %param.4), kind=kLoop, calls=%fused_computation.159 | loop fusion | flops 786432 | bytes 786432 | tf_op jit(solution)/shard_map/concatenate | solution.py:267
  7.6 41.0 %shard_map.59 = bf16[2,3,4,4,2,24,128]{6,5,4,3,2,1,0:T(8,128)(2,1)} custom-call(bf16[4,2,4,2,24,128]{5,4,3,2,1,0:T(8,128)(2,1)} %bitcast.189), custom_call_target="tpu_custom_call" | custom-call | tf_op jit(solution)/shard_map/pallas_call | solution.py:145
  48.7 1.6 copy.30
  50.6 1.3 fusion.194
  52.1 1.4 convert_element_type.39
  53.5 1.3 slice.735
  57.0 1.3 multiply_select_fusion
  58.4 2.0 %multiply_reduce_fusion.7 = (f32[]{:T(128)}, bf16[8,4,2,128,128]{4,3,2,1,0:T(8,128)(2,1)S(1)}) fusion(f32[4,128,128]{2,1,0:T(8,128)S(1)} %get-tuple-element.115, bf16[8,4,48,128,1]{3,2,4,1,0:T(8,128)(2,1)S(1)} %bitcast.216, bf16[8,4,1,48,128]{4,3,2,1,0:T(8,128)(2,1)S(1)} %maximum_bitcast_fusion, bf16[8,4,1,48,128]{4,3,2,1,0:T(8,128)(2,1)S(1)} %bitcast.203), kind=kOutput, calls=%fused_computation.7 | convolution fusion | flops 105250816 | bytes 3538948 | tf_op jit(solution)/shard_map/fbxrc,fbrd->fbxcd/dot_general | solution.py:50
  61.4 2.0 %multiply_reduce_fusion.6 = (f32[]{:T(128)}, bf16[8,4,2,128,128]{4,3,2,1,0:T(8,128)(2,1)S(1)}) fusion(f32[4,128,128]{2,1,0:T(8,128)S(1)} %get-tuple-element.116, bf16[8,4,48,128,1]{3,2,4,1,0:T(8,128)(2,1)S(1)} %bitcast.215, bf16[8,4,1,48,128]{4,3,2,1,0:T(8,128)(2,1)S(1)} %maximum_bitcast_fusion, bf16[8,4,1,48,128]{4,3,2,1,0:T(8,128)(2,1)S(1)} %bitcast.204), kind=kOutput, calls=%fused_computation.6 | convolution fusion | flops 105250816 | bytes 3538948 | tf_op jit(solution)/shard_map/fbxrc,fbrd->fbxcd/dot_general | solution.py:50
  64.9 2.0 %multiply_reduce_fusion.8 = (f32[]{:T(128)}, bf16[8,4,2,128,128]{4,3,2,1,0:T(8,128)(2,1)S(1)}) fusion(f32[4,128,128]{2,1,0:T(8,128)S(1)} %get-tuple-element.122, bf16[8,4,48,128,1]{3,2,4,1,0:T(8,128)(2,1)S(1)} %bitcast.214, bf16[8,4,1,48,128]{4,3,2,1,0:T(8,128)(2,1)S(1)} %maximum_bitcast_fusion, bf16[8,4,1,48,128]{4,3,2,1,0:T(8,128)(2,1)S(1)} %bitcast.205), kind=kOutput, calls=%fused_computation.8 | convolution fusion | flops 105250816 | bytes 3538948 | tf_op jit(solution)/shard_map/fbxrc,fbrd->fbxcd/dot_general | solution.py:50
  67.9 2.0 %multiply_reduce_fusion.5 = (f32[]{:T(128)}, bf16[8,4,2,128,128]{4,3,2,1,0:T(8,128)(2,1)S(1)}) fusion(f32[4,128,128]{2,1,0:T(8,128)S(1)} %get-tuple-element.117, bf16[8,4,48,128,1]{3,2,4,1,0:T(8,128)(2,1)S(1)} %bitcast.213, bf16[8,4,1,48,128]{4,3,2,1,0:T(8,128)(2,1)S(1)} %maximum_bitcast_fusion, bf16[8,4,1,48,128]{4,3,2,1,0:T(8,128)(2,1)S(1)} %bitcast.206), kind=kOutput, calls=%fused_computation.5 | convolution fusion | flops 105250816 | bytes 3538948 | tf_op jit(solution)/shard_map/fbxrc,fbrd->fbxcd/dot_general | solution.py:50
  70.5 0.8 fusion.93
  71.4 2.1 %collective-permute-start = (f32[8,4,2,16,128]{4,3,2,0,1:T(8,128)}, f32[8,4,2,16,128]{4,3,2,0,1:T(8,128)}, u32[]{:S(2)}, u32[]{:S(2)}) collective-permute-start(f32[8,4,2,16,128]{4,3,2,0,1:T(8,128)} %fusion.93), channel_id=1, source_target_pairs={{0,64},{8,72},{16,80},{24,88},{32,96},{40,104},{48,112},{56,120},{... | collective-permute-start | bytes 1572872 | tf_op jit(solution)/shard_map/ppermute | solution.py:17
  74.2 2.1 %multiply_reduce_fusion.2 = (f32[]{:T(128)}, bf16[8,4,2,128,128]{4,3,2,1,0:T(8,128)(2,1)S(1)}) fusion(f32[4,128,128]{2,1,0:T(8,128)S(1)} %get-tuple-element.121, bf16[8,4,48,128,1]{3,2,4,1,0:T(8,128)(2,1)S(1)} %bitcast.202, bf16[8,4,1,48,128]{4,3,1,0,2:T(8,128)(2,1)S(1)} %maximum_bitcast_fusion.1, bf16[8,4,1,48,128]{4,3,1,0,2:T(8,128)(2,1)S(1)} %bitcast.207), kind=kOutput, calls=%fused_computation.2 | convolution fusion | flops 105250816 | bytes 3538948 | tf_op jit(solution)/shard_map/fbxrc,fbrd->fbxcd/dot_general | solution.py:50
  76.8 2.1 %multiply_reduce_fusion.1 = (f32[]{:T(128)}, bf16[8,4,2,128,128]{4,3,2,1,0:T(8,128)(2,1)S(1)}) fusion(f32[4,128,128]{2,1,0:T(8,128)S(1)} %get-tuple-element.120, bf16[8,4,48,128,1]{3,2,4,1,0:T(8,128)(2,1)S(1)} %bitcast.201, bf16[8,4,1,48,128]{4,3,1,0,2:T(8,128)(2,1)S(1)} %maximum_bitcast_fusion.1, bf16[8,4,1,48,128]{4,3,1,0,2:T(8,128)(2,1)S(1)} %bitcast.208), kind=kOutput, calls=%fused_computation.1 | convolution fusion | flops 105250816 | bytes 3538948 | tf_op jit(solution)/shard_map/fbxrc,fbrd->fbxcd/dot_general | solution.py:50
  79.4 2.1 %multiply_reduce_fusion.4 = (f32[]{:T(128)}, bf16[8,4,2,128,128]{4,3,2,1,0:T(8,128)(2,1)S(1)}) fusion(f32[4,128,128]{2,1,0:T(8,128)S(1)} %get-tuple-element.118, bf16[8,4,48,128,1]{3,2,4,1,0:T(8,128)(2,1)S(1)} %bitcast.200, bf16[8,4,1,48,128]{4,3,1,0,2:T(8,128)(2,1)S(1)} %maximum_bitcast_fusion.1, bf16[8,4,1,48,128]{4,3,1,0,2:T(8,128)(2,1)S(1)} %bitcast.209), kind=kOutput, calls=%fused_computation.4 | convolution fusion | flops 105250816 | bytes 3538948 | tf_op jit(solution)/shard_map/fbxrc,fbrd->fbxcd/dot_general | solution.py:50
  81.9 2.0 %multiply_reduce_fusion.3 = (f32[]{:T(128)}, bf16[8,4,2,128,128]{4,3,2,1,0:T(8,128)(2,1)S(1)}) fusion(f32[4,128,128]{2,1,0:T(8,128)S(1)} %get-tuple-element.119, bf16[8,4,48,128,1]{3,2,4,1,0:T(8,128)(2,1)S(1)} %bitcast.199, bf16[8,4,1,48,128]{4,3,1,0,2:T(8,128)(2,1)S(1)} %maximum_bitcast_fusion.1, bf16[8,4,1,48,128]{4,3,1,0,2:T(8,128)(2,1)S(1)} %bitcast.210), kind=kOutput, calls=%fused_computation.3 | convolution fusion | flops 105250816 | bytes 3538948 | tf_op jit(solution)/shard_map/fbxrc,fbrd->fbxcd/dot_general | solution.py:50
  84.6 0.8 pad_maximum_fusion.3
  85.4 2.3 %collective-permute-start.1 = (f32[8,4,2,16,128]{4,3,2,0,1:T(8,128)}, f32[8,4,2,16,128]{4,3,2,0,1:T(8,128)}, u32[]{:S(2)}, u32[]{:S(2)}) collective-permute-start(f32[8,4,2,16,128]{4,3,2,0,1:T(8,128)} %pad_maximum_fusion.3), channel_id=1, source_target_pairs={{0,32},{8,40},{16,48},{24,56},{32,64},{40,72},{48,80},{56,88},{64,... | collective-permute-start | bytes 1572872 | tf_op jit(solution)/shard_map/ppermute | solution.py:17
  88.2 2.1 %multiply_reduce_fusion = (f32[]{:T(128)}, bf16[8,4,2,128,128]{4,3,2,1,0:T(8,128)(2,1)S(1)}) fusion(f32[4,128,128]{2,1,0:T(8,128)S(1)} %get-tuple-element.114, bf16[8,4,48,128,1]{3,2,4,1,0:T(8,128)(2,1)S(1)} %bitcast.212, bf16[8,4,1,48,128]{4,3,1,0,2:T(8,128)(2,1)S(1)} %maximum_bitcast_fusion.2, bf16[8,4,1,48,128]{4,3,1,0,2:T(8,128)(2,1)S(1)} %bitcast.211), kind=kOutput, calls=%fused_computation | convolution fusion | flops 105250816 | bytes 3538948 | tf_op jit(solution)/shard_map/fbxrc,fbrd->fbxcd/dot_general | solution.py:50
  93.7 0.8 fusion.48
  96.2 0.9 slice_subtract_fusion.17
  97.8 0.9 slice_subtract_fusion.14
  98.7 0.8 fusion.72
  99.5 0.9 slice_subtract_fusion.7
  101.2 0.9 slice_subtract_fusion.6
  102.9 0.9 slice_subtract_fusion.9
  104.6 0.9 slice_subtract_fusion.8
  113.4 2.5 %fusion.105.blocks_ref = f32[4,8,2,16,128]{4,3,2,1,0:T(8,128)} fusion(f32[8,4,2,16,128]{4,3,2,0,1:T(8,128)} %collective-permute-done.1, f32[8,4,2,16,128]{4,3,2,0,1:T(8,128)} %collective-permute-done, f32[8,4,1,16,128]{4,3,2,0,1:T(8,128)S(1)} %copy-done.3, f32[8,4,1,16,128]{4,3,2,0,1:T(8,128)S(1)} %copy-done.2, f32[8,4,1,16,128]{4,3,2,0,1:T(8,128)S(1)} %copy-done, ...), kind=kLoop, calls=%fused_computation.148 | loop fusion | flops 3145728 | bytes 6815744 | tf_op jit(solution)/shard_map/transpose | solution.py:311
  116.5 57.4 %shard_map.60 = (f32[4,8,2,16,128]{4,3,2,1,0:T(8,128)}, f32[8,128]{1,0:T(8,128)}) custom-call(f32[4,8,2,16,128]{4,3,2,1,0:T(8,128)} %fusion.105.blocks_ref, f32[8,128]{1,0:T(8,128)} %broadcast_in_dim.2.val_ref), custom_call_target="tpu_custom_call" | custom-call | tf_op jit(solution)/shard_map/pallas_call | solution.py:243
  173.9 1.2 slice.729
  175.7 1.9 %copy.244 = f32[32,2,16,128]{3,2,1,0:T(8,128)} copy(f32[32,2,16,128]{3,2,1,0:T(8,128)} %bitcast.198) | data formatting | bytes 1048576
  (141 shorter events, 25.8 us)
Async XLA Ops:
  50.5 1.3 copy-start.31
  56.2 2.2 %copy-start.20 = (bf16[8,4,2,24,128]{4,3,2,1,0:T(8,128)(2,1)S(1)}, bf16[8,4,2,24,128]{4,3,2,1,0:T(8,128)(2,1)}, u32[]{:S(2)}) copy-start(bf16[8,4,2,24,128]{4,3,2,1,0:T(8,128)(2,1)} %get-tuple-element.58) | copy-start | bytes 1179652
  60.4 1.0 copy-start.19
  63.4 0.9 copy-start.23
  63.4 0.9 copy-start.24
  63.4 0.9 copy-start.25
  63.4 0.9 copy-start.26
  63.4 0.9 copy-start.27
  63.4 0.9 copy-start.28
  63.4 0.9 copy-start.29
  63.9 1.0 copy-start.18
  66.9 1.0 copy-start.17
  70.4 3.0 %copy-start.32 = (bf16[24]{0:T(256)(128)(2,1)S(1)}, bf16[24]{0:T(256)(128)(2,1)}, u32[]{:S(2)}) copy-start(bf16[24]{0:T(256)(128)(2,1)} %constant.46.clone.1) | copy-start | bytes 148
  71.4 40.9 %collective-permute-start = (f32[8,4,2,16,128]{4,3,2,0,1:T(8,128)}, f32[8,4,2,16,128]{4,3,2,0,1:T(8,128)}, u32[]{:S(2)}, u32[]{:S(2)}) collective-permute-start(f32[8,4,2,16,128]{4,3,2,0,1:T(8,128)} %fusion.93), channel_id=1, source_target_pairs={{0,64},{8,72},{16,80},{24,88},{32,96},{40,104},{48,112},{56,120},{... | collective-permute-start | bytes 1572872 | tf_op jit(solution)/shard_map/ppermute | solution.py:17
  85.4 26.9 %collective-permute-start.1 = (f32[8,4,2,16,128]{4,3,2,0,1:T(8,128)}, f32[8,4,2,16,128]{4,3,2,0,1:T(8,128)}, u32[]{:S(2)}, u32[]{:S(2)}) collective-permute-start(f32[8,4,2,16,128]{4,3,2,0,1:T(8,128)} %pad_maximum_fusion.3), channel_id=1, source_target_pairs={{0,32},{8,40},{16,48},{24,56},{32,64},{40,72},{48,80},{56,88},{64,... | collective-permute-start | bytes 1572872 | tf_op jit(solution)/shard_map/ppermute | solution.py:17
  111.2 1.1 copy-start
  111.2 1.1 copy-start.1
  111.3 1.1 copy-start.2
  111.3 1.2 copy-start.3
  111.3 1.2 copy-start.4
  111.3 1.3 copy-start.5
  111.3 1.4 copy-start.6
  111.3 1.4 copy-start.7
  111.3 1.5 copy-start.8
  111.3 1.6 copy-start.9
  111.3 1.7 copy-start.10
  111.3 1.7 copy-start.11
  111.4 1.8 %copy-start.12 = (f32[8,4,1,16,128]{4,3,2,0,1:T(8,128)S(1)}, f32[8,4,1,16,128]{4,3,2,0,1:T(8,128)}, u32[]{:S(2)}) copy-start(f32[8,4,1,16,128]{4,3,2,0,1:T(8,128)} %get-tuple-element.70) | copy-start | bytes 786436
  111.4 1.9 %copy-start.13 = (f32[8,4,1,16,128]{4,3,2,0,1:T(8,128)S(1)}, f32[8,4,1,16,128]{4,3,2,0,1:T(8,128)}, u32[]{:S(2)}) copy-start(f32[8,4,1,16,128]{4,3,2,0,1:T(8,128)} %get-tuple-element.71) | copy-start | bytes 786436
  111.4 1.9 %copy-start.14 = (f32[8,1,2,16,128]{4,3,2,0,1:T(8,128)S(1)}, f32[8,1,2,16,128]{4,3,2,0,1:T(8,128)}, u32[]{:S(2)}) copy-start(f32[8,1,2,16,128]{4,3,2,0,1:T(8,128)} %get-tuple-element.33) | copy-start | bytes 393220
  111.4 1.9 %copy-start.15 = (f32[8,1,2,16,128]{4,3,2,0,1:T(8,128)S(1)}, f32[8,1,2,16,128]{4,3,2,0,1:T(8,128)}, u32[]{:S(2)}) copy-start(f32[8,1,2,16,128]{4,3,2,0,1:T(8,128)} %get-tuple-element.61) | copy-start | bytes 393220
  111.4 2.0 %copy-start.16 = (f32[8,1,2,16,128]{4,3,2,0,1:T(8,128)S(1)}, f32[8,1,2,16,128]{4,3,2,0,1:T(8,128)}, u32[]{:S(2)}) copy-start(f32[8,1,2,16,128]{4,3,2,0,1:T(8,128)} %fusion.137) | copy-start | bytes 393220
  (3 other events, 2.6 us)

commit v10 on v9

--- a/solution.py
+++ b/solution.py
@@ -9,7 +9,7 @@
 F = 256
 W = 16
 BAND = 1024
-HALVES = 2
+HALVES = 4
 GROUP = 4
 
 

time: 180 us -> 178 us (0.989)
  the two profiles are of different devices: /device:TPU:257 before, /device:TPU:1 now
where the time goes in v10:
time: 178 us; the launch traced here: 177 us
  Pallas kernels  95.8 us (54%)
  matrix products  29.4 us (17%)
  other arithmetic  24.7 us (14%)
  local copies, waits for them, and re-layouts  12.8 us (7%)
  between operations  8.89 us (5%)
  starting transfers between devices  5.59 us (3%)
    pallas_call x1, Pallas kernels, finish(): pl.pallas_call(functools.partial(tail_kernel, n_col, n_f), out_shape=(jax...  48.9 us
    pallas_call x1, Pallas kernels, gather_columns(): pl.pallas_call(functools.partial(head_kernel, n_halves, halo_cols), out_s...  46.9 us
    dot_general x9, matrix products, pair_terms(): jnp.einsum('fbxrc,fbrd->fbxcd', stacked_left, right_rows, preferred_eleme...  18.4 us
    dot_general x9, matrix products, pair_terms(): jnp.einsum('fbxcd,fbvd->fbxvc', rounded, far_spec, preferred_element_type...  7.28 us
    sub x9, other arithmetic, pair_terms(): first_real = toward[:, :, 0, :W] - toward[:, :, 1, W:]  6.91 us
    ppermute x2, starting transfers between devices, permute(): return lax.ppermute(x, 'chan', pairs)  5.59 us
    unnamed x67, local copies, waits for them, and re-layouts  4.64 us
    dot_general x9, matrix products, pair_terms(): jnp.einsum('fbxcd,fbvc->fbxvd', rounded, near_spec, preferred_element_typ...  3.73 us
  transfers between devices with their start and end apart: 2, of which 0 were waited for; matrix products, arithmetic and copies ran while one was open for 17% of the time, Pallas kernels for 0%

profile of v10, /device:TPU:1, one launch (start us, length us, event | category | flops | bytes accessed | tf_op | source)
XLA Modules:
  0.0 177.2 jit_solution(5695499485264404990)
XLA Ops:
  5.8 1.8 %pad_maximum_fusion.4 = bf16[32,2,24,128]{3,2,1,0:T(8,128)(2,1)} fusion(bf16[32,2,8,128]{3,2,1,0:T(8,128)(2,1)} %param.5, bf16[32,2,16,128]{3,2,1,0:T(8,128)(2,1)} %param.4), kind=kLoop, calls=%fused_computation.159 | loop fusion | flops 786432 | bytes 786432 | tf_op jit(solution)/shard_map/concatenate | solution.py:267
  7.6 46.9 %shard_map.59 = bf16[4,3,4,2,2,24,128]{6,5,4,3,2,1,0:T(8,128)(2,1)} custom-call(bf16[4,4,2,2,24,128]{5,4,3,2,1,0:T(8,128)(2,1)} %bitcast.189), custom_call_target="tpu_custom_call" | custom-call | tf_op jit(solution)/shard_map/pallas_call | solution.py:145
  54.5 1.6 copy.30
  56.4 1.3 fusion.194
  57.9 1.4 convert_element_type.39
  59.3 1.3 slice.735
  62.8 1.3 multiply_select_fusion
  64.2 2.0 %multiply_reduce_fusion.7 = (f32[]{:T(128)}, bf16[8,4,2,128,128]{4,3,2,1,0:T(8,128)(2,1)S(1)}) fusion(f32[4,128,128]{2,1,0:T(8,128)S(1)} %get-tuple-element.115, bf16[8,4,48,128,1]{3,2,4,1,0:T(8,128)(2,1)S(1)} %bitcast.216, bf16[8,4,1,48,128]{4,3,2,1,0:T(8,128)(2,1)S(1)} %maximum_bitcast_fusion, bf16[8,4,1,48,128]{4,3,2,1,0:T(8,128)(2,1)S(1)} %bitcast.203), kind=kOutput, calls=%fused_computation.7 | convolution fusion | flops 105250816 | bytes 3538948 | tf_op jit(solution)/shard_map/fbxrc,fbrd->fbxcd/dot_general | solution.py:50
  67.2 2.0 %multiply_reduce_fusion.6 = (f32[]{:T(128)}, bf16[8,4,2,128,128]{4,3,2,1,0:T(8,128)(2,1)S(1)}) fusion(f32[4,128,128]{2,1,0:T(8,128)S(1)} %get-tuple-element.116, bf16[8,4,48,128,1]{3,2,4,1,0:T(8,128)(2,1)S(1)} %bitcast.215, bf16[8,4,1,48,128]{4,3,2,1,0:T(8,128)(2,1)S(1)} %maximum_bitcast_fusion, bf16[8,4,1,48,128]{4,3,2,1,0:T(8,128)(2,1)S(1)} %bitcast.204), kind=kOutput, calls=%fused_computation.6 | convolution fusion | flops 105250816 | bytes 3538948 | tf_op jit(solution)/shard_map/fbxrc,fbrd->fbxcd/dot_general | solution.py:50
  70.7 2.0 %multiply_reduce_fusion.8 = (f32[]{:T(128)}, bf16[8,4,2,128,128]{4,3,2,1,0:T(8,128)(2,1)S(1)}) fusion(f32[4,128,128]{2,1,0:T(8,128)S(1)} %get-tuple-element.122, bf16[8,4,48,128,1]{3,2,4,1,0:T(8,128)(2,1)S(1)} %bitcast.214, bf16[8,4,1,48,128]{4,3,2,1,0:T(8,128)(2,1)S(1)} %maximum_bitcast_fusion, bf16[8,4,1,48,128]{4,3,2,1,0:T(8,128)(2,1)S(1)} %bitcast.205), kind=kOutput, calls=%fused_computation.8 | convolution fusion | flops 105250816 | bytes 3538948 | tf_op jit(solution)/shard_map/fbxrc,fbrd->fbxcd/dot_general | solution.py:50
  73.7 2.0 %multiply_reduce_fusion.5 = (f32[]{:T(128)}, bf16[8,4,2,128,128]{4,3,2,1,0:T(8,128)(2,1)S(1)}) fusion(f32[4,128,128]{2,1,0:T(8,128)S(1)} %get-tuple-element.117, bf16[8,4,48,128,1]{3,2,4,1,0:T(8,128)(2,1)S(1)} %bitcast.213, bf16[8,4,1,48,128]{4,3,2,1,0:T(8,128)(2,1)S(1)} %maximum_bitcast_fusion, bf16[8,4,1,48,128]{4,3,2,1,0:T(8,128)(2,1)S(1)} %bitcast.206), kind=kOutput, calls=%fused_computation.5 | convolution fusion | flops 105250816 | bytes 3538948 | tf_op jit(solution)/shard_map/fbxrc,fbrd->fbxcd/dot_general | solution.py:50
  76.3 0.8 fusion.93
  77.2 2.1 %collective-permute-start = (f32[8,4,2,16,128]{4,3,2,0,1:T(8,128)}, f32[8,4,2,16,128]{4,3,2,0,1:T(8,128)}, u32[]{:S(2)}, u32[]{:S(2)}) collective-permute-start(f32[8,4,2,16,128]{4,3,2,0,1:T(8,128)} %fusion.93), channel_id=1, source_target_pairs={{0,64},{8,72},{16,80},{24,88},{32,96},{40,104},{48,112},{56,120},{... | collective-permute-start | bytes 1572872 | tf_op jit(solution)/shard_map/ppermute | solution.py:17
  80.0 2.1 %multiply_reduce_fusion.2 = (f32[]{:T(128)}, bf16[8,4,2,128,128]{4,3,2,1,0:T(8,128)(2,1)S(1)}) fusion(f32[4,128,128]{2,1,0:T(8,128)S(1)} %get-tuple-element.121, bf16[8,4,48,128,1]{3,2,4,1,0:T(8,128)(2,1)S(1)} %bitcast.202, bf16[8,4,1,48,128]{4,3,1,0,2:T(8,128)(2,1)S(1)} %maximum_bitcast_fusion.1, bf16[8,4,1,48,128]{4,3,1,0,2:T(8,128)(2,1)S(1)} %bitcast.207), kind=kOutput, calls=%fused_computation.2 | convolution fusion | flops 105250816 | bytes 3538948 | tf_op jit(solution)/shard_map/fbxrc,fbrd->fbxcd/dot_general | solution.py:50
  82.6 2.1 %multiply_reduce_fusion.1 = (f32[]{:T(128)}, bf16[8,4,2,128,128]{4,3,2,1,0:T(8,128)(2,1)S(1)}) fusion(f32[4,128,128]{2,1,0:T(8,128)S(1)} %get-tuple-element.120, bf16[8,4,48,128,1]{3,2,4,1,0:T(8,128)(2,1)S(1)} %bitcast.201, bf16[8,4,1,48,128]{4,3,1,0,2:T(8,128)(2,1)S(1)} %maximum_bitcast_fusion.1, bf16[8,4,1,48,128]{4,3,1,0,2:T(8,128)(2,1)S(1)} %bitcast.208), kind=kOutput, calls=%fused_computation.1 | convolution fusion | flops 105250816 | bytes 3538948 | tf_op jit(solution)/shard_map/fbxrc,fbrd->fbxcd/dot_general | solution.py:50
  85.2 2.1 %multiply_reduce_fusion.4 = (f32[]{:T(128)}, bf16[8,4,2,128,128]{4,3,2,1,0:T(8,128)(2,1)S(1)}) fusion(f32[4,128,128]{2,1,0:T(8,128)S(1)} %get-tuple-element.118, bf16[8,4,48,128,1]{3,2,4,1,0:T(8,128)(2,1)S(1)} %bitcast.200, bf16[8,4,1,48,128]{4,3,1,0,2:T(8,128)(2,1)S(1)} %maximum_bitcast_fusion.1, bf16[8,4,1,48,128]{4,3,1,0,2:T(8,128)(2,1)S(1)} %bitcast.209), kind=kOutput, calls=%fused_computation.4 | convolution fusion | flops 105250816 | bytes 3538948 | tf_op jit(solution)/shard_map/fbxrc,fbrd->fbxcd/dot_general | solution.py:50
  87.7 2.0 %multiply_reduce_fusion.3 = (f32[]{:T(128)}, bf16[8,4,2,128,128]{4,3,2,1,0:T(8,128)(2,1)S(1)}) fusion(f32[4,128,128]{2,1,0:T(8,128)S(1)} %get-tuple-element.119, bf16[8,4,48,128,1]{3,2,4,1,0:T(8,128)(2,1)S(1)} %bitcast.199, bf16[8,4,1,48,128]{4,3,1,0,2:T(8,128)(2,1)S(1)} %maximum_bitcast_fusion.1, bf16[8,4,1,48,128]{4,3,1,0,2:T(8,128)(2,1)S(1)} %bitcast.210), kind=kOutput, calls=%fused_computation.3 | convolution fusion | flops 105250816 | bytes 3538948 | tf_op jit(solution)/shard_map/fbxrc,fbrd->fbxcd/dot_general | solution.py:50
  90.4 0.8 pad_maximum_fusion.3
  91.2 3.5 %collective-permute-start.1 = (f32[8,4,2,16,128]{4,3,2,0,1:T(8,128)}, f32[8,4,2,16,128]{4,3,2,0,1:T(8,128)}, u32[]{:S(2)}, u32[]{:S(2)}) collective-permute-start(f32[8,4,2,16,128]{4,3,2,0,1:T(8,128)} %pad_maximum_fusion.3), channel_id=1, source_target_pairs={{0,32},{8,40},{16,48},{24,56},{32,64},{40,72},{48,80},{56,88},{64,... | collective-permute-start | bytes 1572872 | tf_op jit(solution)/shard_map/ppermute | solution.py:17
  95.2 2.1 %multiply_reduce_fusion = (f32[]{:T(128)}, bf16[8,4,2,128,128]{4,3,2,1,0:T(8,128)(2,1)S(1)}) fusion(f32[4,128,128]{2,1,0:T(8,128)S(1)} %get-tuple-element.114, bf16[8,4,48,128,1]{3,2,4,1,0:T(8,128)(2,1)S(1)} %bitcast.212, bf16[8,4,1,48,128]{4,3,1,0,2:T(8,128)(2,1)S(1)} %maximum_bitcast_fusion.2, bf16[8,4,1,48,128]{4,3,1,0,2:T(8,128)(2,1)S(1)} %bitcast.211), kind=kOutput, calls=%fused_computation | convolution fusion | flops 105250816 | bytes 3538948 | tf_op jit(solution)/shard_map/fbxrc,fbrd->fbxcd/dot_general | solution.py:50
  100.7 0.8 fusion.48
  103.1 0.9 slice_subtract_fusion.17
  104.8 0.9 slice_subtract_fusion.14
  105.7 0.8 fusion.72
  106.5 0.9 slice_subtract_fusion.7
  108.2 0.9 slice_subtract_fusion.6
  109.9 0.9 slice_subtract_fusion.9
  111.6 0.9 slice_subtract_fusion.8
  120.3 2.5 %fusion.105.blocks_ref = f32[4,8,2,16,128]{4,3,2,1,0:T(8,128)} fusion(f32[8,4,2,16,128]{4,3,2,0,1:T(8,128)} %collective-permute-done.1, f32[8,4,2,16,128]{4,3,2,0,1:T(8,128)} %collective-permute-done, f32[8,4,1,16,128]{4,3,2,0,1:T(8,128)S(1)} %copy-done.3, f32[8,4,1,16,128]{4,3,2,0,1:T(8,128)S(1)} %copy-done.2, f32[8,4,1,16,128]{4,3,2,0,1:T(8,128)S(1)} %copy-done, ...), kind=kLoop, calls=%fused_computation.148 | loop fusion | flops 3145728 | bytes 6815744 | tf_op jit(solution)/shard_map/transpose | solution.py:311
  123.4 48.9 %shard_map.60 = (f32[4,8,2,16,128]{4,3,2,1,0:T(8,128)}, f32[8,128]{1,0:T(8,128)}) custom-call(f32[4,8,2,16,128]{4,3,2,1,0:T(8,128)} %fusion.105.blocks_ref, f32[8,128]{1,0:T(8,128)} %broadcast_in_dim.2.val_ref), custom_call_target="tpu_custom_call" | custom-call | tf_op jit(solution)/shard_map/pallas_call | solution.py:243
  172.3 1.2 slice.729
  174.2 1.9 %copy.244 = f32[32,2,16,128]{3,2,1,0:T(8,128)} copy(f32[32,2,16,128]{3,2,1,0:T(8,128)} %bitcast.198) | data formatting | bytes 1048576
  (141 shorter events, 25.8 us)
Async XLA Ops:
  56.4 1.3 copy-start.31
  62.0 2.2 %copy-start.20 = (bf16[8,4,2,24,128]{4,3,2,1,0:T(8,128)(2,1)S(1)}, bf16[8,4,2,24,128]{4,3,2,1,0:T(8,128)(2,1)}, u32[]{:S(2)}) copy-start(bf16[8,4,2,24,128]{4,3,2,1,0:T(8,128)(2,1)} %get-tuple-element.58) | copy-start | bytes 1179652
  66.2 1.0 copy-start.19
  69.2 0.9 copy-start.23
  69.2 0.9 copy-start.24
  69.2 0.9 copy-start.25
  69.2 0.9 copy-start.26
  69.2 0.9 copy-start.27
  69.2 0.9 copy-start.28
  69.3 0.9 copy-start.29
  69.7 1.0 copy-start.18
  72.7 1.0 copy-start.17
  76.2 3.0 %copy-start.32 = (bf16[24]{0:T(256)(128)(2,1)S(1)}, bf16[24]{0:T(256)(128)(2,1)}, u32[]{:S(2)}) copy-start(bf16[24]{0:T(256)(128)(2,1)} %constant.46.clone.1) | copy-start | bytes 148
  77.2 42.1 %collective-permute-start = (f32[8,4,2,16,128]{4,3,2,0,1:T(8,128)}, f32[8,4,2,16,128]{4,3,2,0,1:T(8,128)}, u32[]{:S(2)}, u32[]{:S(2)}) collective-permute-start(f32[8,4,2,16,128]{4,3,2,0,1:T(8,128)} %fusion.93), channel_id=1, source_target_pairs={{0,64},{8,72},{16,80},{24,88},{32,96},{40,104},{48,112},{56,120},{... | collective-permute-start | bytes 1572872 | tf_op jit(solution)/shard_map/ppermute | solution.py:17
  91.2 28.1 %collective-permute-start.1 = (f32[8,4,2,16,128]{4,3,2,0,1:T(8,128)}, f32[8,4,2,16,128]{4,3,2,0,1:T(8,128)}, u32[]{:S(2)}, u32[]{:S(2)}) collective-permute-start(f32[8,4,2,16,128]{4,3,2,0,1:T(8,128)} %pad_maximum_fusion.3), channel_id=1, source_target_pairs={{0,32},{8,40},{16,48},{24,56},{32,64},{40,72},{48,80},{56,88},{64,... | collective-permute-start | bytes 1572872 | tf_op jit(solution)/shard_map/ppermute | solution.py:17
  118.2 1.1 copy-start
  118.2 1.1 copy-start.1
  118.2 1.1 copy-start.2
  118.2 1.2 copy-start.3
  118.3 1.2 copy-start.4
  118.3 1.3 copy-start.5
  118.3 1.4 copy-start.6
  118.3 1.4 copy-start.7
  118.3 1.5 copy-start.8
  118.3 1.6 copy-start.9
  118.3 1.7 copy-start.10
  118.3 1.7 copy-start.11
  118.3 1.8 %copy-start.12 = (f32[8,4,1,16,128]{4,3,2,0,1:T(8,128)S(1)}, f32[8,4,1,16,128]{4,3,2,0,1:T(8,128)}, u32[]{:S(2)}) copy-start(f32[8,4,1,16,128]{4,3,2,0,1:T(8,128)} %get-tuple-element.70) | copy-start | bytes 786436
  118.3 1.9 %copy-start.13 = (f32[8,4,1,16,128]{4,3,2,0,1:T(8,128)S(1)}, f32[8,4,1,16,128]{4,3,2,0,1:T(8,128)}, u32[]{:S(2)}) copy-start(f32[8,4,1,16,128]{4,3,2,0,1:T(8,128)} %get-tuple-element.71) | copy-start | bytes 786436
  118.4 1.9 %copy-start.14 = (f32[8,1,2,16,128]{4,3,2,0,1:T(8,128)S(1)}, f32[8,1,2,16,128]{4,3,2,0,1:T(8,128)}, u32[]{:S(2)}) copy-start(f32[8,1,2,16,128]{4,3,2,0,1:T(8,128)} %get-tuple-element.33) | copy-start | bytes 393220
  118.4 1.9 %copy-start.15 = (f32[8,1,2,16,128]{4,3,2,0,1:T(8,128)S(1)}, f32[8,1,2,16,128]{4,3,2,0,1:T(8,128)}, u32[]{:S(2)}) copy-start(f32[8,1,2,16,128]{4,3,2,0,1:T(8,128)} %get-tuple-element.61) | copy-start | bytes 393220
  118.4 2.0 %copy-start.16 = (f32[8,1,2,16,128]{4,3,2,0,1:T(8,128)S(1)}, f32[8,1,2,16,128]{4,3,2,0,1:T(8,128)}, u32[]{:S(2)}) copy-start(f32[8,1,2,16,128]{4,3,2,0,1:T(8,128)} %fusion.137) | copy-start | bytes 393220
  (3 other events, 2.6 us)

commit v11 on v10

--- a/solution.py
+++ b/solution.py
@@ -10,6 +10,7 @@
 W = 16
 BAND = 1024
 HALVES = 4
+PIECE = 2
 GROUP = 4
 
 
@@ -297,14 +298,21 @@
         near_acc = near_acc + near_terms
         for bb in range(GROUP):
             far_acc[s + bb] = far_acc[s + bb] + far_terms[:, bb]
-        for h in range(1, halo_cols + 1):
-            if s == max(GROUP * h - GROUP + 1, 0) and h * GROUP < nblk:
-                done = jnp.stack(far_acc[h * GROUP : (h + 1) * GROUP], axis=1)
+        for lo in range(GROUP, nblk, PIECE):
+            if s == max(lo - (GROUP - 1), 0):
+                done = jnp.stack(far_acc[lo : lo + PIECE], axis=1)
                 done, ext = lax.optimization_barrier((done, ext))
                 first = ext[:, :GROUP]
-                sent.append(permute(done, shift_pairs(peers, GROUP * h)))
-    adj = near_acc + jnp.stack(far_acc[:GROUP], axis=1)
-    for part in sent:
+                sent.append((lo % GROUP, permute(done, shift_pairs(peers, GROUP * (lo // GROUP)))))
+    pieces = [jnp.stack(far_acc[:GROUP], axis=1)]
+    for at in range(0, GROUP, PIECE):
+        got = [part for pos, part in sent if pos == at]
+        total = got[0]
+        for part in got[1:]:
+            total = total + part
+        pieces.append(jnp.pad(total, ((0, 0), (at, GROUP - at - PIECE), (0, 0), (0, 0), (0, 0))))
+    adj = near_acc
+    for part in pieces:
         adj = adj + part
     adj = adj * (1.0 / W)
 

time: 178 us -> 183 us (1.028)
  starting transfers between devices: 5.59 us -> 9.41 us
  Pallas kernels: 95.8 us -> 99.4 us
  local copies, waits for them, and re-layouts: 12.8 us -> 10.8 us
    ppermute x2 -> x4, starting transfers between devices: 5.59 us -> 9.41 us  [permute(): return lax.ppermute(x, 'chan', pairs)]
    pallas_call x1, Pallas kernels: 48.9 us -> 52.5 us  [finish(): pl.pallas_call(functools.partial(tail_kernel, n_col, n_f), out_shape=(jax...]
    sub x9, other arithmetic: 6.91 us -> 3.78 us  [pair_terms(): first_real = toward[:, :, 0, :W] - toward[:, :, 1, W:]]
    add x0 -> x2, other arithmetic: none -> 2.25 us  [shards(): total = total + part]
    unnamed x67 -> x51, local copies, waits for them, and re-layouts: 4.64 us -> 3.35 us
  transfers between devices with their start and end apart: 2 -> 4, of which waited for: 0 -> 0; matrix products, arithmetic and copies ran while one was open for 17% -> 20% of each run, Pallas kernels for 0% -> 0%
where the time goes in v11:
time: 183 us; the launch traced here: 182 us
  Pallas kernels  99.4 us (54%)
  matrix products  30.3 us (17%)
  other arithmetic  23.1 us (13%)
  local copies, waits for them, and re-layouts  10.8 us (6%)
  starting transfers between devices  9.41 us (5%)
  between operations  8.89 us (5%)
    pallas_call x1, Pallas kernels, finish(): pl.pallas_call(functools.partial(tail_kernel, n_col, n_f), out_shape=(jax...  52.5 us
    pallas_call x1, Pallas kernels, gather_columns(): pl.pallas_call(functools.partial(head_kernel, n_halves, halo_cols), out_s...  46.9 us
    dot_general x9, matrix products, pair_terms(): jnp.einsum('fbxrc,fbrd->fbxcd', stacked_left, right_rows, preferred_eleme...  19.3 us
    ppermute x4, starting transfers between devices, permute(): return lax.ppermute(x, 'chan', pairs)  9.41 us
    dot_general x9, matrix products, pair_terms(): jnp.einsum('fbxcd,fbvd->fbxvc', rounded, far_spec, preferred_element_type...  7.31 us
    sub x9, other arithmetic, pair_terms(): first_real = toward[:, :, 0, :W] - toward[:, :, 1, W:]  3.78 us
    dot_general x9, matrix products, pair_terms(): jnp.einsum('fbxcd,fbvc->fbxvd', rounded, near_spec, preferred_element_typ...  3.71 us
  transfers between devices with their start and end apart: 4, of which 0 were waited for; matrix products, arithmetic and copies ran while one was open for 20% of the time, Pallas kernels for 0%

profile of v11, /device:TPU:1, one launch (start us, length us, event | category | flops | bytes accessed | tf_op | source)
XLA Modules:
  0.0 181.8 jit_solution(6071825705537275655)
XLA Ops:
  5.2 1.8 pad_maximum_fusion.7
  7.0 46.9 %shard_map.59 = bf16[4,3,4,2,2,24,128]{6,5,4,3,2,1,0:T(8,128)(2,1)} custom-call(bf16[4,4,2,2,24,128]{5,4,3,2,1,0:T(8,128)(2,1)} %bitcast.215), custom_call_target="tpu_custom_call" | custom-call | tf_op jit(solution)/shard_map/pallas_call | solution.py:146
  53.9 1.6 copy.32
  61.3 1.2 multiply_select_fusion.1
  62.5 3.0 %multiply_reduce_fusion.8 = (f32[]{:T(128)}, bf16[8,4,2,128,128]{4,3,2,1,0:T(8,128)(2,1)S(1)}) fusion(f32[4,128,128]{2,1,0:T(8,128)S(1)} %get-tuple-element.137, bf16[8,4,48,128,1]{3,2,4,1,0:T(8,128)(2,1)S(1)} %bitcast.226, bf16[8,4,1,48,128]{4,3,2,1,0:T(8,128)(2,1)S(1)} %maximum_bitcast_fusion, bf16[8,4,1,48,128]{4,3,2,1,0:T(8,128)(2,1)} %bitcast.227), kind=kOutput, calls=%fused_computation.8 | convolution fusion | flops 105250816 | bytes 3538948 | tf_op jit(solution)/shard_map/fbxrc,fbrd->fbxcd/dot_general | solution.py:51
  67.0 2.0 %multiply_reduce_fusion.7 = (f32[]{:T(128)}, bf16[8,4,2,128,128]{4,3,2,1,0:T(8,128)(2,1)S(1)}) fusion(f32[4,128,128]{2,1,0:T(8,128)S(1)} %get-tuple-element.130, bf16[8,4,48,128,1]{3,2,4,1,0:T(8,128)(2,1)S(1)} %bitcast.225, bf16[8,4,1,48,128]{4,3,2,1,0:T(8,128)(2,1)S(1)} %maximum_bitcast_fusion, bf16[8,4,1,48,128]{4,3,2,1,0:T(8,128)(2,1)S(1)} %bitcast.228), kind=kOutput, calls=%fused_computation.7 | convolution fusion | flops 105250816 | bytes 3538948 | tf_op jit(solution)/shard_map/fbxrc,fbrd->fbxcd/dot_general | solution.py:51
  70.2 1.9 %collective-permute-start.2 = (f32[8,2,2,16,128]{4,3,2,0,1:T(8,128)}, f32[8,2,2,16,128]{4,3,2,0,1:T(8,128)}, u32[]{:S(2)}, u32[]{:S(2)}) collective-permute-start(f32[8,2,2,16,128]{4,3,2,0,1:T(8,128)} %pad_maximum_fusion.8), channel_id=1, source_target_pairs={{0,64},{8,72},{16,80},{24,88},{32,96},{40,104},{48,112},{56,120},{... | collective-permute-start | bytes 786440 | tf_op jit(solution)/shard_map/ppermute | solution.py:18
  72.8 2.1 %multiply_reduce_fusion.5 = (f32[]{:T(128)}, bf16[8,4,2,128,128]{4,3,2,1,0:T(8,128)(2,1)S(1)}) fusion(f32[4,128,128]{2,1,0:T(8,128)S(1)} %get-tuple-element.132, bf16[8,4,48,128,1]{3,2,4,1,0:T(8,128)(2,1)S(1)} %bitcast.240, bf16[8,4,1,48,128]{4,3,1,0,2:T(8,128)(2,1)S(1)} %maximum_bitcast_fusion.1, bf16[8,4,1,48,128]{4,3,1,0,2:T(8,128)(2,1)S(1)} %bitcast.231), kind=kOutput, calls=%fused_computation.5 | convolution fusion | flops 105250816 | bytes 3538948 | tf_op jit(solution)/shard_map/fbxrc,fbrd->fbxcd/dot_general | solution.py:51
  75.3 2.0 %multiply_reduce_fusion.6 = (f32[]{:T(128)}, bf16[8,4,2,128,128]{4,3,2,1,0:T(8,128)(2,1)S(1)}) fusion(f32[4,128,128]{2,1,0:T(8,128)S(1)} %get-tuple-element.131, bf16[8,4,48,128,1]{3,2,4,1,0:T(8,128)(2,1)S(1)} %bitcast.238, bf16[8,4,1,48,128]{4,3,1,0,2:T(8,128)(2,1)S(1)} %maximum_bitcast_fusion.1, bf16[8,4,1,48,128]{4,3,1,0,2:T(8,128)(2,1)S(1)} %bitcast.232), kind=kOutput, calls=%fused_computation.6 | convolution fusion | flops 105250816 | bytes 3538948 | tf_op jit(solution)/shard_map/fbxrc,fbrd->fbxcd/dot_general | solution.py:51
  78.6 2.1 %collective-permute-start = (f32[8,2,2,16,128]{4,3,2,0,1:T(8,128)}, f32[8,2,2,16,128]{4,3,2,0,1:T(8,128)}, u32[]{:S(2)}, u32[]{:S(2)}) collective-permute-start(f32[8,2,2,16,128]{4,3,2,0,1:T(8,128)} %pad_maximum_fusion.9), channel_id=1, source_target_pairs={{0,64},{8,72},{16,80},{24,88},{32,96},{40,104},{48,112},{56,120},{... | collective-permute-start | bytes 786440 | tf_op jit(solution)/shard_map/ppermute | solution.py:18
  81.3 2.0 %multiply_reduce_fusion.3 = (f32[]{:T(128)}, bf16[8,4,2,128,128]{4,3,2,1,0:T(8,128)(2,1)S(1)}) fusion(f32[4,128,128]{2,1,0:T(8,128)S(1)} %get-tuple-element.134, bf16[8,4,48,128,1]{3,2,4,1,0:T(8,128)(2,1)S(1)} %bitcast.241, bf16[8,4,1,48,128]{4,3,1,0,2:T(8,128)(2,1)S(1)} %maximum_bitcast_fusion.2, bf16[8,4,1,48,128]{4,3,1,0,2:T(8,128)(2,1)S(1)} %bitcast.233), kind=kOutput, calls=%fused_computation.3 | convolution fusion | flops 105250816 | bytes 3538948 | tf_op jit(solution)/shard_map/fbxrc,fbrd->fbxcd/dot_general | solution.py:51
  83.8 2.1 %multiply_reduce_fusion.4 = (f32[]{:T(128)}, bf16[8,4,2,128,128]{4,3,2,1,0:T(8,128)(2,1)S(1)}) fusion(f32[4,128,128]{2,1,0:T(8,128)S(1)} %get-tuple-element.133, bf16[8,4,48,128,1]{3,2,4,1,0:T(8,128)(2,1)S(1)} %bitcast.239, bf16[8,4,1,48,128]{4,3,1,0,2:T(8,128)(2,1)S(1)} %maximum_bitcast_fusion.2, bf16[8,4,1,48,128]{4,3,1,0,2:T(8,128)(2,1)S(1)} %bitcast.234), kind=kOutput, calls=%fused_computation.4 | convolution fusion | flops 105250816 | bytes 3538948 | tf_op jit(solution)/shard_map/fbxrc,fbrd->fbxcd/dot_general | solution.py:51
  87.1 3.3 %collective-permute-start.3 = (f32[8,2,2,16,128]{4,3,2,0,1:T(8,128)}, f32[8,2,2,16,128]{4,3,2,0,1:T(8,128)}, u32[]{:S(2)}, u32[]{:S(2)}) collective-permute-start(f32[8,2,2,16,128]{4,3,2,0,1:T(8,128)} %pad_maximum_fusion.10), channel_id=1, source_target_pairs={{0,32},{8,40},{16,48},{24,56},{32,64},{40,72},{48,80},{56,88},{64,... | collective-permute-start | bytes 786440 | tf_op jit(solution)/shard_map/ppermute | solution.py:18
  91.0 2.1 %multiply_reduce_fusion.1 = (f32[]{:T(128)}, bf16[8,4,2,128,128]{4,3,2,1,0:T(8,128)(2,1)S(1)}) fusion(f32[4,128,128]{2,1,0:T(8,128)S(1)} %get-tuple-element.135, bf16[8,4,48,128,1]{3,2,4,1,0:T(8,128)(2,1)S(1)} %bitcast.242, bf16[8,4,1,48,128]{4,3,1,0,2:T(8,128)(2,1)S(1)} %maximum_bitcast_fusion.3, bf16[8,4,1,48,128]{4,3,1,0,2:T(8,128)(2,1)S(1)} %bitcast.229), kind=kOutput, calls=%fused_computation.1 | convolution fusion | flops 105250816 | bytes 3538948 | tf_op jit(solution)/shard_map/fbxrc,fbrd->fbxcd/dot_general | solution.py:51
  93.5 2.0 %multiply_reduce_fusion.2 = (f32[]{:T(128)}, bf16[8,4,2,128,128]{4,3,2,1,0:T(8,128)(2,1)S(1)}) fusion(f32[4,128,128]{2,1,0:T(8,128)S(1)} %get-tuple-element.136, bf16[8,4,48,128,1]{3,2,4,1,0:T(8,128)(2,1)S(1)} %bitcast.237, bf16[8,4,1,48,128]{4,3,1,0,2:T(8,128)(2,1)S(1)} %maximum_bitcast_fusion.3, bf16[8,4,1,48,128]{4,3,1,0,2:T(8,128)(2,1)S(1)} %bitcast.230), kind=kOutput, calls=%fused_computation.2 | convolution fusion | flops 105250816 | bytes 3538948 | tf_op jit(solution)/shard_map/fbxrc,fbrd->fbxcd/dot_general | solution.py:51
  96.9 2.1 %collective-permute-start.1 = (f32[8,2,2,16,128]{4,3,2,0,1:T(8,128)}, f32[8,2,2,16,128]{4,3,2,0,1:T(8,128)}, u32[]{:S(2)}, u32[]{:S(2)}) collective-permute-start(f32[8,2,2,16,128]{4,3,2,0,1:T(8,128)} %pad_maximum_fusion.11), channel_id=1, source_target_pairs={{0,32},{8,40},{16,48},{24,56},{32,64},{40,72},{48,80},{56,88},{64,... | collective-permute-start | bytes 786440 | tf_op jit(solution)/shard_map/ppermute | solution.py:18
  99.4 2.0 %multiply_reduce_fusion = (f32[]{:T(128)}, bf16[8,4,2,128,128]{4,3,2,1,0:T(8,128)(2,1)S(1)}) fusion(f32[4,128,128]{2,1,0:T(8,128)S(1)} %get-tuple-element.129, bf16[8,4,48,128,1]{3,2,4,1,0:T(8,128)(2,1)S(1)} %bitcast.236, bf16[8,4,1,48,128]{4,3,1,0,2:T(8,128)(2,1)S(1)} %maximum_bitcast_fusion.4, bf16[8,4,1,48,128]{4,3,1,0,2:T(8,128)(2,1)S(1)} %bitcast.235), kind=kOutput, calls=%fused_computation | convolution fusion | flops 105250816 | bytes 3538948 | tf_op jit(solution)/shard_map/fbxrc,fbrd->fbxcd/dot_general | solution.py:51
  101.9 0.8 fusion.84
  102.7 0.8 fusion.36
  103.6 0.8 fusion.42
  104.5 0.8 fusion.54
  106.3 0.8 fusion.66
  108.7 0.9 slice_subtract_fusion.9
  109.5 0.8 fusion.78
  110.3 0.9 slice_subtract_fusion.4
  112.0 0.9 slice_subtract_fusion.5
  120.3 1.2 add.393
  121.5 1.1 add.391
  122.7 1.3 fusion.115.blocks_ref
  124.5 52.5 %shard_map.60 = (f32[4,8,2,16,128]{4,3,2,1,0:T(8,128)}, f32[8,128]{1,0:T(8,128)}) custom-call(f32[4,8,2,16,128]{4,3,2,1,0:T(8,128)} %fusion.115.blocks_ref, f32[8,128]{1,0:T(8,128)} %broadcast_in_dim.2.val_ref), custom_call_target="tpu_custom_call" | custom-call | tf_op jit(solution)/shard_map/pallas_call | solution.py:244
  177.0 1.2 slice.757
  178.8 1.9 %copy.266 = f32[32,2,16,128]{3,2,1,0:T(8,128)} copy(f32[32,2,16,128]{3,2,1,0:T(8,128)} %bitcast.224) | data formatting | bytes 1048576
  (146 shorter events, 26.3 us)
Async XLA Ops:
  55.5 0.7 copy-start.18
  57.9 0.6 copy-start.11
  65.5 0.7 copy-start.12
  65.5 0.7 copy-start.13
  65.5 0.7 copy-start.14
  65.5 0.8 copy-start.15
  65.5 0.8 copy-start.16
  65.5 0.8 copy-start.17
  65.5 0.8 copy-start.20
  65.5 0.8 copy-start.21
  65.5 0.8 copy-start.22
  65.5 0.7 copy-start.23
  65.6 0.7 copy-start.24
  66.0 1.0 copy-start.10
  69.4 2.8 %copy-start.19 = (bf16[24]{0:T(256)(128)(2,1)S(1)}, bf16[24]{0:T(256)(128)(2,1)}, u32[]{:S(2)}) copy-start(bf16[24]{0:T(256)(128)(2,1)} %constant.47.clone.1) | copy-start | bytes 148
  70.2 50.0 %collective-permute-start.2 = (f32[8,2,2,16,128]{4,3,2,0,1:T(8,128)}, f32[8,2,2,16,128]{4,3,2,0,1:T(8,128)}, u32[]{:S(2)}, u32[]{:S(2)}) collective-permute-start(f32[8,2,2,16,128]{4,3,2,0,1:T(8,128)} %pad_maximum_fusion.8), channel_id=1, source_target_pairs={{0,64},{8,72},{16,80},{24,88},{32,96},{40,104},{48,112},{56,120},{... | collective-permute-start | bytes 786440 | tf_op jit(solution)/shard_map/ppermute | solution.py:18
  78.6 42.9 %collective-permute-start = (f32[8,2,2,16,128]{4,3,2,0,1:T(8,128)}, f32[8,2,2,16,128]{4,3,2,0,1:T(8,128)}, u32[]{:S(2)}, u32[]{:S(2)}) collective-permute-start(f32[8,2,2,16,128]{4,3,2,0,1:T(8,128)} %pad_maximum_fusion.9), channel_id=1, source_target_pairs={{0,64},{8,72},{16,80},{24,88},{32,96},{40,104},{48,112},{56,120},{... | collective-permute-start | bytes 786440 | tf_op jit(solution)/shard_map/ppermute | solution.py:18
  87.1 33.1 %collective-permute-start.3 = (f32[8,2,2,16,128]{4,3,2,0,1:T(8,128)}, f32[8,2,2,16,128]{4,3,2,0,1:T(8,128)}, u32[]{:S(2)}, u32[]{:S(2)}) collective-permute-start(f32[8,2,2,16,128]{4,3,2,0,1:T(8,128)} %pad_maximum_fusion.10), channel_id=1, source_target_pairs={{0,32},{8,40},{16,48},{24,56},{32,64},{40,72},{48,80},{56,88},{64,... | collective-permute-start | bytes 786440 | tf_op jit(solution)/shard_map/ppermute | solution.py:18
  96.9 24.6 %collective-permute-start.1 = (f32[8,2,2,16,128]{4,3,2,0,1:T(8,128)}, f32[8,2,2,16,128]{4,3,2,0,1:T(8,128)}, u32[]{:S(2)}, u32[]{:S(2)}) collective-permute-start(f32[8,2,2,16,128]{4,3,2,0,1:T(8,128)} %pad_maximum_fusion.11), channel_id=1, source_target_pairs={{0,32},{8,40},{16,48},{24,56},{32,64},{40,72},{48,80},{56,88},{64,... | collective-permute-start | bytes 786440 | tf_op jit(solution)/shard_map/ppermute | solution.py:18
  120.1 2.5 %copy-start = (f32[8,4,1,16,128]{4,3,2,0,1:T(8,128)S(1)}, f32[8,4,1,16,128]{4,3,2,0,1:T(8,128)}, u32[]{:S(2)}) copy-start(f32[8,4,1,16,128]{4,3,2,0,1:T(8,128)} %get-tuple-element.89) | copy-start | bytes 786436
  120.1 2.5 %copy-start.1 = (f32[8,4,1,16,128]{4,3,2,0,1:T(8,128)S(1)}, f32[8,4,1,16,128]{4,3,2,0,1:T(8,128)}, u32[]{:S(2)}) copy-start(f32[8,4,1,16,128]{4,3,2,0,1:T(8,128)} %get-tuple-element.90) | copy-start | bytes 786436
  120.1 2.5 %copy-start.2 = (f32[8,4,1,16,128]{4,3,2,0,1:T(8,128)S(1)}, f32[8,4,1,16,128]{4,3,2,0,1:T(8,128)}, u32[]{:S(2)}) copy-start(f32[8,4,1,16,128]{4,3,2,0,1:T(8,128)} %get-tuple-element.91) | copy-start | bytes 786436
  120.1 2.5 %copy-start.3 = (f32[8,4,1,16,128]{4,3,2,0,1:T(8,128)S(1)}, f32[8,4,1,16,128]{4,3,2,0,1:T(8,128)}, u32[]{:S(2)}) copy-start(f32[8,4,1,16,128]{4,3,2,0,1:T(8,128)} %get-tuple-element.80) | copy-start | bytes 786436
  120.1 2.5 %copy-start.4 = (f32[8,4,1,16,128]{4,3,2,0,1:T(8,128)S(1)}, f32[8,4,1,16,128]{4,3,2,0,1:T(8,128)}, u32[]{:S(2)}) copy-start(f32[8,4,1,16,128]{4,3,2,0,1:T(8,128)} %get-tuple-element.81) | copy-start | bytes 786436
  120.1 2.5 %copy-start.5 = (f32[8,4,1,16,128]{4,3,2,0,1:T(8,128)S(1)}, f32[8,4,1,16,128]{4,3,2,0,1:T(8,128)}, u32[]{:S(2)}) copy-start(f32[8,4,1,16,128]{4,3,2,0,1:T(8,128)} %get-tuple-element.82) | copy-start | bytes 786436
  120.2 2.5 %copy-start.6 = (f32[8,4,1,16,128]{4,3,2,0,1:T(8,128)S(1)}, f32[8,4,1,16,128]{4,3,2,0,1:T(8,128)}, u32[]{:S(2)}) copy-start(f32[8,4,1,16,128]{4,3,2,0,1:T(8,128)} %get-tuple-element.83) | copy-start | bytes 786436
  120.2 2.5 %copy-start.7 = (f32[8,1,2,16,128]{4,3,2,0,1:T(8,128)S(1)}, f32[8,1,2,16,128]{4,3,2,0,1:T(8,128)}, u32[]{:S(2)}) copy-start(f32[8,1,2,16,128]{4,3,2,0,1:T(8,128)} %get-tuple-element.41) | copy-start | bytes 393220
  120.2 2.5 %copy-start.8 = (f32[8,1,2,16,128]{4,3,2,0,1:T(8,128)S(1)}, f32[8,1,2,16,128]{4,3,2,0,1:T(8,128)}, u32[]{:S(2)}) copy-start(f32[8,1,2,16,128]{4,3,2,0,1:T(8,128)} %get-tuple-element.71) | copy-start | bytes 393220
  120.2 2.5 %copy-start.9 = (f32[8,1,2,16,128]{4,3,2,0,1:T(8,128)S(1)}, f32[8,1,2,16,128]{4,3,2,0,1:T(8,128)}, u32[]{:S(2)}) copy-start(f32[8,1,2,16,128]{4,3,2,0,1:T(8,128)} %fusion.143) | copy-start | bytes 393220

commit v12 on v10

--- a/solution.py
+++ b/solution.py
@@ -56,7 +56,8 @@
     inside = ((offset[None] >= 1) & (offset[None] <= limit_first[:, None, None])).astype(jnp.float32)
     live_mask = ok_first[:, :, None] * ok_second[:, None, :] * inside
     residual = cross_spec * live_mask[None, :, None]
-    piece_loss = 0.5 * jnp.sum(residual * residual)
+    squares = (residual * residual).reshape(-1, block_width // 8, 8, block_width)
+    piece_loss = jnp.sum(squares, axis=(0, 1))
     rounded = residual.astype(jnp.bfloat16)
     far_spec = second[:, :, :, :W].reshape(fb, nb, 2 * W, block_width)
     near_spec = first[:, :, :, :W].reshape(fb, nb, 2 * W, block_width)
@@ -284,7 +285,7 @@
 
     first = ext[:, :GROUP]
     ok_first = ok_ext[:GROUP]
-    misfit_sum = jnp.zeros((), jnp.float32)
+    misfit_part = jnp.zeros((8, bw), jnp.float32)
     near_acc = jnp.zeros((sub, GROUP, 2, W, bw), jnp.float32)
     far_acc = [jnp.zeros((sub, 2, W, bw), jnp.float32) for _ in range(nblk)]
     sent = []
@@ -293,7 +294,7 @@
         piece_loss, near_terms, far_terms = pair_terms(
             first, second, ok_first, ok_ext[s : s + GROUP], lim, s
         )
-        misfit_sum = misfit_sum + piece_loss
+        misfit_part = misfit_part + piece_loss
         near_acc = near_acc + near_terms
         for bb in range(GROUP):
             far_acc[s + bb] = far_acc[s + bb] + far_terms[:, bb]
@@ -303,6 +304,7 @@
                 done, ext = lax.optimization_barrier((done, ext))
                 first = ext[:, :GROUP]
                 sent.append(permute(done, shift_pairs(peers, GROUP * h)))
+    misfit_sum = 0.5 * jnp.sum(misfit_part)
     adj = near_acc + jnp.stack(far_acc[:GROUP], axis=1)
     for part in sent:
         adj = adj + part

time: 178 us -> 166 us (0.933)
  matrix products: 29.4 us -> 21.2 us
  between operations: 8.89 us -> 3.88 us
    dot_general x9, matrix products: 18.4 us -> 10.2 us  [pair_terms(): jnp.einsum('fbxrc,fbrd->fbxcd', stacked_left, right_rows, preferred_eleme...]
  transfers between devices with their start and end apart: 2 -> 2, of which waited for: 0 -> 0; matrix products, arithmetic and copies ran while one was open for 17% -> 16% of each run, Pallas kernels for 0% -> 0%
where the time goes in v12:
time: 166 us; the launch traced here: 165 us
  Pallas kernels  95.7 us (58%)
  other arithmetic  25.5 us (15%)
  matrix products  21.2 us (13%)
  local copies, waits for them, and re-layouts  12.8 us (8%)
  starting transfers between devices  5.59 us (3%)
  between operations  3.88 us (2%)
    pallas_call x1, Pallas kernels, finish(): pl.pallas_call(functools.partial(tail_kernel, n_col, n_f), out_shape=(jax...  48.9 us
    pallas_call x1, Pallas kernels, gather_columns(): pl.pallas_call(functools.partial(head_kernel, n_halves, halo_cols), out_s...  46.9 us
    dot_general x9, matrix products, pair_terms(): jnp.einsum('fbxrc,fbrd->fbxcd', stacked_left, right_rows, preferred_eleme...  10.2 us
    dot_general x9, matrix products, pair_terms(): jnp.einsum('fbxcd,fbvd->fbxvc', rounded, far_spec, preferred_element_type...  7.27 us
    sub x9, other arithmetic, pair_terms(): first_real = toward[:, :, 0, :W] - toward[:, :, 1, W:]  6.89 us
    ppermute x2, starting transfers between devices, permute(): return lax.ppermute(x, 'chan', pairs)  5.59 us
    unnamed x67, local copies, waits for them, and re-layouts  4.63 us
    dot_general x9, matrix products, pair_terms(): jnp.einsum('fbxcd,fbvc->fbxvd', rounded, near_spec, preferred_element_typ...  3.75 us
  transfers between devices with their start and end apart: 2, of which 0 were waited for; matrix products, arithmetic and copies ran while one was open for 16% of the time, Pallas kernels for 0%

profile of v12, /device:TPU:1, one launch (start us, length us, event | category | flops | bytes accessed | tf_op | source)
XLA Modules:
  0.0 164.8 jit_solution(18370821012767395581)
XLA Ops:
  5.9 1.8 %pad_maximum_fusion.4 = bf16[32,2,24,128]{3,2,1,0:T(8,128)(2,1)} fusion(bf16[32,2,8,128]{3,2,1,0:T(8,128)(2,1)} %param.5, bf16[32,2,16,128]{3,2,1,0:T(8,128)(2,1)} %param.4), kind=kLoop, calls=%fused_computation.159 | loop fusion | flops 786432 | bytes 786432 | tf_op jit(solution)/shard_map/concatenate | solution.py:268
  7.7 46.9 %shard_map.59 = bf16[4,3,4,2,2,24,128]{6,5,4,3,2,1,0:T(8,128)(2,1)} custom-call(bf16[4,4,2,2,24,128]{5,4,3,2,1,0:T(8,128)(2,1)} %bitcast.207), custom_call_target="tpu_custom_call" | custom-call | tf_op jit(solution)/shard_map/pallas_call | solution.py:146
  54.5 1.6 copy.62
  56.4 1.3 fusion.194
  57.9 1.4 convert_element_type.39
  59.3 1.3 slice.735
  62.8 1.3 multiply_select_fusion
  64.2 1.1 multiply_reduce_fusion.7
  66.3 1.1 multiply_reduce_fusion.6
  69.0 1.1 multiply_reduce_fusion.8
  71.1 1.1 multiply_reduce_fusion.5
  72.8 0.9 fusion.93
  73.7 2.1 %collective-permute-start = (f32[8,4,2,16,128]{4,3,2,0,1:T(8,128)}, f32[8,4,2,16,128]{4,3,2,0,1:T(8,128)}, u32[]{:S(2)}, u32[]{:S(2)}) collective-permute-start(f32[8,4,2,16,128]{4,3,2,0,1:T(8,128)} %fusion.93), channel_id=1, source_target_pairs={{0,64},{8,72},{16,80},{24,88},{32,96},{40,104},{48,112},{56,120},{... | collective-permute-start | bytes 1572872 | tf_op jit(solution)/shard_map/ppermute | solution.py:17
  76.6 1.1 multiply_reduce_fusion.2
  78.2 1.1 multiply_reduce_fusion.1
  79.8 1.1 multiply_reduce_fusion.4
  81.5 1.1 multiply_reduce_fusion.3
  83.3 0.8 pad_maximum_fusion.3
  84.1 3.5 %collective-permute-start.1 = (f32[8,4,2,16,128]{4,3,2,0,1:T(8,128)}, f32[8,4,2,16,128]{4,3,2,0,1:T(8,128)}, u32[]{:S(2)}, u32[]{:S(2)}) collective-permute-start(f32[8,4,2,16,128]{4,3,2,0,1:T(8,128)} %pad_maximum_fusion.3), channel_id=1, source_target_pairs={{0,32},{8,40},{16,48},{24,56},{32,64},{40,72},{48,80},{56,88},{64,... | collective-permute-start | bytes 1572872 | tf_op jit(solution)/shard_map/ppermute | solution.py:17
  88.0 1.1 multiply_reduce_fusion
  95.2 0.9 slice_subtract_fusion.17
  96.8 0.9 slice_subtract_fusion.14
  98.5 0.9 slice_subtract_fusion.7
  99.4 0.8 fusion.78
  100.3 0.9 slice_subtract_fusion.6
  102.0 0.9 slice_subtract_fusion.9
  103.7 0.9 slice_subtract_fusion.8
  106.0 0.8 fusion.84
  107.9 2.5 %fusion.105.blocks_ref = f32[4,8,2,16,128]{4,3,2,1,0:T(8,128)} fusion(f32[8,4,2,16,128]{4,3,2,0,1:T(8,128)} %collective-permute-done.1, f32[8,4,2,16,128]{4,3,2,0,1:T(8,128)} %collective-permute-done, f32[8,4,1,16,128]{4,3,2,0,1:T(8,128)S(1)} %copy-done.3, f32[8,4,1,16,128]{4,3,2,0,1:T(8,128)S(1)} %copy-done.2, f32[8,4,1,16,128]{4,3,2,0,1:T(8,128)S(1)} %copy-done, ...), kind=kLoop, calls=%fused_computation.148 | loop fusion | flops 3145728 | bytes 6815744 | tf_op jit(solution)/shard_map/transpose | solution.py:313
  111.0 48.9 %shard_map.60 = (f32[4,8,2,16,128]{4,3,2,1,0:T(8,128)}, f32[8,128]{1,0:T(8,128)}) custom-call(f32[4,8,2,16,128]{4,3,2,1,0:T(8,128)} %fusion.105.blocks_ref, f32[8,128]{1,0:T(8,128)} %broadcast_in_dim.2.val_ref), custom_call_target="tpu_custom_call" | custom-call | tf_op jit(solution)/shard_map/pallas_call | solution.py:244
  159.9 1.2 slice.729
  161.8 1.9 %copy.276 = f32[32,2,16,128]{3,2,1,0:T(8,128)} copy(f32[32,2,16,128]{3,2,1,0:T(8,128)} %bitcast.216) | data formatting | bytes 1048576
  (151 shorter events, 26.6 us)
Async XLA Ops:
  56.4 1.3 copy-start.31
  62.0 2.2 %copy-start.20 = (bf16[8,4,2,24,128]{4,3,2,1,0:T(8,128)(2,1)S(1)}, bf16[8,4,2,24,128]{4,3,2,1,0:T(8,128)(2,1)}, u32[]{:S(2)}) copy-start(bf16[8,4,2,24,128]{4,3,2,1,0:T(8,128)(2,1)} %get-tuple-element.58) | copy-start | bytes 1179652
  65.3 1.0 copy-start.19
  67.4 0.9 copy-start.22
  67.4 0.9 copy-start.23
  67.5 0.9 copy-start.24
  67.5 0.9 copy-start.25
  67.5 0.9 copy-start.26
  67.5 0.9 copy-start.27
  67.5 0.9 copy-start.28
  67.9 1.0 copy-start.18
  70.1 1.0 copy-start.17
  72.7 3.1 %copy-start.32 = (bf16[24]{0:T(256)(128)(2,1)S(1)}, bf16[24]{0:T(256)(128)(2,1)}, u32[]{:S(2)}) copy-start(bf16[24]{0:T(256)(128)(2,1)} %constant.46.clone.1) | copy-start | bytes 148
  73.7 33.2 %collective-permute-start = (f32[8,4,2,16,128]{4,3,2,0,1:T(8,128)}, f32[8,4,2,16,128]{4,3,2,0,1:T(8,128)}, u32[]{:S(2)}, u32[]{:S(2)}) collective-permute-start(f32[8,4,2,16,128]{4,3,2,0,1:T(8,128)} %fusion.93), channel_id=1, source_target_pairs={{0,64},{8,72},{16,80},{24,88},{32,96},{40,104},{48,112},{56,120},{... | collective-permute-start | bytes 1572872 | tf_op jit(solution)/shard_map/ppermute | solution.py:17
  84.1 22.8 %collective-permute-start.1 = (f32[8,4,2,16,128]{4,3,2,0,1:T(8,128)}, f32[8,4,2,16,128]{4,3,2,0,1:T(8,128)}, u32[]{:S(2)}, u32[]{:S(2)}) collective-permute-start(f32[8,4,2,16,128]{4,3,2,0,1:T(8,128)} %pad_maximum_fusion.3), channel_id=1, source_target_pairs={{0,32},{8,40},{16,48},{24,56},{32,64},{40,72},{48,80},{56,88},{64,... | collective-permute-start | bytes 1572872 | tf_op jit(solution)/shard_map/ppermute | solution.py:17
  105.8 1.1 copy-start
  105.8 1.1 copy-start.1
  105.8 1.1 copy-start.2
  105.8 1.2 copy-start.3
  105.8 1.2 copy-start.4
  105.9 1.3 copy-start.5
  105.9 1.4 copy-start.6
  105.9 1.4 copy-start.7
  105.9 1.5 copy-start.8
  105.9 1.6 copy-start.9
  105.9 1.7 %copy-start.10 = (f32[8,4,1,16,128]{4,3,2,0,1:T(8,128)S(1)}, f32[8,4,1,16,128]{4,3,2,0,1:T(8,128)}, u32[]{:S(2)}) copy-start(f32[8,4,1,16,128]{4,3,2,0,1:T(8,128)} %get-tuple-element.72) | copy-start | bytes 786436
  105.9 1.7 %copy-start.11 = (f32[8,4,1,16,128]{4,3,2,0,1:T(8,128)S(1)}, f32[8,4,1,16,128]{4,3,2,0,1:T(8,128)}, u32[]{:S(2)}) copy-start(f32[8,4,1,16,128]{4,3,2,0,1:T(8,128)} %get-tuple-element.73) | copy-start | bytes 786436
  105.9 1.8 %copy-start.12 = (f32[8,4,1,16,128]{4,3,2,0,1:T(8,128)S(1)}, f32[8,4,1,16,128]{4,3,2,0,1:T(8,128)}, u32[]{:S(2)}) copy-start(f32[8,4,1,16,128]{4,3,2,0,1:T(8,128)} %get-tuple-element.70) | copy-start | bytes 786436
  105.9 1.9 %copy-start.13 = (f32[8,4,1,16,128]{4,3,2,0,1:T(8,128)S(1)}, f32[8,4,1,16,128]{4,3,2,0,1:T(8,128)}, u32[]{:S(2)}) copy-start(f32[8,4,1,16,128]{4,3,2,0,1:T(8,128)} %get-tuple-element.71) | copy-start | bytes 786436
  105.9 1.9 %copy-start.14 = (f32[8,1,2,16,128]{4,3,2,0,1:T(8,128)S(1)}, f32[8,1,2,16,128]{4,3,2,0,1:T(8,128)}, u32[]{:S(2)}) copy-start(f32[8,1,2,16,128]{4,3,2,0,1:T(8,128)} %get-tuple-element.33) | copy-start | bytes 393220
  106.0 1.9 %copy-start.15 = (f32[8,1,2,16,128]{4,3,2,0,1:T(8,128)S(1)}, f32[8,1,2,16,128]{4,3,2,0,1:T(8,128)}, u32[]{:S(2)}) copy-start(f32[8,1,2,16,128]{4,3,2,0,1:T(8,128)} %get-tuple-element.61) | copy-start | bytes 393220
  106.0 2.0 %copy-start.16 = (f32[8,1,2,16,128]{4,3,2,0,1:T(8,128)S(1)}, f32[8,1,2,16,128]{4,3,2,0,1:T(8,128)}, u32[]{:S(2)}) copy-start(f32[8,1,2,16,128]{4,3,2,0,1:T(8,128)} %fusion.137) | copy-start | bytes 393220
  (3 other events, 2.5 us)

commit v13 on v12

--- a/solution.py
+++ b/solution.py
@@ -82,6 +82,7 @@
     peers = lax.axis_size("chan")
     k = c // GROUP
     j = c % GROUP
+    back = 1 + halo_cols
 
     def devg(b):
         return (k * GROUP + b, f)
@@ -126,12 +127,22 @@
                 device_id=devh(h, -1), device_id_type=MESH)
             cp.start()
             sends.append(cp)
+        cp = pltpu.make_async_remote_copy(
+            src_ref=held.at[half, 0], dst_ref=held.at[half, back],
+            send_sem=send_h.at[half, back], recv_sem=recv_h.at[half, back],
+            device_id=devh(halo_cols, 1), device_id_type=MESH)
+        cp.start()
+        sends.append(cp)
     for half in range(n_halves):
         for h in range(1, halo_cols + 1):
             pltpu.make_async_remote_copy(
                 src_ref=held.at[half, 0], dst_ref=held.at[half, h],
                 send_sem=send_h.at[half, h], recv_sem=recv_h.at[half, h],
                 device_id=devh(h, 1), device_id_type=MESH).wait_recv()
+        pltpu.make_async_remote_copy(
+            src_ref=held.at[half, 0], dst_ref=held.at[half, back],
+            send_sem=send_h.at[half, back], recv_sem=recv_h.at[half, back],
+            device_id=devh(halo_cols, -1), device_id_type=MESH).wait_recv()
     for cp in sends:
         cp.wait_send()
     out_ref[...] = held[...]
@@ -141,7 +152,7 @@
     fl, two, rows, bw = payload.shape
     q = fl // GROUP // n_halves
     chunks = payload.reshape(GROUP, n_halves, q, two, rows, bw)
-    shape = (n_halves, 1 + halo_cols, GROUP, q, two, rows, bw)
+    shape = (n_halves, 2 + halo_cols, GROUP, q, two, rows, bw)
     vmem = pl.BlockSpec(memory_space=pltpu.VMEM)
     held = pl.pallas_call(
         functools.partial(head_kernel, n_halves, halo_cols),
@@ -152,14 +163,14 @@
             pltpu.VMEM(shape, payload.dtype),
             pltpu.SemaphoreType.DMA((n_halves, GROUP)),
             pltpu.SemaphoreType.DMA((n_halves, GROUP)),
-            pltpu.SemaphoreType.DMA((n_halves, 1 + halo_cols)),
-            pltpu.SemaphoreType.DMA((n_halves, 1 + halo_cols)),
+            pltpu.SemaphoreType.DMA((n_halves, 2 + halo_cols)),
+            pltpu.SemaphoreType.DMA((n_halves, 2 + halo_cols)),
             pltpu.SemaphoreType.DMA((n_halves,)),
         ],
         compiler_params=pltpu.CompilerParams(collective_id=1, has_side_effects=True),
     )(chunks)
     held = jnp.transpose(held, (0, 3, 1, 2, 4, 5, 6))
-    return held.reshape(n_halves * q, (1 + halo_cols) * GROUP, two, rows, bw)
+    return held.reshape(n_halves * q, (2 + halo_cols) * GROUP, two, rows, bw)
 
 
 def tail_kernel(n_col, n_f, blocks_ref, val_ref, out_ref, sum_ref,
@@ -276,12 +287,17 @@
     halo_cols = -(-band_blocks // GROUP)
     nblk = GROUP * (1 + halo_cols)
 
-    ext = gather_columns(payload, halo_cols, HALVES)
+    full = gather_columns(payload, halo_cols, HALVES)
+    ext = full[:, :nblk]
+    behind = full[:, nblk:]
 
     ok_all = channel_ok.astype(jnp.float32)
     ok_wide = jnp.concatenate([ok_all, ok_all[: nblk * bw]])
     ok_ext = lax.dynamic_slice_in_dim(ok_wide, column * GROUP * bw, nblk * bw).reshape(nblk, bw)
     lim = lax.dynamic_slice_in_dim(limits, column * GROUP, GROUP)
+    back_col = (column - halo_cols) % (peers // GROUP)
+    ok_back = lax.dynamic_slice_in_dim(ok_all, back_col * GROUP * bw, GROUP * bw).reshape(GROUP, bw)
+    lim_back = lax.dynamic_slice_in_dim(limits, back_col * GROUP, GROUP)
 
     first = ext[:, :GROUP]
     ok_first = ok_ext[:GROUP]
@@ -298,13 +314,19 @@
         near_acc = near_acc + near_terms
         for bb in range(GROUP):
             far_acc[s + bb] = far_acc[s + bb] + far_terms[:, bb]
-        for h in range(1, halo_cols + 1):
-            if s == max(GROUP * h - GROUP + 1, 0) and h * GROUP < nblk:
+        for h in range(1, halo_cols):
+            if s == max(GROUP * h - GROUP + 1, 0):
                 done = jnp.stack(far_acc[h * GROUP : (h + 1) * GROUP], axis=1)
                 done, ext = lax.optimization_barrier((done, ext))
                 first = ext[:, :GROUP]
                 sent.append(permute(done, shift_pairs(peers, GROUP * h)))
     misfit_sum = 0.5 * jnp.sum(misfit_part)
+    for d in range(GROUP):
+        _, _, back_terms = pair_terms(
+            behind[:, d:], ext[:, : GROUP - d], ok_back[d:], ok_ext[: GROUP - d],
+            lim_back[d:], GROUP * halo_cols - d,
+        )
+        sent.append(jnp.pad(back_terms, ((0, 0), (0, d), (0, 0), (0, 0), (0, 0))))
     adj = near_acc + jnp.stack(far_acc[:GROUP], axis=1)
     for part in sent:
         adj = adj + part

time: 166 us -> 207 us (1.25)
  local copies, waits for them, and re-layouts: 12.8 us -> 28.5 us
  other arithmetic: 25.5 us -> 38 us
  Pallas kernels: 95.7 us -> 102 us
  matrix products: 21.2 us -> 26.9 us
    slice x0 -> x23, local copies, waits for them, and re-layouts: none -> 9.87 us  [the longest x4 2.99 us: pair_terms(): near_spec = first[:, :, :, :W].reshape(fb, nb, 2 * W, block_width)]
    reduce_sum x9, other arithmetic: 0.16 us -> 4.84 us  [pair_terms(): piece_loss = jnp.sum(squares, axis=(0, 1))]
    pallas_call x1, Pallas kernels: 46.9 us -> 51.3 us  [gather_columns(): pl.pallas_call(functools.partial(head_kernel, n_halves, halo_cols), out_s...]
    add x2 -> x9, other arithmetic: 0.14 us -> 3.63 us  [pair_terms(): second_real = backward[:, :, 0, :W] + backward[:, :, 1, W:]]
    mul x2 -> x5, other arithmetic: 1.57 us -> 4.7 us  [pair_terms(): live_mask = ok_first[:, :, None] * ok_second[:, None, :] * inside]
    dot_general x9 -> x12, matrix products: 3.75 us -> 6.76 us  [pair_terms(): jnp.einsum('fbxcd,fbvc->fbxvd', rounded, near_spec, preferred_element_typ...]
    mul x3 -> x6, local copies, waits for them, and re-layouts: 0.12 us -> 2.95 us  [pair_terms(): scaled = first * row_scale[None, None, None, :, None]]
    dot_general x9 -> x12, matrix products: 10.2 us -> 12.8 us  [pair_terms(): jnp.einsum('fbxrc,fbrd->fbxcd', stacked_left, right_rows, preferred_eleme...]
  transfers between devices with their start and end apart: 2 -> 1, of which waited for: 0 -> 0; matrix products, arithmetic and copies ran while one was open for 16% -> 23% of each run, Pallas kernels for 0% -> 0%
where the time goes in v13:
time: 207 us; the launch traced here: 206 us
  Pallas kernels  102 us (49%)
  other arithmetic  38 us (18%)
  local copies, waits for them, and re-layouts  28.5 us (14%)
  matrix products  26.9 us (13%)
  starting transfers between devices  5.38 us (3%)
  between operations  4.43 us (2%)
    pallas_call x1, Pallas kernels, gather_columns(): pl.pallas_call(functools.partial(head_kernel, n_halves, halo_cols), out_s...  51.3 us
    pallas_call x1, Pallas kernels, finish(): pl.pallas_call(functools.partial(tail_kernel, n_col, n_f), out_shape=(jax...  51.1 us
    dot_general x12, matrix products, pair_terms(): jnp.einsum('fbxrc,fbrd->fbxcd', stacked_left, right_rows, preferred_eleme...  12.8 us
    dot_general x9, matrix products, pair_terms(): jnp.einsum('fbxcd,fbvd->fbxvc', rounded, far_spec, preferred_element_type...  7.28 us
    unnamed x175, local copies, waits for them, and re-layouts  7.25 us
    sub x9, other arithmetic, pair_terms(): first_real = toward[:, :, 0, :W] - toward[:, :, 1, W:]  7.21 us
    dot_general x12, matrix products, pair_terms(): jnp.einsum('fbxcd,fbvc->fbxvd', rounded, near_spec, preferred_element_typ...  6.76 us
    ppermute x1, starting transfers between devices, permute(): return lax.ppermute(x, 'chan', pairs)  5.38 us
  transfers between devices with their start and end apart: 1, of which 0 were waited for; matrix products, arithmetic and copies ran while one was open for 23% of the time, Pallas kernels for 0%

profile of v13, /device:TPU:1, one launch (start us, length us, event | category | flops | bytes accessed | tf_op | source)
XLA Modules:
  0.0 205.6 jit_solution(13089398534243051157)
XLA Ops:
  6.6 1.8 pad_maximum_fusion.4
  8.4 51.3 %shard_map.59 = bf16[4,4,4,2,2,24,128]{6,5,4,3,2,1,0:T(8,128)(2,1)} custom-call(bf16[4,4,2,2,24,128]{5,4,3,2,1,0:T(8,128)(2,1)} %bitcast.292), custom_call_target="tpu_custom_call" | custom-call | tf_op jit(solution)/shard_map/pallas_call | solution.py:157
  59.7 1.8 copy.66
  61.5 1.2 slice.1015
  62.8 1.7 fusion.200
  64.4 1.9 fusion.201
  69.3 1.5 copy.169
  70.9 1.2 fusion.202
  72.1 2.0 multiply_select_fusion
  74.1 1.1 multiply_reduce_fusion.7
  76.2 1.1 multiply_reduce_fusion.6
  78.4 1.1 multiply_reduce_fusion.5
  80.5 1.1 multiply_reduce_fusion.4
  83.3 1.1 multiply_reduce_fusion.3
  85.4 1.1 multiply_reduce_fusion.2
  87.6 1.1 multiply_reduce_fusion.1
  90.2 5.4 %collective-permute-start = (f32[8,4,2,16,128]{4,3,2,0,1:T(8,128)}, f32[8,4,2,16,128]{4,3,2,0,1:T(8,128)}, u32[]{:S(2)}, u32[]{:S(2)}) collective-permute-start(f32[8,4,2,16,128]{4,3,2,0,1:T(8,128)} %pad_maximum_fusion.3), channel_id=1, source_target_pairs={{0,32},{8,40},{16,48},{24,56},{32,64},{40,72},{48,80},{56,88},{64,... | collective-permute-start | bytes 1572872 | tf_op jit(solution)/shard_map/ppermute | solution.py:17
  105.8 1.8 multiply_reduce_fusion
  115.5 0.9 slice_subtract_fusion.14
  120.2 0.9 slice_subtract_fusion.12
  124.0 1.1 multiply_reduce_fusion.8
  126.6 0.9 slice_subtract_fusion.17
  128.3 0.9 slice_subtract_fusion.10
  129.9 1.4 multiply_select_fusion.12
  131.3 2.2 %fusion.97 = f32[8,1,2,32,128]{4,3,2,0,1:T(8,128)} fusion(bf16[8,32,128,1]{2,1,3,0:T(8,128)(2,1)} %bitcast.328, bf16[8,48,128,1]{2,1,3,0:T(8,128)(2,1)} %bitcast.327, f32[128,128]{1,0:T(8,128)} %multiply_select_fusion.12, bf16[8,1,1,48,128]{4,3,2,0,1:T(8,128)(2,1)S(1)} %maximum_bitcast_fusion.8, bf16[8,1,1,48,128]{4,3,2,0,1:T(8,128)(2,1)} %bitcast.326), kind=kOutput, calls=%fused_computation.82 | convolution fusion | flops 42565632 | bytes 688128 | tf_op jit(solution)/shard_map/fbxcd,fbvc->fbxvd/dot_general | solution.py:67
  133.5 1.6 slice_add_fusion.20
  135.2 1.0 maximum_bitcast_fusion.4
  136.2 1.0 multiply_select_fusion.11
  146.4 2.6 %fusion.107.blocks_ref = f32[4,8,2,16,128]{4,3,2,1,0:T(8,128)} fusion(f32[8,1,1,16,128]{4,3,2,0,1:T(8,128)} %get-tuple-element.106, f32[8,1,1,16,128]{4,3,2,0,1:T(8,128)S(1)} %copy-done.58, f32[8,2,1,16,128]{4,3,2,0,1:T(8,128)} %get-tuple-element.96, f32[8,2,1,16,128]{4,3,2,0,1:T(8,128)} %get-tuple-element.95, f32[8,3,1,16,128]{4,3,2,0,1:T(8,128)S(1)} %copy-done.35, ...), kind=kLoop, calls=%fused_computation.126 | loop fusion | flops 5242880 | bytes 7602176 | tf_op jit(solution)/shard_map/transpose | solution.py:335
  149.6 51.1 %shard_map.60 = (f32[4,8,2,16,128]{4,3,2,1,0:T(8,128)}, f32[8,128]{1,0:T(8,128)}) custom-call(f32[4,8,2,16,128]{4,3,2,1,0:T(8,128)} %fusion.107.blocks_ref, f32[8,128]{1,0:T(8,128)} %broadcast_in_dim.2.val_ref), custom_call_target="tpu_custom_call" | custom-call | tf_op jit(solution)/shard_map/pallas_call | solution.py:255
  200.7 1.2 slice.906
  202.6 1.9 copy.304
  (301 shorter events, 52.9 us)
Async XLA Ops:
  0.7 2.6 %copy-start.84 = (s32[128]{0:T(128)}, s32[128]{0:T(128)S(1)}, u32[]{:S(2)}) copy-start(s32[128]{0:T(128)S(1)} %iota_add_fusion.4) | copy-start | bytes 1540
  4.0 68.1 %copy-start.36 = (s32[128,128]{1,0:T(8,128)}, s32[128,128]{1,0:T(8,128)S(1)}, u32[]{:S(2)}) copy-start(s32[128,128]{1,0:T(8,128)S(1)} %get-tuple-element.144) | copy-start | bytes 196612
  4.0 68.1 %copy-start.38 = (s32[128,128]{1,0:T(8,128)}, s32[128,128]{1,0:T(8,128)S(1)}, u32[]{:S(2)}) copy-start(s32[128,128]{1,0:T(8,128)S(1)} %get-tuple-element.143) | copy-start | bytes 196612
  64.4 1.9 copy-start.77
  70.8 33.8 %copy-start = (bf16[8,12,2,24,128]{4,3,1,0,2:T(8,128)(2,1)}, bf16[8,12,2,24,128]{4,3,1,0,2:T(8,128)(2,1)S(1)}, u32[]{:S(2)}) copy-start(bf16[8,12,2,24,128]{4,3,1,0,2:T(8,128)(2,1)S(1)} %copy.169) | copy-start | bytes 3538948
  70.8 3.3 %copy-start.45 = (bf16[8,4,2,24,128]{4,3,2,1,0:T(8,128)(2,1)S(1)}, bf16[8,4,2,24,128]{4,3,2,1,0:T(8,128)(2,1)}, u32[]{:S(2)}) copy-start(bf16[8,4,2,24,128]{4,3,2,1,0:T(8,128)(2,1)} %copy.68) | copy-start | bytes 1179652
  70.8 3.3 %copy-start.53 = (bf16[8,4,2,24,128]{4,3,2,1,0:T(8,128)(2,1)S(1)}, bf16[8,4,2,24,128]{4,3,2,1,0:T(8,128)(2,1)}, u32[]{:S(2)}) copy-start(bf16[8,4,2,24,128]{4,3,2,1,0:T(8,128)(2,1)} %get-tuple-element.46) | copy-start | bytes 1179652
  89.3 8.9 %copy-start.61 = (f32[1536]{0:T(1024)S(1)}, f32[1536]{0:T(1024)}, u32[]{:S(2)}) copy-start(f32[1536]{0:T(1024)} %copy-done.60) | copy-start | bytes 18436
  89.3 10.7 %copy-start.78 = (bf16[24]{0:T(256)(128)(2,1)S(1)}, bf16[24]{0:T(256)(128)(2,1)}, u32[]{:S(2)}) copy-start(bf16[24]{0:T(256)(128)(2,1)} %constant.66.clone.1) | copy-start | bytes 148
  90.2 54.9 %collective-permute-start = (f32[8,4,2,16,128]{4,3,2,0,1:T(8,128)}, f32[8,4,2,16,128]{4,3,2,0,1:T(8,128)}, u32[]{:S(2)}, u32[]{:S(2)}) collective-permute-start(f32[8,4,2,16,128]{4,3,2,0,1:T(8,128)} %pad_maximum_fusion.3), channel_id=1, source_target_pairs={{0,32},{8,40},{16,48},{24,56},{32,64},{40,72},{48,80},{56,88},{64,... | collective-permute-start | bytes 1572872 | tf_op jit(solution)/shard_map/ppermute | solution.py:17
  102.3 2.4 %copy-start.3 = (bf16[8,4,2,24,128]{4,3,2,1,0:T(8,128)(2,1)S(1)}, bf16[8,4,2,24,128]{4,3,2,1,0:T(8,128)(2,1)}, u32[]{:S(2)}) copy-start(bf16[8,4,2,24,128]{4,3,2,1,0:T(8,128)(2,1)} %get-tuple-element.38) | copy-start | bytes 1179652
  108.0 2.1 %copy-start.14 = (bf16[8,4,2,16,128]{4,3,2,1,0:T(8,128)(2,1)S(1)}, bf16[8,4,2,16,128]{4,3,2,1,0:T(8,128)(2,1)}, u32[]{:S(2)}) copy-start(bf16[8,4,2,16,128]{4,3,2,1,0:T(8,128)(2,1)} %get-tuple-element.36) | copy-start | bytes 786436
  110.1 2.3 %copy-start.13 = (bf16[8,4,2,16,128]{4,3,2,1,0:T(8,128)(2,1)S(1)}, bf16[8,4,2,16,128]{4,3,2,1,0:T(8,128)(2,1)}, u32[]{:S(2)}) copy-start(bf16[8,4,2,16,128]{4,3,2,1,0:T(8,128)(2,1)} %get-tuple-element.35) | copy-start | bytes 786436
  112.4 2.3 %copy-start.12 = (bf16[8,4,2,16,128]{4,3,2,1,0:T(8,128)(2,1)S(1)}, bf16[8,4,2,16,128]{4,3,2,1,0:T(8,128)(2,1)}, u32[]{:S(2)}) copy-start(bf16[8,4,2,16,128]{4,3,2,1,0:T(8,128)(2,1)} %get-tuple-element.34) | copy-start | bytes 786436
  114.7 2.3 %copy-start.11 = (bf16[8,4,2,16,128]{4,3,2,1,0:T(8,128)(2,1)S(1)}, bf16[8,4,2,16,128]{4,3,2,1,0:T(8,128)(2,1)}, u32[]{:S(2)}) copy-start(bf16[8,4,2,16,128]{4,3,2,1,0:T(8,128)(2,1)} %get-tuple-element.33) | copy-start | bytes 786436
  117.1 2.3 %copy-start.10 = (bf16[8,4,2,16,128]{4,3,2,1,0:T(8,128)(2,1)S(1)}, bf16[8,4,2,16,128]{4,3,2,1,0:T(8,128)(2,1)}, u32[]{:S(2)}) copy-start(bf16[8,4,2,16,128]{4,3,2,1,0:T(8,128)(2,1)} %get-tuple-element.32) | copy-start | bytes 786436
  119.4 2.4 %copy-start.9 = (bf16[8,4,2,16,128]{4,3,2,1,0:T(8,128)(2,1)S(1)}, bf16[8,4,2,16,128]{4,3,2,1,0:T(8,128)(2,1)}, u32[]{:S(2)}) copy-start(bf16[8,4,2,16,128]{4,3,2,1,0:T(8,128)(2,1)} %get-tuple-element.31) | copy-start | bytes 786436
  121.7 2.3 %copy-start.46 = (bf16[8,4,2,24,128]{4,3,2,1,0:T(8,128)(2,1)S(1)}, bf16[8,4,2,24,128]{4,3,2,1,0:T(8,128)(2,1)}, u32[]{:S(2)}) copy-start(bf16[8,4,2,24,128]{4,3,2,1,0:T(8,128)(2,1)} %get-tuple-element.47) | copy-start | bytes 1179652
  127.5 2.4 %slice-start.3 = ((f32[1536]{0:T(1024)}), f32[128]{0:T(128)S(1)}, s32[]{:S(2)}) async-start(f32[1536]{0:T(1024)} %copy-done.60), calls=%async_computation.3 | async-start | bytes 1024 | tf_op jit(solution)/shard_map/slice | solution.py:326
  127.5 2.4 %copy-start.85 = (s32[128]{0:T(128)S(1)}, s32[128]{0:T(128)}, u32[]{:S(2)}) copy-start(s32[128]{0:T(128)} %copy-done.84) | copy-start | bytes 1540
  128.3 6.8 %slice-start.1 = ((bf16[8,12,2,24,128]{4,3,1,0,2:T(8,128)(2,1)}), bf16[8,2,2,24,128]{4,3,1,0,2:T(8,128)(2,1)S(1)}, s32[]{:S(2)}) async-start(bf16[8,12,2,24,128]{4,3,1,0,2:T(8,128)(2,1)} %copy-done), calls=%async_computation.1 | async-start | bytes 393216 | tf_op jit(solution)/shard_map/slice | solution.py:326
  128.3 6.8 %slice-start.2 = ((bf16[8,12,2,24,128]{4,3,1,0,2:T(8,128)(2,1)}), bf16[8,3,2,24,128]{4,3,1,0,2:T(8,128)(2,1)S(1)}, s32[]{:S(2)}) async-start(bf16[8,12,2,24,128]{4,3,1,0,2:T(8,128)(2,1)} %copy-done), calls=%async_computation.2 | async-start | bytes 589824 | tf_op jit(solution)/shard_map/slice | solution.py:326
  133.5 3.7 %copy-start.31 = (bf16[8,2,2,24,128]{4,3,2,1,0:T(8,128)(2,1)S(1)}, bf16[8,2,2,24,128]{4,3,2,1,0:T(8,128)(2,1)}, u32[]{:S(2)}) copy-start(bf16[8,2,2,24,128]{4,3,2,1,0:T(8,128)(2,1)} %copy.102) | copy-start | bytes 589828
  133.5 4.2 %copy-start.41 = (bf16[8,2,2,16,128]{4,3,2,1,0:T(8,128)(2,1)S(1)}, bf16[8,2,2,16,128]{4,3,2,1,0:T(8,128)(2,1)}, u32[]{:S(2)}) copy-start(bf16[8,2,2,16,128]{4,3,2,1,0:T(8,128)(2,1)} %slice.1055) | copy-start | bytes 393220
  142.3 2.8 %copy-start.58 = (f32[8,1,1,16,128]{4,3,2,0,1:T(8,128)S(1)}, f32[8,1,1,16,128]{4,3,2,0,1:T(8,128)}, u32[]{:S(2)}) copy-start(f32[8,1,1,16,128]{4,3,2,0,1:T(8,128)} %get-tuple-element.105) | copy-start | bytes 196612
  144.1 1.9 copy-start.29
  144.2 2.0 copy-start.30
  144.2 2.1 %copy-start.34 = (f32[8,3,1,16,128]{4,3,2,0,1:T(8,128)S(1)}, f32[8,3,1,16,128]{4,3,2,0,1:T(8,128)}, u32[]{:S(2)}) copy-start(f32[8,3,1,16,128]{4,3,2,0,1:T(8,128)} %get-tuple-element.93) | copy-start | bytes 589828
  144.2 2.1 %copy-start.35 = (f32[8,3,1,16,128]{4,3,2,0,1:T(8,128)S(1)}, f32[8,3,1,16,128]{4,3,2,0,1:T(8,128)}, u32[]{:S(2)}) copy-start(f32[8,3,1,16,128]{4,3,2,0,1:T(8,128)} %get-tuple-element.94) | copy-start | bytes 589828
  144.2 2.1 %copy-start.42 = (f32[8,1,2,16,128]{4,3,2,0,1:T(8,128)S(1)}, f32[8,1,2,16,128]{4,3,2,0,1:T(8,128)}, u32[]{:S(2)}) copy-start(f32[8,1,2,16,128]{4,3,2,0,1:T(8,128)} %get-tuple-element.48) | copy-start | bytes 393220
  144.2 2.2 %copy-start.43 = (f32[8,1,2,16,128]{4,3,2,0,1:T(8,128)S(1)}, f32[8,1,2,16,128]{4,3,2,0,1:T(8,128)}, u32[]{:S(2)}) copy-start(f32[8,1,2,16,128]{4,3,2,0,1:T(8,128)} %get-tuple-element.49) | copy-start | bytes 393220
  144.2 2.2 %copy-start.44 = (f32[8,1,2,16,128]{4,3,2,0,1:T(8,128)S(1)}, f32[8,1,2,16,128]{4,3,2,0,1:T(8,128)}, u32[]{:S(2)}) copy-start(f32[8,1,2,16,128]{4,3,2,0,1:T(8,128)} %get-tuple-element.58) | copy-start | bytes 393220
  (60 other events, 70.6 us)

commit v14 on v12

--- a/solution.py
+++ b/solution.py
@@ -308,11 +308,10 @@
     adj = near_acc + jnp.stack(far_acc[:GROUP], axis=1)
     for part in sent:
         adj = adj + part
-    adj = adj * (1.0 / W)
 
     blocks = jnp.transpose(adj, (1, 0, 2, 3, 4))
     back, misfit_total = finish(blocks, misfit_sum, mesh_shape)
-    adjoint = back.reshape(fl, 2, W, bw)
+    adjoint = back.reshape(fl, 2, W, bw) * (1.0 / W)
 
     misfit = misfit_total / float(F * bw * peers * BAND)
     return adjoint, misfit

time: 166 us -> 166 us (level)
  other arithmetic: 25.5 us -> 27.4 us
  local copies, waits for them, and re-layouts: 12.8 us -> 11 us
    mul x0 -> x1, other arithmetic: none -> 1.88 us  [shards(): adjoint = back.reshape(fl, 2, W, bw) * (1.0 / W)]
    unnamed x67 -> x66, local copies, waits for them, and re-layouts: 4.63 us -> 2.76 us
where the time goes in v14:
time: 166 us; the launch traced here: 165 us
  Pallas kernels  95.7 us (58%)
  other arithmetic  27.4 us (17%)
  matrix products  21.2 us (13%)
  local copies, waits for them, and re-layouts  11 us (7%)
  starting transfers between devices  5.59 us (3%)
  between operations  3.87 us (2%)
    pallas_call x1, Pallas kernels, finish(): pl.pallas_call(functools.partial(tail_kernel, n_col, n_f), out_shape=(jax...  48.9 us
    pallas_call x1, Pallas kernels, gather_columns(): pl.pallas_call(functools.partial(head_kernel, n_halves, halo_cols), out_s...  46.9 us
    dot_general x9, matrix products, pair_terms(): jnp.einsum('fbxrc,fbrd->fbxcd', stacked_left, right_rows, preferred_eleme...  10.2 us
    dot_general x9, matrix products, pair_terms(): jnp.einsum('fbxcd,fbvd->fbxvc', rounded, far_spec, preferred_element_type...  7.27 us
    sub x9, other arithmetic, pair_terms(): first_real = toward[:, :, 0, :W] - toward[:, :, 1, W:]  6.89 us
    ppermute x2, starting transfers between devices, permute(): return lax.ppermute(x, 'chan', pairs)  5.59 us
    dot_general x9, matrix products, pair_terms(): jnp.einsum('fbxcd,fbvc->fbxvd', rounded, near_spec, preferred_element_typ...  3.75 us
  transfers between devices with their start and end apart: 2, of which 0 were waited for; matrix products, arithmetic and copies ran while one was open for 16% of the time, Pallas kernels for 0%

profile of v14, /device:TPU:1, one launch (start us, length us, event | category | flops | bytes accessed | tf_op | source)
XLA Modules:
  0.0 164.8 jit_solution(8946322593874854385)
XLA Ops:
  5.9 1.8 %pad_maximum_fusion.4 = bf16[32,2,24,128]{3,2,1,0:T(8,128)(2,1)} fusion(bf16[32,2,8,128]{3,2,1,0:T(8,128)(2,1)} %param.5, bf16[32,2,16,128]{3,2,1,0:T(8,128)(2,1)} %param.4), kind=kLoop, calls=%fused_computation.158 | loop fusion | flops 786432 | bytes 786432 | tf_op jit(solution)/shard_map/concatenate | solution.py:268
  7.7 46.9 %shard_map.59 = bf16[4,3,4,2,2,24,128]{6,5,4,3,2,1,0:T(8,128)(2,1)} custom-call(bf16[4,4,2,2,24,128]{5,4,3,2,1,0:T(8,128)(2,1)} %bitcast.207), custom_call_target="tpu_custom_call" | custom-call | tf_op jit(solution)/shard_map/pallas_call | solution.py:146
  54.5 1.6 copy.62
  56.4 1.3 fusion.193
  57.9 1.4 convert_element_type.39
  59.3 1.3 slice.735
  62.8 1.3 multiply_select_fusion
  64.2 1.1 multiply_reduce_fusion.7
  66.3 1.1 multiply_reduce_fusion.6
  69.0 1.1 multiply_reduce_fusion.8
  71.1 1.1 multiply_reduce_fusion.5
  72.8 0.9 fusion.93
  73.7 2.1 %collective-permute-start = (f32[8,4,2,16,128]{4,3,2,0,1:T(8,128)}, f32[8,4,2,16,128]{4,3,2,0,1:T(8,128)}, u32[]{:S(2)}, u32[]{:S(2)}) collective-permute-start(f32[8,4,2,16,128]{4,3,2,0,1:T(8,128)} %fusion.93), channel_id=1, source_target_pairs={{0,64},{8,72},{16,80},{24,88},{32,96},{40,104},{48,112},{56,120},{... | collective-permute-start | bytes 1572872 | tf_op jit(solution)/shard_map/ppermute | solution.py:17
  76.6 1.1 multiply_reduce_fusion.2
  78.2 1.1 multiply_reduce_fusion.1
  79.8 1.1 multiply_reduce_fusion.4
  81.5 1.1 multiply_reduce_fusion.3
  83.3 0.8 pad_maximum_fusion.3
  84.1 3.5 %collective-permute-start.1 = (f32[8,4,2,16,128]{4,3,2,0,1:T(8,128)}, f32[8,4,2,16,128]{4,3,2,0,1:T(8,128)}, u32[]{:S(2)}, u32[]{:S(2)}) collective-permute-start(f32[8,4,2,16,128]{4,3,2,0,1:T(8,128)} %pad_maximum_fusion.3), channel_id=1, source_target_pairs={{0,32},{8,40},{16,48},{24,56},{32,64},{40,72},{48,80},{56,88},{64,... | collective-permute-start | bytes 1572872 | tf_op jit(solution)/shard_map/ppermute | solution.py:17
  88.0 1.1 multiply_reduce_fusion
  95.2 0.9 slice_subtract_fusion.17
  96.8 0.9 slice_subtract_fusion.14
  98.5 0.9 slice_subtract_fusion.7
  99.4 0.8 fusion.78
  100.3 0.9 slice_subtract_fusion.6
  102.0 0.9 slice_subtract_fusion.9
  103.7 0.9 slice_subtract_fusion.8
  106.0 0.8 fusion.84
  107.9 2.5 %fusion.104.blocks_ref = f32[4,8,2,16,128]{4,3,2,1,0:T(8,128)} fusion(f32[8,4,2,16,128]{4,3,2,0,1:T(8,128)} %collective-permute-done.1, f32[8,4,2,16,128]{4,3,2,0,1:T(8,128)} %collective-permute-done, f32[8,4,1,16,128]{4,3,2,0,1:T(8,128)S(1)} %copy-done.3, f32[8,4,1,16,128]{4,3,2,0,1:T(8,128)S(1)} %copy-done.2, f32[8,4,1,16,128]{4,3,2,0,1:T(8,128)S(1)} %copy-done, ...), kind=kLoop, calls=%fused_computation.147 | loop fusion | flops 3014656 | bytes 6815744 | tf_op jit(solution)/shard_map/transpose | solution.py:312
  111.0 48.9 %shard_map.60 = (f32[4,8,2,16,128]{4,3,2,1,0:T(8,128)}, f32[8,128]{1,0:T(8,128)}) custom-call(f32[4,8,2,16,128]{4,3,2,1,0:T(8,128)} %fusion.104.blocks_ref, f32[8,128]{1,0:T(8,128)} %broadcast_in_dim.2.val_ref), custom_call_target="tpu_custom_call" | custom-call | tf_op jit(solution)/shard_map/pallas_call | solution.py:244
  159.9 1.2 slice.729
  161.1 1.9 %broadcast_multiply_fusion = f32[4,8,2,16,128]{4,3,2,1,0:T(8,128)} fusion(f32[4,8,2,16,128]{4,3,2,1,0:T(8,128)} %get-tuple-element.12), kind=kLoop, calls=%fused_computation.207 | loop fusion | flops 131072 | bytes 1048576 | tf_op jit(solution)/shard_map/mul | solution.py:314
  (151 shorter events, 26.6 us)
Async XLA Ops:
  56.4 1.3 copy-start.31
  62.0 2.2 %copy-start.20 = (bf16[8,4,2,24,128]{4,3,2,1,0:T(8,128)(2,1)S(1)}, bf16[8,4,2,24,128]{4,3,2,1,0:T(8,128)(2,1)}, u32[]{:S(2)}) copy-start(bf16[8,4,2,24,128]{4,3,2,1,0:T(8,128)(2,1)} %get-tuple-element.58) | copy-start | bytes 1179652
  65.3 1.0 copy-start.19
  67.4 0.9 copy-start.22
  67.4 0.9 copy-start.23
  67.5 0.9 copy-start.24
  67.5 0.9 copy-start.25
  67.5 0.9 copy-start.26
  67.5 0.9 copy-start.27
  67.5 0.9 copy-start.28
  67.9 1.0 copy-start.18
  70.1 1.0 copy-start.17
  72.7 3.1 %copy-start.32 = (bf16[24]{0:T(256)(128)(2,1)S(1)}, bf16[24]{0:T(256)(128)(2,1)}, u32[]{:S(2)}) copy-start(bf16[24]{0:T(256)(128)(2,1)} %constant.46.clone.1) | copy-start | bytes 148
  73.7 33.2 %collective-permute-start = (f32[8,4,2,16,128]{4,3,2,0,1:T(8,128)}, f32[8,4,2,16,128]{4,3,2,0,1:T(8,128)}, u32[]{:S(2)}, u32[]{:S(2)}) collective-permute-start(f32[8,4,2,16,128]{4,3,2,0,1:T(8,128)} %fusion.93), channel_id=1, source_target_pairs={{0,64},{8,72},{16,80},{24,88},{32,96},{40,104},{48,112},{56,120},{... | collective-permute-start | bytes 1572872 | tf_op jit(solution)/shard_map/ppermute | solution.py:17
  84.1 22.8 %collective-permute-start.1 = (f32[8,4,2,16,128]{4,3,2,0,1:T(8,128)}, f32[8,4,2,16,128]{4,3,2,0,1:T(8,128)}, u32[]{:S(2)}, u32[]{:S(2)}) collective-permute-start(f32[8,4,2,16,128]{4,3,2,0,1:T(8,128)} %pad_maximum_fusion.3), channel_id=1, source_target_pairs={{0,32},{8,40},{16,48},{24,56},{32,64},{40,72},{48,80},{56,88},{64,... | collective-permute-start | bytes 1572872 | tf_op jit(solution)/shard_map/ppermute | solution.py:17
  105.8 1.1 copy-start
  105.8 1.1 copy-start.1
  105.8 1.1 copy-start.2
  105.8 1.2 copy-start.3
  105.8 1.2 copy-start.4
  105.9 1.3 copy-start.5
  105.9 1.4 copy-start.6
  105.9 1.4 copy-start.7
  105.9 1.5 copy-start.8
  105.9 1.6 copy-start.9
  105.9 1.7 %copy-start.10 = (f32[8,4,1,16,128]{4,3,2,0,1:T(8,128)S(1)}, f32[8,4,1,16,128]{4,3,2,0,1:T(8,128)}, u32[]{:S(2)}) copy-start(f32[8,4,1,16,128]{4,3,2,0,1:T(8,128)} %get-tuple-element.72) | copy-start | bytes 786436
  105.9 1.7 %copy-start.11 = (f32[8,4,1,16,128]{4,3,2,0,1:T(8,128)S(1)}, f32[8,4,1,16,128]{4,3,2,0,1:T(8,128)}, u32[]{:S(2)}) copy-start(f32[8,4,1,16,128]{4,3,2,0,1:T(8,128)} %get-tuple-element.73) | copy-start | bytes 786436
  105.9 1.8 %copy-start.12 = (f32[8,4,1,16,128]{4,3,2,0,1:T(8,128)S(1)}, f32[8,4,1,16,128]{4,3,2,0,1:T(8,128)}, u32[]{:S(2)}) copy-start(f32[8,4,1,16,128]{4,3,2,0,1:T(8,128)} %get-tuple-element.70) | copy-start | bytes 786436
  105.9 1.9 %copy-start.13 = (f32[8,4,1,16,128]{4,3,2,0,1:T(8,128)S(1)}, f32[8,4,1,16,128]{4,3,2,0,1:T(8,128)}, u32[]{:S(2)}) copy-start(f32[8,4,1,16,128]{4,3,2,0,1:T(8,128)} %get-tuple-element.71) | copy-start | bytes 786436
  105.9 1.9 %copy-start.14 = (f32[8,1,2,16,128]{4,3,2,0,1:T(8,128)S(1)}, f32[8,1,2,16,128]{4,3,2,0,1:T(8,128)}, u32[]{:S(2)}) copy-start(f32[8,1,2,16,128]{4,3,2,0,1:T(8,128)} %get-tuple-element.33) | copy-start | bytes 393220
  106.0 1.9 %copy-start.15 = (f32[8,1,2,16,128]{4,3,2,0,1:T(8,128)S(1)}, f32[8,1,2,16,128]{4,3,2,0,1:T(8,128)}, u32[]{:S(2)}) copy-start(f32[8,1,2,16,128]{4,3,2,0,1:T(8,128)} %get-tuple-element.61) | copy-start | bytes 393220
  106.0 2.0 %copy-start.16 = (f32[8,1,2,16,128]{4,3,2,0,1:T(8,128)S(1)}, f32[8,1,2,16,128]{4,3,2,0,1:T(8,128)}, u32[]{:S(2)}) copy-start(f32[8,1,2,16,128]{4,3,2,0,1:T(8,128)} %fusion.136) | copy-start | bytes 393220
  (3 other events, 2.5 us)

commit v15 on v14

--- a/solution.py
+++ b/solution.py
@@ -9,7 +9,7 @@
 F = 256
 W = 16
 BAND = 1024
-HALVES = 4
+HALVES = 8
 GROUP = 4
 
 

time: 166 us -> 165 us (level)
  no operation moved by 1% of the time
where the time goes in v15:
time: 165 us; the launch traced here: 164 us
  Pallas kernels  96 us (58%)
  other arithmetic  27.5 us (17%)
  matrix products  21.2 us (13%)
  local copies, waits for them, and re-layouts  10.8 us (7%)
  starting transfers between devices  4.22 us (3%)
  between operations  3.88 us (2%)
    pallas_call x1, Pallas kernels, finish(): pl.pallas_call(functools.partial(tail_kernel, n_col, n_f), out_shape=(jax...  48.1 us
    pallas_call x1, Pallas kernels, gather_columns(): pl.pallas_call(functools.partial(head_kernel, n_halves, halo_cols), out_s...  47.9 us
    dot_general x9, matrix products, pair_terms(): jnp.einsum('fbxrc,fbrd->fbxcd', stacked_left, right_rows, preferred_eleme...  10.2 us
    dot_general x9, matrix products, pair_terms(): jnp.einsum('fbxcd,fbvd->fbxvc', rounded, far_spec, preferred_element_type...  7.27 us
    sub x9, other arithmetic, pair_terms(): first_real = toward[:, :, 0, :W] - toward[:, :, 1, W:]  6.96 us
    ppermute x2, starting transfers between devices, permute(): return lax.ppermute(x, 'chan', pairs)  4.22 us
    dot_general x9, matrix products, pair_terms(): jnp.einsum('fbxcd,fbvc->fbxvd', rounded, near_spec, preferred_element_typ...  3.75 us
  transfers between devices with their start and end apart: 2, of which 0 were waited for; matrix products, arithmetic and copies ran while one was open for 16% of the time, Pallas kernels for 0%

profile of v15, /device:TPU:1, one launch (start us, length us, event | category | flops | bytes accessed | tf_op | source)
XLA Modules:
  0.0 163.6 jit_solution(13691799178820339498)
XLA Ops:
  5.9 1.8 %pad_maximum_fusion.4 = bf16[32,2,24,128]{3,2,1,0:T(8,128)(2,1)} fusion(bf16[32,2,8,128]{3,2,1,0:T(8,128)(2,1)} %param.5, bf16[32,2,16,128]{3,2,1,0:T(8,128)(2,1)} %param.4), kind=kLoop, calls=%fused_computation.158 | loop fusion | flops 786432 | bytes 786432 | tf_op jit(solution)/shard_map/concatenate | solution.py:268
  7.7 47.9 %shard_map.59 = bf16[8,3,4,1,2,24,128]{6,5,4,3,2,1,0:T(8,128)(2,1)} custom-call(bf16[4,8,1,2,24,128]{5,4,3,2,1,0:T(8,128)(2,1)} %bitcast.205), custom_call_target="tpu_custom_call" | custom-call | tf_op jit(solution)/shard_map/pallas_call | solution.py:146
  55.6 1.7 %fusion.191 = (bf16[8,4,2,16,128]{4,3,2,1,0:T(8,128)(2,1)S(1)}, bf16[8,4,2,16,128]{4,3,2,1,0:T(8,128)(2,1)S(1)}, bf16[8,4,2,16,128]{4,3,2,1,0:T(8,128)(2,1)S(1)}...) fusion(bf16[8,12,2,24,128]{4,3,2,1,0:T(8,128)(2,1)} %bitcast.188), kind=kLoop, calls=%fused_computation.349 | loop fusion | bytes 2621440 | tf_op jit(solution)/shard_map/slice | solution.py:62
  57.3 1.3 fusion.193
  58.9 1.4 convert_element_type.39
  60.2 1.3 slice.735
  63.8 1.3 multiply_select_fusion
  65.1 1.1 multiply_reduce_fusion.7
  67.2 1.1 multiply_reduce_fusion.6
  69.9 1.1 multiply_reduce_fusion.8
  72.1 1.1 multiply_reduce_fusion.5
  73.8 0.9 fusion.93
  74.7 2.1 %collective-permute-start = (f32[8,4,2,16,128]{4,3,2,0,1:T(8,128)}, f32[8,4,2,16,128]{4,3,2,0,1:T(8,128)}, u32[]{:S(2)}, u32[]{:S(2)}) collective-permute-start(f32[8,4,2,16,128]{4,3,2,0,1:T(8,128)} %fusion.93), channel_id=1, source_target_pairs={{0,64},{8,72},{16,80},{24,88},{32,96},{40,104},{48,112},{56,120},{... | collective-permute-start | bytes 1572872 | tf_op jit(solution)/shard_map/ppermute | solution.py:17
  77.5 1.1 multiply_reduce_fusion.2
  79.2 1.1 multiply_reduce_fusion.1
  80.8 1.1 multiply_reduce_fusion.4
  82.5 1.1 multiply_reduce_fusion.3
  84.2 0.8 pad_maximum_fusion.3
  85.1 2.1 %collective-permute-start.1 = (f32[8,4,2,16,128]{4,3,2,0,1:T(8,128)}, f32[8,4,2,16,128]{4,3,2,0,1:T(8,128)}, u32[]{:S(2)}, u32[]{:S(2)}) collective-permute-start(f32[8,4,2,16,128]{4,3,2,0,1:T(8,128)} %pad_maximum_fusion.3), channel_id=1, source_target_pairs={{0,32},{8,40},{16,48},{24,56},{32,64},{40,72},{48,80},{56,88},{64,... | collective-permute-start | bytes 1572872 | tf_op jit(solution)/shard_map/ppermute | solution.py:17
  87.6 1.1 multiply_reduce_fusion
  94.0 0.8 fusion.36
  94.8 0.9 slice_subtract_fusion.17
  95.7 0.8 fusion.54
  96.5 0.9 slice_subtract_fusion.14
  98.2 0.9 slice_subtract_fusion.7
  99.9 0.9 slice_subtract_fusion.6
  101.6 0.9 slice_subtract_fusion.9
  103.3 0.9 slice_subtract_fusion.8
  107.6 2.5 %fusion.104.blocks_ref = f32[4,8,2,16,128]{4,3,2,1,0:T(8,128)} fusion(f32[8,4,2,16,128]{4,3,2,0,1:T(8,128)} %collective-permute-done.1, f32[8,4,2,16,128]{4,3,2,0,1:T(8,128)} %collective-permute-done, f32[8,4,1,16,128]{4,3,2,0,1:T(8,128)S(1)} %copy-done.4, f32[8,4,1,16,128]{4,3,2,0,1:T(8,128)S(1)} %copy-done.3, f32[8,4,1,16,128]{4,3,2,0,1:T(8,128)S(1)} %copy-done.1, ...), kind=kLoop, calls=%fused_computation.147 | loop fusion | flops 3014656 | bytes 6815744 | tf_op jit(solution)/shard_map/transpose | solution.py:312
  110.7 48.1 %shard_map.60 = (f32[4,8,2,16,128]{4,3,2,1,0:T(8,128)}, f32[8,128]{1,0:T(8,128)}) custom-call(f32[4,8,2,16,128]{4,3,2,1,0:T(8,128)} %fusion.104.blocks_ref, f32[8,128]{1,0:T(8,128)} %broadcast_in_dim.2.val_ref), custom_call_target="tpu_custom_call" | custom-call | tf_op jit(solution)/shard_map/pallas_call | solution.py:244
  158.8 1.2 slice.729
  160.0 1.9 %broadcast_multiply_fusion = f32[4,8,2,16,128]{4,3,2,1,0:T(8,128)} fusion(f32[4,8,2,16,128]{4,3,2,1,0:T(8,128)} %get-tuple-element.12), kind=kLoop, calls=%fused_computation.207 | loop fusion | flops 131072 | bytes 1048576 | tf_op jit(solution)/shard_map/mul | solution.py:314
  (152 shorter events, 26.4 us)
Async XLA Ops:
  55.6 1.7 %copy-start = (bf16[8,3,4,1,2,24,128]{6,5,4,3,2,1,0:T(8,128)(2,1)S(1)}, bf16[8,3,4,1,2,24,128]{6,5,4,3,2,1,0:T(8,128)(2,1)}, u32[]{:S(2)}) copy-start(bf16[8,3,4,1,2,24,128]{6,5,4,3,2,1,0:T(8,128)(2,1)} %shard_map.59) | copy-start | bytes 3538948
  57.3 1.3 copy-start.32
  63.0 2.2 %copy-start.21 = (bf16[8,4,2,24,128]{4,3,2,1,0:T(8,128)(2,1)S(1)}, bf16[8,4,2,24,128]{4,3,2,1,0:T(8,128)(2,1)}, u32[]{:S(2)}) copy-start(bf16[8,4,2,24,128]{4,3,2,1,0:T(8,128)(2,1)} %get-tuple-element.58) | copy-start | bytes 1179652
  66.2 1.0 copy-start.20
  68.4 0.9 copy-start.23
  68.4 0.9 copy-start.24
  68.4 0.9 copy-start.25
  68.4 0.9 copy-start.26
  68.4 0.9 copy-start.27
  68.4 0.9 copy-start.28
  68.9 1.0 copy-start.19
  71.1 1.0 copy-start.18
  73.7 3.1 %copy-start.33 = (bf16[24]{0:T(256)(128)(2,1)S(1)}, bf16[24]{0:T(256)(128)(2,1)}, u32[]{:S(2)}) copy-start(bf16[24]{0:T(256)(128)(2,1)} %constant.46.clone.1) | copy-start | bytes 148
  74.7 31.9 %collective-permute-start = (f32[8,4,2,16,128]{4,3,2,0,1:T(8,128)}, f32[8,4,2,16,128]{4,3,2,0,1:T(8,128)}, u32[]{:S(2)}, u32[]{:S(2)}) collective-permute-start(f32[8,4,2,16,128]{4,3,2,0,1:T(8,128)} %fusion.93), channel_id=1, source_target_pairs={{0,64},{8,72},{16,80},{24,88},{32,96},{40,104},{48,112},{56,120},{... | collective-permute-start | bytes 1572872 | tf_op jit(solution)/shard_map/ppermute | solution.py:17
  85.1 21.5 %collective-permute-start.1 = (f32[8,4,2,16,128]{4,3,2,0,1:T(8,128)}, f32[8,4,2,16,128]{4,3,2,0,1:T(8,128)}, u32[]{:S(2)}, u32[]{:S(2)}) collective-permute-start(f32[8,4,2,16,128]{4,3,2,0,1:T(8,128)} %pad_maximum_fusion.3), channel_id=1, source_target_pairs={{0,32},{8,40},{16,48},{24,56},{32,64},{40,72},{48,80},{56,88},{64,... | collective-permute-start | bytes 1572872 | tf_op jit(solution)/shard_map/ppermute | solution.py:17
  105.5 1.1 copy-start.1
  105.5 1.1 copy-start.2
  105.5 1.1 copy-start.3
  105.5 1.2 copy-start.4
  105.5 1.2 copy-start.5
  105.5 1.3 copy-start.6
  105.6 1.4 copy-start.7
  105.6 1.4 copy-start.8
  105.6 1.5 copy-start.9
  105.6 1.6 copy-start.10
  105.6 1.7 %copy-start.11 = (f32[8,4,1,16,128]{4,3,2,0,1:T(8,128)S(1)}, f32[8,4,1,16,128]{4,3,2,0,1:T(8,128)}, u32[]{:S(2)}) copy-start(f32[8,4,1,16,128]{4,3,2,0,1:T(8,128)} %get-tuple-element.72) | copy-start | bytes 786436
  105.6 1.7 %copy-start.12 = (f32[8,4,1,16,128]{4,3,2,0,1:T(8,128)S(1)}, f32[8,4,1,16,128]{4,3,2,0,1:T(8,128)}, u32[]{:S(2)}) copy-start(f32[8,4,1,16,128]{4,3,2,0,1:T(8,128)} %get-tuple-element.73) | copy-start | bytes 786436
  105.6 1.8 %copy-start.13 = (f32[8,4,1,16,128]{4,3,2,0,1:T(8,128)S(1)}, f32[8,4,1,16,128]{4,3,2,0,1:T(8,128)}, u32[]{:S(2)}) copy-start(f32[8,4,1,16,128]{4,3,2,0,1:T(8,128)} %get-tuple-element.70) | copy-start | bytes 786436
  105.6 1.9 %copy-start.14 = (f32[8,4,1,16,128]{4,3,2,0,1:T(8,128)S(1)}, f32[8,4,1,16,128]{4,3,2,0,1:T(8,128)}, u32[]{:S(2)}) copy-start(f32[8,4,1,16,128]{4,3,2,0,1:T(8,128)} %get-tuple-element.71) | copy-start | bytes 786436
  105.6 1.9 %copy-start.15 = (f32[8,1,2,16,128]{4,3,2,0,1:T(8,128)S(1)}, f32[8,1,2,16,128]{4,3,2,0,1:T(8,128)}, u32[]{:S(2)}) copy-start(f32[8,1,2,16,128]{4,3,2,0,1:T(8,128)} %get-tuple-element.33) | copy-start | bytes 393220
  105.6 1.9 %copy-start.16 = (f32[8,1,2,16,128]{4,3,2,0,1:T(8,128)S(1)}, f32[8,1,2,16,128]{4,3,2,0,1:T(8,128)}, u32[]{:S(2)}) copy-start(f32[8,1,2,16,128]{4,3,2,0,1:T(8,128)} %get-tuple-element.61) | copy-start | bytes 393220
  105.7 2.0 %copy-start.17 = (f32[8,1,2,16,128]{4,3,2,0,1:T(8,128)S(1)}, f32[8,1,2,16,128]{4,3,2,0,1:T(8,128)}, u32[]{:S(2)}) copy-start(f32[8,1,2,16,128]{4,3,2,0,1:T(8,128)} %fusion.136) | copy-start | bytes 393220
  (4 other events, 3.4 us)

commit v16 on v14

--- a/solution.py
+++ b/solution.py
@@ -134,7 +134,10 @@
                 device_id=devh(h, 1), device_id_type=MESH).wait_recv()
     for cp in sends:
         cp.wait_send()
-    out_ref[...] = held[...]
+    for half in range(n_halves):
+        for col in range(1 + halo_cols):
+            for blk in range(GROUP):
+                out_ref[half, :, col, blk] = held[half, col, blk]
 
 
 def gather_columns(payload, halo_cols, n_halves):
@@ -143,9 +146,10 @@
     chunks = payload.reshape(GROUP, n_halves, q, two, rows, bw)
     shape = (n_halves, 1 + halo_cols, GROUP, q, two, rows, bw)
     vmem = pl.BlockSpec(memory_space=pltpu.VMEM)
+    out_layout = (n_halves, q, 1 + halo_cols, GROUP, two, rows, bw)
     held = pl.pallas_call(
         functools.partial(head_kernel, n_halves, halo_cols),
-        out_shape=jax.ShapeDtypeStruct(shape, payload.dtype),
+        out_shape=jax.ShapeDtypeStruct(out_layout, payload.dtype),
         in_specs=[vmem],
         out_specs=vmem,
         scratch_shapes=[
@@ -158,7 +162,6 @@
         ],
         compiler_params=pltpu.CompilerParams(collective_id=1, has_side_effects=True),
     )(chunks)
-    held = jnp.transpose(held, (0, 3, 1, 2, 4, 5, 6))
     return held.reshape(n_halves * q, (1 + halo_cols) * GROUP, two, rows, bw)
 
 
@@ -212,7 +215,6 @@
             acc = acc + slots[s]
         return acc
 
-    first = start_gather(val_ref, slots1, send1, recv1, g1, me1, dev1)
     outgoing = []
     for t in range(1, GROUP):
         b = (j + t) % GROUP
@@ -221,6 +223,7 @@
             recv_sem=recv_o.at[j], device_id=devg(b), device_id_type=MESH)
         cp.start()
         outgoing.append(cp)
+    first = start_gather(val_ref, slots1, send1, recv1, g1, me1, dev1)
     stage[...] = finish_gather(val_ref, slots1, send1, recv1, g1, me1, dev1, first)
     second = start_gather(stage, slots2, send2, recv2, n_col, k, dev2)
     sum_ref[...] = finish_gather(stage, slots2, send2, recv2, n_col, k, dev2, second)

time: 166 us -> 171 us (1.030)
  Pallas kernels: 95.7 us -> 101 us
    pallas_call x1, Pallas kernels: 48.9 us -> 54.4 us  [finish(): pl.pallas_call(functools.partial(tail_kernel, n_col, n_f), out_shape=(jax...]
where the time goes in v16:
time: 171 us; the launch traced here: 170 us
  Pallas kernels  101 us (59%)
  other arithmetic  27.5 us (16%)
  matrix products  21.2 us (12%)
  local copies, waits for them, and re-layouts  10.8 us (6%)
  starting transfers between devices  5.59 us (3%)
  between operations  3.88 us (2%)
    pallas_call x1, Pallas kernels, finish(): pl.pallas_call(functools.partial(tail_kernel, n_col, n_f), out_shape=(jax...  54.4 us
    pallas_call x1, Pallas kernels, gather_columns(): pl.pallas_call(functools.partial(head_kernel, n_halves, halo_cols), out_s...  46.9 us
    dot_general x9, matrix products, pair_terms(): jnp.einsum('fbxrc,fbrd->fbxcd', stacked_left, right_rows, preferred_eleme...  10.2 us
    dot_general x9, matrix products, pair_terms(): jnp.einsum('fbxcd,fbvd->fbxvc', rounded, far_spec, preferred_element_type...  7.27 us
    sub x9, other arithmetic, pair_terms(): first_real = toward[:, :, 0, :W] - toward[:, :, 1, W:]  6.96 us
    ppermute x2, starting transfers between devices, permute(): return lax.ppermute(x, 'chan', pairs)  5.59 us
    dot_general x9, matrix products, pair_terms(): jnp.einsum('fbxcd,fbvc->fbxvd', rounded, near_spec, preferred_element_typ...  3.74 us
  transfers between devices with their start and end apart: 2, of which 0 were waited for; matrix products, arithmetic and copies ran while one was open for 16% of the time, Pallas kernels for 0%

profile of v16, /device:TPU:1, one launch (start us, length us, event | category | flops | bytes accessed | tf_op | source)
XLA Modules:
  0.0 170.3 jit_solution(5742753502128277540)
XLA Ops:
  5.9 1.8 %pad_maximum_fusion.4 = bf16[32,2,24,128]{3,2,1,0:T(8,128)(2,1)} fusion(bf16[32,2,8,128]{3,2,1,0:T(8,128)(2,1)} %param.5, bf16[32,2,16,128]{3,2,1,0:T(8,128)(2,1)} %param.4), kind=kLoop, calls=%fused_computation.158 | loop fusion | flops 786432 | bytes 786432 | tf_op jit(solution)/shard_map/concatenate | solution.py:271
  7.7 46.9 %shard_map.59 = bf16[4,2,3,4,2,24,128]{6,5,4,3,2,1,0:T(8,128)(2,1)} custom-call(bf16[4,4,2,2,24,128]{5,4,3,2,1,0:T(8,128)(2,1)} %bitcast.205), custom_call_target="tpu_custom_call" | custom-call | tf_op jit(solution)/shard_map/pallas_call | solution.py:150
  54.6 1.7 fusion.191
  56.3 1.3 fusion.193
  57.8 1.4 convert_element_type.39
  59.2 1.3 slice.735
  62.7 1.3 multiply_select_fusion
  64.1 1.1 multiply_reduce_fusion.7
  66.2 1.1 multiply_reduce_fusion.6
  68.9 1.1 multiply_reduce_fusion.8
  71.0 1.1 multiply_reduce_fusion.5
  72.7 0.9 fusion.93
  73.6 2.1 %collective-permute-start = (f32[8,4,2,16,128]{4,3,2,0,1:T(8,128)}, f32[8,4,2,16,128]{4,3,2,0,1:T(8,128)}, u32[]{:S(2)}, u32[]{:S(2)}) collective-permute-start(f32[8,4,2,16,128]{4,3,2,0,1:T(8,128)} %fusion.93), channel_id=1, source_target_pairs={{0,64},{8,72},{16,80},{24,88},{32,96},{40,104},{48,112},{56,120},{... | collective-permute-start | bytes 1572872 | tf_op jit(solution)/shard_map/ppermute | solution.py:17
  76.5 1.1 multiply_reduce_fusion.2
  78.1 1.1 multiply_reduce_fusion.1
  79.8 1.1 multiply_reduce_fusion.4
  81.4 1.1 multiply_reduce_fusion.3
  83.2 0.8 pad_maximum_fusion.3
  84.0 3.5 %collective-permute-start.1 = (f32[8,4,2,16,128]{4,3,2,0,1:T(8,128)}, f32[8,4,2,16,128]{4,3,2,0,1:T(8,128)}, u32[]{:S(2)}, u32[]{:S(2)}) collective-permute-start(f32[8,4,2,16,128]{4,3,2,0,1:T(8,128)} %pad_maximum_fusion.3), channel_id=1, source_target_pairs={{0,32},{8,40},{16,48},{24,56},{32,64},{40,72},{48,80},{56,88},{64,... | collective-permute-start | bytes 1572872 | tf_op jit(solution)/shard_map/ppermute | solution.py:17
  87.9 1.1 multiply_reduce_fusion
  94.3 0.8 fusion.36
  95.1 0.9 slice_subtract_fusion.17
  96.0 0.8 fusion.54
  96.8 0.9 slice_subtract_fusion.14
  98.5 0.9 slice_subtract_fusion.7
  100.2 0.9 slice_subtract_fusion.6
  101.9 0.9 slice_subtract_fusion.9
  103.6 0.9 slice_subtract_fusion.8
  107.9 2.5 %fusion.104.blocks_ref = f32[4,8,2,16,128]{4,3,2,1,0:T(8,128)} fusion(f32[8,4,2,16,128]{4,3,2,0,1:T(8,128)} %collective-permute-done.1, f32[8,4,2,16,128]{4,3,2,0,1:T(8,128)} %collective-permute-done, f32[8,4,1,16,128]{4,3,2,0,1:T(8,128)S(1)} %copy-done.4, f32[8,4,1,16,128]{4,3,2,0,1:T(8,128)S(1)} %copy-done.3, f32[8,4,1,16,128]{4,3,2,0,1:T(8,128)S(1)} %copy-done.1, ...), kind=kLoop, calls=%fused_computation.147 | loop fusion | flops 3014656 | bytes 6815744 | tf_op jit(solution)/shard_map/transpose | solution.py:315
  111.0 54.4 %shard_map.60 = (f32[4,8,2,16,128]{4,3,2,1,0:T(8,128)}, f32[8,128]{1,0:T(8,128)}) custom-call(f32[4,8,2,16,128]{4,3,2,1,0:T(8,128)} %fusion.104.blocks_ref, f32[8,128]{1,0:T(8,128)} %broadcast_in_dim.2.val_ref), custom_call_target="tpu_custom_call" | custom-call | tf_op jit(solution)/shard_map/pallas_call | solution.py:247
  165.5 1.2 slice.729
  166.6 1.9 %broadcast_multiply_fusion = f32[4,8,2,16,128]{4,3,2,1,0:T(8,128)} fusion(f32[4,8,2,16,128]{4,3,2,1,0:T(8,128)} %get-tuple-element.12), kind=kLoop, calls=%fused_computation.207 | loop fusion | flops 131072 | bytes 1048576 | tf_op jit(solution)/shard_map/mul | solution.py:317
  (152 shorter events, 26.4 us)
Async XLA Ops:
  54.6 1.7 copy-start
  56.2 1.3 copy-start.32
  61.9 2.2 %copy-start.21 = (bf16[8,4,2,24,128]{4,3,2,1,0:T(8,128)(2,1)S(1)}, bf16[8,4,2,24,128]{4,3,2,1,0:T(8,128)(2,1)}, u32[]{:S(2)}) copy-start(bf16[8,4,2,24,128]{4,3,2,1,0:T(8,128)(2,1)} %get-tuple-element.58) | copy-start | bytes 1179652
  65.2 1.0 copy-start.20
  67.3 0.9 copy-start.23
  67.3 0.9 copy-start.24
  67.3 0.9 copy-start.25
  67.4 0.9 copy-start.26
  67.4 0.9 copy-start.27
  67.4 0.9 copy-start.28
  67.8 1.0 copy-start.19
  70.0 1.0 copy-start.18
  72.6 3.1 %copy-start.33 = (bf16[24]{0:T(256)(128)(2,1)S(1)}, bf16[24]{0:T(256)(128)(2,1)}, u32[]{:S(2)}) copy-start(bf16[24]{0:T(256)(128)(2,1)} %constant.46.clone.1) | copy-start | bytes 148
  73.6 33.2 %collective-permute-start = (f32[8,4,2,16,128]{4,3,2,0,1:T(8,128)}, f32[8,4,2,16,128]{4,3,2,0,1:T(8,128)}, u32[]{:S(2)}, u32[]{:S(2)}) collective-permute-start(f32[8,4,2,16,128]{4,3,2,0,1:T(8,128)} %fusion.93), channel_id=1, source_target_pairs={{0,64},{8,72},{16,80},{24,88},{32,96},{40,104},{48,112},{56,120},{... | collective-permute-start | bytes 1572872 | tf_op jit(solution)/shard_map/ppermute | solution.py:17
  84.0 22.9 %collective-permute-start.1 = (f32[8,4,2,16,128]{4,3,2,0,1:T(8,128)}, f32[8,4,2,16,128]{4,3,2,0,1:T(8,128)}, u32[]{:S(2)}, u32[]{:S(2)}) collective-permute-start(f32[8,4,2,16,128]{4,3,2,0,1:T(8,128)} %pad_maximum_fusion.3), channel_id=1, source_target_pairs={{0,32},{8,40},{16,48},{24,56},{32,64},{40,72},{48,80},{56,88},{64,... | collective-permute-start | bytes 1572872 | tf_op jit(solution)/shard_map/ppermute | solution.py:17
  105.8 1.1 copy-start.1
  105.8 1.1 copy-start.2
  105.8 1.1 copy-start.3
  105.8 1.2 copy-start.4
  105.8 1.2 copy-start.5
  105.9 1.3 copy-start.6
  105.9 1.4 copy-start.7
  105.9 1.4 copy-start.8
  105.9 1.5 copy-start.9
  105.9 1.6 copy-start.10
  105.9 1.7 copy-start.11
  105.9 1.7 %copy-start.12 = (f32[8,4,1,16,128]{4,3,2,0,1:T(8,128)S(1)}, f32[8,4,1,16,128]{4,3,2,0,1:T(8,128)}, u32[]{:S(2)}) copy-start(f32[8,4,1,16,128]{4,3,2,0,1:T(8,128)} %get-tuple-element.73) | copy-start | bytes 786436
  105.9 1.8 %copy-start.13 = (f32[8,4,1,16,128]{4,3,2,0,1:T(8,128)S(1)}, f32[8,4,1,16,128]{4,3,2,0,1:T(8,128)}, u32[]{:S(2)}) copy-start(f32[8,4,1,16,128]{4,3,2,0,1:T(8,128)} %get-tuple-element.70) | copy-start | bytes 786436
  105.9 1.9 %copy-start.14 = (f32[8,4,1,16,128]{4,3,2,0,1:T(8,128)S(1)}, f32[8,4,1,16,128]{4,3,2,0,1:T(8,128)}, u32[]{:S(2)}) copy-start(f32[8,4,1,16,128]{4,3,2,0,1:T(8,128)} %get-tuple-element.71) | copy-start | bytes 786436
  105.9 1.9 %copy-start.15 = (f32[8,1,2,16,128]{4,3,2,0,1:T(8,128)S(1)}, f32[8,1,2,16,128]{4,3,2,0,1:T(8,128)}, u32[]{:S(2)}) copy-start(f32[8,1,2,16,128]{4,3,2,0,1:T(8,128)} %get-tuple-element.33) | copy-start | bytes 393220
  106.0 1.9 %copy-start.16 = (f32[8,1,2,16,128]{4,3,2,0,1:T(8,128)S(1)}, f32[8,1,2,16,128]{4,3,2,0,1:T(8,128)}, u32[]{:S(2)}) copy-start(f32[8,1,2,16,128]{4,3,2,0,1:T(8,128)} %get-tuple-element.61) | copy-start | bytes 393220
  106.0 2.0 %copy-start.17 = (f32[8,1,2,16,128]{4,3,2,0,1:T(8,128)S(1)}, f32[8,1,2,16,128]{4,3,2,0,1:T(8,128)}, u32[]{:S(2)}) copy-start(f32[8,1,2,16,128]{4,3,2,0,1:T(8,128)} %fusion.136) | copy-start | bytes 393220
  (4 other events, 3.4 us)

commit v17 on v16

--- a/solution.py
+++ b/solution.py
@@ -215,6 +215,7 @@
             acc = acc + slots[s]
         return acc
 
+    first = start_gather(val_ref, slots1, send1, recv1, g1, me1, dev1)
     outgoing = []
     for t in range(1, GROUP):
         b = (j + t) % GROUP
@@ -223,7 +224,6 @@
             recv_sem=recv_o.at[j], device_id=devg(b), device_id_type=MESH)
         cp.start()
         outgoing.append(cp)
-    first = start_gather(val_ref, slots1, send1, recv1, g1, me1, dev1)
     stage[...] = finish_gather(val_ref, slots1, send1, recv1, g1, me1, dev1, first)
     second = start_gather(stage, slots2, send2, recv2, n_col, k, dev2)
     sum_ref[...] = finish_gather(stage, slots2, send2, recv2, n_col, k, dev2, second)

time: 171 us -> 166 us (0.971)
  Pallas kernels: 101 us -> 95.7 us
    pallas_call x1, Pallas kernels: 54.4 us -> 48.9 us  [finish(): pl.pallas_call(functools.partial(tail_kernel, n_col, n_f), out_shape=(jax...]
where the time goes in v17:
time: 166 us; the launch traced here: 165 us
  Pallas kernels  95.7 us (58%)
  other arithmetic  27.5 us (17%)
  matrix products  21.2 us (13%)
  local copies, waits for them, and re-layouts  10.8 us (7%)
  starting transfers between devices  5.59 us (3%)
  between operations  3.88 us (2%)
    pallas_call x1, Pallas kernels, finish(): pl.pallas_call(functools.partial(tail_kernel, n_col, n_f), out_shape=(jax...  48.9 us
    pallas_call x1, Pallas kernels, gather_columns(): pl.pallas_call(functools.partial(head_kernel, n_halves, halo_cols), out_s...  46.9 us
    dot_general x9, matrix products, pair_terms(): jnp.einsum('fbxrc,fbrd->fbxcd', stacked_left, right_rows, preferred_eleme...  10.2 us
    dot_general x9, matrix products, pair_terms(): jnp.einsum('fbxcd,fbvd->fbxvc', rounded, far_spec, preferred_element_type...  7.27 us
    sub x9, other arithmetic, pair_terms(): first_real = toward[:, :, 0, :W] - toward[:, :, 1, W:]  6.96 us
    ppermute x2, starting transfers between devices, permute(): return lax.ppermute(x, 'chan', pairs)  5.59 us
    dot_general x9, matrix products, pair_terms(): jnp.einsum('fbxcd,fbvc->fbxvd', rounded, near_spec, preferred_element_typ...  3.74 us
  transfers between devices with their start and end apart: 2, of which 0 were waited for; matrix products, arithmetic and copies ran while one was open for 16% of the time, Pallas kernels for 0%

profile of v17, /device:TPU:1, one launch (start us, length us, event | category | flops | bytes accessed | tf_op | source)
XLA Modules:
  0.0 164.8 jit_solution(1946565288225378476)
XLA Ops:
  5.9 1.8 %pad_maximum_fusion.4 = bf16[32,2,24,128]{3,2,1,0:T(8,128)(2,1)} fusion(bf16[32,2,8,128]{3,2,1,0:T(8,128)(2,1)} %param.5, bf16[32,2,16,128]{3,2,1,0:T(8,128)(2,1)} %param.4), kind=kLoop, calls=%fused_computation.158 | loop fusion | flops 786432 | bytes 786432 | tf_op jit(solution)/shard_map/concatenate | solution.py:271
  7.7 46.9 %shard_map.59 = bf16[4,2,3,4,2,24,128]{6,5,4,3,2,1,0:T(8,128)(2,1)} custom-call(bf16[4,4,2,2,24,128]{5,4,3,2,1,0:T(8,128)(2,1)} %bitcast.205), custom_call_target="tpu_custom_call" | custom-call | tf_op jit(solution)/shard_map/pallas_call | solution.py:150
  54.6 1.7 %fusion.191 = (bf16[8,4,2,16,128]{4,3,2,1,0:T(8,128)(2,1)S(1)}, bf16[8,4,2,16,128]{4,3,2,1,0:T(8,128)(2,1)S(1)}, bf16[8,4,2,16,128]{4,3,2,1,0:T(8,128)(2,1)S(1)}...) fusion(bf16[8,12,2,24,128]{4,3,2,1,0:T(8,128)(2,1)} %bitcast.188), kind=kLoop, calls=%fused_computation.349 | loop fusion | bytes 2621440 | tf_op jit(solution)/shard_map/slice | solution.py:62
  56.3 1.3 fusion.193
  57.8 1.4 convert_element_type.39
  59.2 1.3 slice.735
  62.7 1.3 multiply_select_fusion
  64.1 1.1 multiply_reduce_fusion.7
  66.2 1.1 multiply_reduce_fusion.6
  68.9 1.1 multiply_reduce_fusion.8
  71.0 1.1 multiply_reduce_fusion.5
  72.7 0.9 fusion.93
  73.6 2.1 %collective-permute-start = (f32[8,4,2,16,128]{4,3,2,0,1:T(8,128)}, f32[8,4,2,16,128]{4,3,2,0,1:T(8,128)}, u32[]{:S(2)}, u32[]{:S(2)}) collective-permute-start(f32[8,4,2,16,128]{4,3,2,0,1:T(8,128)} %fusion.93), channel_id=1, source_target_pairs={{0,64},{8,72},{16,80},{24,88},{32,96},{40,104},{48,112},{56,120},{... | collective-permute-start | bytes 1572872 | tf_op jit(solution)/shard_map/ppermute | solution.py:17
  76.5 1.1 multiply_reduce_fusion.2
  78.1 1.1 multiply_reduce_fusion.1
  79.8 1.1 multiply_reduce_fusion.4
  81.4 1.1 multiply_reduce_fusion.3
  83.2 0.8 pad_maximum_fusion.3
  84.0 3.5 %collective-permute-start.1 = (f32[8,4,2,16,128]{4,3,2,0,1:T(8,128)}, f32[8,4,2,16,128]{4,3,2,0,1:T(8,128)}, u32[]{:S(2)}, u32[]{:S(2)}) collective-permute-start(f32[8,4,2,16,128]{4,3,2,0,1:T(8,128)} %pad_maximum_fusion.3), channel_id=1, source_target_pairs={{0,32},{8,40},{16,48},{24,56},{32,64},{40,72},{48,80},{56,88},{64,... | collective-permute-start | bytes 1572872 | tf_op jit(solution)/shard_map/ppermute | solution.py:17
  87.9 1.1 multiply_reduce_fusion
  94.3 0.8 fusion.36
  95.1 0.9 slice_subtract_fusion.17
  96.0 0.8 fusion.54
  96.8 0.9 slice_subtract_fusion.14
  98.5 0.9 slice_subtract_fusion.7
  100.2 0.9 slice_subtract_fusion.6
  101.9 0.9 slice_subtract_fusion.9
  103.6 0.9 slice_subtract_fusion.8
  107.9 2.5 %fusion.104.blocks_ref = f32[4,8,2,16,128]{4,3,2,1,0:T(8,128)} fusion(f32[8,4,2,16,128]{4,3,2,0,1:T(8,128)} %collective-permute-done.1, f32[8,4,2,16,128]{4,3,2,0,1:T(8,128)} %collective-permute-done, f32[8,4,1,16,128]{4,3,2,0,1:T(8,128)S(1)} %copy-done.4, f32[8,4,1,16,128]{4,3,2,0,1:T(8,128)S(1)} %copy-done.3, f32[8,4,1,16,128]{4,3,2,0,1:T(8,128)S(1)} %copy-done.1, ...), kind=kLoop, calls=%fused_computation.147 | loop fusion | flops 3014656 | bytes 6815744 | tf_op jit(solution)/shard_map/transpose | solution.py:315
  111.0 48.9 %shard_map.60 = (f32[4,8,2,16,128]{4,3,2,1,0:T(8,128)}, f32[8,128]{1,0:T(8,128)}) custom-call(f32[4,8,2,16,128]{4,3,2,1,0:T(8,128)} %fusion.104.blocks_ref, f32[8,128]{1,0:T(8,128)} %broadcast_in_dim.2.val_ref), custom_call_target="tpu_custom_call" | custom-call | tf_op jit(solution)/shard_map/pallas_call | solution.py:247
  159.9 1.2 slice.729
  161.1 1.9 %broadcast_multiply_fusion = f32[4,8,2,16,128]{4,3,2,1,0:T(8,128)} fusion(f32[4,8,2,16,128]{4,3,2,1,0:T(8,128)} %get-tuple-element.12), kind=kLoop, calls=%fused_computation.207 | loop fusion | flops 131072 | bytes 1048576 | tf_op jit(solution)/shard_map/mul | solution.py:317
  (152 shorter events, 26.4 us)
Async XLA Ops:
  54.6 1.7 %copy-start = (bf16[4,2,3,4,2,24,128]{6,5,4,3,2,1,0:T(8,128)(2,1)S(1)}, bf16[4,2,3,4,2,24,128]{6,5,4,3,2,1,0:T(8,128)(2,1)}, u32[]{:S(2)}) copy-start(bf16[4,2,3,4,2,24,128]{6,5,4,3,2,1,0:T(8,128)(2,1)} %shard_map.59) | copy-start | bytes 3538948
  56.2 1.3 copy-start.32
  61.9 2.2 %copy-start.21 = (bf16[8,4,2,24,128]{4,3,2,1,0:T(8,128)(2,1)S(1)}, bf16[8,4,2,24,128]{4,3,2,1,0:T(8,128)(2,1)}, u32[]{:S(2)}) copy-start(bf16[8,4,2,24,128]{4,3,2,1,0:T(8,128)(2,1)} %get-tuple-element.58) | copy-start | bytes 1179652
  65.2 1.0 copy-start.20
  67.3 0.9 copy-start.23
  67.3 0.9 copy-start.24
  67.3 0.9 copy-start.25
  67.4 0.9 copy-start.26
  67.4 0.9 copy-start.27
  67.4 0.9 copy-start.28
  67.8 1.0 copy-start.19
  70.0 1.0 copy-start.18
  72.6 3.1 %copy-start.33 = (bf16[24]{0:T(256)(128)(2,1)S(1)}, bf16[24]{0:T(256)(128)(2,1)}, u32[]{:S(2)}) copy-start(bf16[24]{0:T(256)(128)(2,1)} %constant.46.clone.1) | copy-start | bytes 148
  73.6 33.2 %collective-permute-start = (f32[8,4,2,16,128]{4,3,2,0,1:T(8,128)}, f32[8,4,2,16,128]{4,3,2,0,1:T(8,128)}, u32[]{:S(2)}, u32[]{:S(2)}) collective-permute-start(f32[8,4,2,16,128]{4,3,2,0,1:T(8,128)} %fusion.93), channel_id=1, source_target_pairs={{0,64},{8,72},{16,80},{24,88},{32,96},{40,104},{48,112},{56,120},{... | collective-permute-start | bytes 1572872 | tf_op jit(solution)/shard_map/ppermute | solution.py:17
  84.0 22.9 %collective-permute-start.1 = (f32[8,4,2,16,128]{4,3,2,0,1:T(8,128)}, f32[8,4,2,16,128]{4,3,2,0,1:T(8,128)}, u32[]{:S(2)}, u32[]{:S(2)}) collective-permute-start(f32[8,4,2,16,128]{4,3,2,0,1:T(8,128)} %pad_maximum_fusion.3), channel_id=1, source_target_pairs={{0,32},{8,40},{16,48},{24,56},{32,64},{40,72},{48,80},{56,88},{64,... | collective-permute-start | bytes 1572872 | tf_op jit(solution)/shard_map/ppermute | solution.py:17
  105.8 1.1 copy-start.1
  105.8 1.1 copy-start.2
  105.8 1.1 copy-start.3
  105.8 1.2 copy-start.4
  105.8 1.2 copy-start.5
  105.9 1.3 copy-start.6
  105.9 1.4 copy-start.7
  105.9 1.4 copy-start.8
  105.9 1.5 copy-start.9
  105.9 1.6 copy-start.10
  105.9 1.7 %copy-start.11 = (f32[8,4,1,16,128]{4,3,2,0,1:T(8,128)S(1)}, f32[8,4,1,16,128]{4,3,2,0,1:T(8,128)}, u32[]{:S(2)}) copy-start(f32[8,4,1,16,128]{4,3,2,0,1:T(8,128)} %get-tuple-element.72) | copy-start | bytes 786436
  105.9 1.7 %copy-start.12 = (f32[8,4,1,16,128]{4,3,2,0,1:T(8,128)S(1)}, f32[8,4,1,16,128]{4,3,2,0,1:T(8,128)}, u32[]{:S(2)}) copy-start(f32[8,4,1,16,128]{4,3,2,0,1:T(8,128)} %get-tuple-element.73) | copy-start | bytes 786436
  105.9 1.8 %copy-start.13 = (f32[8,4,1,16,128]{4,3,2,0,1:T(8,128)S(1)}, f32[8,4,1,16,128]{4,3,2,0,1:T(8,128)}, u32[]{:S(2)}) copy-start(f32[8,4,1,16,128]{4,3,2,0,1:T(8,128)} %get-tuple-element.70) | copy-start | bytes 786436
  105.9 1.9 %copy-start.14 = (f32[8,4,1,16,128]{4,3,2,0,1:T(8,128)S(1)}, f32[8,4,1,16,128]{4,3,2,0,1:T(8,128)}, u32[]{:S(2)}) copy-start(f32[8,4,1,16,128]{4,3,2,0,1:T(8,128)} %get-tuple-element.71) | copy-start | bytes 786436
  105.9 1.9 %copy-start.15 = (f32[8,1,2,16,128]{4,3,2,0,1:T(8,128)S(1)}, f32[8,1,2,16,128]{4,3,2,0,1:T(8,128)}, u32[]{:S(2)}) copy-start(f32[8,1,2,16,128]{4,3,2,0,1:T(8,128)} %get-tuple-element.33) | copy-start | bytes 393220
  106.0 1.9 %copy-start.16 = (f32[8,1,2,16,128]{4,3,2,0,1:T(8,128)S(1)}, f32[8,1,2,16,128]{4,3,2,0,1:T(8,128)}, u32[]{:S(2)}) copy-start(f32[8,1,2,16,128]{4,3,2,0,1:T(8,128)} %get-tuple-element.61) | copy-start | bytes 393220
  106.0 2.0 %copy-start.17 = (f32[8,1,2,16,128]{4,3,2,0,1:T(8,128)S(1)}, f32[8,1,2,16,128]{4,3,2,0,1:T(8,128)}, u32[]{:S(2)}) copy-start(f32[8,1,2,16,128]{4,3,2,0,1:T(8,128)} %fusion.136) | copy-start | bytes 393220
  (4 other events, 3.4 us)

commit v18 on v14

--- a/solution.py
+++ b/solution.py
@@ -119,7 +119,7 @@
                 src_ref=chunks_ref.at[b, half], dst_ref=held.at[half, 0, b],
                 send_sem=send_e.at[half, b], recv_sem=recv_e.at[half, b],
                 device_id=devg(b), device_id_type=MESH).wait_recv()
-        for h in range(1, halo_cols + 1):
+        for h in range(halo_cols, 0, -1):
             cp = pltpu.make_async_remote_copy(
                 src_ref=held.at[half, 0], dst_ref=held.at[half, h],
                 send_sem=send_h.at[half, h], recv_sem=recv_h.at[half, h],

time: 166 us -> 167 us (level)
  Pallas kernels: 95.7 us -> 98.1 us
    pallas_call x1, Pallas kernels: 46.9 us -> 49 us  [gather_columns(): pl.pallas_call(functools.partial(head_kernel, n_halves, halo_cols), out_s...]
where the time goes in v18:
time: 167 us; the launch traced here: 166 us
  Pallas kernels  98.1 us (59%)
  other arithmetic  27.4 us (16%)
  matrix products  21.2 us (13%)
  local copies, waits for them, and re-layouts  11 us (7%)
  starting transfers between devices  4.22 us (3%)
  between operations  3.87 us (2%)
    pallas_call x1, Pallas kernels, finish(): pl.pallas_call(functools.partial(tail_kernel, n_col, n_f), out_shape=(jax...  49.1 us
    pallas_call x1, Pallas kernels, gather_columns(): pl.pallas_call(functools.partial(head_kernel, n_halves, halo_cols), out_s...  49 us
    dot_general x9, matrix products, pair_terms(): jnp.einsum('fbxrc,fbrd->fbxcd', stacked_left, right_rows, preferred_eleme...  10.2 us
    dot_general x9, matrix products, pair_terms(): jnp.einsum('fbxcd,fbvd->fbxvc', rounded, far_spec, preferred_element_type...  7.27 us
    sub x9, other arithmetic, pair_terms(): first_real = toward[:, :, 0, :W] - toward[:, :, 1, W:]  6.9 us
    ppermute x2, starting transfers between devices, permute(): return lax.ppermute(x, 'chan', pairs)  4.22 us
    dot_general x9, matrix products, pair_terms(): jnp.einsum('fbxcd,fbvc->fbxvd', rounded, near_spec, preferred_element_typ...  3.74 us
  transfers between devices with their start and end apart: 2, of which 0 were waited for; matrix products, arithmetic and copies ran while one was open for 16% of the time, Pallas kernels for 0%

profile of v18, /device:TPU:1, one launch (start us, length us, event | category | flops | bytes accessed | tf_op | source)
XLA Modules:
  0.0 165.8 jit_solution(8887831182039846543)
XLA Ops:
  5.9 1.8 %pad_maximum_fusion.4 = bf16[32,2,24,128]{3,2,1,0:T(8,128)(2,1)} fusion(bf16[32,2,8,128]{3,2,1,0:T(8,128)(2,1)} %param.5, bf16[32,2,16,128]{3,2,1,0:T(8,128)(2,1)} %param.4), kind=kLoop, calls=%fused_computation.158 | loop fusion | flops 786432 | bytes 786432 | tf_op jit(solution)/shard_map/concatenate | solution.py:268
  7.7 49.0 %shard_map.59 = bf16[4,3,4,2,2,24,128]{6,5,4,3,2,1,0:T(8,128)(2,1)} custom-call(bf16[4,4,2,2,24,128]{5,4,3,2,1,0:T(8,128)(2,1)} %bitcast.207), custom_call_target="tpu_custom_call" | custom-call | tf_op jit(solution)/shard_map/pallas_call | solution.py:146
  56.7 1.6 copy.62
  58.5 1.3 fusion.193
  60.1 1.4 convert_element_type.39
  61.4 1.3 slice.735
  65.0 1.3 multiply_select_fusion
  66.3 1.1 multiply_reduce_fusion.7
  68.4 1.1 multiply_reduce_fusion.6
  71.1 1.1 multiply_reduce_fusion.8
  73.3 1.1 multiply_reduce_fusion.5
  75.0 0.9 fusion.93
  75.8 2.1 %collective-permute-start = (f32[8,4,2,16,128]{4,3,2,0,1:T(8,128)}, f32[8,4,2,16,128]{4,3,2,0,1:T(8,128)}, u32[]{:S(2)}, u32[]{:S(2)}) collective-permute-start(f32[8,4,2,16,128]{4,3,2,0,1:T(8,128)} %fusion.93), channel_id=1, source_target_pairs={{0,64},{8,72},{16,80},{24,88},{32,96},{40,104},{48,112},{56,120},{... | collective-permute-start | bytes 1572872 | tf_op jit(solution)/shard_map/ppermute | solution.py:17
  78.7 1.1 multiply_reduce_fusion.2
  80.3 1.1 multiply_reduce_fusion.1
  82.0 1.1 multiply_reduce_fusion.4
  83.6 1.1 multiply_reduce_fusion.3
  85.4 0.8 pad_maximum_fusion.3
  86.2 2.1 %collective-permute-start.1 = (f32[8,4,2,16,128]{4,3,2,0,1:T(8,128)}, f32[8,4,2,16,128]{4,3,2,0,1:T(8,128)}, u32[]{:S(2)}, u32[]{:S(2)}) collective-permute-start(f32[8,4,2,16,128]{4,3,2,0,1:T(8,128)} %pad_maximum_fusion.3), channel_id=1, source_target_pairs={{0,32},{8,40},{16,48},{24,56},{32,64},{40,72},{48,80},{56,88},{64,... | collective-permute-start | bytes 1572872 | tf_op jit(solution)/shard_map/ppermute | solution.py:17
  88.8 1.1 multiply_reduce_fusion
  95.9 0.9 slice_subtract_fusion.17
  97.6 0.9 slice_subtract_fusion.14
  99.3 0.9 slice_subtract_fusion.7
  100.2 0.8 fusion.78
  101.0 0.9 slice_subtract_fusion.6
  102.7 0.9 slice_subtract_fusion.9
  104.4 0.9 slice_subtract_fusion.8
  106.7 0.8 fusion.84
  108.7 2.5 %fusion.104.blocks_ref = f32[4,8,2,16,128]{4,3,2,1,0:T(8,128)} fusion(f32[8,4,2,16,128]{4,3,2,0,1:T(8,128)} %collective-permute-done.1, f32[8,4,2,16,128]{4,3,2,0,1:T(8,128)} %collective-permute-done, f32[8,4,1,16,128]{4,3,2,0,1:T(8,128)S(1)} %copy-done.3, f32[8,4,1,16,128]{4,3,2,0,1:T(8,128)S(1)} %copy-done.2, f32[8,4,1,16,128]{4,3,2,0,1:T(8,128)S(1)} %copy-done, ...), kind=kLoop, calls=%fused_computation.147 | loop fusion | flops 3014656 | bytes 6815744 | tf_op jit(solution)/shard_map/transpose | solution.py:312
  111.8 49.1 %shard_map.60 = (f32[4,8,2,16,128]{4,3,2,1,0:T(8,128)}, f32[8,128]{1,0:T(8,128)}) custom-call(f32[4,8,2,16,128]{4,3,2,1,0:T(8,128)} %fusion.104.blocks_ref, f32[8,128]{1,0:T(8,128)} %broadcast_in_dim.2.val_ref), custom_call_target="tpu_custom_call" | custom-call | tf_op jit(solution)/shard_map/pallas_call | solution.py:244
  160.9 1.2 slice.729
  162.1 1.9 %broadcast_multiply_fusion = f32[4,8,2,16,128]{4,3,2,1,0:T(8,128)} fusion(f32[4,8,2,16,128]{4,3,2,1,0:T(8,128)} %get-tuple-element.12), kind=kLoop, calls=%fused_computation.207 | loop fusion | flops 131072 | bytes 1048576 | tf_op jit(solution)/shard_map/mul | solution.py:314
  (151 shorter events, 26.6 us)
Async XLA Ops:
  58.5 1.3 copy-start.31
  64.1 2.2 %copy-start.20 = (bf16[8,4,2,24,128]{4,3,2,1,0:T(8,128)(2,1)S(1)}, bf16[8,4,2,24,128]{4,3,2,1,0:T(8,128)(2,1)}, u32[]{:S(2)}) copy-start(bf16[8,4,2,24,128]{4,3,2,1,0:T(8,128)(2,1)} %get-tuple-element.58) | copy-start | bytes 1179652
  67.4 1.0 copy-start.19
  69.6 0.9 copy-start.22
  69.6 0.9 copy-start.23
  69.6 0.9 copy-start.24
  69.6 0.9 copy-start.25
  69.6 0.9 copy-start.26
  69.6 0.9 copy-start.27
  69.6 0.9 copy-start.28
  70.1 1.0 copy-start.18
  72.3 1.0 copy-start.17
  74.9 3.1 %copy-start.32 = (bf16[24]{0:T(256)(128)(2,1)S(1)}, bf16[24]{0:T(256)(128)(2,1)}, u32[]{:S(2)}) copy-start(bf16[24]{0:T(256)(128)(2,1)} %constant.46.clone.1) | copy-start | bytes 148
  75.8 31.8 %collective-permute-start = (f32[8,4,2,16,128]{4,3,2,0,1:T(8,128)}, f32[8,4,2,16,128]{4,3,2,0,1:T(8,128)}, u32[]{:S(2)}, u32[]{:S(2)}) collective-permute-start(f32[8,4,2,16,128]{4,3,2,0,1:T(8,128)} %fusion.93), channel_id=1, source_target_pairs={{0,64},{8,72},{16,80},{24,88},{32,96},{40,104},{48,112},{56,120},{... | collective-permute-start | bytes 1572872 | tf_op jit(solution)/shard_map/ppermute | solution.py:17
  86.2 21.4 %collective-permute-start.1 = (f32[8,4,2,16,128]{4,3,2,0,1:T(8,128)}, f32[8,4,2,16,128]{4,3,2,0,1:T(8,128)}, u32[]{:S(2)}, u32[]{:S(2)}) collective-permute-start(f32[8,4,2,16,128]{4,3,2,0,1:T(8,128)} %pad_maximum_fusion.3), channel_id=1, source_target_pairs={{0,32},{8,40},{16,48},{24,56},{32,64},{40,72},{48,80},{56,88},{64,... | collective-permute-start | bytes 1572872 | tf_op jit(solution)/shard_map/ppermute | solution.py:17
  106.6 1.1 copy-start
  106.6 1.1 copy-start.1
  106.6 1.1 copy-start.2
  106.6 1.2 copy-start.3
  106.6 1.2 copy-start.4
  106.6 1.3 copy-start.5
  106.6 1.4 copy-start.6
  106.6 1.4 copy-start.7
  106.7 1.5 copy-start.8
  106.7 1.6 copy-start.9
  106.7 1.7 %copy-start.10 = (f32[8,4,1,16,128]{4,3,2,0,1:T(8,128)S(1)}, f32[8,4,1,16,128]{4,3,2,0,1:T(8,128)}, u32[]{:S(2)}) copy-start(f32[8,4,1,16,128]{4,3,2,0,1:T(8,128)} %get-tuple-element.72) | copy-start | bytes 786436
  106.7 1.7 %copy-start.11 = (f32[8,4,1,16,128]{4,3,2,0,1:T(8,128)S(1)}, f32[8,4,1,16,128]{4,3,2,0,1:T(8,128)}, u32[]{:S(2)}) copy-start(f32[8,4,1,16,128]{4,3,2,0,1:T(8,128)} %get-tuple-element.73) | copy-start | bytes 786436
  106.7 1.8 %copy-start.12 = (f32[8,4,1,16,128]{4,3,2,0,1:T(8,128)S(1)}, f32[8,4,1,16,128]{4,3,2,0,1:T(8,128)}, u32[]{:S(2)}) copy-start(f32[8,4,1,16,128]{4,3,2,0,1:T(8,128)} %get-tuple-element.70) | copy-start | bytes 786436
  106.7 1.9 %copy-start.13 = (f32[8,4,1,16,128]{4,3,2,0,1:T(8,128)S(1)}, f32[8,4,1,16,128]{4,3,2,0,1:T(8,128)}, u32[]{:S(2)}) copy-start(f32[8,4,1,16,128]{4,3,2,0,1:T(8,128)} %get-tuple-element.71) | copy-start | bytes 786436
  106.7 1.9 %copy-start.14 = (f32[8,1,2,16,128]{4,3,2,0,1:T(8,128)S(1)}, f32[8,1,2,16,128]{4,3,2,0,1:T(8,128)}, u32[]{:S(2)}) copy-start(f32[8,1,2,16,128]{4,3,2,0,1:T(8,128)} %get-tuple-element.33) | copy-start | bytes 393220
  106.7 1.9 %copy-start.15 = (f32[8,1,2,16,128]{4,3,2,0,1:T(8,128)S(1)}, f32[8,1,2,16,128]{4,3,2,0,1:T(8,128)}, u32[]{:S(2)}) copy-start(f32[8,1,2,16,128]{4,3,2,0,1:T(8,128)} %get-tuple-element.61) | copy-start | bytes 393220
  106.7 2.0 %copy-start.16 = (f32[8,1,2,16,128]{4,3,2,0,1:T(8,128)S(1)}, f32[8,1,2,16,128]{4,3,2,0,1:T(8,128)}, u32[]{:S(2)}) copy-start(f32[8,1,2,16,128]{4,3,2,0,1:T(8,128)} %fusion.136) | copy-start | bytes 393220
  (3 other events, 2.5 us)
